TPU v7x, 256 devices: a whole 4x4x8 slice. The times are simulated.
256 devices in a mesh: seq: 4 (over x), ctx: 64 (over z, y, core).
Axes of the slice: x: 4, y: 4, z: 8, core: 2. Of those that a mesh axis runs over, the one named last changes fastest.
Arguments:
- inputs: bfloat16 [4, 8192, 1024], P('seq', 'ctx'), may hold values from -16 to 16
- w_query: bfloat16 [1024, 1024], replicated, may hold values from -0.1875 to 0.1875
- w_key: bfloat16 [1024, 1024], replicated, as said below
- w_value: bfloat16 [1024, 1024], replicated, may hold values from -0.1875 to 0.1875
- damping: float32 [8, 128], replicated, may hold values from 0.25 to 4
- grad_out: bfloat16 [4, 8192, 1024], P('seq', 'ctx'), may hold values from -6 to 6
Outputs:
- grad_inputs: bfloat16 [4, 8192, 1024], P('seq', 'ctx')
- grad_weights: float32 [1024, 1024], P(('seq', 'ctx'))
Inputs may be any that keep to these rules, and one draw needn't show every extreme that they name: `w_key`: entries scaled by a random factor per column.
All inputs are finite; a program needn't handle non-finite values.
Results may differ from a plain program's by a relative error of at most 0.013.
Values sent between devices are 32-bit elements; how exact they have to be, the bound alone decides.
No kernel may reach another device: no remote copies, remote signals or barrier semaphores. Data moves between devices by JAX's collectives and lax.ppermute only.
A program may use at most 256 MiB of HBM per device.

v0:
```python
import functools

import jax
import jax.numpy as jnp
from jax import lax
from jax.experimental import pallas as pl
from jax.experimental.pallas import tpu as pltpu
from jax.sharding import Mesh, PartitionSpec as P


ITERS = 2
EPSILON = 1e-06
F32 = jnp.float32
BF16 = jnp.bfloat16
HEADS = 8
DK = 128
CHUNKS = 8
PLANE = ("y", "core")


def halves(x):
    hi = x.astype(BF16)
    return hi, (x - hi.astype(F32)).astype(BF16)


def nn(a, b):
    return lax.dot_general(a, b, (((1,), (0,)), ((), ())), preferred_element_type=F32)


def nt(a, b):
    return lax.dot_general(a, b, (((1,), (1,)), ((), ())), preferred_element_type=F32)


def tn(a, b):
    return lax.dot_general(a, b, (((0,), (0,)), ((), ())), preferred_element_type=F32)


def wide(x):
    return jnp.concatenate(halves(x), axis=1)


def tall(x):
    return jnp.concatenate(halves(x), axis=0)


def twice_wide(b):
    return jnp.concatenate([b, b], axis=1)


def twice_tall(b):
    return jnp.concatenate([b, b], axis=0)


def fold_cols(m):
    half = m.shape[1] // 2
    return m[:, :half] + m[:, half:]


def fold_rows(m):
    half = m.shape[0] // 2
    return m[:half] + m[half:]


def rowsum(x):
    return jnp.sum(x, axis=-1, keepdims=True)


def causal(size):
    rows = lax.broadcasted_iota(jnp.int32, (size, size), 0)
    cols = lax.broadcasted_iota(jnp.int32, (size, size), 1)
    return rows >= cols


def inv_norm(block):
    wide_block = block.astype(F32)
    return lax.rsqrt(rowsum(wide_block * wide_block) + EPSILON)


def across(column):
    size = column.shape[0]
    return jnp.transpose(jnp.broadcast_to(column, (size, size)))


def apply_all(vectors, keys, grams, scale2, damp):
    splits = [halves(p) for p in vectors]
    cats = [jnp.concatenate(s, axis=1) for s in splits]
    raw = [nt(c, twice_wide(k)) for c, k in zip(cats, keys)]
    prior = []
    for c, s, g in zip(cats, splits, grams):
        g_hi, g_lo = halves(g)
        prior.append(nn(c, twice_tall(g_hi)) + nn(s[0], g_lo))
    inner = [wide(r * m) for r, m in zip(raw, scale2)]
    return [
        o + nn(i, twice_tall(k)) + damp * p
        for o, i, k, p in zip(prior, inner, keys, vectors)
    ]


def conjugate(targets, keys, grams, scale2, damp):
    residual = list(targets)
    direction = list(targets)
    norm_now = [rowsum(r * r) for r in residual]
    solution = None
    for sweep in range(ITERS):
        image = apply_all(direction, keys, grams, scale2, damp)
        step = [n / (rowsum(p * w) + EPSILON) for n, p, w in zip(norm_now, direction, image)]
        moved = [a * p for a, p in zip(step, direction)]
        solution = moved if solution is None else [x + m for x, m in zip(solution, moved)]
        if sweep + 1 < ITERS:
            residual = [r - a * w for r, a, w in zip(residual, step, image)]
            norm_next = [rowsum(r * r) for r in residual]
            direction = [
                r + n / (o + EPSILON) * p
                for r, n, o, p in zip(residual, norm_next, norm_now, direction)
            ]
            norm_now = norm_next
    return solution


def staged(body, counts, tables, *refs):
    n_in, n_out = counts
    sources, refs = refs[:n_in], refs[n_in:]
    targets, refs = refs[:n_out], refs[n_out:]
    held, refs = refs[:n_in], refs[n_in:]
    made, (in_sems, out_sems, *rest) = refs[:n_out], refs[n_out:]
    loads = [
        pltpu.make_async_copy(s, h, in_sems.at[n]) for n, (s, h) in enumerate(zip(sources, held))
    ]
    stores = [
        pltpu.make_async_copy(m, t, out_sems.at[n]) for n, (m, t) in enumerate(zip(made, targets))
    ]
    for load in loads:
        load.start()
    arrived, sent = set(), set()

    def need(n):
        if n not in arrived:
            arrived.add(n)
            loads[n].wait()
        return held[n]

    def put(n):
        sent.add(n)
        stores[n].start()

    body(tables, need, made, put, *rest)
    for n in range(n_in):
        need(n)
    for n in range(n_out):
        if n not in sent:
            put(n)
    for store in stores:
        store.wait()


def shaped(*dims, dtype=F32):
    return jax.ShapeDtypeStruct(dims, dtype)


def call(body, outs, args, flops, tables=(), raw=(), scratch=()):
    def kernel(*refs):
        t, r = len(tables), len(raw)
        operands = refs[t + r :]
        staged(
            functools.partial(body, *refs[t : t + r]), (len(args), len(outs)), refs[:t], *operands
        )

    moved = sum(a.size * a.dtype.itemsize for a in args) + sum(
        o.size * jnp.dtype(o.dtype).itemsize for o in outs
    )
    anywhere = pl.BlockSpec(memory_space=pl.ANY)
    return pl.pallas_call(
        kernel,
        out_shape=tuple(outs),
        in_specs=[pl.BlockSpec(memory_space=pltpu.SMEM)] * len(tables)
        + [anywhere] * (len(raw) + len(args)),
        out_specs=tuple([anywhere] * len(outs)),
        scratch_shapes=[pltpu.VMEM(a.shape, a.dtype) for a in args]
        + [pltpu.VMEM(o.shape, o.dtype) for o in outs]
        + [pltpu.SemaphoreType.DMA((len(args),)), pltpu.SemaphoreType.DMA((len(outs),))]
        + list(scratch),
        compiler_params=pltpu.CompilerParams(vmem_limit_bytes=60 << 20),
        cost_estimate=pl.CostEstimate(flops=flops, bytes_accessed=moved, transcendentals=0),
    )(*tables, *raw, *args)


def prepare_body(tables, need, made, put):
    x, (low, high, upstream) = need(0), made
    rows = low.shape[0]
    low[...] = x[:rows].astype(F32)
    put(0)
    high[...] = x[rows:].astype(F32)
    put(1)
    g = need(1)
    for h in range(HEADS):
        upstream[h] = g[:, h * DK : (h + 1) * DK].astype(F32)


def project_body(slots, wq_hbm, wk_hbm, wv_hbm, tables, need, made, put, w_buf, w_sem):
    (where,) = tables
    xb, q_out, k_out, v_out, gram_out, cross_out, tot = made
    cols = pl.ds(pl.multiple_of(where[len(where) - 1] * DK, DK), DK)
    weights = [
        pltpu.make_async_copy(w.at[:, cols], w_buf.at[n], w_sem.at[n])
        for n, w in enumerate((wq_hbm, wk_hbm, wv_hbm))
    ]
    for copy in weights:
        copy.start()
    for n, (slot, start) in enumerate(slots):
        piece = need(n)
        row = pl.multiple_of(where[slot] * DK + start, DK // 2)
        xb[pl.ds(row, piece.shape[0]), :] = piece[...].astype(BF16)
    put(0)
    for copy in weights:
        copy.wait()
    wq, wk, wv = w_buf[0], w_buf[1], w_buf[2]
    gram = jnp.zeros((DK, DK), F32)
    cross = jnp.zeros((DK, DK), F32)
    for j in range(CHUNKS):
        x = xb[j * DK : (j + 1) * DK, :]
        k = nn(x, wk).astype(BF16)
        v = nn(x, wv).astype(BF16)
        k_out[j] = k
        v_out[j] = v
        rk = inv_norm(k)
        kn = k.astype(F32) * rk
        gram_out[j] = gram
        cross_out[j] = cross
        gram = gram + fold_cols(tn(k, wide(kn * rk)))
        cross = cross + fold_cols(tn(v, wide(kn)))
    tot[0] = gram
    tot[1] = cross
    put(6)
    for n in (2, 3, 4, 5):
        put(n)
    for j in range(CHUNKS):
        q_out[j] = nn(xb[j * DK : (j + 1) * DK, :], wq).astype(BF16)


def total_of(need, first):
    near = [need(first + n) for n in range(4)]
    return [(near[0][i] + near[1][i]) + (near[2][i] + near[3][i]) for i in range(2)]


def solve_body(tables, need, made, put):
    (where,) = tables
    q_in, k_in, v_in, gram_in, cross_in, damp_in, g_in = [need(n) for n in range(7)]
    gram_prior, cross_prior = total_of(need, 7)
    z_out, u_out, dq_out, suf, tot = made
    damp = damp_in[pl.ds(where[len(where) - 1], 1), :]
    keep = causal(DK)
    keys = [k_in[j] for j in range(CHUNKS)]
    grams = [gram_in[j] + gram_prior for j in range(CHUNKS)]
    scale2, targets = [], []
    for j, k in enumerate(keys):
        row = jnp.where(keep, across(inv_norm(k)), 0.0)
        scale2.append(twice_tall(row * row))
        g = g_in[j].astype(BF16)
        scores = nt(g, v_in[j]) * row
        state = cross_in[j] + cross_prior
        right = nn(twice_wide(g), tall(state)) + nn(wide(scores), twice_tall(k))
        qn = q_in[j].astype(F32) * inv_norm(q_in[j])
        targets.append(jnp.concatenate([qn, right], axis=0))
    both = conjugate(targets, keys, grams, scale2, damp)
    gram = jnp.zeros((DK, DK), F32)
    cross = jnp.zeros((DK, DK), F32)
    for j in reversed(range(CHUNKS)):
        z, u = both[j][:DK], both[j][DK:]
        z_out[j] = z
        u_out[j] = u
        suf[0, j] = gram
        suf[1, j] = cross
        left = jnp.concatenate([wide(u), wide(z)], axis=0)
        right = jnp.concatenate([wide(z), wide(u)], axis=0)
        gram = gram + fold_rows(fold_cols(tn(left, right)))
        cross = cross + fold_cols(tn(g_in[j].astype(BF16), wide(z)))
    tot[0] = gram
    tot[1] = cross
    put(4)
    for n in (0, 1, 3):
        put(n)
    for j in range(CHUNKS):
        q = q_in[j]
        rq = inv_norm(q)
        qn = q.astype(F32) * rq
        u = u_out[j]
        dq_out[j] = ((u - qn * rowsum(qn * u)) * rq).astype(BF16).astype(F32)


def grads_body(seq, tables, need, made, put, dk_buf, dw_buf, out):
    (place,) = tables
    k_in, v_in, z_in, u_in, suf, g_in = [need(n) for n in range(6)]
    gram_after, cross_after = total_of(need, 6)
    keep = causal(DK)
    for j in range(CHUNKS):
        k, v = k_in[j], v_in[j]
        rk = inv_norm(k)
        kn = k.astype(F32) * rk
        row = jnp.where(keep, across(rk), 0.0)
        g = g_in[j].astype(BF16)
        scores = jnp.where(keep, nt(g, v), 0.0)
        u, z = u_in[j], z_in[j]
        both = jnp.concatenate([u, z], axis=0)
        pair = nt(wide(both), twice_wide(k)) * twice_tall(row)
        left = jnp.concatenate([scores - pair[:DK], -pair[DK:]], axis=0)
        right = jnp.concatenate([z, u], axis=0)
        kk = twice_wide(k)
        cross = suf[1, j] + cross_after
        dkn = fold_rows(fold_cols(tn(wide(left), wide(right))))
        dkn = dkn + nn(twice_wide(v), tall(cross))
        dkn = dkn - rk * nn(kk, tall(suf[0, j] + gram_after))
        dk = ((dkn - kn * rowsum(kn * dkn)) * rk).astype(BF16)
        dk_buf[j * DK : (j + 1) * DK, :] = dk
        out[j, :DK] = dk.astype(F32)
        dv = rk * nt(kk, wide(cross)) + tn(tall(pair[DK:]), twice_tall(g))
        out[j, DK:] = dv.astype(BF16).astype(F32)
    for step in range(CHUNKS):
        made[seq + step][...] = out[lax.rem(place[1] + step, CHUNKS)]
        put(seq + step)
    dw_buf[...] = jnp.transpose(tn(dk_buf[...], need(10)[...]))
    rows = made[0].shape[0]
    for step in range(seq):
        start = pl.multiple_of(lax.rem(place[0] + step, seq) * rows, rows)
        made[step][...] = dw_buf[pl.ds(start, rows), :]
        put(step)


def input_grad_body(tables, need, made, put, dk_cat, dv_cat):
    (place,) = tables
    dq_cat = jnp.concatenate([need(0)[h].astype(BF16) for h in range(HEADS)], axis=1)
    total = nt(dq_cat, need(1)[...])
    for step in range(HEADS):
        piece = need(4 + step)
        head = lax.rem(place[1] + HEADS - step, HEADS)
        cols = pl.ds(pl.multiple_of(head * DK, DK), DK)
        dk_cat[:, cols] = piece[:DK].astype(BF16)
        dv_cat[:, cols] = piece[DK:].astype(BF16)
    total = total + nt(dk_cat[...], need(2)[...])
    total = total + nt(dv_cat[...], need(3)[...])
    made[0][...] = total.astype(BF16)


def shift(x, axis, by, wrap):
    size = lax.axis_size(axis)
    pairs = [(i, (i + by) % size) for i in range(size) if wrap or 0 <= i + by < size]
    return lax.ppermute(x, axis, pairs)


def exclusive(total, sign):
    one, two = shift(total, "z", sign, False), shift(total, "z", 2 * sign, False)
    third = total + one + two
    return one, two, shift(third, "z", 3 * sign, False), shift(third, "z", 6 * sign, False)


def exchange(x, axis):
    return lax.all_to_all(x, axis, 0, 0)


def gather_plane(low, high):
    y, core = lax.axis_index("y"), lax.axis_index("core")
    rows = low.shape[0]
    prev_low = shift(low, "y", 1, True)
    next_high = shift(high, "y", -1, True)
    prev_high = shift(high, "y", 1, True)
    next_low = shift(low, "y", -1, True)
    far_low = shift(prev_low, "y", 1, True)
    far_high = shift(next_high, "y", -1, True)
    pieces = [(low, 0, 0), (high, 0, rows)]
    pieces += [(shift(low, "core", 1, True), 4, 0), (shift(high, "core", 1, True), 4, rows)]
    for piece, slot, start in (
        (prev_low, 1, 0), (next_high, 2, rows), (prev_high, 1, rows), (next_low, 2, 0),
        (far_low, 3, 0), (far_high, 3, rows),
    ):
        pieces.append((piece, slot, start))
        pieces.append((shift(piece, "core", 1, True), slot + 4, start))
    ysize = lax.axis_size("y")
    places = [
        ((y + step) % ysize) * 2 + c for c in (core, 1 - core) for step in (0, -1, 1, 2)
    ] + [y * 2 + core]
    return pieces, jnp.stack(places).astype(jnp.int32)


def on_device(inputs, w_query, w_key, w_value, damping, grad_out):
    mine = inputs[0]
    tokens, width = mine.shape
    blocks = shaped(CHUNKS, tokens, DK)
    brick = shaped(CHUNKS, tokens, DK, dtype=BF16)
    pair = shaped(2, DK, DK)
    states = shaped(CHUNKS, DK, DK)
    unit = 2 * CHUNKS * tokens * DK * DK

    half = shaped(tokens // 2, width)
    low, high, upstream = call(
        prepare_body, [half, half, shaped(HEADS, tokens, DK)], [mine, grad_out[0]], 0
    )
    pieces, where = gather_plane(low, high)
    slots = tuple((slot, start) for _, slot, start in pieces)
    xb, q, k, v, gram_pre, cross_pre, first_tot = call(
        functools.partial(project_body, slots),
        [shaped(CHUNKS * tokens, width, dtype=BF16), brick, brick, brick, states, states, pair],
        [p for p, _, _ in pieces],
        unit * 28,
        tables=[where], raw=[w_query, w_key, w_value],
        scratch=[pltpu.VMEM((3, width, DK), BF16), pltpu.SemaphoreType.DMA((3,))],
    )
    prior = exclusive(first_tot, 1)
    upstream, _ = lax.optimization_barrier((upstream, first_tot))
    g = exchange(upstream, PLANE)

    z, u, dq, suf, second_tot = call(
        solve_body, [blocks, blocks, blocks, shaped(2, CHUNKS, DK, DK), pair],
        [q, k, v, gram_pre, cross_pre, damping, g, *prior], unit * 40, tables=[where],
    )
    after = exclusive(second_tot, -1)
    dq_all = exchange(dq, PLANE)

    seq = lax.axis_size("seq")
    ctx = ("z", "y", "core")
    spread = lax.axis_size(ctx)
    rows = width // (seq * spread)
    place = jnp.stack(
        [lax.axis_index("seq"), lax.axis_index("y") * 2 + lax.axis_index("core")]
    ).astype(jnp.int32)
    pieces = call(
        functools.partial(grads_body, seq),
        [shaped(width // seq, DK)] * seq + [shaped(2 * tokens, DK)] * CHUNKS,
        [k, v, z, u, suf, g, *after, xb], unit * 30, tables=[place],
        scratch=[
            pltpu.VMEM((CHUNKS * tokens, DK), BF16), pltpu.VMEM((width, DK), F32),
            pltpu.VMEM((CHUNKS, 2 * tokens, DK), F32),
        ],
    )
    dw, dkv = pieces[:seq], pieces[seq:]
    dw = sum((shift(part, "seq", step, True) for step, part in enumerate(dw) if step), dw[0])
    dkv = [shift(p, PLANE, step, True) if step else p for step, p in enumerate(dkv)]
    dw = exchange(dw.reshape(spread, rows, DK), ctx)
    dw = dw.reshape(spread // HEADS, HEADS, rows, DK)
    grad_weights = jnp.sum(dw, axis=0).transpose(1, 0, 2).reshape(rows, HEADS * DK)

    (grad_inputs,) = call(
        input_grad_body, [shaped(tokens, width, dtype=BF16)],
        [dq_all, w_query, w_key, w_value, *dkv], unit * 24, tables=[place],
        scratch=[pltpu.VMEM((tokens, width), BF16)] * 2,
    )
    return (grad_inputs[None], grad_weights)


def solution(mesh):
    grid = Mesh(mesh.devices.reshape(4, 8, 4, 2), ("seq", "z", "y", "core"))
    ctx = ("z", "y", "core")
    in_specs = (P("seq", ctx, None), P(), P(), P(), P(), P("seq", ctx, None))
    out_specs = (P("seq", ctx, None), P(("seq",) + ctx, None))

    return jax.shard_map(on_device, mesh=grid, in_specs=in_specs, out_specs=out_specs, check_vma=False)
```

profile of v0, /device:TPU:2, one launch (start us, length us, event | category | flops | bytes accessed | tf_op | source)
XLA Modules:
  0.0 156.5 jit_solution(8020835034444167741)
XLA Ops:
  0.6 2.0 %shard_map.77 = (f32[64,1024]{1,0:T(8,128)}, f32[64,1024]{1,0:T(8,128)}, f32[8,128,128]{2,1,0:T(8,128)}) custom-call(bf16[128,1024]{1,0:T(8,128)(2,1)} %bitcast.20, bf16[128,1024]{1,0:T(8,128)(2,1)} %bitcast.21), custom_call_target="tpu_custom_call" | custom-call | bytes 1572864 | tf_op jit(solution)/shard_map/pallas_call | solution.py:172
  2.6 3.1 %collective-permute-start.8 = (f32[64,1024]{1,0:T(8,128)}, f32[64,1024]{1,0:T(8,128)S(1)}, u32[]{:S(2)}, u32[]{:S(2)}) collective-permute-start(f32[64,1024]{1,0:T(8,128)} %get-tuple-element.30.refs_4_), channel_id=1, source_target_pairs={{0,6},{2,0},{4,2},{6,4},{1,7},{3,1},{5,3},{7,5},{8,14},{10,8},{12,... | collective-permute-start | bytes 786440 | tf_op jit(solution)/shard_map/ppermute | solution.py:346
  5.7 3.2 %collective-permute-start.4 = (f32[64,1024]{1,0:T(8,128)}, f32[64,1024]{1,0:T(8,128)S(1)}, u32[]{:S(2)}, u32[]{:S(2)}) collective-permute-start(f32[64,1024]{1,0:T(8,128)} %get-tuple-element.31.refs_5_), channel_id=1, source_target_pairs={{0,6},{2,0},{4,2},{6,4},{1,7},{3,1},{5,3},{7,5},{8,14},{10,8},{12,... | collective-permute-start | bytes 786440 | tf_op jit(solution)/shard_map/ppermute | solution.py:346
  9.0 3.8 %collective-permute-done.8.refs_14_ = f32[64,1024]{1,0:T(8,128)S(1)} collective-permute-done((f32[64,1024]{1,0:T(8,128)}, f32[64,1024]{1,0:T(8,128)S(1)}, u32[]{:S(2)}, u32[]{:S(2)}) %collective-permute-start.8) | collective-permute-done | bytes 262176 | tf_op jit(solution)/shard_map/ppermute | solution.py:346
  12.7 3.6 %collective-permute-done.2.refs_8_ = f32[64,1024]{1,0:T(8,128)S(1)} collective-permute-done((f32[64,1024]{1,0:T(8,128)}, f32[64,1024]{1,0:T(8,128)S(1)}, u32[]{:S(2)}, u32[]{:S(2)}) %collective-permute-start.2) | collective-permute-done | bytes 262176 | tf_op jit(solution)/shard_map/ppermute | solution.py:346
  17.2 3.6 %collective-permute-start.12 = (f32[64,1024]{1,0:T(8,128)S(1)}, f32[64,1024]{1,0:T(8,128)S(1)}, u32[]{:S(2)}, u32[]{:S(2)}) collective-permute-start(f32[64,1024]{1,0:T(8,128)S(1)} %collective-permute-done.4.refs_10_), channel_id=1, source_target_pairs={{0,6},{2,0},{4,2},{6,4},{1,7},{3,1},{5,3},{7,5},{8,14},{10,8},{12,... | collective-permute-start | bytes 786440 | tf_op jit(solution)/shard_map/ppermute | solution.py:346
  21.4 4.8 %collective-permute-done.10.refs_16_ = f32[64,1024]{1,0:T(8,128)S(1)} collective-permute-done((f32[64,1024]{1,0:T(8,128)S(1)}, f32[64,1024]{1,0:T(8,128)S(1)}, u32[]{:S(2)}, u32[]{:S(2)}) %collective-permute-start.10) | collective-permute-done | bytes 262176 | tf_op jit(solution)/shard_map/ppermute | solution.py:346
  28.5 7.7 %shard_map.78 = (bf16[1024,1024]{1,0:T(8,128)(2,1)}, bf16[8,128,128]{2,1,0:T(8,128)(2,1)}, bf16[8,128,128]{2,1,0:T(8,128)(2,1)}, bf16[8,128,128]{2,1,0:T(8,128)(...) custom-call(s32[9]{0:T(128)} %stack.48.refs_0_, bf16[1024,1024]{1,0:T(8,128)(2,1)} %refs_2_.3, ...), custom_call_target="tpu_custom_call" | custom-call | flops 939524096 | bytes 8257536 | tf_op jit(solution)/shard_map/pallas_call | solution.py:172
  36.2 5.2 %collective-permute-start.15 = (f32[2,128,128]{2,1,0:T(8,128)}, f32[2,128,128]{2,1,0:T(8,128)S(1)}, u32[]{:S(2)}, u32[]{:S(2)}) collective-permute-start(f32[2,128,128]{2,1,0:T(8,128)} %get-tuple-element.38), channel_id=1, source_target_pairs={{0,16},{8,24},{16,32},{24,40},{32,48},{40,56},{1,17},{9,25},{17,33... | collective-permute-start | bytes 393224 | tf_op jit(solution)/shard_map/ppermute | solution.py:346
  41.4 3.8 %collective-permute-start.14 = (f32[2,128,128]{2,1,0:T(8,128)}, f32[2,128,128]{2,1,0:T(8,128)S(1)}, u32[]{:S(2)}, u32[]{:S(2)}) collective-permute-start(f32[2,128,128]{2,1,0:T(8,128)} %get-tuple-element.38), channel_id=1, source_target_pairs={{0,8},{8,16},{16,24},{24,32},{32,40},{40,48},{48,56},{1,9},{9,17},... | collective-permute-start | bytes 393224 | tf_op jit(solution)/shard_map/ppermute | solution.py:346
  45.2 3.9 %all-to-all-start = ((f32[8,128,128]{2,1,0:T(8,128)}), f32[8,128,128]{2,1,0:T(8,128)S(1)}, u32[]{:S(2)}, u32[]{:S(2)}) async-start(f32[8,128,128]{2,1,0:T(8,128)} %get-tuple-element.39), calls=%async_computation | async-start | bytes 1048576 | tf_op jit(solution)/shard_map/all_to_all | solution.py:356
  50.2 9.0 %collective-permute-start.17 = (f32[2,128,128]{2,1,0:T(8,128)S(1)}, f32[2,128,128]{2,1,0:T(8,128)S(1)}, u32[]{:S(2)}, u32[]{:S(2)}) collective-permute-start(f32[2,128,128]{2,1,0:T(8,128)S(1)} %add_add_fusion.2), channel_id=1, source_target_pairs={{0,48},{8,56},{1,49},{9,57},{2,50},{10,58},{3,51},{11,59},{4,52},{... | collective-permute-start | bytes 393224 | tf_op jit(solution)/shard_map/ppermute | solution.py:346
  59.2 1.3 collective-permute-start.16
  60.5 2.2 %collective-permute-done.17.refs_11_ = f32[2,128,128]{2,1,0:T(8,128)S(1)} collective-permute-done((f32[2,128,128]{2,1,0:T(8,128)S(1)}, f32[2,128,128]{2,1,0:T(8,128)S(1)}, u32[]{:S(2)}, u32[]{:S(2)}) %collective-permute-start.17) | collective-permute-done | bytes 131104 | tf_op jit(solution)/shard_map/ppermute | solution.py:346
  63.9 8.8 %shard_map.79 = (f32[8,128,128]{2,1,0:T(8,128)}, f32[8,128,128]{2,1,0:T(8,128)}, f32[8,128,128]{2,1,0:T(8,128)}, f32[2,8,128,128]{3,2,1,0:T(8,128)}, f32[2,128,128]{2,1,0:T(8,128)}) custom-call(s32[9]{0:T(128)} %stack.48.refs_0_, bf16[8,128,128]{2,1,0:T(8,128)(2,1)} %get-tuple-element.32.refs_1_, bf16[8,128,128]{2,1,0:T(8,128)(2,1)} %get-tuple-element.33.refs_2_.refs_1_, ...), custom_call_target="tpu_custom_call" | custom-call | flops 1342177280 | bytes 5640192 | tf_op jit(solution)/shard_map/pallas_call | solution.py:172
  75.3 12.3 %collective-permute-done.19.refs_8_ = f32[2,128,128]{2,1,0:T(8,128)S(1)} collective-permute-done((f32[2,128,128]{2,1,0:T(8,128)}, f32[2,128,128]{2,1,0:T(8,128)S(1)}, u32[]{:S(2)}, u32[]{:S(2)}) %collective-permute-start.19) | collective-permute-done | bytes 131104 | tf_op jit(solution)/shard_map/ppermute | solution.py:346
  91.9 4.0 %all-to-all-start.1 = ((f32[8,128,128]{2,1,0:T(8,128)}), f32[8,128,128]{2,1,0:T(8,128)S(1)}, u32[]{:S(2)}, u32[]{:S(2)}) async-start(f32[8,128,128]{2,1,0:T(8,128)} %get-tuple-element.40), calls=%async_computation.1 | async-start | bytes 1048576 | tf_op jit(solution)/shard_map/all_to_all | solution.py:356
  95.9 2.6 %collective-permute-done.21.refs_10_ = f32[2,128,128]{2,1,0:T(8,128)S(1)} collective-permute-done((f32[2,128,128]{2,1,0:T(8,128)S(1)}, f32[2,128,128]{2,1,0:T(8,128)S(1)}, u32[]{:S(2)}, u32[]{:S(2)}) %collective-permute-start.21) | collective-permute-done | bytes 131104 | tf_op jit(solution)/shard_map/ppermute | solution.py:346
  98.4 5.7 %collective-permute-done.20.refs_9_ = f32[2,128,128]{2,1,0:T(8,128)S(1)} collective-permute-done((f32[2,128,128]{2,1,0:T(8,128)S(1)}, f32[2,128,128]{2,1,0:T(8,128)S(1)}, u32[]{:S(2)}, u32[]{:S(2)}) %collective-permute-start.20) | collective-permute-done | bytes 131104 | tf_op jit(solution)/shard_map/ppermute | solution.py:346
  104.8 7.7 %shard_map.80 = (f32[256,128]{1,0:T(8,128)}, f32[256,128]{1,0:T(8,128)}, f32[256,128]{1,0:T(8,128)}, f32[256,128]{1,0:T(8,128)}, f32[256,128]{1,0:T(8,128)}, /*i...) custom-call(s32[2]{0:T(128)} %pad_add_fusion.refs_0_, ...), custom_call_target="tpu_custom_call" | custom-call | flops 1006632960 | bytes 7340032 | tf_op jit(solution)/shard_map/pallas_call | solution.py:172
  112.5 1.7 %collective-permute-start.29 = (f32[256,128]{1,0:T(8,128)}, f32[256,128]{1,0:T(8,128)S(1)}, u32[]{:S(2)}, u32[]{:S(2)}) collective-permute-start(f32[256,128]{1,0:T(8,128)} %get-tuple-element.55), channel_id=1, source_target_pairs={{0,64},{64,128},{128,192},{192,0},{1,65},{65,129},{129,193},{193,1... | collective-permute-start | bytes 393224 | tf_op jit(solution)/shard_map/ppermute | solution.py:346
  115.2 2.2 %collective-permute-start.31 = (f32[256,128]{1,0:T(8,128)}, f32[256,128]{1,0:T(8,128)S(1)}, u32[]{:S(2)}, u32[]{:S(2)}) collective-permute-start(f32[256,128]{1,0:T(8,128)} %get-tuple-element.57), channel_id=1, source_target_pairs={{0,192},{64,0},{128,64},{192,128},{1,193},{65,1},{129,65},{193,129... | collective-permute-start | bytes 393224 | tf_op jit(solution)/shard_map/ppermute | solution.py:346
  117.7 3.3 %collective-permute-done.30 = f32[256,128]{1,0:T(8,128)S(1)} collective-permute-done((f32[256,128]{1,0:T(8,128)}, f32[256,128]{1,0:T(8,128)S(1)}, u32[]{:S(2)}, u32[]{:S(2)}) %collective-permute-start.30) | collective-permute-done | bytes 131104 | tf_op jit(solution)/shard_map/ppermute | solution.py:346
  121.8 1.6 %add_add_fusion = f32[256,128]{1,0:T(8,128)} fusion(f32[256,128]{1,0:T(8,128)S(1)} %collective-permute-done.31, f32[256,128]{1,0:T(8,128)S(1)} %collective-permute-done.30, f32[256,128]{1,0:T(8,128)} %get-tuple-element.54, f32[256,128]{1,0:T(8,128)S(1)} %collective-permute-done.29), kind=kLoop, calls=%fused_computation | loop fusion | flops 98304 | bytes 655360 | tf_op jit(solution)/shard_map/add | solution.py:434
  123.3 8.8 %all-to-all-start.2 = ((f32[64,4,128]{2,1,0:T(4,128)}), f32[64,4,128]{2,1,0:T(4,128)S(1)}, u32[]{:S(2)}, u32[]{:S(2)}) async-start(f32[64,4,128]{2,1,0:T(4,128)} %bitcast.13), calls=%async_computation.2 | async-start | bytes 262144 | tf_op jit(solution)/shard_map/all_to_all | solution.py:356
  132.2 1.4 collective-permute-start.24
  133.5 2.7 %collective-permute-start.25 = (f32[256,128]{1,0:T(8,128)}, f32[256,128]{1,0:T(8,128)S(1)}, u32[]{:S(2)}, u32[]{:S(2)}) collective-permute-start(f32[256,128]{1,0:T(8,128)} %get-tuple-element.50), channel_id=1, source_target_pairs={{0,4},{1,5},{2,6},{3,7},{4,0},{5,1},{6,2},{7,3},{8,12},{9,13},{10,... | collective-permute-start | bytes 393224 | tf_op jit(solution)/shard_map/ppermute | solution.py:346
  136.2 2.1 %collective-permute-start.26 = (f32[256,128]{1,0:T(8,128)}, f32[256,128]{1,0:T(8,128)S(1)}, u32[]{:S(2)}, u32[]{:S(2)}) collective-permute-start(f32[256,128]{1,0:T(8,128)} %get-tuple-element.51), channel_id=1, source_target_pairs={{0,5},{1,6},{2,7},{3,0},{4,1},{5,2},{6,3},{7,4},{8,13},{9,14},{10,... | collective-permute-start | bytes 393224 | tf_op jit(solution)/shard_map/ppermute | solution.py:346
  139.5 4.3 %collective-permute-done.25.refs_9_ = f32[256,128]{1,0:T(8,128)S(1)} collective-permute-done((f32[256,128]{1,0:T(8,128)}, f32[256,128]{1,0:T(8,128)S(1)}, u32[]{:S(2)}, u32[]{:S(2)}) %collective-permute-start.25) | collective-permute-done | bytes 131104 | tf_op jit(solution)/shard_map/ppermute | solution.py:346
  143.8 2.2 %collective-permute-done.26.refs_10_ = f32[256,128]{1,0:T(8,128)S(1)} collective-permute-done((f32[256,128]{1,0:T(8,128)}, f32[256,128]{1,0:T(8,128)S(1)}, u32[]{:S(2)}, u32[]{:S(2)}) %collective-permute-start.26) | collective-permute-done | bytes 131104 | tf_op jit(solution)/shard_map/ppermute | solution.py:346
  146.9 1.4 collective-permute-done.28.refs_12_
  148.9 6.9 %shard_map.81 = bf16[128,1024]{1,0:T(8,128)(2,1)} custom-call(s32[2]{0:T(128)} %pad_add_fusion.refs_0_, f32[8,128,128]{2,1,0:T(8,128)} %copy-done, bf16[1024,1024]{1,0:T(8,128)(2,1)} %refs_2_.3, bf16[1024,1024]{1,0:T(8,128)(2,1)} %refs_3_.3, bf16[1024,1024]{1,0:T(8,128)(2,1)} %refs_4_.1, f32[256,128]{1,0:T(8,128)} %get-tuple-element.46.refs_5_, ...), custom_call_target="tpu_custom_call" | custom-call | flops 805306368 | bytes 8126464 | tf_op jit(solution)/shard_map/pallas_call | solution.py:172
  (109 shorter events, 18.7 us)
Async XLA Ops:
  2.6 10.1 %collective-permute-start.8 = (f32[64,1024]{1,0:T(8,128)}, f32[64,1024]{1,0:T(8,128)S(1)}, u32[]{:S(2)}, u32[]{:S(2)}) collective-permute-start(f32[64,1024]{1,0:T(8,128)} %get-tuple-element.30.refs_4_), channel_id=1, source_target_pairs={{0,6},{2,0},{4,2},{6,4},{1,7},{3,1},{5,3},{7,5},{8,14},{10,8},{12,... | collective-permute-start | bytes 786440 | tf_op jit(solution)/shard_map/ppermute | solution.py:346
  5.7 10.6 %collective-permute-start.2 = (f32[64,1024]{1,0:T(8,128)}, f32[64,1024]{1,0:T(8,128)S(1)}, u32[]{:S(2)}, u32[]{:S(2)}) collective-permute-start(f32[64,1024]{1,0:T(8,128)} %get-tuple-element.30.refs_4_), channel_id=1, source_target_pairs={{0,2},{2,4},{4,6},{6,0},{1,3},{3,5},{5,7},{7,1},{8,10},{10,12},{12... | collective-permute-start | bytes 786440 | tf_op jit(solution)/shard_map/ppermute | solution.py:346
  5.7 10.6 %collective-permute-start = (f32[64,1024]{1,0:T(8,128)}, f32[64,1024]{1,0:T(8,128)S(1)}, u32[]{:S(2)}, u32[]{:S(2)}) collective-permute-start(f32[64,1024]{1,0:T(8,128)} %get-tuple-element.30.refs_4_), channel_id=1, source_target_pairs={{0,1},{1,0},{2,3},{3,2},{4,5},{5,4},{6,7},{7,6},{8,9},{9,8},{10,11... | collective-permute-start | bytes 786440 | tf_op jit(solution)/shard_map/ppermute | solution.py:346
  5.7 11.5 %collective-permute-start.4 = (f32[64,1024]{1,0:T(8,128)}, f32[64,1024]{1,0:T(8,128)S(1)}, u32[]{:S(2)}, u32[]{:S(2)}) collective-permute-start(f32[64,1024]{1,0:T(8,128)} %get-tuple-element.31.refs_5_), channel_id=1, source_target_pairs={{0,6},{2,0},{4,2},{6,4},{1,7},{3,1},{5,3},{7,5},{8,14},{10,8},{12,... | collective-permute-start | bytes 786440 | tf_op jit(solution)/shard_map/ppermute | solution.py:346
  8.9 11.8 %collective-permute-start.6 = (f32[64,1024]{1,0:T(8,128)}, f32[64,1024]{1,0:T(8,128)S(1)}, u32[]{:S(2)}, u32[]{:S(2)}) collective-permute-start(f32[64,1024]{1,0:T(8,128)} %get-tuple-element.31.refs_5_), channel_id=1, source_target_pairs={{0,2},{2,4},{4,6},{6,0},{1,3},{3,5},{5,7},{7,1},{8,10},{10,12},{12... | collective-permute-start | bytes 786440 | tf_op jit(solution)/shard_map/ppermute | solution.py:346
  12.7 8.1 %collective-permute-start.1 = (f32[64,1024]{1,0:T(8,128)}, f32[64,1024]{1,0:T(8,128)S(1)}, u32[]{:S(2)}, u32[]{:S(2)}) collective-permute-start(f32[64,1024]{1,0:T(8,128)} %get-tuple-element.31.refs_5_), channel_id=1, source_target_pairs={{0,1},{1,0},{2,3},{3,2},{4,5},{5,4},{6,7},{7,6},{8,9},{9,8},{10,11... | collective-permute-start | bytes 786440 | tf_op jit(solution)/shard_map/ppermute | solution.py:346
  16.3 5.0 %collective-permute-start.9 = (f32[64,1024]{1,0:T(8,128)S(1)}, f32[64,1024]{1,0:T(8,128)S(1)}, u32[]{:S(2)}, u32[]{:S(2)}) collective-permute-start(f32[64,1024]{1,0:T(8,128)S(1)} %collective-permute-done.8.refs_14_), channel_id=1, source_target_pairs={{0,1},{1,0},{2,3},{3,2},{4,5},{5,4},{6,7},{7,6},{8,9},{9,8},{10,11... | collective-permute-start | bytes 786440 | tf_op jit(solution)/shard_map/ppermute | solution.py:346
  16.3 9.9 %collective-permute-start.10 = (f32[64,1024]{1,0:T(8,128)S(1)}, f32[64,1024]{1,0:T(8,128)S(1)}, u32[]{:S(2)}, u32[]{:S(2)}) collective-permute-start(f32[64,1024]{1,0:T(8,128)S(1)} %collective-permute-done.2.refs_8_), channel_id=1, source_target_pairs={{0,2},{2,4},{4,6},{6,0},{1,3},{3,5},{5,7},{7,1},{8,10},{10,12},{12... | collective-permute-start | bytes 786440 | tf_op jit(solution)/shard_map/ppermute | solution.py:346
  17.2 9.0 %collective-permute-start.12 = (f32[64,1024]{1,0:T(8,128)S(1)}, f32[64,1024]{1,0:T(8,128)S(1)}, u32[]{:S(2)}, u32[]{:S(2)}) collective-permute-start(f32[64,1024]{1,0:T(8,128)S(1)} %collective-permute-done.4.refs_10_), channel_id=1, source_target_pairs={{0,6},{2,0},{4,2},{6,4},{1,7},{3,1},{5,3},{7,5},{8,14},{10,8},{12,... | collective-permute-start | bytes 786440 | tf_op jit(solution)/shard_map/ppermute | solution.py:346
  20.8 6.6 %collective-permute-start.3 = (f32[64,1024]{1,0:T(8,128)S(1)}, f32[64,1024]{1,0:T(8,128)S(1)}, u32[]{:S(2)}, u32[]{:S(2)}) collective-permute-start(f32[64,1024]{1,0:T(8,128)S(1)} %collective-permute-done.2.refs_8_), channel_id=1, source_target_pairs={{0,1},{1,0},{2,3},{3,2},{4,5},{5,4},{6,7},{7,6},{8,9},{9,8},{10,11... | collective-permute-start | bytes 786440 | tf_op jit(solution)/shard_map/ppermute | solution.py:346
  20.8 6.6 %collective-permute-start.5 = (f32[64,1024]{1,0:T(8,128)S(1)}, f32[64,1024]{1,0:T(8,128)S(1)}, u32[]{:S(2)}, u32[]{:S(2)}) collective-permute-start(f32[64,1024]{1,0:T(8,128)S(1)} %collective-permute-done.4.refs_10_), channel_id=1, source_target_pairs={{0,1},{1,0},{2,3},{3,2},{4,5},{5,4},{6,7},{7,6},{8,9},{9,8},{10,11... | collective-permute-start | bytes 786440 | tf_op jit(solution)/shard_map/ppermute | solution.py:346
  21.3 6.1 %collective-permute-start.7 = (f32[64,1024]{1,0:T(8,128)S(1)}, f32[64,1024]{1,0:T(8,128)S(1)}, u32[]{:S(2)}, u32[]{:S(2)}) collective-permute-start(f32[64,1024]{1,0:T(8,128)S(1)} %collective-permute-done.6.refs_12_), channel_id=1, source_target_pairs={{0,1},{1,0},{2,3},{3,2},{4,5},{5,4},{6,7},{7,6},{8,9},{9,8},{10,11... | collective-permute-start | bytes 786440 | tf_op jit(solution)/shard_map/ppermute | solution.py:346
  36.2 12.9 %collective-permute-start.15 = (f32[2,128,128]{2,1,0:T(8,128)}, f32[2,128,128]{2,1,0:T(8,128)S(1)}, u32[]{:S(2)}, u32[]{:S(2)}) collective-permute-start(f32[2,128,128]{2,1,0:T(8,128)} %get-tuple-element.38), channel_id=1, source_target_pairs={{0,16},{8,24},{16,32},{24,40},{32,48},{40,56},{1,17},{9,25},{17,33... | collective-permute-start | bytes 393224 | tf_op jit(solution)/shard_map/ppermute | solution.py:346
  41.4 7.8 %collective-permute-start.14 = (f32[2,128,128]{2,1,0:T(8,128)}, f32[2,128,128]{2,1,0:T(8,128)S(1)}, u32[]{:S(2)}, u32[]{:S(2)}) collective-permute-start(f32[2,128,128]{2,1,0:T(8,128)} %get-tuple-element.38), channel_id=1, source_target_pairs={{0,8},{8,16},{16,24},{24,32},{32,40},{40,48},{48,56},{1,9},{9,17},... | collective-permute-start | bytes 393224 | tf_op jit(solution)/shard_map/ppermute | solution.py:346
  45.2 17.8 %all-to-all-start = ((f32[8,128,128]{2,1,0:T(8,128)}), f32[8,128,128]{2,1,0:T(8,128)S(1)}, u32[]{:S(2)}, u32[]{:S(2)}) async-start(f32[8,128,128]{2,1,0:T(8,128)} %get-tuple-element.39), calls=%async_computation | async-start | bytes 1048576 | tf_op jit(solution)/shard_map/all_to_all | solution.py:356
  50.2 12.6 %collective-permute-start.17 = (f32[2,128,128]{2,1,0:T(8,128)S(1)}, f32[2,128,128]{2,1,0:T(8,128)S(1)}, u32[]{:S(2)}, u32[]{:S(2)}) collective-permute-start(f32[2,128,128]{2,1,0:T(8,128)S(1)} %add_add_fusion.2), channel_id=1, source_target_pairs={{0,48},{8,56},{1,49},{9,57},{2,50},{10,58},{3,51},{11,59},{4,52},{... | collective-permute-start | bytes 393224 | tf_op jit(solution)/shard_map/ppermute | solution.py:346
  72.7 14.9 %collective-permute-start.19 = (f32[2,128,128]{2,1,0:T(8,128)}, f32[2,128,128]{2,1,0:T(8,128)S(1)}, u32[]{:S(2)}, u32[]{:S(2)}) collective-permute-start(f32[2,128,128]{2,1,0:T(8,128)} %get-tuple-element.44), channel_id=1, source_target_pairs={{16,0},{24,8},{32,16},{40,24},{48,32},{56,40},{17,1},{25,9},{33,17... | collective-permute-start | bytes 393224 | tf_op jit(solution)/shard_map/ppermute | solution.py:346
  74.0 13.6 %collective-permute-start.18 = (f32[2,128,128]{2,1,0:T(8,128)}, f32[2,128,128]{2,1,0:T(8,128)S(1)}, u32[]{:S(2)}, u32[]{:S(2)}) collective-permute-start(f32[2,128,128]{2,1,0:T(8,128)} %get-tuple-element.44), channel_id=1, source_target_pairs={{8,0},{16,8},{24,16},{32,24},{40,32},{48,40},{56,48},{9,1},{17,9},... | collective-permute-start | bytes 393224 | tf_op jit(solution)/shard_map/ppermute | solution.py:346
  88.6 9.8 %collective-permute-start.21 = (f32[2,128,128]{2,1,0:T(8,128)S(1)}, f32[2,128,128]{2,1,0:T(8,128)S(1)}, u32[]{:S(2)}, u32[]{:S(2)}) collective-permute-start(f32[2,128,128]{2,1,0:T(8,128)S(1)} %add_add_fusion.1), channel_id=1, source_target_pairs={{48,0},{56,8},{49,1},{57,9},{50,2},{58,10},{51,3},{59,11},{52,4},{... | collective-permute-start | bytes 393224 | tf_op jit(solution)/shard_map/ppermute | solution.py:346
  89.9 14.2 %collective-permute-start.20 = (f32[2,128,128]{2,1,0:T(8,128)S(1)}, f32[2,128,128]{2,1,0:T(8,128)S(1)}, u32[]{:S(2)}, u32[]{:S(2)}) collective-permute-start(f32[2,128,128]{2,1,0:T(8,128)S(1)} %add_add_fusion.1), channel_id=1, source_target_pairs={{24,0},{32,8},{40,16},{48,24},{56,32},{25,1},{33,9},{41,17},{49,25... | collective-permute-start | bytes 393224 | tf_op jit(solution)/shard_map/ppermute | solution.py:346
  91.9 31.4 %all-to-all-start.1 = ((f32[8,128,128]{2,1,0:T(8,128)}), f32[8,128,128]{2,1,0:T(8,128)S(1)}, u32[]{:S(2)}, u32[]{:S(2)}) async-start(f32[8,128,128]{2,1,0:T(8,128)} %get-tuple-element.40), calls=%async_computation.1 | async-start | bytes 1048576 | tf_op jit(solution)/shard_map/all_to_all | solution.py:356
  112.5 5.3 %collective-permute-start.29 = (f32[256,128]{1,0:T(8,128)}, f32[256,128]{1,0:T(8,128)S(1)}, u32[]{:S(2)}, u32[]{:S(2)}) collective-permute-start(f32[256,128]{1,0:T(8,128)} %get-tuple-element.55), channel_id=1, source_target_pairs={{0,64},{64,128},{128,192},{192,0},{1,65},{65,129},{129,193},{193,1... | collective-permute-start | bytes 393224 | tf_op jit(solution)/shard_map/ppermute | solution.py:346
  114.2 6.8 %collective-permute-start.30 = (f32[256,128]{1,0:T(8,128)}, f32[256,128]{1,0:T(8,128)S(1)}, u32[]{:S(2)}, u32[]{:S(2)}) collective-permute-start(f32[256,128]{1,0:T(8,128)} %get-tuple-element.56), channel_id=1, source_target_pairs={{0,128},{64,192},{128,0},{192,64},{1,129},{65,193},{129,1},{193,65... | collective-permute-start | bytes 393224 | tf_op jit(solution)/shard_map/ppermute | solution.py:346
  115.2 6.6 %collective-permute-start.31 = (f32[256,128]{1,0:T(8,128)}, f32[256,128]{1,0:T(8,128)S(1)}, u32[]{:S(2)}, u32[]{:S(2)}) collective-permute-start(f32[256,128]{1,0:T(8,128)} %get-tuple-element.57), channel_id=1, source_target_pairs={{0,192},{64,0},{128,64},{192,128},{1,193},{65,1},{129,65},{193,129... | collective-permute-start | bytes 393224 | tf_op jit(solution)/shard_map/ppermute | solution.py:346
  117.3 20.9 %collective-permute-start.22 = (f32[256,128]{1,0:T(8,128)}, f32[256,128]{1,0:T(8,128)S(1)}, u32[]{:S(2)}, u32[]{:S(2)}) collective-permute-start(f32[256,128]{1,0:T(8,128)} %get-tuple-element.47), channel_id=1, source_target_pairs={{0,1},{1,2},{2,3},{3,4},{4,5},{5,6},{6,7},{7,0},{8,9},{9,10},{10,1... | collective-permute-start | bytes 393224 | tf_op jit(solution)/shard_map/ppermute | solution.py:346
  117.3 22.1 %collective-permute-start.23 = (f32[256,128]{1,0:T(8,128)}, f32[256,128]{1,0:T(8,128)S(1)}, u32[]{:S(2)}, u32[]{:S(2)}) collective-permute-start(f32[256,128]{1,0:T(8,128)} %get-tuple-element.48), channel_id=1, source_target_pairs={{0,2},{1,3},{2,4},{3,5},{4,6},{5,7},{6,0},{7,1},{8,10},{9,11},{10,... | collective-permute-start | bytes 393224 | tf_op jit(solution)/shard_map/ppermute | solution.py:346
  123.3 32.5 %all-to-all-start.2 = ((f32[64,4,128]{2,1,0:T(4,128)}), f32[64,4,128]{2,1,0:T(4,128)S(1)}, u32[]{:S(2)}, u32[]{:S(2)}) async-start(f32[64,4,128]{2,1,0:T(4,128)} %bitcast.13), calls=%async_computation.2 | async-start | bytes 262144 | tf_op jit(solution)/shard_map/all_to_all | solution.py:356
  132.2 7.3 %collective-permute-start.24 = (f32[256,128]{1,0:T(8,128)}, f32[256,128]{1,0:T(8,128)S(1)}, u32[]{:S(2)}, u32[]{:S(2)}) collective-permute-start(f32[256,128]{1,0:T(8,128)} %get-tuple-element.49), channel_id=1, source_target_pairs={{0,3},{1,4},{2,5},{3,6},{4,7},{5,0},{6,1},{7,2},{8,11},{9,12},{10,... | collective-permute-start | bytes 393224 | tf_op jit(solution)/shard_map/ppermute | solution.py:346
  133.5 10.3 %collective-permute-start.25 = (f32[256,128]{1,0:T(8,128)}, f32[256,128]{1,0:T(8,128)S(1)}, u32[]{:S(2)}, u32[]{:S(2)}) collective-permute-start(f32[256,128]{1,0:T(8,128)} %get-tuple-element.50), channel_id=1, source_target_pairs={{0,4},{1,5},{2,6},{3,7},{4,0},{5,1},{6,2},{7,3},{8,12},{9,13},{10,... | collective-permute-start | bytes 393224 | tf_op jit(solution)/shard_map/ppermute | solution.py:346
  136.2 9.8 %collective-permute-start.26 = (f32[256,128]{1,0:T(8,128)}, f32[256,128]{1,0:T(8,128)S(1)}, u32[]{:S(2)}, u32[]{:S(2)}) collective-permute-start(f32[256,128]{1,0:T(8,128)} %get-tuple-element.51), channel_id=1, source_target_pairs={{0,5},{1,6},{2,7},{3,0},{4,1},{5,2},{6,3},{7,4},{8,13},{9,14},{10,... | collective-permute-start | bytes 393224 | tf_op jit(solution)/shard_map/ppermute | solution.py:346
  138.3 8.6 %collective-permute-start.27 = (f32[256,128]{1,0:T(8,128)}, f32[256,128]{1,0:T(8,128)S(1)}, u32[]{:S(2)}, u32[]{:S(2)}) collective-permute-start(f32[256,128]{1,0:T(8,128)} %get-tuple-element.52), channel_id=1, source_target_pairs={{0,6},{1,7},{2,0},{3,1},{4,2},{5,3},{6,4},{7,5},{8,14},{9,15},{10,... | collective-permute-start | bytes 393224 | tf_op jit(solution)/shard_map/ppermute | solution.py:346
  139.5 8.8 %collective-permute-start.28 = (f32[256,128]{1,0:T(8,128)}, f32[256,128]{1,0:T(8,128)S(1)}, u32[]{:S(2)}, u32[]{:S(2)}) collective-permute-start(f32[256,128]{1,0:T(8,128)} %get-tuple-element.53), channel_id=1, source_target_pairs={{0,7},{1,0},{2,1},{3,2},{4,3},{5,4},{6,5},{7,6},{8,15},{9,8},{10,9... | collective-permute-start | bytes 393224 | tf_op jit(solution)/shard_map/ppermute | solution.py:346
  (33 other events, 218.6 us)
where the time goes:
time: 159 us; the launch traced here: 156 us
  starting transfers between devices  64.4 us (41%)
  waiting for transfers between devices  50.1 us (32%)
  Pallas kernels  33.1 us (21%)
  other arithmetic  4.92 us (3%)
  local copies, waits for them, and re-layouts  2.94 us (2%)
    ppermute x32, waiting for transfers between devices, shift(): return lax.ppermute(x, axis, pairs)  50.1 us
    ppermute x32, starting transfers between devices, shift(): return lax.ppermute(x, axis, pairs)  47.8 us
    pallas_call x5, Pallas kernels, call(): pl.pallas_call(kernel, out_shape=tuple(outs), in_specs=[pl.BlockSpec(memo...  33.1 us
    all_to_all x3, starting transfers between devices, exchange(): return lax.all_to_all(x, axis, 0, 0)  16.7 us
  transfers between devices with their start and end apart: 35, of which 18 were waited for; matrix products, arithmetic and copies ran while one was open for 3% of the time, Pallas kernels for 9%

commit v1 on v0

--- a/solution.py
+++ b/solution.py
@@ -184,25 +184,62 @@
     )(*tables, *raw, *args)
 
 
+def fold_symmetric(m):
+    half = m.shape[0] // 2
+    rows = lax.broadcasted_iota(jnp.int32, (half, 2 * half), 0)
+    cols = lax.broadcasted_iota(jnp.int32, (half, 2 * half), 1)
+    low = pltpu.roll(m[half:], half, 1)
+    diagonal = jnp.sum(jnp.where(rows == cols, low, 0.0), axis=0, keepdims=True)
+    mixed = jnp.where((cols > rows) & (cols < half), low, m[:half])
+    return jnp.concatenate([mixed, jnp.broadcast_to(diagonal, (8, 2 * half))], axis=0)
+
+
+def unfold_symmetric(f):
+    half = f.shape[1] // 2
+    rows = lax.broadcasted_iota(jnp.int32, (half, 2 * half), 0)
+    cols = lax.broadcasted_iota(jnp.int32, (half, 2 * half), 1)
+    mixed, diagonal = f[:half], f[half : half + 1]
+    turned = jnp.transpose(jnp.concatenate([mixed, jnp.zeros_like(mixed)], axis=0))
+    top = jnp.where((cols > rows) & (cols < half), turned[:half], mixed)
+    last = jnp.where(cols > rows, mixed, jnp.where(cols < rows, turned[:half], diagonal))
+    low = jnp.where(cols < half, turned[half:], pltpu.roll(last, half, 1))
+    return jnp.concatenate([top, low], axis=0)
+
+
+FOLDED = DK // 2 + 8
+STATE = FOLDED + DK
+
+
+def total_of(need, first):
+    near = [need(first + n) for n in range(4)]
+    state = (near[0][...] + near[1][...]) + (near[2][...] + near[3][...])
+    return unfold_symmetric(state[:FOLDED]), state[FOLDED:]
+
+
+def chunk(j):
+    return slice(j * DK, (j + 1) * DK)
+
+
 def prepare_body(tables, need, made, put):
-    x, (low, high, upstream) = need(0), made
+    x, (low, high) = need(0), made
     rows = low.shape[0]
     low[...] = x[:rows].astype(F32)
     put(0)
     high[...] = x[rows:].astype(F32)
-    put(1)
-    g = need(1)
+
+
+def upstream_body(tables, need, made, put):
     for h in range(HEADS):
-        upstream[h] = g[:, h * DK : (h + 1) * DK].astype(F32)
-
-
-def project_body(slots, wq_hbm, wk_hbm, wv_hbm, tables, need, made, put, w_buf, w_sem):
+        made[0][h] = need(0)[:, chunk(h)].astype(F32)
+
+
+def project_body(slots, wk_hbm, wv_hbm, tables, need, made, put, w_buf, w_sem):
     (where,) = tables
-    xb, q_out, k_out, v_out, gram_out, cross_out, tot = made
+    xb, k_out, v_out, tot = made
     cols = pl.ds(pl.multiple_of(where[len(where) - 1] * DK, DK), DK)
     weights = [
-        pltpu.make_async_copy(w.at[:, cols], w_buf.at[n], w_sem.at[n])
-        for n, w in enumerate((wq_hbm, wk_hbm, wv_hbm))
+        pltpu.make_async_copy(w.at[:, cols], w_buf.at[:, chunk(n)], w_sem.at[n])
+        for n, w in enumerate((wk_hbm, wv_hbm))
     ]
     for copy in weights:
         copy.start()
@@ -213,116 +250,143 @@
     put(0)
     for copy in weights:
         copy.wait()
-    wq, wk, wv = w_buf[0], w_buf[1], w_buf[2]
+    both = nn(xb[...], w_buf[...]).astype(BF16)
+    k, v = both[:, :DK], both[:, DK:]
+    k_out[...] = k
+    v_out[...] = v
+    put(1)
+    put(2)
+    rk = inv_norm(k)
+    kn = k.astype(F32) * rk
+    tot[:FOLDED] = fold_symmetric(fold_cols(tn(k, wide(kn * rk))))
+    tot[FOLDED:] = fold_cols(tn(v, wide(kn)))
+
+
+def states_body(wq_hbm, tables, need, made, put, w_buf, w_sem):
+    (where,) = tables
+    q_out, gram_out = made
+    cols = pl.ds(pl.multiple_of(where[len(where) - 1] * DK, DK), DK)
+    weight = pltpu.make_async_copy(wq_hbm.at[:, cols], w_buf, w_sem.at[0])
+    weight.start()
+    k_in = need(0)
+    gram = jnp.zeros((DK, DK), F32)
+    for j in range(CHUNKS):
+        gram_out[j] = gram
+        if j + 1 < CHUNKS:
+            k = k_in[chunk(j), :]
+            rk = inv_norm(k)
+            gram = gram + fold_cols(tn(k, wide(k.astype(F32) * (rk * rk))))
+    put(1)
+    weight.wait()
+    q_out[...] = nn(need(1)[...], w_buf[...]).astype(BF16)
+
+
+def targets_body(tables, need, made, put):
+    k_in, v_in, g_in = need(0), need(1), need(2)
+    keep = causal(DK)
+    cross = jnp.zeros((DK, DK), F32)
+    for j in range(CHUNKS):
+        k, v, g = k_in[chunk(j), :], v_in[chunk(j), :], g_in[j].astype(BF16)
+        rk = inv_norm(k)
+        scores = nt(g, v) * jnp.where(keep, across(rk), 0.0)
+        made[0][j] = nn(twice_wide(g), tall(cross)) + nn(wide(scores), twice_tall(k))
+        if j + 1 < CHUNKS:
+            cross = cross + fold_cols(tn(v, wide(k.astype(F32) * rk)))
+
+
+def solve_body(tables, need, made, put):
+    (where,) = tables
+    q_in, k_in, gram_in, part, g_in, damp_in = [need(n) for n in range(6)]
+    gram_prior, cross_prior = total_of(need, 6)
+    z_out, u_out, tot = made
+    damp = damp_in[pl.ds(where[len(where) - 1], 1), :]
+    keep = causal(DK)
+    keys = [k_in[chunk(j), :] for j in range(CHUNKS)]
+    grams = [gram_in[j] + gram_prior for j in range(CHUNKS)]
+    cross_tall = tall(cross_prior)
+    scale2, targets = [], []
+    for j, k in enumerate(keys):
+        rk = inv_norm(k)
+        row = jnp.where(keep, across(rk * rk), 0.0)
+        scale2.append(twice_tall(row))
+        right = part[j] + nn(twice_wide(g_in[j].astype(BF16)), cross_tall)
+        q = q_in[chunk(j), :]
+        targets.append(jnp.concatenate([q.astype(F32) * inv_norm(q), right], axis=0))
+    both = conjugate(targets, keys, grams, scale2, damp)
     gram = jnp.zeros((DK, DK), F32)
     cross = jnp.zeros((DK, DK), F32)
     for j in range(CHUNKS):
-        x = xb[j * DK : (j + 1) * DK, :]
-        k = nn(x, wk).astype(BF16)
-        v = nn(x, wv).astype(BF16)
-        k_out[j] = k
-        v_out[j] = v
-        rk = inv_norm(k)
-        kn = k.astype(F32) * rk
-        gram_out[j] = gram
-        cross_out[j] = cross
-        gram = gram + fold_cols(tn(k, wide(kn * rk)))
-        cross = cross + fold_cols(tn(v, wide(kn)))
-    tot[0] = gram
-    tot[1] = cross
-    put(6)
-    for n in (2, 3, 4, 5):
-        put(n)
+        z, u = both[j][:DK], both[j][DK:]
+        z_out[j] = z
+        u_out[j] = u
+        z_wide, u_wide = wide(z), wide(u)
+        left = jnp.concatenate([u_wide, z_wide], axis=0)
+        right = jnp.concatenate([z_wide, u_wide], axis=0)
+        gram = gram + fold_rows(fold_cols(tn(left, right)))
+        cross = cross + fold_cols(tn(g_in[j].astype(BF16), z_wide))
+    tot[:FOLDED] = fold_symmetric(gram)
+    tot[FOLDED:] = cross
+
+
+def local_body(tables, need, made, put):
+    q_in, k_in, v_in, g_in, z_in, u_in = [need(n) for n in range(6)]
+    dq_out, dk_out, dv_out = made
+    keep = causal(DK)
     for j in range(CHUNKS):
-        q_out[j] = nn(xb[j * DK : (j + 1) * DK, :], wq).astype(BF16)
-
-
-def total_of(need, first):
-    near = [need(first + n) for n in range(4)]
-    return [(near[0][i] + near[1][i]) + (near[2][i] + near[3][i]) for i in range(2)]
-
-
-def solve_body(tables, need, made, put):
-    (where,) = tables
-    q_in, k_in, v_in, gram_in, cross_in, damp_in, g_in = [need(n) for n in range(7)]
-    gram_prior, cross_prior = total_of(need, 7)
-    z_out, u_out, dq_out, suf, tot = made
-    damp = damp_in[pl.ds(where[len(where) - 1], 1), :]
-    keep = causal(DK)
-    keys = [k_in[j] for j in range(CHUNKS)]
-    grams = [gram_in[j] + gram_prior for j in range(CHUNKS)]
-    scale2, targets = [], []
-    for j, k in enumerate(keys):
-        row = jnp.where(keep, across(inv_norm(k)), 0.0)
-        scale2.append(twice_tall(row * row))
-        g = g_in[j].astype(BF16)
-        scores = nt(g, v_in[j]) * row
-        state = cross_in[j] + cross_prior
-        right = nn(twice_wide(g), tall(state)) + nn(wide(scores), twice_tall(k))
-        qn = q_in[j].astype(F32) * inv_norm(q_in[j])
-        targets.append(jnp.concatenate([qn, right], axis=0))
-    both = conjugate(targets, keys, grams, scale2, damp)
+        q, u = q_in[chunk(j), :], u_in[j]
+        rq = inv_norm(q)
+        qn = q.astype(F32) * rq
+        dq_out[j] = ((u - qn * rowsum(qn * u)) * rq).astype(BF16).astype(F32)
+    put(0)
     gram = jnp.zeros((DK, DK), F32)
     cross = jnp.zeros((DK, DK), F32)
     for j in reversed(range(CHUNKS)):
-        z, u = both[j][:DK], both[j][DK:]
-        z_out[j] = z
-        u_out[j] = u
-        suf[0, j] = gram
-        suf[1, j] = cross
-        left = jnp.concatenate([wide(u), wide(z)], axis=0)
-        right = jnp.concatenate([wide(z), wide(u)], axis=0)
-        gram = gram + fold_rows(fold_cols(tn(left, right)))
-        cross = cross + fold_cols(tn(g_in[j].astype(BF16), wide(z)))
-    tot[0] = gram
-    tot[1] = cross
-    put(4)
-    for n in (0, 1, 3):
-        put(n)
-    for j in range(CHUNKS):
-        q = q_in[j]
-        rq = inv_norm(q)
-        qn = q.astype(F32) * rq
-        u = u_out[j]
-        dq_out[j] = ((u - qn * rowsum(qn * u)) * rq).astype(BF16).astype(F32)
-
-
-def grads_body(seq, tables, need, made, put, dk_buf, dw_buf, out):
-    (place,) = tables
-    k_in, v_in, z_in, u_in, suf, g_in = [need(n) for n in range(6)]
-    gram_after, cross_after = total_of(need, 6)
-    keep = causal(DK)
-    for j in range(CHUNKS):
-        k, v = k_in[j], v_in[j]
+        k, v = k_in[chunk(j), :], v_in[chunk(j), :]
         rk = inv_norm(k)
-        kn = k.astype(F32) * rk
         row = jnp.where(keep, across(rk), 0.0)
         g = g_in[j].astype(BF16)
         scores = jnp.where(keep, nt(g, v), 0.0)
         u, z = u_in[j], z_in[j]
-        both = jnp.concatenate([u, z], axis=0)
-        pair = nt(wide(both), twice_wide(k)) * twice_tall(row)
+        u_wide, z_wide = wide(u), wide(z)
+        kk = twice_wide(k)
+        pair = nt(jnp.concatenate([u_wide, z_wide], axis=0), kk) * twice_tall(row)
         left = jnp.concatenate([scores - pair[:DK], -pair[DK:]], axis=0)
-        right = jnp.concatenate([z, u], axis=0)
+        right = jnp.concatenate([z_wide, u_wide], axis=0)
+        dkn = fold_rows(fold_cols(tn(wide(left), right)))
+        dkn = dkn + nn(twice_wide(v), tall(cross))
+        dk_out[j] = dkn - rk * nn(kk, tall(gram))
+        dv_out[j] = rk * nt(kk, wide(cross)) + tn(tall(pair[DK:]), twice_tall(g))
+        if j:
+            swapped = jnp.concatenate([u_wide, z_wide], axis=0)
+            gram = gram + fold_rows(fold_cols(tn(swapped, right)))
+            cross = cross + fold_cols(tn(g, z_wide))
+
+
+def grads_body(seq, tables, need, made, put, dk_buf, dw_buf, out):
+    (place,) = tables
+    k_in, v_in, dk_part, dv_part = [need(n) for n in range(4)]
+    gram_after, cross_after = total_of(need, 4)
+    gram_tall, cross_tall, cross_wide = tall(gram_after), tall(cross_after), wide(cross_after)
+    for j in range(CHUNKS):
+        k, v = k_in[chunk(j), :], v_in[chunk(j), :]
+        rk = inv_norm(k)
+        kn = k.astype(F32) * rk
         kk = twice_wide(k)
-        cross = suf[1, j] + cross_after
-        dkn = fold_rows(fold_cols(tn(wide(left), wide(right))))
-        dkn = dkn + nn(twice_wide(v), tall(cross))
-        dkn = dkn - rk * nn(kk, tall(suf[0, j] + gram_after))
+        dkn = dk_part[j] + nn(twice_wide(v), cross_tall) - rk * nn(kk, gram_tall)
         dk = ((dkn - kn * rowsum(kn * dkn)) * rk).astype(BF16)
-        dk_buf[j * DK : (j + 1) * DK, :] = dk
+        dk_buf[chunk(j), :] = dk
         out[j, :DK] = dk.astype(F32)
-        dv = rk * nt(kk, wide(cross)) + tn(tall(pair[DK:]), twice_tall(g))
+        dv = dv_part[j] + rk * nt(kk, cross_wide)
         out[j, DK:] = dv.astype(BF16).astype(F32)
-    for step in range(CHUNKS):
-        made[seq + step][...] = out[lax.rem(place[1] + step, CHUNKS)]
-        put(seq + step)
-    dw_buf[...] = jnp.transpose(tn(dk_buf[...], need(10)[...]))
+    dw_buf[...] = jnp.transpose(tn(dk_buf[...], need(8)[...]))
     rows = made[0].shape[0]
     for step in range(seq):
         start = pl.multiple_of(lax.rem(place[0] + step, seq) * rows, rows)
         made[step][...] = dw_buf[pl.ds(start, rows), :]
         put(step)
+    for step in range(CHUNKS):
+        made[seq + step][...] = out[lax.rem(place[1] + step, CHUNKS)]
+        put(seq + step)
 
 
 def input_grad_body(tables, need, made, put, dk_cat, dv_cat):
@@ -383,35 +447,41 @@
 def on_device(inputs, w_query, w_key, w_value, damping, grad_out):
     mine = inputs[0]
     tokens, width = mine.shape
+    plane = CHUNKS * tokens
     blocks = shaped(CHUNKS, tokens, DK)
-    brick = shaped(CHUNKS, tokens, DK, dtype=BF16)
-    pair = shaped(2, DK, DK)
-    states = shaped(CHUNKS, DK, DK)
-    unit = 2 * CHUNKS * tokens * DK * DK
+    brick = shaped(plane, DK, dtype=BF16)
+    state = shaped(STATE, DK)
+    unit = 2 * plane * DK * DK
 
     half = shaped(tokens // 2, width)
-    low, high, upstream = call(
-        prepare_body, [half, half, shaped(HEADS, tokens, DK)], [mine, grad_out[0]], 0
-    )
+    low, high = call(prepare_body, [half, half], [mine], 0)
     pieces, where = gather_plane(low, high)
     slots = tuple((slot, start) for _, slot, start in pieces)
-    xb, q, k, v, gram_pre, cross_pre, first_tot = call(
+    pieces = [p for p, _, _ in pieces]
+    upstream, _ = lax.optimization_barrier((grad_out[0], pieces[4]))
+    (upstream,) = call(upstream_body, [shaped(HEADS, tokens, DK)], [upstream], 0)
+    xb, k, v, first_tot = call(
         functools.partial(project_body, slots),
-        [shaped(CHUNKS * tokens, width, dtype=BF16), brick, brick, brick, states, states, pair],
-        [p for p, _, _ in pieces],
-        unit * 28,
-        tables=[where], raw=[w_query, w_key, w_value],
-        scratch=[pltpu.VMEM((3, width, DK), BF16), pltpu.SemaphoreType.DMA((3,))],
+        [shaped(plane, width, dtype=BF16), brick, brick, state],
+        pieces, unit * 28, tables=[where], raw=[w_key, w_value],
+        scratch=[pltpu.VMEM((width, 2 * DK), BF16), pltpu.SemaphoreType.DMA((2,))],
     )
     prior = exclusive(first_tot, 1)
     upstream, _ = lax.optimization_barrier((upstream, first_tot))
     g = exchange(upstream, PLANE)
-
-    z, u, dq, suf, second_tot = call(
-        solve_body, [blocks, blocks, blocks, shaped(2, CHUNKS, DK, DK), pair],
-        [q, k, v, gram_pre, cross_pre, damping, g, *prior], unit * 40, tables=[where],
+    q, gram_pre = call(
+        states_body, [brick, shaped(CHUNKS, DK, DK)], [k, xb], unit * 10,
+        tables=[where], raw=[w_query],
+        scratch=[pltpu.VMEM((width, DK), BF16), pltpu.SemaphoreType.DMA((1,))],
+    )
+    (part,) = call(targets_body, [blocks], [k, v, g], unit * 8)
+
+    z, u, second_tot = call(
+        solve_body, [blocks, blocks, state],
+        [q, k, gram_pre, part, g, damping, *prior], unit * 40, tables=[where],
     )
     after = exclusive(second_tot, -1)
+    dq, dk_part, dv_part = call(local_body, [blocks, blocks, blocks], [q, k, v, g, z, u], unit * 30)
     dq_all = exchange(dq, PLANE)
 
     seq = lax.axis_size("seq")
@@ -424,9 +494,9 @@
     pieces = call(
         functools.partial(grads_body, seq),
         [shaped(width // seq, DK)] * seq + [shaped(2 * tokens, DK)] * CHUNKS,
-        [k, v, z, u, suf, g, *after, xb], unit * 30, tables=[place],
+        [k, v, dk_part, dv_part, *after, xb], unit * 14, tables=[place],
         scratch=[
-            pltpu.VMEM((CHUNKS * tokens, DK), BF16), pltpu.VMEM((width, DK), F32),
+            pltpu.VMEM((plane, DK), BF16), pltpu.VMEM((width, DK), F32),
             pltpu.VMEM((CHUNKS, 2 * tokens, DK), F32),
         ],
     )

time: 159 us -> 159 us (level)
  waiting for transfers between devices: 50.1 us -> 37.5 us
  Pallas kernels: 33.1 us -> 41 us
  starting transfers between devices: 64.4 us -> 68.8 us
    ppermute x32, waiting for transfers between devices: 50.1 us -> 37.5 us  [shift(): return lax.ppermute(x, axis, pairs)]
    pallas_call x5 -> x9, Pallas kernels: 33.1 us -> 41 us  [call(): pl.pallas_call(kernel, out_shape=tuple(outs), in_specs=[pl.BlockSpec(memo...]
    all_to_all x3, starting transfers between devices: 16.7 us -> 19.7 us  [exchange(): return lax.all_to_all(x, axis, 0, 0)]
    unnamed x60 -> x62, local copies, waits for them, and re-layouts: 2.29 us -> 3.6 us
  transfers between devices with their start and end apart: 35 -> 35, of which waited for: 18 -> 13; matrix products, arithmetic and copies ran while one was open for 3% -> 2% of each run, Pallas kernels for 9% -> 18%
where the time goes in v1:
time: 159 us; the launch traced here: 156 us
  starting transfers between devices  68.8 us (43%)
  Pallas kernels  41 us (26%)
  waiting for transfers between devices  37.5 us (24%)
  local copies, waits for them, and re-layouts  4.17 us (3%)
  other arithmetic  3.76 us (2%)
    ppermute x32, starting transfers between devices, shift(): return lax.ppermute(x, axis, pairs)  49.1 us
    pallas_call x9, Pallas kernels, call(): pl.pallas_call(kernel, out_shape=tuple(outs), in_specs=[pl.BlockSpec(memo...  41 us
    ppermute x32, waiting for transfers between devices, shift(): return lax.ppermute(x, axis, pairs)  37.5 us
    all_to_all x3, starting transfers between devices, exchange(): return lax.all_to_all(x, axis, 0, 0)  19.7 us
    unnamed x62, local copies, waits for them, and re-layouts  3.6 us
  transfers between devices with their start and end apart: 35, of which 13 were waited for; matrix products, arithmetic and copies ran while one was open for 2% of the time, Pallas kernels for 18%

profile of v1, /device:TPU:2, one launch (start us, length us, event | category | flops | bytes accessed | tf_op | source)
XLA Modules:
  0.0 156.4 jit_solution(17347507740543127678)
XLA Ops:
  0.6 1.8 %shard_map.77 = (f32[64,1024]{1,0:T(8,128)}, f32[64,1024]{1,0:T(8,128)}) custom-call(bf16[128,1024]{1,0:T(8,128)(2,1)} %bitcast.21), custom_call_target="tpu_custom_call" | custom-call | bytes 786432 | tf_op jit(solution)/shard_map/pallas_call | solution.py:172
  2.4 3.1 %collective-permute-start.8 = (f32[64,1024]{1,0:T(8,128)}, f32[64,1024]{1,0:T(8,128)S(1)}, u32[]{:S(2)}, u32[]{:S(2)}) collective-permute-start(f32[64,1024]{1,0:T(8,128)} %get-tuple-element.30.refs_3_), channel_id=1, source_target_pairs={{0,6},{2,0},{4,2},{6,4},{1,7},{3,1},{5,3},{7,5},{8,14},{10,8},{12,... | collective-permute-start | bytes 786440 | tf_op jit(solution)/shard_map/ppermute | solution.py:410
  5.5 3.2 %collective-permute-start.4 = (f32[64,1024]{1,0:T(8,128)}, f32[64,1024]{1,0:T(8,128)S(1)}, u32[]{:S(2)}, u32[]{:S(2)}) collective-permute-start(f32[64,1024]{1,0:T(8,128)} %get-tuple-element.31.refs_4_), channel_id=1, source_target_pairs={{0,6},{2,0},{4,2},{6,4},{1,7},{3,1},{5,3},{7,5},{8,14},{10,8},{12,... | collective-permute-start | bytes 786440 | tf_op jit(solution)/shard_map/ppermute | solution.py:410
  8.7 3.8 %collective-permute-done.8.refs_13_ = f32[64,1024]{1,0:T(8,128)S(1)} collective-permute-done((f32[64,1024]{1,0:T(8,128)}, f32[64,1024]{1,0:T(8,128)S(1)}, u32[]{:S(2)}, u32[]{:S(2)}) %collective-permute-start.8) | collective-permute-done | bytes 262176 | tf_op jit(solution)/shard_map/ppermute | solution.py:410
  12.5 3.6 %collective-permute-done.2.refs_7_ = f32[64,1024]{1,0:T(8,128)S(1)} collective-permute-done((f32[64,1024]{1,0:T(8,128)}, f32[64,1024]{1,0:T(8,128)S(1)}, u32[]{:S(2)}, u32[]{:S(2)}) %collective-permute-start.2) | collective-permute-done | bytes 262176 | tf_op jit(solution)/shard_map/ppermute | solution.py:410
  17.0 3.6 %collective-permute-start.12 = (f32[64,1024]{1,0:T(8,128)S(1)}, f32[64,1024]{1,0:T(8,128)S(1)}, u32[]{:S(2)}, u32[]{:S(2)}) collective-permute-start(f32[64,1024]{1,0:T(8,128)S(1)} %collective-permute-done.4.refs_9_), channel_id=1, source_target_pairs={{0,6},{2,0},{4,2},{6,4},{1,7},{3,1},{5,3},{7,5},{8,14},{10,8},{12,... | collective-permute-start | bytes 786440 | tf_op jit(solution)/shard_map/ppermute | solution.py:410
  21.2 4.8 %collective-permute-done.10.refs_15_ = f32[64,1024]{1,0:T(8,128)S(1)} collective-permute-done((f32[64,1024]{1,0:T(8,128)S(1)}, f32[64,1024]{1,0:T(8,128)S(1)}, u32[]{:S(2)}, u32[]{:S(2)}) %collective-permute-start.10) | collective-permute-done | bytes 262176 | tf_op jit(solution)/shard_map/ppermute | solution.py:410
  27.1 1.8 %shard_map.80 = f32[8,128,128]{2,1,0:T(8,128)} custom-call(bf16[128,1024]{1,0:T(8,128)(2,1)} %bitcast.19), custom_call_target="tpu_custom_call" | custom-call | bytes 786432 | tf_op jit(solution)/shard_map/pallas_call | solution.py:172
  29.9 5.0 %shard_map.78 = (bf16[1024,1024]{1,0:T(8,128)(2,1)}, bf16[1024,128]{1,0:T(8,128)(2,1)}, bf16[1024,128]{1,0:T(8,128)(2,1)}, f32[200,128]{1,0:T(8,128)}) custom-call(s32[9]{0:T(128)} %stack.48.refs_0_, bf16[1024,1024]{1,0:T(8,128)(2,1)} %refs_3_.1, bf16[1024,1024]{1,0:T(8,128)(2,1)} %refs_4_.1, f32[64,1024]{1,0:T(8,128)} %get-tuple-element.30.refs_3_, ...), custom_call_target="tpu_custom_call" | custom-call | flops 939524096 | bytes 6918144 | tf_op jit(solution)/shard_map/pallas_call | solution.py:172
  35.0 3.8 %all-to-all-start = ((f32[8,128,128]{2,1,0:T(8,128)}), f32[8,128,128]{2,1,0:T(8,128)S(1)}, u32[]{:S(2)}, u32[]{:S(2)}) async-start(f32[8,128,128]{2,1,0:T(8,128)} %shard_map.80), calls=%async_computation | async-start | bytes 1048576 | tf_op jit(solution)/shard_map/all_to_all | solution.py:420
  38.8 5.2 %collective-permute-start.15 = (f32[200,128]{1,0:T(8,128)}, f32[200,128]{1,0:T(8,128)S(1)}, u32[]{:S(2)}, u32[]{:S(2)}) collective-permute-start(f32[200,128]{1,0:T(8,128)} %get-tuple-element.37), channel_id=1, source_target_pairs={{0,16},{8,24},{16,32},{24,40},{32,48},{40,56},{1,17},{9,25},{17,33... | collective-permute-start | bytes 307208 | tf_op jit(solution)/shard_map/ppermute | solution.py:410
  44.0 3.8 %collective-permute-start.14 = (f32[200,128]{1,0:T(8,128)}, f32[200,128]{1,0:T(8,128)S(1)}, u32[]{:S(2)}, u32[]{:S(2)}) collective-permute-start(f32[200,128]{1,0:T(8,128)} %get-tuple-element.37), channel_id=1, source_target_pairs={{0,8},{8,16},{16,24},{24,32},{32,40},{40,48},{48,56},{1,9},{9,17},... | collective-permute-start | bytes 307208 | tf_op jit(solution)/shard_map/ppermute | solution.py:410
  47.8 2.8 %collective-permute-done.14.refs_7_ = f32[200,128]{1,0:T(8,128)S(1)} collective-permute-done((f32[200,128]{1,0:T(8,128)}, f32[200,128]{1,0:T(8,128)S(1)}, u32[]{:S(2)}, u32[]{:S(2)}) %collective-permute-start.14) | collective-permute-done | bytes 102432 | tf_op jit(solution)/shard_map/ppermute | solution.py:410
  51.6 8.6 %collective-permute-start.17 = (f32[200,128]{1,0:T(8,128)S(1)}, f32[200,128]{1,0:T(8,128)S(1)}, u32[]{:S(2)}, u32[]{:S(2)}) collective-permute-start(f32[200,128]{1,0:T(8,128)S(1)} %add_add_fusion.2), channel_id=1, source_target_pairs={{0,48},{8,56},{1,49},{9,57},{2,50},{10,58},{3,51},{11,59},{4,52},{... | collective-permute-start | bytes 307208 | tf_op jit(solution)/shard_map/ppermute | solution.py:410
  61.7 3.8 %shard_map.79 = (bf16[1024,128]{1,0:T(8,128)(2,1)}, f32[8,128,128]{2,1,0:T(8,128)}) custom-call(s32[9]{0:T(128)} %stack.48.refs_0_, bf16[1024,1024]{1,0:T(8,128)(2,1)} %refs_2_.3, bf16[1024,128]{1,0:T(8,128)(2,1)} %get-tuple-element.32.refs_2_.refs_0_.refs_1_, bf16[1024,1024]{1,0:T(8,128)(2,1)} %get-tuple-element.33.refs_3_.refs_9_), custom_call_target="tpu_custom_call" | custom-call | flops 335544320 | bytes 3145728 | tf_op jit(solution)/shard_map/pallas_call | solution.py:172
  66.4 3.6 %shard_map.81.refs_4_ = f32[8,128,128]{2,1,0:T(8,128)} custom-call(bf16[1024,128]{1,0:T(8,128)(2,1)} %get-tuple-element.32.refs_2_.refs_0_.refs_1_, bf16[1024,128]{1,0:T(8,128)(2,1)} %get-tuple-element.35.refs_1_.refs_2_, f32[8,128,128]{2,1,0:T(8,128)} %copy-done.1), custom_call_target="tpu_custom_call" | custom-call | flops 268435456 | bytes 1572864 | tf_op jit(solution)/shard_map/pallas_call | solution.py:172
  70.7 6.7 %shard_map.82 = (f32[8,128,128]{2,1,0:T(8,128)}, f32[8,128,128]{2,1,0:T(8,128)}, f32[200,128]{1,0:T(8,128)}) custom-call(s32[9]{0:T(128)} %stack.48.refs_0_, bf16[1024,128]{1,0:T(8,128)(2,1)} %get-tuple-element.34.refs_1_.refs_0_, bf16[1024,128]{1,0:T(8,128)(2,1)} %get-tuple-element.32.refs_2_.refs_0_.refs_1_, f32[8,128,128]{2,1,0:T(8,128)} %get-tuple-element.39.refs_3_, ...), custom_call_target="tpu_custom_call" | custom-call | flops 1342177280 | bytes 3661824 | tf_op jit(solution)/shard_map/pallas_call | solution.py:172
  80.0 6.3 %shard_map.83 = (f32[8,128,128]{2,1,0:T(8,128)}, f32[8,128,128]{2,1,0:T(8,128)}, f32[8,128,128]{2,1,0:T(8,128)}) custom-call(bf16[1024,128]{1,0:T(8,128)(2,1)} %get-tuple-element.34.refs_1_.refs_0_, bf16[1024,128]{1,0:T(8,128)(2,1)} %get-tuple-element.32.refs_2_.refs_0_.refs_1_, bf16[1024,128]{1,0:T(8,128)(2,1)} %get-tuple-element.35.refs_1_.refs_2_, ...), custom_call_target="tpu_custom_call" | custom-call | flops 1006632960 | bytes 3932160 | tf_op jit(solution)/shard_map/pallas_call | solution.py:172
  86.4 4.4 %all-to-all-start.1 = ((f32[8,128,128]{2,1,0:T(8,128)}), f32[8,128,128]{2,1,0:T(8,128)S(1)}, u32[]{:S(2)}, u32[]{:S(2)}) async-start(f32[8,128,128]{2,1,0:T(8,128)} %get-tuple-element.42), calls=%async_computation.1 | async-start | bytes 1048576 | tf_op jit(solution)/shard_map/all_to_all | solution.py:420
  94.0 8.6 %collective-permute-done.21.refs_8_ = f32[200,128]{1,0:T(8,128)S(1)} collective-permute-done((f32[200,128]{1,0:T(8,128)S(1)}, f32[200,128]{1,0:T(8,128)S(1)}, u32[]{:S(2)}, u32[]{:S(2)}) %collective-permute-start.21) | collective-permute-done | bytes 102432 | tf_op jit(solution)/shard_map/ppermute | solution.py:410
  103.4 5.0 %shard_map.84 = (f32[256,128]{1,0:T(8,128)}, f32[256,128]{1,0:T(8,128)}, f32[256,128]{1,0:T(8,128)}, f32[256,128]{1,0:T(8,128)}, f32[256,128]{1,0:T(8,128)}, /*i...) custom-call(s32[2]{0:T(128)} %pad_add_fusion.refs_0_, ...), custom_call_target="tpu_custom_call" | custom-call | flops 469762048 | bytes 5652480 | tf_op jit(solution)/shard_map/pallas_call | solution.py:172
  108.4 1.6 %collective-permute-start.29 = (f32[256,128]{1,0:T(8,128)}, f32[256,128]{1,0:T(8,128)S(1)}, u32[]{:S(2)}, u32[]{:S(2)}) collective-permute-start(f32[256,128]{1,0:T(8,128)} %get-tuple-element.55), channel_id=1, source_target_pairs={{0,64},{64,128},{128,192},{192,0},{1,65},{65,129},{129,193},{193,1... | collective-permute-start | bytes 393224 | tf_op jit(solution)/shard_map/ppermute | solution.py:410
  111.1 2.2 %collective-permute-start.31 = (f32[256,128]{1,0:T(8,128)}, f32[256,128]{1,0:T(8,128)S(1)}, u32[]{:S(2)}, u32[]{:S(2)}) collective-permute-start(f32[256,128]{1,0:T(8,128)} %get-tuple-element.57), channel_id=1, source_target_pairs={{0,192},{64,0},{128,64},{192,128},{1,193},{65,1},{129,65},{193,129... | collective-permute-start | bytes 393224 | tf_op jit(solution)/shard_map/ppermute | solution.py:410
  113.2 1.6 %collective-permute-start.23 = (f32[256,128]{1,0:T(8,128)}, f32[256,128]{1,0:T(8,128)S(1)}, u32[]{:S(2)}, u32[]{:S(2)}) collective-permute-start(f32[256,128]{1,0:T(8,128)} %get-tuple-element.48), channel_id=1, source_target_pairs={{0,2},{1,3},{2,4},{3,5},{4,6},{5,7},{6,0},{7,1},{8,10},{9,11},{10,... | collective-permute-start | bytes 393224 | tf_op jit(solution)/shard_map/ppermute | solution.py:410
  114.8 3.2 %collective-permute-done.30 = f32[256,128]{1,0:T(8,128)S(1)} collective-permute-done((f32[256,128]{1,0:T(8,128)}, f32[256,128]{1,0:T(8,128)S(1)}, u32[]{:S(2)}, u32[]{:S(2)}) %collective-permute-start.30) | collective-permute-done | bytes 131104 | tf_op jit(solution)/shard_map/ppermute | solution.py:410
  118.9 1.6 %add_add_fusion = f32[256,128]{1,0:T(8,128)} fusion(f32[256,128]{1,0:T(8,128)S(1)} %collective-permute-done.31, f32[256,128]{1,0:T(8,128)S(1)} %collective-permute-done.30, f32[256,128]{1,0:T(8,128)} %get-tuple-element.54, f32[256,128]{1,0:T(8,128)S(1)} %collective-permute-done.29), kind=kLoop, calls=%fused_computation | loop fusion | flops 98304 | bytes 655360 | tf_op jit(solution)/shard_map/add | solution.py:504
  120.5 11.4 %all-to-all-start.2 = ((f32[64,4,128]{2,1,0:T(4,128)}), f32[64,4,128]{2,1,0:T(4,128)S(1)}, u32[]{:S(2)}, u32[]{:S(2)}) async-start(f32[64,4,128]{2,1,0:T(4,128)} %bitcast.13), calls=%async_computation.2 | async-start | bytes 262144 | tf_op jit(solution)/shard_map/all_to_all | solution.py:420
  133.3 2.7 %collective-permute-start.25 = (f32[256,128]{1,0:T(8,128)}, f32[256,128]{1,0:T(8,128)S(1)}, u32[]{:S(2)}, u32[]{:S(2)}) collective-permute-start(f32[256,128]{1,0:T(8,128)} %get-tuple-element.50), channel_id=1, source_target_pairs={{0,4},{1,5},{2,6},{3,7},{4,0},{5,1},{6,2},{7,3},{8,12},{9,13},{10,... | collective-permute-start | bytes 393224 | tf_op jit(solution)/shard_map/ppermute | solution.py:410
  136.0 2.1 %collective-permute-start.26 = (f32[256,128]{1,0:T(8,128)}, f32[256,128]{1,0:T(8,128)S(1)}, u32[]{:S(2)}, u32[]{:S(2)}) collective-permute-start(f32[256,128]{1,0:T(8,128)} %get-tuple-element.51), channel_id=1, source_target_pairs={{0,5},{1,6},{2,7},{3,0},{4,1},{5,2},{6,3},{7,4},{8,13},{9,14},{10,... | collective-permute-start | bytes 393224 | tf_op jit(solution)/shard_map/ppermute | solution.py:410
  139.3 4.3 %collective-permute-done.25.refs_9_ = f32[256,128]{1,0:T(8,128)S(1)} collective-permute-done((f32[256,128]{1,0:T(8,128)}, f32[256,128]{1,0:T(8,128)S(1)}, u32[]{:S(2)}, u32[]{:S(2)}) %collective-permute-start.25) | collective-permute-done | bytes 131104 | tf_op jit(solution)/shard_map/ppermute | solution.py:410
  143.6 2.2 %collective-permute-done.26.refs_10_ = f32[256,128]{1,0:T(8,128)S(1)} collective-permute-done((f32[256,128]{1,0:T(8,128)}, f32[256,128]{1,0:T(8,128)S(1)}, u32[]{:S(2)}, u32[]{:S(2)}) %collective-permute-start.26) | collective-permute-done | bytes 131104 | tf_op jit(solution)/shard_map/ppermute | solution.py:410
  148.8 7.0 %shard_map.85 = bf16[128,1024]{1,0:T(8,128)(2,1)} custom-call(s32[2]{0:T(128)} %pad_add_fusion.refs_0_, f32[8,128,128]{2,1,0:T(8,128)} %copy-done, bf16[1024,1024]{1,0:T(8,128)(2,1)} %refs_2_.3, bf16[1024,1024]{1,0:T(8,128)(2,1)} %refs_3_.1, bf16[1024,1024]{1,0:T(8,128)(2,1)} %refs_4_.1, f32[256,128]{1,0:T(8,128)} %get-tuple-element.46.refs_5_, ...), custom_call_target="tpu_custom_call" | custom-call | flops 805306368 | bytes 8126464 | tf_op jit(solution)/shard_map/pallas_call | solution.py:172
  (115 shorter events, 22.0 us)
Async XLA Ops:
  2.4 10.1 %collective-permute-start.8 = (f32[64,1024]{1,0:T(8,128)}, f32[64,1024]{1,0:T(8,128)S(1)}, u32[]{:S(2)}, u32[]{:S(2)}) collective-permute-start(f32[64,1024]{1,0:T(8,128)} %get-tuple-element.30.refs_3_), channel_id=1, source_target_pairs={{0,6},{2,0},{4,2},{6,4},{1,7},{3,1},{5,3},{7,5},{8,14},{10,8},{12,... | collective-permute-start | bytes 786440 | tf_op jit(solution)/shard_map/ppermute | solution.py:410
  5.5 10.6 %collective-permute-start.2 = (f32[64,1024]{1,0:T(8,128)}, f32[64,1024]{1,0:T(8,128)S(1)}, u32[]{:S(2)}, u32[]{:S(2)}) collective-permute-start(f32[64,1024]{1,0:T(8,128)} %get-tuple-element.30.refs_3_), channel_id=1, source_target_pairs={{0,2},{2,4},{4,6},{6,0},{1,3},{3,5},{5,7},{7,1},{8,10},{10,12},{12... | collective-permute-start | bytes 786440 | tf_op jit(solution)/shard_map/ppermute | solution.py:410
  5.5 10.6 %collective-permute-start = (f32[64,1024]{1,0:T(8,128)}, f32[64,1024]{1,0:T(8,128)S(1)}, u32[]{:S(2)}, u32[]{:S(2)}) collective-permute-start(f32[64,1024]{1,0:T(8,128)} %get-tuple-element.30.refs_3_), channel_id=1, source_target_pairs={{0,1},{1,0},{2,3},{3,2},{4,5},{5,4},{6,7},{7,6},{8,9},{9,8},{10,11... | collective-permute-start | bytes 786440 | tf_op jit(solution)/shard_map/ppermute | solution.py:410
  5.5 11.5 %collective-permute-start.4 = (f32[64,1024]{1,0:T(8,128)}, f32[64,1024]{1,0:T(8,128)S(1)}, u32[]{:S(2)}, u32[]{:S(2)}) collective-permute-start(f32[64,1024]{1,0:T(8,128)} %get-tuple-element.31.refs_4_), channel_id=1, source_target_pairs={{0,6},{2,0},{4,2},{6,4},{1,7},{3,1},{5,3},{7,5},{8,14},{10,8},{12,... | collective-permute-start | bytes 786440 | tf_op jit(solution)/shard_map/ppermute | solution.py:410
  8.7 11.8 %collective-permute-start.6 = (f32[64,1024]{1,0:T(8,128)}, f32[64,1024]{1,0:T(8,128)S(1)}, u32[]{:S(2)}, u32[]{:S(2)}) collective-permute-start(f32[64,1024]{1,0:T(8,128)} %get-tuple-element.31.refs_4_), channel_id=1, source_target_pairs={{0,2},{2,4},{4,6},{6,0},{1,3},{3,5},{5,7},{7,1},{8,10},{10,12},{12... | collective-permute-start | bytes 786440 | tf_op jit(solution)/shard_map/ppermute | solution.py:410
  12.5 8.1 %collective-permute-start.1 = (f32[64,1024]{1,0:T(8,128)}, f32[64,1024]{1,0:T(8,128)S(1)}, u32[]{:S(2)}, u32[]{:S(2)}) collective-permute-start(f32[64,1024]{1,0:T(8,128)} %get-tuple-element.31.refs_4_), channel_id=1, source_target_pairs={{0,1},{1,0},{2,3},{3,2},{4,5},{5,4},{6,7},{7,6},{8,9},{9,8},{10,11... | collective-permute-start | bytes 786440 | tf_op jit(solution)/shard_map/ppermute | solution.py:410
  16.1 9.9 %collective-permute-start.10 = (f32[64,1024]{1,0:T(8,128)S(1)}, f32[64,1024]{1,0:T(8,128)S(1)}, u32[]{:S(2)}, u32[]{:S(2)}) collective-permute-start(f32[64,1024]{1,0:T(8,128)S(1)} %collective-permute-done.2.refs_7_), channel_id=1, source_target_pairs={{0,2},{2,4},{4,6},{6,0},{1,3},{3,5},{5,7},{7,1},{8,10},{10,12},{12... | collective-permute-start | bytes 786440 | tf_op jit(solution)/shard_map/ppermute | solution.py:410
  17.0 9.0 %collective-permute-start.12 = (f32[64,1024]{1,0:T(8,128)S(1)}, f32[64,1024]{1,0:T(8,128)S(1)}, u32[]{:S(2)}, u32[]{:S(2)}) collective-permute-start(f32[64,1024]{1,0:T(8,128)S(1)} %collective-permute-done.4.refs_9_), channel_id=1, source_target_pairs={{0,6},{2,0},{4,2},{6,4},{1,7},{3,1},{5,3},{7,5},{8,14},{10,8},{12,... | collective-permute-start | bytes 786440 | tf_op jit(solution)/shard_map/ppermute | solution.py:410
  20.6 8.3 %collective-permute-start.3 = (f32[64,1024]{1,0:T(8,128)S(1)}, f32[64,1024]{1,0:T(8,128)S(1)}, u32[]{:S(2)}, u32[]{:S(2)}) collective-permute-start(f32[64,1024]{1,0:T(8,128)S(1)} %collective-permute-done.2.refs_7_), channel_id=1, source_target_pairs={{0,1},{1,0},{2,3},{3,2},{4,5},{5,4},{6,7},{7,6},{8,9},{9,8},{10,11... | collective-permute-start | bytes 786440 | tf_op jit(solution)/shard_map/ppermute | solution.py:410
  20.6 8.4 %collective-permute-start.5 = (f32[64,1024]{1,0:T(8,128)S(1)}, f32[64,1024]{1,0:T(8,128)S(1)}, u32[]{:S(2)}, u32[]{:S(2)}) collective-permute-start(f32[64,1024]{1,0:T(8,128)S(1)} %collective-permute-done.4.refs_9_), channel_id=1, source_target_pairs={{0,1},{1,0},{2,3},{3,2},{4,5},{5,4},{6,7},{7,6},{8,9},{9,8},{10,11... | collective-permute-start | bytes 786440 | tf_op jit(solution)/shard_map/ppermute | solution.py:410
  21.1 7.8 %collective-permute-start.7 = (f32[64,1024]{1,0:T(8,128)S(1)}, f32[64,1024]{1,0:T(8,128)S(1)}, u32[]{:S(2)}, u32[]{:S(2)}) collective-permute-start(f32[64,1024]{1,0:T(8,128)S(1)} %collective-permute-done.6.refs_11_), channel_id=1, source_target_pairs={{0,1},{1,0},{2,3},{3,2},{4,5},{5,4},{6,7},{7,6},{8,9},{9,8},{10,11... | collective-permute-start | bytes 786440 | tf_op jit(solution)/shard_map/ppermute | solution.py:410
  35.0 30.6 %all-to-all-start = ((f32[8,128,128]{2,1,0:T(8,128)}), f32[8,128,128]{2,1,0:T(8,128)S(1)}, u32[]{:S(2)}, u32[]{:S(2)}) async-start(f32[8,128,128]{2,1,0:T(8,128)} %shard_map.80), calls=%async_computation | async-start | bytes 1048576 | tf_op jit(solution)/shard_map/all_to_all | solution.py:420
  38.8 9.0 %collective-permute-start.15 = (f32[200,128]{1,0:T(8,128)}, f32[200,128]{1,0:T(8,128)S(1)}, u32[]{:S(2)}, u32[]{:S(2)}) collective-permute-start(f32[200,128]{1,0:T(8,128)} %get-tuple-element.37), channel_id=1, source_target_pairs={{0,16},{8,24},{16,32},{24,40},{32,48},{40,56},{1,17},{9,25},{17,33... | collective-permute-start | bytes 307208 | tf_op jit(solution)/shard_map/ppermute | solution.py:410
  44.0 6.7 %collective-permute-start.14 = (f32[200,128]{1,0:T(8,128)}, f32[200,128]{1,0:T(8,128)S(1)}, u32[]{:S(2)}, u32[]{:S(2)}) collective-permute-start(f32[200,128]{1,0:T(8,128)} %get-tuple-element.37), channel_id=1, source_target_pairs={{0,8},{8,16},{16,24},{24,32},{32,40},{40,48},{48,56},{1,9},{9,17},... | collective-permute-start | bytes 307208 | tf_op jit(solution)/shard_map/ppermute | solution.py:410
  51.6 18.4 %collective-permute-start.17 = (f32[200,128]{1,0:T(8,128)S(1)}, f32[200,128]{1,0:T(8,128)S(1)}, u32[]{:S(2)}, u32[]{:S(2)}) collective-permute-start(f32[200,128]{1,0:T(8,128)S(1)} %add_add_fusion.2), channel_id=1, source_target_pairs={{0,48},{8,56},{1,49},{9,57},{2,50},{10,58},{3,51},{11,59},{4,52},{... | collective-permute-start | bytes 307208 | tf_op jit(solution)/shard_map/ppermute | solution.py:410
  60.2 9.8 %collective-permute-start.16 = (f32[200,128]{1,0:T(8,128)S(1)}, f32[200,128]{1,0:T(8,128)S(1)}, u32[]{:S(2)}, u32[]{:S(2)}) collective-permute-start(f32[200,128]{1,0:T(8,128)S(1)} %add_add_fusion.2), channel_id=1, source_target_pairs={{0,24},{8,32},{16,40},{24,48},{32,56},{1,25},{9,33},{17,41},{25,49... | collective-permute-start | bytes 307208 | tf_op jit(solution)/shard_map/ppermute | solution.py:410
  77.4 13.4 %collective-permute-start.19 = (f32[200,128]{1,0:T(8,128)}, f32[200,128]{1,0:T(8,128)S(1)}, u32[]{:S(2)}, u32[]{:S(2)}) collective-permute-start(f32[200,128]{1,0:T(8,128)} %get-tuple-element.45), channel_id=1, source_target_pairs={{16,0},{24,8},{32,16},{40,24},{48,32},{56,40},{17,1},{25,9},{33,17... | collective-permute-start | bytes 307208 | tf_op jit(solution)/shard_map/ppermute | solution.py:410
  78.7 12.1 %collective-permute-start.18 = (f32[200,128]{1,0:T(8,128)}, f32[200,128]{1,0:T(8,128)S(1)}, u32[]{:S(2)}, u32[]{:S(2)}) collective-permute-start(f32[200,128]{1,0:T(8,128)} %get-tuple-element.45), channel_id=1, source_target_pairs={{8,0},{16,8},{24,16},{32,24},{40,32},{48,40},{56,48},{9,1},{17,9},... | collective-permute-start | bytes 307208 | tf_op jit(solution)/shard_map/ppermute | solution.py:410
  86.4 34.2 %all-to-all-start.1 = ((f32[8,128,128]{2,1,0:T(8,128)}), f32[8,128,128]{2,1,0:T(8,128)S(1)}, u32[]{:S(2)}, u32[]{:S(2)}) async-start(f32[8,128,128]{2,1,0:T(8,128)} %get-tuple-element.42), calls=%async_computation.1 | async-start | bytes 1048576 | tf_op jit(solution)/shard_map/all_to_all | solution.py:420
  90.9 11.7 %collective-permute-start.21 = (f32[200,128]{1,0:T(8,128)S(1)}, f32[200,128]{1,0:T(8,128)S(1)}, u32[]{:S(2)}, u32[]{:S(2)}) collective-permute-start(f32[200,128]{1,0:T(8,128)S(1)} %add_add_fusion.1), channel_id=1, source_target_pairs={{48,0},{56,8},{49,1},{57,9},{50,2},{58,10},{51,3},{59,11},{52,4},{... | collective-permute-start | bytes 307208 | tf_op jit(solution)/shard_map/ppermute | solution.py:410
  92.2 10.6 %collective-permute-start.20 = (f32[200,128]{1,0:T(8,128)S(1)}, f32[200,128]{1,0:T(8,128)S(1)}, u32[]{:S(2)}, u32[]{:S(2)}) collective-permute-start(f32[200,128]{1,0:T(8,128)S(1)} %add_add_fusion.1), channel_id=1, source_target_pairs={{24,0},{32,8},{40,16},{48,24},{56,32},{25,1},{33,9},{41,17},{49,25... | collective-permute-start | bytes 307208 | tf_op jit(solution)/shard_map/ppermute | solution.py:410
  108.4 6.5 %collective-permute-start.29 = (f32[256,128]{1,0:T(8,128)}, f32[256,128]{1,0:T(8,128)S(1)}, u32[]{:S(2)}, u32[]{:S(2)}) collective-permute-start(f32[256,128]{1,0:T(8,128)} %get-tuple-element.55), channel_id=1, source_target_pairs={{0,64},{64,128},{128,192},{192,0},{1,65},{65,129},{129,193},{193,1... | collective-permute-start | bytes 393224 | tf_op jit(solution)/shard_map/ppermute | solution.py:410
  109.9 8.1 %collective-permute-start.30 = (f32[256,128]{1,0:T(8,128)}, f32[256,128]{1,0:T(8,128)S(1)}, u32[]{:S(2)}, u32[]{:S(2)}) collective-permute-start(f32[256,128]{1,0:T(8,128)} %get-tuple-element.56), channel_id=1, source_target_pairs={{0,128},{64,192},{128,0},{192,64},{1,129},{65,193},{129,1},{193,65... | collective-permute-start | bytes 393224 | tf_op jit(solution)/shard_map/ppermute | solution.py:410
  111.1 7.9 %collective-permute-start.31 = (f32[256,128]{1,0:T(8,128)}, f32[256,128]{1,0:T(8,128)S(1)}, u32[]{:S(2)}, u32[]{:S(2)}) collective-permute-start(f32[256,128]{1,0:T(8,128)} %get-tuple-element.57), channel_id=1, source_target_pairs={{0,192},{64,0},{128,64},{192,128},{1,193},{65,1},{129,65},{193,129... | collective-permute-start | bytes 393224 | tf_op jit(solution)/shard_map/ppermute | solution.py:410
  113.2 24.9 %collective-permute-start.22 = (f32[256,128]{1,0:T(8,128)}, f32[256,128]{1,0:T(8,128)S(1)}, u32[]{:S(2)}, u32[]{:S(2)}) collective-permute-start(f32[256,128]{1,0:T(8,128)} %get-tuple-element.47), channel_id=1, source_target_pairs={{0,1},{1,2},{2,3},{3,4},{4,5},{5,6},{6,7},{7,0},{8,9},{9,10},{10,1... | collective-permute-start | bytes 393224 | tf_op jit(solution)/shard_map/ppermute | solution.py:410
  113.2 26.1 %collective-permute-start.23 = (f32[256,128]{1,0:T(8,128)}, f32[256,128]{1,0:T(8,128)S(1)}, u32[]{:S(2)}, u32[]{:S(2)}) collective-permute-start(f32[256,128]{1,0:T(8,128)} %get-tuple-element.48), channel_id=1, source_target_pairs={{0,2},{1,3},{2,4},{3,5},{4,6},{5,7},{6,0},{7,1},{8,10},{9,11},{10,... | collective-permute-start | bytes 393224 | tf_op jit(solution)/shard_map/ppermute | solution.py:410
  120.5 35.2 %all-to-all-start.2 = ((f32[64,4,128]{2,1,0:T(4,128)}), f32[64,4,128]{2,1,0:T(4,128)S(1)}, u32[]{:S(2)}, u32[]{:S(2)}) async-start(f32[64,4,128]{2,1,0:T(4,128)} %bitcast.13), calls=%async_computation.2 | async-start | bytes 262144 | tf_op jit(solution)/shard_map/all_to_all | solution.py:420
  132.0 7.3 %collective-permute-start.24 = (f32[256,128]{1,0:T(8,128)}, f32[256,128]{1,0:T(8,128)S(1)}, u32[]{:S(2)}, u32[]{:S(2)}) collective-permute-start(f32[256,128]{1,0:T(8,128)} %get-tuple-element.49), channel_id=1, source_target_pairs={{0,3},{1,4},{2,5},{3,6},{4,7},{5,0},{6,1},{7,2},{8,11},{9,12},{10,... | collective-permute-start | bytes 393224 | tf_op jit(solution)/shard_map/ppermute | solution.py:410
  133.3 10.3 %collective-permute-start.25 = (f32[256,128]{1,0:T(8,128)}, f32[256,128]{1,0:T(8,128)S(1)}, u32[]{:S(2)}, u32[]{:S(2)}) collective-permute-start(f32[256,128]{1,0:T(8,128)} %get-tuple-element.50), channel_id=1, source_target_pairs={{0,4},{1,5},{2,6},{3,7},{4,0},{5,1},{6,2},{7,3},{8,12},{9,13},{10,... | collective-permute-start | bytes 393224 | tf_op jit(solution)/shard_map/ppermute | solution.py:410
  136.0 9.8 %collective-permute-start.26 = (f32[256,128]{1,0:T(8,128)}, f32[256,128]{1,0:T(8,128)S(1)}, u32[]{:S(2)}, u32[]{:S(2)}) collective-permute-start(f32[256,128]{1,0:T(8,128)} %get-tuple-element.51), channel_id=1, source_target_pairs={{0,5},{1,6},{2,7},{3,0},{4,1},{5,2},{6,3},{7,4},{8,13},{9,14},{10,... | collective-permute-start | bytes 393224 | tf_op jit(solution)/shard_map/ppermute | solution.py:410
  138.1 8.6 %collective-permute-start.27 = (f32[256,128]{1,0:T(8,128)}, f32[256,128]{1,0:T(8,128)S(1)}, u32[]{:S(2)}, u32[]{:S(2)}) collective-permute-start(f32[256,128]{1,0:T(8,128)} %get-tuple-element.52), channel_id=1, source_target_pairs={{0,6},{1,7},{2,0},{3,1},{4,2},{5,3},{6,4},{7,5},{8,14},{9,15},{10,... | collective-permute-start | bytes 393224 | tf_op jit(solution)/shard_map/ppermute | solution.py:410
  139.3 8.8 %collective-permute-start.28 = (f32[256,128]{1,0:T(8,128)}, f32[256,128]{1,0:T(8,128)S(1)}, u32[]{:S(2)}, u32[]{:S(2)}) collective-permute-start(f32[256,128]{1,0:T(8,128)} %get-tuple-element.53), channel_id=1, source_target_pairs={{0,7},{1,0},{2,1},{3,2},{4,3},{5,4},{6,5},{7,6},{8,15},{9,8},{10,9... | collective-permute-start | bytes 393224 | tf_op jit(solution)/shard_map/ppermute | solution.py:410
  (34 other events, 234.6 us)

commit v2 on v1

--- a/solution.py
+++ b/solution.py
@@ -81,28 +81,30 @@
     return jnp.transpose(jnp.broadcast_to(column, (size, size)))
 
 
-def apply_all(vectors, keys, grams, scale2, damp):
-    splits = [halves(p) for p in vectors]
-    cats = [jnp.concatenate(s, axis=1) for s in splits]
-    raw = [nt(c, twice_wide(k)) for c, k in zip(cats, keys)]
-    prior = []
-    for c, s, g in zip(cats, splits, grams):
-        g_hi, g_lo = halves(g)
-        prior.append(nn(c, twice_tall(g_hi)) + nn(s[0], g_lo))
-    inner = [wide(r * m) for r, m in zip(raw, scale2)]
+def system(key, gram):
+    turned = jnp.transpose(key)
+    hi, lo = halves(gram)
+    upper = jnp.concatenate([turned, hi, lo], axis=1)
+    lower = jnp.concatenate([turned, hi, jnp.zeros_like(lo)], axis=1)
+    return jnp.concatenate([upper, lower], axis=0), twice_tall(key)
+
+
+def apply_all(vectors, systems, scale2, damp):
+    firsts = [nn(wide(p), s[0]) for p, s in zip(vectors, systems)]
+    inner = [wide(f[:, :DK] * m) for f, m in zip(firsts, scale2)]
     return [
-        o + nn(i, twice_tall(k)) + damp * p
-        for o, i, k, p in zip(prior, inner, keys, vectors)
+        nn(i, s[1]) + (f[:, DK : 2 * DK] + f[:, 2 * DK :]) + damp * p
+        for i, s, f, p in zip(inner, systems, firsts, vectors)
     ]
 
 
-def conjugate(targets, keys, grams, scale2, damp):
+def conjugate(targets, systems, scale2, damp):
     residual = list(targets)
     direction = list(targets)
     norm_now = [rowsum(r * r) for r in residual]
     solution = None
     for sweep in range(ITERS):
-        image = apply_all(direction, keys, grams, scale2, damp)
+        image = apply_all(direction, systems, scale2, damp)
         step = [n / (rowsum(p * w) + EPSILON) for n, p, w in zip(norm_now, direction, image)]
         moved = [a * p for a, p in zip(step, direction)]
         solution = moved if solution is None else [x + m for x, m in zip(solution, moved)]
@@ -117,7 +119,7 @@
     return solution
 
 
-def staged(body, counts, tables, *refs):
+def staged(body, counts, late, tables, *refs):
     n_in, n_out = counts
     sources, refs = refs[:n_in], refs[n_in:]
     targets, refs = refs[:n_out], refs[n_out:]
@@ -129,15 +131,24 @@
     stores = [
         pltpu.make_async_copy(m, t, out_sems.at[n]) for n, (m, t) in enumerate(zip(made, targets))
     ]
-    for load in loads:
-        load.start()
-    arrived, sent = set(), set()
+    begun, arrived, sent = set(), set(), set()
+
+    def begin(n):
+        if n not in begun:
+            begun.add(n)
+            loads[n].start()
+
+    for n in range(n_in - late):
+        begin(n)
 
     def need(n):
+        begin(n)
         if n not in arrived:
             arrived.add(n)
             loads[n].wait()
         return held[n]
+
+    need.begin = begin
 
     def put(n):
         sent.add(n)
@@ -157,29 +168,32 @@
     return jax.ShapeDtypeStruct(dims, dtype)
 
 
-def call(body, outs, args, flops, tables=(), raw=(), scratch=()):
+ANYWHERE = pl.BlockSpec(memory_space=pl.ANY)
+
+
+def call(body, outs, args, flops, tables=(), raw=(), scratch=(), late=0, raw_spec=ANYWHERE, grant=60):
     def kernel(*refs):
         t, r = len(tables), len(raw)
         operands = refs[t + r :]
         staged(
-            functools.partial(body, *refs[t : t + r]), (len(args), len(outs)), refs[:t], *operands
+            functools.partial(body, *refs[t : t + r]), (len(args), len(outs)), late, refs[:t],
+            *operands,
         )
 
     moved = sum(a.size * a.dtype.itemsize for a in args) + sum(
         o.size * jnp.dtype(o.dtype).itemsize for o in outs
     )
-    anywhere = pl.BlockSpec(memory_space=pl.ANY)
     return pl.pallas_call(
         kernel,
         out_shape=tuple(outs),
         in_specs=[pl.BlockSpec(memory_space=pltpu.SMEM)] * len(tables)
-        + [anywhere] * (len(raw) + len(args)),
-        out_specs=tuple([anywhere] * len(outs)),
+        + [raw_spec] * len(raw) + [ANYWHERE] * len(args),
+        out_specs=tuple([ANYWHERE] * len(outs)),
         scratch_shapes=[pltpu.VMEM(a.shape, a.dtype) for a in args]
         + [pltpu.VMEM(o.shape, o.dtype) for o in outs]
         + [pltpu.SemaphoreType.DMA((len(args),)), pltpu.SemaphoreType.DMA((len(outs),))]
         + list(scratch),
-        compiler_params=pltpu.CompilerParams(vmem_limit_bytes=60 << 20),
+        compiler_params=pltpu.CompilerParams(vmem_limit_bytes=grant << 20),
         cost_estimate=pl.CostEstimate(flops=flops, bytes_accessed=moved, transcendentals=0),
     )(*tables, *raw, *args)
 
@@ -233,13 +247,13 @@
         made[0][h] = need(0)[:, chunk(h)].astype(F32)
 
 
-def project_body(slots, wk_hbm, wv_hbm, tables, need, made, put, w_buf, w_sem):
+def project_body(slots, wk_hbm, wv_hbm, wq_hbm, tables, need, made, put, w_buf, w_sem):
     (where,) = tables
-    xb, k_out, v_out, tot = made
+    xb, k_out, v_out, q_out, tot = made
     cols = pl.ds(pl.multiple_of(where[len(where) - 1] * DK, DK), DK)
     weights = [
         pltpu.make_async_copy(w.at[:, cols], w_buf.at[:, chunk(n)], w_sem.at[n])
-        for n, w in enumerate((wk_hbm, wv_hbm))
+        for n, w in enumerate((wk_hbm, wv_hbm, wq_hbm))
     ]
     for copy in weights:
         copy.start()
@@ -250,7 +264,7 @@
     put(0)
     for copy in weights:
         copy.wait()
-    both = nn(xb[...], w_buf[...]).astype(BF16)
+    both = nn(xb[...], w_buf[:, : 2 * DK]).astype(BF16)
     k, v = both[:, :DK], both[:, DK:]
     k_out[...] = k
     v_out[...] = v
@@ -260,15 +274,13 @@
     kn = k.astype(F32) * rk
     tot[:FOLDED] = fold_symmetric(fold_cols(tn(k, wide(kn * rk))))
     tot[FOLDED:] = fold_cols(tn(v, wide(kn)))
-
-
-def states_body(wq_hbm, tables, need, made, put, w_buf, w_sem):
-    (where,) = tables
-    q_out, gram_out = made
-    cols = pl.ds(pl.multiple_of(where[len(where) - 1] * DK, DK), DK)
-    weight = pltpu.make_async_copy(wq_hbm.at[:, cols], w_buf, w_sem.at[0])
-    weight.start()
+    put(4)
+    q_out[...] = nn(xb[...], w_buf[:, 2 * DK :]).astype(BF16)
+
+
+def targets_body(tables, need, made, put):
     k_in = need(0)
+    part, gram_out = made
     gram = jnp.zeros((DK, DK), F32)
     for j in range(CHUNKS):
         gram_out[j] = gram
@@ -277,19 +289,14 @@
             rk = inv_norm(k)
             gram = gram + fold_cols(tn(k, wide(k.astype(F32) * (rk * rk))))
     put(1)
-    weight.wait()
-    q_out[...] = nn(need(1)[...], w_buf[...]).astype(BF16)
-
-
-def targets_body(tables, need, made, put):
-    k_in, v_in, g_in = need(0), need(1), need(2)
+    v_in, g_in = need(1), need(2)
     keep = causal(DK)
     cross = jnp.zeros((DK, DK), F32)
     for j in range(CHUNKS):
         k, v, g = k_in[chunk(j), :], v_in[chunk(j), :], g_in[j].astype(BF16)
         rk = inv_norm(k)
         scores = nt(g, v) * jnp.where(keep, across(rk), 0.0)
-        made[0][j] = nn(twice_wide(g), tall(cross)) + nn(wide(scores), twice_tall(k))
+        part[j] = nn(twice_wide(g), tall(cross)) + nn(wide(scores), twice_tall(k))
         if j + 1 < CHUNKS:
             cross = cross + fold_cols(tn(v, wide(k.astype(F32) * rk)))
 
@@ -302,7 +309,7 @@
     damp = damp_in[pl.ds(where[len(where) - 1], 1), :]
     keep = causal(DK)
     keys = [k_in[chunk(j), :] for j in range(CHUNKS)]
-    grams = [gram_in[j] + gram_prior for j in range(CHUNKS)]
+    systems = [system(k, gram_in[j] + gram_prior) for j, k in enumerate(keys)]
     cross_tall = tall(cross_prior)
     scale2, targets = [], []
     for j, k in enumerate(keys):
@@ -312,7 +319,7 @@
         right = part[j] + nn(twice_wide(g_in[j].astype(BF16)), cross_tall)
         q = q_in[chunk(j), :]
         targets.append(jnp.concatenate([q.astype(F32) * inv_norm(q), right], axis=0))
-    both = conjugate(targets, keys, grams, scale2, damp)
+    both = conjugate(targets, systems, scale2, damp)
     gram = jnp.zeros((DK, DK), F32)
     cross = jnp.zeros((DK, DK), F32)
     for j in range(CHUNKS):
@@ -366,6 +373,7 @@
     (place,) = tables
     k_in, v_in, dk_part, dv_part = [need(n) for n in range(4)]
     gram_after, cross_after = total_of(need, 4)
+    need.begin(8)
     gram_tall, cross_tall, cross_wide = tall(gram_after), tall(cross_after), wide(cross_after)
     for j in range(CHUNKS):
         k, v = k_in[chunk(j), :], v_in[chunk(j), :]
@@ -389,18 +397,18 @@
         put(seq + step)
 
 
-def input_grad_body(tables, need, made, put, dk_cat, dv_cat):
+def input_grad_body(wq, tables, need, made, put, dk_cat, dv_cat):
     (place,) = tables
     dq_cat = jnp.concatenate([need(0)[h].astype(BF16) for h in range(HEADS)], axis=1)
-    total = nt(dq_cat, need(1)[...])
+    total = nt(dq_cat, wq[...])
     for step in range(HEADS):
-        piece = need(4 + step)
+        piece = need(1 + step)
         head = lax.rem(place[1] + HEADS - step, HEADS)
         cols = pl.ds(pl.multiple_of(head * DK, DK), DK)
         dk_cat[:, cols] = piece[:DK].astype(BF16)
         dv_cat[:, cols] = piece[DK:].astype(BF16)
-    total = total + nt(dk_cat[...], need(2)[...])
-    total = total + nt(dv_cat[...], need(3)[...])
+    total = total + nt(dk_cat[...], need(1 + HEADS)[...])
+    total = total + nt(dv_cat[...], need(2 + HEADS)[...])
     made[0][...] = total.astype(BF16)
 
 
@@ -458,23 +466,17 @@
     pieces, where = gather_plane(low, high)
     slots = tuple((slot, start) for _, slot, start in pieces)
     pieces = [p for p, _, _ in pieces]
-    upstream, _ = lax.optimization_barrier((grad_out[0], pieces[4]))
-    (upstream,) = call(upstream_body, [shaped(HEADS, tokens, DK)], [upstream], 0)
-    xb, k, v, first_tot = call(
+    (upstream,) = call(upstream_body, [shaped(HEADS, tokens, DK)], [grad_out[0]], 0)
+    xb, k, v, q, first_tot = call(
         functools.partial(project_body, slots),
-        [shaped(plane, width, dtype=BF16), brick, brick, state],
-        pieces, unit * 28, tables=[where], raw=[w_key, w_value],
-        scratch=[pltpu.VMEM((width, 2 * DK), BF16), pltpu.SemaphoreType.DMA((2,))],
+        [shaped(plane, width, dtype=BF16), brick, brick, brick, state],
+        pieces, unit * 28, tables=[where], raw=[w_key, w_value, w_query],
+        scratch=[pltpu.VMEM((width, 3 * DK), BF16), pltpu.SemaphoreType.DMA((3,))],
     )
     prior = exclusive(first_tot, 1)
     upstream, _ = lax.optimization_barrier((upstream, first_tot))
     g = exchange(upstream, PLANE)
-    q, gram_pre = call(
-        states_body, [brick, shaped(CHUNKS, DK, DK)], [k, xb], unit * 10,
-        tables=[where], raw=[w_query],
-        scratch=[pltpu.VMEM((width, DK), BF16), pltpu.SemaphoreType.DMA((1,))],
-    )
-    (part,) = call(targets_body, [blocks], [k, v, g], unit * 8)
+    part, gram_pre = call(targets_body, [blocks, shaped(CHUNKS, DK, DK)], [k, v, g], unit * 10)
 
     z, u, second_tot = call(
         solve_body, [blocks, blocks, state],
@@ -494,7 +496,7 @@
     pieces = call(
         functools.partial(grads_body, seq),
         [shaped(width // seq, DK)] * seq + [shaped(2 * tokens, DK)] * CHUNKS,
-        [k, v, dk_part, dv_part, *after, xb], unit * 14, tables=[place],
+        [k, v, dk_part, dv_part, *after, xb], unit * 14, tables=[place], late=1,
         scratch=[
             pltpu.VMEM((plane, DK), BF16), pltpu.VMEM((width, DK), F32),
             pltpu.VMEM((CHUNKS, 2 * tokens, DK), F32),
@@ -509,7 +511,8 @@
 
     (grad_inputs,) = call(
         input_grad_body, [shaped(tokens, width, dtype=BF16)],
-        [dq_all, w_query, w_key, w_value, *dkv], unit * 24, tables=[place],
+        [dq_all, *dkv, w_key, w_value], unit * 24, tables=[place], raw=[w_query],
+        raw_spec=pl.BlockSpec(memory_space=pltpu.VMEM), grant=24,
         scratch=[pltpu.VMEM((tokens, width), BF16)] * 2,
     )
     return (grad_inputs[None], grad_weights)

time: 159 us -> 161 us (1.013)
  the two profiles are of different devices: /device:TPU:2 before, /device:TPU:1 now
where the time goes in v2:
time: 161 us
  starting transfers between devices  73.5 us (46%)
  Pallas kernels  38 us (24%)
  waiting for transfers between devices  36.4 us (23%)
  local copies, waits for them, and re-layouts  7.75 us (5%)
  other arithmetic  3.87 us (2%)
    ppermute x32, starting transfers between devices, shift(): return lax.ppermute(x, axis, pairs)  53.9 us
    pallas_call x8, Pallas kernels, call(): pl.pallas_call(kernel, out_shape=tuple(outs), in_specs=[pl.BlockSpec(memo...  38 us
    ppermute x32, waiting for transfers between devices, shift(): return lax.ppermute(x, axis, pairs)  36.4 us
    all_to_all x3, starting transfers between devices, exchange(): return lax.all_to_all(x, axis, 0, 0)  19.6 us
    unnamed x56, local copies, waits for them, and re-layouts  7.06 us
  transfers between devices with their start and end apart: 35, of which 13 were waited for; matrix products, arithmetic and copies ran while one was open for 2% of the time, Pallas kernels for 14%

profile of v2, /device:TPU:1, one launch (start us, length us, event | category | flops | bytes accessed | tf_op | source)
XLA Modules:
  0.0 160.6 jit_solution(17746262933026772809)
XLA Ops:
  0.6 1.8 %shard_map.77 = (f32[64,1024]{1,0:T(8,128)}, f32[64,1024]{1,0:T(8,128)}) custom-call(bf16[128,1024]{1,0:T(8,128)(2,1)} %bitcast.21), custom_call_target="tpu_custom_call" | custom-call | bytes 786432 | tf_op jit(solution)/shard_map/pallas_call | solution.py:186
  2.4 3.3 %collective-permute-start = (f32[64,1024]{1,0:T(8,128)}, f32[64,1024]{1,0:T(8,128)S(1)}, u32[]{:S(2)}, u32[]{:S(2)}) collective-permute-start(f32[64,1024]{1,0:T(8,128)} %get-tuple-element.30.refs_4_), channel_id=1, source_target_pairs={{0,1},{1,0},{2,3},{3,2},{4,5},{5,4},{6,7},{7,6},{8,9},{9,8},{10,11... | collective-permute-start | bytes 786440 | tf_op jit(solution)/shard_map/ppermute | solution.py:418
  5.9 2.9 %collective-permute-start.4 = (f32[64,1024]{1,0:T(8,128)}, f32[64,1024]{1,0:T(8,128)S(1)}, u32[]{:S(2)}, u32[]{:S(2)}) collective-permute-start(f32[64,1024]{1,0:T(8,128)} %get-tuple-element.31.refs_5_), channel_id=1, source_target_pairs={{0,6},{2,0},{4,2},{6,4},{1,7},{3,1},{5,3},{7,5},{8,14},{10,8},{12,... | collective-permute-start | bytes 786440 | tf_op jit(solution)/shard_map/ppermute | solution.py:418
  8.8 2.7 %collective-permute-start.8 = (f32[64,1024]{1,0:T(8,128)}, f32[64,1024]{1,0:T(8,128)S(1)}, u32[]{:S(2)}, u32[]{:S(2)}) collective-permute-start(f32[64,1024]{1,0:T(8,128)} %get-tuple-element.30.refs_4_), channel_id=1, source_target_pairs={{0,6},{2,0},{4,2},{6,4},{1,7},{3,1},{5,3},{7,5},{8,14},{10,8},{12,... | collective-permute-start | bytes 786440 | tf_op jit(solution)/shard_map/ppermute | solution.py:418
  11.4 3.5 %collective-permute-done.2.refs_8_ = f32[64,1024]{1,0:T(8,128)S(1)} collective-permute-done((f32[64,1024]{1,0:T(8,128)}, f32[64,1024]{1,0:T(8,128)S(1)}, u32[]{:S(2)}, u32[]{:S(2)}) %collective-permute-start.2) | collective-permute-done | bytes 262176 | tf_op jit(solution)/shard_map/ppermute | solution.py:418
  16.4 2.7 %collective-permute-start.12 = (f32[64,1024]{1,0:T(8,128)S(1)}, f32[64,1024]{1,0:T(8,128)S(1)}, u32[]{:S(2)}, u32[]{:S(2)}) collective-permute-start(f32[64,1024]{1,0:T(8,128)S(1)} %collective-permute-done.4.refs_10_), channel_id=1, source_target_pairs={{0,6},{2,0},{4,2},{6,4},{1,7},{3,1},{5,3},{7,5},{8,14},{10,8},{12,... | collective-permute-start | bytes 786440 | tf_op jit(solution)/shard_map/ppermute | solution.py:418
  22.5 3.6 %collective-permute-done.10.refs_16_ = f32[64,1024]{1,0:T(8,128)S(1)} collective-permute-done((f32[64,1024]{1,0:T(8,128)S(1)}, f32[64,1024]{1,0:T(8,128)S(1)}, u32[]{:S(2)}, u32[]{:S(2)}) %collective-permute-start.10) | collective-permute-done | bytes 262176 | tf_op jit(solution)/shard_map/ppermute | solution.py:418
  27.2 1.8 %shard_map.79 = f32[8,128,128]{2,1,0:T(8,128)} custom-call(bf16[128,1024]{1,0:T(8,128)(2,1)} %bitcast.19), custom_call_target="tpu_custom_call" | custom-call | bytes 786432 | tf_op jit(solution)/shard_map/pallas_call | solution.py:186
  30.7 6.6 %shard_map.78 = (bf16[1024,1024]{1,0:T(8,128)(2,1)}, bf16[1024,128]{1,0:T(8,128)(2,1)}, bf16[1024,128]{1,0:T(8,128)(2,1)}, bf16[1024,128]{1,0:T(8,128)(2,1)}, f32[200,128]{1,0:T(8,128)}) custom-call(s32[9]{0:T(128)} %stack.48.refs_0_, bf16[1024,1024]{1,0:T(8,128)(2,1)} %refs_11_.1, bf16[1024,1024]{1,0:T(8,128)(2,1)} %refs_12_.1, bf16[1024,1024]{1,0:T(8,128)(2,1)} %refs_1_.3, ...), custom_call_target="tpu_custom_call" | custom-call | flops 939524096 | bytes 7180288 | tf_op jit(solution)/shard_map/pallas_call | solution.py:186
  37.2 4.6 %all-to-all-start = ((f32[8,128,128]{2,1,0:T(8,128)}), f32[8,128,128]{2,1,0:T(8,128)S(1)}, u32[]{:S(2)}, u32[]{:S(2)}) async-start(f32[8,128,128]{2,1,0:T(8,128)} %shard_map.79), calls=%async_computation | async-start | bytes 1048576 | tf_op jit(solution)/shard_map/all_to_all | solution.py:428
  41.9 1.9 %collective-permute-start.14 = (f32[200,128]{1,0:T(8,128)}, f32[200,128]{1,0:T(8,128)S(1)}, u32[]{:S(2)}, u32[]{:S(2)}) collective-permute-start(f32[200,128]{1,0:T(8,128)} %get-tuple-element.35), channel_id=1, source_target_pairs={{0,8},{8,16},{16,24},{24,32},{32,40},{40,48},{48,56},{1,9},{9,17},... | collective-permute-start | bytes 307208 | tf_op jit(solution)/shard_map/ppermute | solution.py:418
  43.7 4.9 %collective-permute-start.15 = (f32[200,128]{1,0:T(8,128)}, f32[200,128]{1,0:T(8,128)S(1)}, u32[]{:S(2)}, u32[]{:S(2)}) collective-permute-start(f32[200,128]{1,0:T(8,128)} %get-tuple-element.35), channel_id=1, source_target_pairs={{0,16},{8,24},{16,32},{24,40},{32,48},{40,56},{1,17},{9,25},{17,33... | collective-permute-start | bytes 307208 | tf_op jit(solution)/shard_map/ppermute | solution.py:418
  48.7 2.2 %collective-permute-done.15.refs_8_ = f32[200,128]{1,0:T(8,128)S(1)} collective-permute-done((f32[200,128]{1,0:T(8,128)}, f32[200,128]{1,0:T(8,128)S(1)}, u32[]{:S(2)}, u32[]{:S(2)}) %collective-permute-start.15) | collective-permute-done | bytes 102432 | tf_op jit(solution)/shard_map/ppermute | solution.py:418
  51.8 8.6 %collective-permute-start.16 = (f32[200,128]{1,0:T(8,128)S(1)}, f32[200,128]{1,0:T(8,128)S(1)}, u32[]{:S(2)}, u32[]{:S(2)}) collective-permute-start(f32[200,128]{1,0:T(8,128)S(1)} %add_add_fusion.2), channel_id=1, source_target_pairs={{0,24},{8,32},{16,40},{24,48},{32,56},{1,25},{9,33},{17,41},{25,49... | collective-permute-start | bytes 307208 | tf_op jit(solution)/shard_map/ppermute | solution.py:418
  62.7 3.8 %shard_map.80 = (f32[8,128,128]{2,1,0:T(8,128)}, f32[8,128,128]{2,1,0:T(8,128)}) custom-call(bf16[1024,128]{1,0:T(8,128)(2,1)} %get-tuple-element.33.refs_0_.refs_2_.refs_1_, bf16[1024,128]{1,0:T(8,128)(2,1)} %get-tuple-element.34.refs_1_.refs_2_, f32[8,128,128]{2,1,0:T(8,128)} %copy-done.5), custom_call_target="tpu_custom_call" | custom-call | flops 335544320 | bytes 2097152 | tf_op jit(solution)/shard_map/pallas_call | solution.py:186
  67.2 6.5 %shard_map.81 = (f32[8,128,128]{2,1,0:T(8,128)}, f32[8,128,128]{2,1,0:T(8,128)}, f32[200,128]{1,0:T(8,128)}) custom-call(s32[9]{0:T(128)} %stack.48.refs_0_, bf16[1024,128]{1,0:T(8,128)(2,1)} %get-tuple-element.32.refs_1_.refs_0_, bf16[1024,128]{1,0:T(8,128)(2,1)} %get-tuple-element.33.refs_0_.refs_2_.refs_1_, f32[8,128,128]{2,1,0:T(8,128)} %get-tuple-element.37.refs_3_, ...), custom_call_target="tpu_custom_call" | custom-call | flops 1342177280 | bytes 3661824 | tf_op jit(solution)/shard_map/pallas_call | solution.py:186
  76.3 6.3 %shard_map.82 = (f32[8,128,128]{2,1,0:T(8,128)}, f32[8,128,128]{2,1,0:T(8,128)}, f32[8,128,128]{2,1,0:T(8,128)}) custom-call(bf16[1024,128]{1,0:T(8,128)(2,1)} %get-tuple-element.32.refs_1_.refs_0_, bf16[1024,128]{1,0:T(8,128)(2,1)} %get-tuple-element.33.refs_0_.refs_2_.refs_1_, bf16[1024,128]{1,0:T(8,128)(2,1)} %get-tuple-element.34.refs_1_.refs_2_, ...), custom_call_target="tpu_custom_call" | custom-call | flops 1006632960 | bytes 3932160 | tf_op jit(solution)/shard_map/pallas_call | solution.py:186
  82.6 5.4 %all-to-all-start.1 = ((f32[8,128,128]{2,1,0:T(8,128)}), f32[8,128,128]{2,1,0:T(8,128)S(1)}, u32[]{:S(2)}, u32[]{:S(2)}) async-start(f32[8,128,128]{2,1,0:T(8,128)} %get-tuple-element.41), calls=%async_computation.1 | async-start | bytes 1048576 | tf_op jit(solution)/shard_map/all_to_all | solution.py:428
  91.3 9.0 %collective-permute-done.20.refs_7_ = f32[200,128]{1,0:T(8,128)S(1)} collective-permute-done((f32[200,128]{1,0:T(8,128)S(1)}, f32[200,128]{1,0:T(8,128)S(1)}, u32[]{:S(2)}, u32[]{:S(2)}) %collective-permute-start.20) | collective-permute-done | bytes 102432 | tf_op jit(solution)/shard_map/ppermute | solution.py:418
  100.3 3.4 %collective-permute-done.21.refs_8_ = f32[200,128]{1,0:T(8,128)S(1)} collective-permute-done((f32[200,128]{1,0:T(8,128)S(1)}, f32[200,128]{1,0:T(8,128)S(1)}, u32[]{:S(2)}, u32[]{:S(2)}) %collective-permute-start.21) | collective-permute-done | bytes 102432 | tf_op jit(solution)/shard_map/ppermute | solution.py:418
  104.3 5.8 %shard_map.83 = (f32[256,128]{1,0:T(8,128)}, f32[256,128]{1,0:T(8,128)}, f32[256,128]{1,0:T(8,128)}, f32[256,128]{1,0:T(8,128)}, f32[256,128]{1,0:T(8,128)}, /*i...) custom-call(s32[2]{0:T(128)} %pad_add_fusion.refs_0_, ...), custom_call_target="tpu_custom_call" | custom-call | flops 469762048 | bytes 5652480 | tf_op jit(solution)/shard_map/pallas_call | solution.py:186
  110.1 2.5 %collective-permute-start.31 = (f32[256,128]{1,0:T(8,128)}, f32[256,128]{1,0:T(8,128)S(1)}, u32[]{:S(2)}, u32[]{:S(2)}) collective-permute-start(f32[256,128]{1,0:T(8,128)} %get-tuple-element.57), channel_id=1, source_target_pairs={{0,192},{64,0},{128,64},{192,128},{1,193},{65,1},{129,65},{193,129... | collective-permute-start | bytes 393224 | tf_op jit(solution)/shard_map/ppermute | solution.py:418
  113.8 3.0 %collective-permute-start.22 = (f32[256,128]{1,0:T(8,128)}, f32[256,128]{1,0:T(8,128)S(1)}, u32[]{:S(2)}, u32[]{:S(2)}) collective-permute-start(f32[256,128]{1,0:T(8,128)} %get-tuple-element.47), channel_id=1, source_target_pairs={{0,1},{1,2},{2,3},{3,4},{4,5},{5,6},{6,7},{7,0},{8,9},{9,10},{10,1... | collective-permute-start | bytes 393224 | tf_op jit(solution)/shard_map/ppermute | solution.py:418
  118.3 3.8 %collective-permute-done.29 = f32[256,128]{1,0:T(8,128)S(1)} collective-permute-done((f32[256,128]{1,0:T(8,128)}, f32[256,128]{1,0:T(8,128)S(1)}, u32[]{:S(2)}, u32[]{:S(2)}) %collective-permute-start.29) | collective-permute-done | bytes 131104 | tf_op jit(solution)/shard_map/ppermute | solution.py:418
  123.8 9.6 %all-to-all-start.2 = ((f32[64,4,128]{2,1,0:T(4,128)}), f32[64,4,128]{2,1,0:T(4,128)S(1)}, u32[]{:S(2)}, u32[]{:S(2)}) async-start(f32[64,4,128]{2,1,0:T(4,128)} %bitcast.13), calls=%async_computation.2 | async-start | bytes 262144 | tf_op jit(solution)/shard_map/all_to_all | solution.py:428
  133.3 3.2 %collective-permute-start.24 = (f32[256,128]{1,0:T(8,128)}, f32[256,128]{1,0:T(8,128)S(1)}, u32[]{:S(2)}, u32[]{:S(2)}) collective-permute-start(f32[256,128]{1,0:T(8,128)} %get-tuple-element.49), channel_id=1, source_target_pairs={{0,3},{1,4},{2,5},{3,6},{4,7},{5,0},{6,1},{7,2},{8,11},{9,12},{10,... | collective-permute-start | bytes 393224 | tf_op jit(solution)/shard_map/ppermute | solution.py:418
  136.7 2.2 %collective-permute-start.26 = (f32[256,128]{1,0:T(8,128)}, f32[256,128]{1,0:T(8,128)S(1)}, u32[]{:S(2)}, u32[]{:S(2)}) collective-permute-start(f32[256,128]{1,0:T(8,128)} %get-tuple-element.51), channel_id=1, source_target_pairs={{0,5},{1,6},{2,7},{3,0},{4,1},{5,2},{6,3},{7,4},{8,13},{9,14},{10,... | collective-permute-start | bytes 393224 | tf_op jit(solution)/shard_map/ppermute | solution.py:418
  139.2 1.9 %collective-permute-start.28 = (f32[256,128]{1,0:T(8,128)}, f32[256,128]{1,0:T(8,128)S(1)}, u32[]{:S(2)}, u32[]{:S(2)}) collective-permute-start(f32[256,128]{1,0:T(8,128)} %get-tuple-element.53), channel_id=1, source_target_pairs={{0,7},{1,0},{2,1},{3,2},{4,3},{5,4},{6,5},{7,6},{8,15},{9,8},{10,9... | collective-permute-start | bytes 393224 | tf_op jit(solution)/shard_map/ppermute | solution.py:418
  142.5 1.8 %collective-permute-done.25.refs_7_ = f32[256,128]{1,0:T(8,128)S(1)} collective-permute-done((f32[256,128]{1,0:T(8,128)}, f32[256,128]{1,0:T(8,128)S(1)}, u32[]{:S(2)}, u32[]{:S(2)}) %collective-permute-start.25) | collective-permute-done | bytes 131104 | tf_op jit(solution)/shard_map/ppermute | solution.py:418
  144.3 2.3 %collective-permute-done.26.refs_8_ = f32[256,128]{1,0:T(8,128)S(1)} collective-permute-done((f32[256,128]{1,0:T(8,128)}, f32[256,128]{1,0:T(8,128)S(1)}, u32[]{:S(2)}, u32[]{:S(2)}) %collective-permute-start.26) | collective-permute-done | bytes 131104 | tf_op jit(solution)/shard_map/ppermute | solution.py:418
  146.6 3.2 %collective-permute-done.27.refs_9_ = f32[256,128]{1,0:T(8,128)S(1)} collective-permute-done((f32[256,128]{1,0:T(8,128)}, f32[256,128]{1,0:T(8,128)S(1)}, u32[]{:S(2)}, u32[]{:S(2)}) %collective-permute-start.27) | collective-permute-done | bytes 131104 | tf_op jit(solution)/shard_map/ppermute | solution.py:418
  154.3 5.6 %shard_map.84 = bf16[128,1024]{1,0:T(8,128)(2,1)} custom-call(s32[2]{0:T(128)S(1)} %copy-done.4, bf16[1024,1024]{1,0:T(8,128)(2,1)S(1)} %copy-done, f32[8,128,128]{2,1,0:T(8,128)S(1)} %all-to-all-done.1.refs_2_, f32[256,128]{1,0:T(8,128)S(1)} %copy-done.3, f32[256,128]{1,0:T(8,128)S(1)} %collective-permute-done.22.refs_4_, ...), custom_call_target="tpu_custom_call" | custom-call | flops 805306368 | bytes 6029312 | tf_op jit(solution)/shard_map/pallas_call | solution.py:186
  (108 shorter events, 29.5 us)
Async XLA Ops:
  2.4 6.3 %collective-permute-start = (f32[64,1024]{1,0:T(8,128)}, f32[64,1024]{1,0:T(8,128)S(1)}, u32[]{:S(2)}, u32[]{:S(2)}) collective-permute-start(f32[64,1024]{1,0:T(8,128)} %get-tuple-element.30.refs_4_), channel_id=1, source_target_pairs={{0,1},{1,0},{2,3},{3,2},{4,5},{5,4},{6,7},{7,6},{8,9},{9,8},{10,11... | collective-permute-start | bytes 786440 | tf_op jit(solution)/shard_map/ppermute | solution.py:418
  5.7 9.2 %collective-permute-start.2 = (f32[64,1024]{1,0:T(8,128)}, f32[64,1024]{1,0:T(8,128)S(1)}, u32[]{:S(2)}, u32[]{:S(2)}) collective-permute-start(f32[64,1024]{1,0:T(8,128)} %get-tuple-element.30.refs_4_), channel_id=1, source_target_pairs={{0,2},{2,4},{4,6},{6,0},{1,3},{3,5},{5,7},{7,1},{8,10},{10,12},{12... | collective-permute-start | bytes 786440 | tf_op jit(solution)/shard_map/ppermute | solution.py:418
  5.7 10.7 %collective-permute-start.1 = (f32[64,1024]{1,0:T(8,128)}, f32[64,1024]{1,0:T(8,128)S(1)}, u32[]{:S(2)}, u32[]{:S(2)}) collective-permute-start(f32[64,1024]{1,0:T(8,128)} %get-tuple-element.31.refs_5_), channel_id=1, source_target_pairs={{0,1},{1,0},{2,3},{3,2},{4,5},{5,4},{6,7},{7,6},{8,9},{9,8},{10,11... | collective-permute-start | bytes 786440 | tf_op jit(solution)/shard_map/ppermute | solution.py:418
  5.9 10.5 %collective-permute-start.4 = (f32[64,1024]{1,0:T(8,128)}, f32[64,1024]{1,0:T(8,128)S(1)}, u32[]{:S(2)}, u32[]{:S(2)}) collective-permute-start(f32[64,1024]{1,0:T(8,128)} %get-tuple-element.31.refs_5_), channel_id=1, source_target_pairs={{0,6},{2,0},{4,2},{6,4},{1,7},{3,1},{5,3},{7,5},{8,14},{10,8},{12,... | collective-permute-start | bytes 786440 | tf_op jit(solution)/shard_map/ppermute | solution.py:418
  8.7 11.8 %collective-permute-start.6 = (f32[64,1024]{1,0:T(8,128)}, f32[64,1024]{1,0:T(8,128)S(1)}, u32[]{:S(2)}, u32[]{:S(2)}) collective-permute-start(f32[64,1024]{1,0:T(8,128)} %get-tuple-element.31.refs_5_), channel_id=1, source_target_pairs={{0,2},{2,4},{4,6},{6,0},{1,3},{3,5},{5,7},{7,1},{8,10},{10,12},{12... | collective-permute-start | bytes 786440 | tf_op jit(solution)/shard_map/ppermute | solution.py:418
  8.8 13.3 %collective-permute-start.8 = (f32[64,1024]{1,0:T(8,128)}, f32[64,1024]{1,0:T(8,128)S(1)}, u32[]{:S(2)}, u32[]{:S(2)}) collective-permute-start(f32[64,1024]{1,0:T(8,128)} %get-tuple-element.30.refs_4_), channel_id=1, source_target_pairs={{0,6},{2,0},{4,2},{6,4},{1,7},{3,1},{5,3},{7,5},{8,14},{10,8},{12,... | collective-permute-start | bytes 786440 | tf_op jit(solution)/shard_map/ppermute | solution.py:418
  14.9 7.2 %collective-permute-start.3 = (f32[64,1024]{1,0:T(8,128)S(1)}, f32[64,1024]{1,0:T(8,128)S(1)}, u32[]{:S(2)}, u32[]{:S(2)}) collective-permute-start(f32[64,1024]{1,0:T(8,128)S(1)} %collective-permute-done.2.refs_8_), channel_id=1, source_target_pairs={{0,1},{1,0},{2,3},{3,2},{4,5},{5,4},{6,7},{7,6},{8,9},{9,8},{10,11... | collective-permute-start | bytes 786440 | tf_op jit(solution)/shard_map/ppermute | solution.py:418
  16.4 9.7 %collective-permute-start.10 = (f32[64,1024]{1,0:T(8,128)S(1)}, f32[64,1024]{1,0:T(8,128)S(1)}, u32[]{:S(2)}, u32[]{:S(2)}) collective-permute-start(f32[64,1024]{1,0:T(8,128)S(1)} %collective-permute-done.2.refs_8_), channel_id=1, source_target_pairs={{0,2},{2,4},{4,6},{6,0},{1,3},{3,5},{5,7},{7,1},{8,10},{10,12},{12... | collective-permute-start | bytes 786440 | tf_op jit(solution)/shard_map/ppermute | solution.py:418
  16.4 10.7 %collective-permute-start.12 = (f32[64,1024]{1,0:T(8,128)S(1)}, f32[64,1024]{1,0:T(8,128)S(1)}, u32[]{:S(2)}, u32[]{:S(2)}) collective-permute-start(f32[64,1024]{1,0:T(8,128)S(1)} %collective-permute-done.4.refs_10_), channel_id=1, source_target_pairs={{0,6},{2,0},{4,2},{6,4},{1,7},{3,1},{5,3},{7,5},{8,14},{10,8},{12,... | collective-permute-start | bytes 786440 | tf_op jit(solution)/shard_map/ppermute | solution.py:418
  20.5 9.2 %collective-permute-start.5 = (f32[64,1024]{1,0:T(8,128)S(1)}, f32[64,1024]{1,0:T(8,128)S(1)}, u32[]{:S(2)}, u32[]{:S(2)}) collective-permute-start(f32[64,1024]{1,0:T(8,128)S(1)} %collective-permute-done.4.refs_10_), channel_id=1, source_target_pairs={{0,1},{1,0},{2,3},{3,2},{4,5},{5,4},{6,7},{7,6},{8,9},{9,8},{10,11... | collective-permute-start | bytes 786440 | tf_op jit(solution)/shard_map/ppermute | solution.py:418
  22.0 7.7 %collective-permute-start.7 = (f32[64,1024]{1,0:T(8,128)S(1)}, f32[64,1024]{1,0:T(8,128)S(1)}, u32[]{:S(2)}, u32[]{:S(2)}) collective-permute-start(f32[64,1024]{1,0:T(8,128)S(1)} %collective-permute-done.6.refs_12_), channel_id=1, source_target_pairs={{0,1},{1,0},{2,3},{3,2},{4,5},{5,4},{6,7},{7,6},{8,9},{9,8},{10,11... | collective-permute-start | bytes 786440 | tf_op jit(solution)/shard_map/ppermute | solution.py:418
  22.1 7.6 %collective-permute-start.9 = (f32[64,1024]{1,0:T(8,128)S(1)}, f32[64,1024]{1,0:T(8,128)S(1)}, u32[]{:S(2)}, u32[]{:S(2)}) collective-permute-start(f32[64,1024]{1,0:T(8,128)S(1)} %collective-permute-done.8.refs_14_), channel_id=1, source_target_pairs={{0,1},{1,0},{2,3},{3,2},{4,5},{5,4},{6,7},{7,6},{8,9},{9,8},{10,11... | collective-permute-start | bytes 786440 | tf_op jit(solution)/shard_map/ppermute | solution.py:418
  37.2 24.7 %all-to-all-start = ((f32[8,128,128]{2,1,0:T(8,128)}), f32[8,128,128]{2,1,0:T(8,128)S(1)}, u32[]{:S(2)}, u32[]{:S(2)}) async-start(f32[8,128,128]{2,1,0:T(8,128)} %shard_map.79), calls=%async_computation | async-start | bytes 1048576 | tf_op jit(solution)/shard_map/all_to_all | solution.py:428
  41.9 6.8 %collective-permute-start.14 = (f32[200,128]{1,0:T(8,128)}, f32[200,128]{1,0:T(8,128)S(1)}, u32[]{:S(2)}, u32[]{:S(2)}) collective-permute-start(f32[200,128]{1,0:T(8,128)} %get-tuple-element.35), channel_id=1, source_target_pairs={{0,8},{8,16},{16,24},{24,32},{32,40},{40,48},{48,56},{1,9},{9,17},... | collective-permute-start | bytes 307208 | tf_op jit(solution)/shard_map/ppermute | solution.py:418
  43.7 7.2 %collective-permute-start.15 = (f32[200,128]{1,0:T(8,128)}, f32[200,128]{1,0:T(8,128)S(1)}, u32[]{:S(2)}, u32[]{:S(2)}) collective-permute-start(f32[200,128]{1,0:T(8,128)} %get-tuple-element.35), channel_id=1, source_target_pairs={{0,16},{8,24},{16,32},{24,40},{32,48},{40,56},{1,17},{9,25},{17,33... | collective-permute-start | bytes 307208 | tf_op jit(solution)/shard_map/ppermute | solution.py:418
  51.8 14.7 %collective-permute-start.16 = (f32[200,128]{1,0:T(8,128)S(1)}, f32[200,128]{1,0:T(8,128)S(1)}, u32[]{:S(2)}, u32[]{:S(2)}) collective-permute-start(f32[200,128]{1,0:T(8,128)S(1)} %add_add_fusion.2), channel_id=1, source_target_pairs={{0,24},{8,32},{16,40},{24,48},{32,56},{1,25},{9,33},{17,41},{25,49... | collective-permute-start | bytes 307208 | tf_op jit(solution)/shard_map/ppermute | solution.py:418
  60.4 6.1 %collective-permute-start.17 = (f32[200,128]{1,0:T(8,128)S(1)}, f32[200,128]{1,0:T(8,128)S(1)}, u32[]{:S(2)}, u32[]{:S(2)}) collective-permute-start(f32[200,128]{1,0:T(8,128)S(1)} %add_add_fusion.2), channel_id=1, source_target_pairs={{0,48},{8,56},{1,49},{9,57},{2,50},{10,58},{3,51},{11,59},{4,52},{... | collective-permute-start | bytes 307208 | tf_op jit(solution)/shard_map/ppermute | solution.py:418
  73.7 14.3 %collective-permute-start.18 = (f32[200,128]{1,0:T(8,128)}, f32[200,128]{1,0:T(8,128)S(1)}, u32[]{:S(2)}, u32[]{:S(2)}) collective-permute-start(f32[200,128]{1,0:T(8,128)} %get-tuple-element.44), channel_id=1, source_target_pairs={{8,0},{16,8},{24,16},{32,24},{40,32},{48,40},{56,48},{9,1},{17,9},... | collective-permute-start | bytes 307208 | tf_op jit(solution)/shard_map/ppermute | solution.py:418
  75.0 13.0 %collective-permute-start.19 = (f32[200,128]{1,0:T(8,128)}, f32[200,128]{1,0:T(8,128)S(1)}, u32[]{:S(2)}, u32[]{:S(2)}) collective-permute-start(f32[200,128]{1,0:T(8,128)} %get-tuple-element.44), channel_id=1, source_target_pairs={{16,0},{24,8},{32,16},{40,24},{48,32},{56,40},{17,1},{25,9},{33,17... | collective-permute-start | bytes 307208 | tf_op jit(solution)/shard_map/ppermute | solution.py:418
  82.6 41.1 %all-to-all-start.1 = ((f32[8,128,128]{2,1,0:T(8,128)}), f32[8,128,128]{2,1,0:T(8,128)S(1)}, u32[]{:S(2)}, u32[]{:S(2)}) async-start(f32[8,128,128]{2,1,0:T(8,128)} %get-tuple-element.41), calls=%async_computation.1 | async-start | bytes 1048576 | tf_op jit(solution)/shard_map/all_to_all | solution.py:428
  88.1 12.2 %collective-permute-start.20 = (f32[200,128]{1,0:T(8,128)S(1)}, f32[200,128]{1,0:T(8,128)S(1)}, u32[]{:S(2)}, u32[]{:S(2)}) collective-permute-start(f32[200,128]{1,0:T(8,128)S(1)} %add_add_fusion.1), channel_id=1, source_target_pairs={{24,0},{32,8},{40,16},{48,24},{56,32},{25,1},{33,9},{41,17},{49,25... | collective-permute-start | bytes 307208 | tf_op jit(solution)/shard_map/ppermute | solution.py:418
  89.4 14.3 %collective-permute-start.21 = (f32[200,128]{1,0:T(8,128)S(1)}, f32[200,128]{1,0:T(8,128)S(1)}, u32[]{:S(2)}, u32[]{:S(2)}) collective-permute-start(f32[200,128]{1,0:T(8,128)S(1)} %add_add_fusion.1), channel_id=1, source_target_pairs={{48,0},{56,8},{49,1},{57,9},{50,2},{58,10},{51,3},{59,11},{52,4},{... | collective-permute-start | bytes 307208 | tf_op jit(solution)/shard_map/ppermute | solution.py:418
  110.1 7.9 %collective-permute-start.31 = (f32[256,128]{1,0:T(8,128)}, f32[256,128]{1,0:T(8,128)S(1)}, u32[]{:S(2)}, u32[]{:S(2)}) collective-permute-start(f32[256,128]{1,0:T(8,128)} %get-tuple-element.57), channel_id=1, source_target_pairs={{0,192},{64,0},{128,64},{192,128},{1,193},{65,1},{129,65},{193,129... | collective-permute-start | bytes 393224 | tf_op jit(solution)/shard_map/ppermute | solution.py:418
  113.2 8.9 %collective-permute-start.29 = (f32[256,128]{1,0:T(8,128)}, f32[256,128]{1,0:T(8,128)S(1)}, u32[]{:S(2)}, u32[]{:S(2)}) collective-permute-start(f32[256,128]{1,0:T(8,128)} %get-tuple-element.55), channel_id=1, source_target_pairs={{0,64},{64,128},{128,192},{192,0},{1,65},{65,129},{129,193},{193,1... | collective-permute-start | bytes 393224 | tf_op jit(solution)/shard_map/ppermute | solution.py:418
  113.8 25.1 %collective-permute-start.22 = (f32[256,128]{1,0:T(8,128)}, f32[256,128]{1,0:T(8,128)S(1)}, u32[]{:S(2)}, u32[]{:S(2)}) collective-permute-start(f32[256,128]{1,0:T(8,128)} %get-tuple-element.47), channel_id=1, source_target_pairs={{0,1},{1,2},{2,3},{3,4},{4,5},{5,6},{6,7},{7,0},{8,9},{9,10},{10,1... | collective-permute-start | bytes 393224 | tf_op jit(solution)/shard_map/ppermute | solution.py:418
  116.9 22.4 %collective-permute-start.23 = (f32[256,128]{1,0:T(8,128)}, f32[256,128]{1,0:T(8,128)S(1)}, u32[]{:S(2)}, u32[]{:S(2)}) collective-permute-start(f32[256,128]{1,0:T(8,128)} %get-tuple-element.48), channel_id=1, source_target_pairs={{0,2},{1,3},{2,4},{3,5},{4,6},{5,7},{6,0},{7,1},{8,10},{9,11},{10,... | collective-permute-start | bytes 393224 | tf_op jit(solution)/shard_map/ppermute | solution.py:418
  123.8 36.2 %all-to-all-start.2 = ((f32[64,4,128]{2,1,0:T(4,128)}), f32[64,4,128]{2,1,0:T(4,128)S(1)}, u32[]{:S(2)}, u32[]{:S(2)}) async-start(f32[64,4,128]{2,1,0:T(4,128)} %bitcast.13), calls=%async_computation.2 | async-start | bytes 262144 | tf_op jit(solution)/shard_map/all_to_all | solution.py:428
  133.3 9.2 %collective-permute-start.24 = (f32[256,128]{1,0:T(8,128)}, f32[256,128]{1,0:T(8,128)S(1)}, u32[]{:S(2)}, u32[]{:S(2)}) collective-permute-start(f32[256,128]{1,0:T(8,128)} %get-tuple-element.49), channel_id=1, source_target_pairs={{0,3},{1,4},{2,5},{3,6},{4,7},{5,0},{6,1},{7,2},{8,11},{9,12},{10,... | collective-permute-start | bytes 393224 | tf_op jit(solution)/shard_map/ppermute | solution.py:418
  136.6 7.8 %collective-permute-start.25 = (f32[256,128]{1,0:T(8,128)}, f32[256,128]{1,0:T(8,128)S(1)}, u32[]{:S(2)}, u32[]{:S(2)}) collective-permute-start(f32[256,128]{1,0:T(8,128)} %get-tuple-element.50), channel_id=1, source_target_pairs={{0,4},{1,5},{2,6},{3,7},{4,0},{5,1},{6,2},{7,3},{8,12},{9,13},{10,... | collective-permute-start | bytes 393224 | tf_op jit(solution)/shard_map/ppermute | solution.py:418
  136.7 9.9 %collective-permute-start.26 = (f32[256,128]{1,0:T(8,128)}, f32[256,128]{1,0:T(8,128)S(1)}, u32[]{:S(2)}, u32[]{:S(2)}) collective-permute-start(f32[256,128]{1,0:T(8,128)} %get-tuple-element.51), channel_id=1, source_target_pairs={{0,5},{1,6},{2,7},{3,0},{4,1},{5,2},{6,3},{7,4},{8,13},{9,14},{10,... | collective-permute-start | bytes 393224 | tf_op jit(solution)/shard_map/ppermute | solution.py:418
  138.9 10.9 %collective-permute-start.27 = (f32[256,128]{1,0:T(8,128)}, f32[256,128]{1,0:T(8,128)S(1)}, u32[]{:S(2)}, u32[]{:S(2)}) collective-permute-start(f32[256,128]{1,0:T(8,128)} %get-tuple-element.52), channel_id=1, source_target_pairs={{0,6},{1,7},{2,0},{3,1},{4,2},{5,3},{6,4},{7,5},{8,14},{9,15},{10,... | collective-permute-start | bytes 393224 | tf_op jit(solution)/shard_map/ppermute | solution.py:418
  139.2 11.0 %collective-permute-start.28 = (f32[256,128]{1,0:T(8,128)}, f32[256,128]{1,0:T(8,128)S(1)}, u32[]{:S(2)}, u32[]{:S(2)}) collective-permute-start(f32[256,128]{1,0:T(8,128)} %get-tuple-element.53), channel_id=1, source_target_pairs={{0,7},{1,0},{2,1},{3,2},{4,3},{5,4},{6,5},{7,6},{8,15},{9,8},{10,9... | collective-permute-start | bytes 393224 | tf_op jit(solution)/shard_map/ppermute | solution.py:418
  (31 other events, 287.8 us)

commit v3 on v1

--- a/solution.py
+++ b/solution.py
@@ -81,28 +81,30 @@
     return jnp.transpose(jnp.broadcast_to(column, (size, size)))
 
 
-def apply_all(vectors, keys, grams, scale2, damp):
-    splits = [halves(p) for p in vectors]
-    cats = [jnp.concatenate(s, axis=1) for s in splits]
-    raw = [nt(c, twice_wide(k)) for c, k in zip(cats, keys)]
-    prior = []
-    for c, s, g in zip(cats, splits, grams):
-        g_hi, g_lo = halves(g)
-        prior.append(nn(c, twice_tall(g_hi)) + nn(s[0], g_lo))
-    inner = [wide(r * m) for r, m in zip(raw, scale2)]
+def system(key, gram):
+    turned = jnp.transpose(key)
+    hi, lo = halves(gram)
+    upper = jnp.concatenate([turned, hi, lo], axis=1)
+    lower = jnp.concatenate([turned, hi, jnp.zeros_like(lo)], axis=1)
+    return jnp.concatenate([upper, lower], axis=0), twice_tall(key)
+
+
+def apply_all(vectors, systems, scale2, damp):
+    firsts = [nn(wide(p), s[0]) for p, s in zip(vectors, systems)]
+    inner = [wide(f[:, :DK] * m) for f, m in zip(firsts, scale2)]
     return [
-        o + nn(i, twice_tall(k)) + damp * p
-        for o, i, k, p in zip(prior, inner, keys, vectors)
+        nn(i, s[1]) + (f[:, DK : 2 * DK] + f[:, 2 * DK :]) + damp * p
+        for i, s, f, p in zip(inner, systems, firsts, vectors)
     ]
 
 
-def conjugate(targets, keys, grams, scale2, damp):
+def conjugate(targets, systems, scale2, damp):
     residual = list(targets)
     direction = list(targets)
     norm_now = [rowsum(r * r) for r in residual]
     solution = None
     for sweep in range(ITERS):
-        image = apply_all(direction, keys, grams, scale2, damp)
+        image = apply_all(direction, systems, scale2, damp)
         step = [n / (rowsum(p * w) + EPSILON) for n, p, w in zip(norm_now, direction, image)]
         moved = [a * p for a, p in zip(step, direction)]
         solution = moved if solution is None else [x + m for x, m in zip(solution, moved)]
@@ -157,24 +159,27 @@
     return jax.ShapeDtypeStruct(dims, dtype)
 
 
+ANYWHERE = pl.BlockSpec(memory_space=pl.ANY)
+
+
 def call(body, outs, args, flops, tables=(), raw=(), scratch=()):
     def kernel(*refs):
         t, r = len(tables), len(raw)
         operands = refs[t + r :]
         staged(
-            functools.partial(body, *refs[t : t + r]), (len(args), len(outs)), refs[:t], *operands
+            functools.partial(body, *refs[t : t + r]), (len(args), len(outs)), refs[:t],
+            *operands,
         )
 
     moved = sum(a.size * a.dtype.itemsize for a in args) + sum(
         o.size * jnp.dtype(o.dtype).itemsize for o in outs
     )
-    anywhere = pl.BlockSpec(memory_space=pl.ANY)
     return pl.pallas_call(
         kernel,
         out_shape=tuple(outs),
         in_specs=[pl.BlockSpec(memory_space=pltpu.SMEM)] * len(tables)
-        + [anywhere] * (len(raw) + len(args)),
-        out_specs=tuple([anywhere] * len(outs)),
+        + [ANYWHERE] * (len(raw) + len(args)),
+        out_specs=tuple([ANYWHERE] * len(outs)),
         scratch_shapes=[pltpu.VMEM(a.shape, a.dtype) for a in args]
         + [pltpu.VMEM(o.shape, o.dtype) for o in outs]
         + [pltpu.SemaphoreType.DMA((len(args),)), pltpu.SemaphoreType.DMA((len(outs),))]
@@ -302,7 +307,7 @@
     damp = damp_in[pl.ds(where[len(where) - 1], 1), :]
     keep = causal(DK)
     keys = [k_in[chunk(j), :] for j in range(CHUNKS)]
-    grams = [gram_in[j] + gram_prior for j in range(CHUNKS)]
+    systems = [system(k, gram_in[j] + gram_prior) for j, k in enumerate(keys)]
     cross_tall = tall(cross_prior)
     scale2, targets = [], []
     for j, k in enumerate(keys):
@@ -312,7 +317,7 @@
         right = part[j] + nn(twice_wide(g_in[j].astype(BF16)), cross_tall)
         q = q_in[chunk(j), :]
         targets.append(jnp.concatenate([q.astype(F32) * inv_norm(q), right], axis=0))
-    both = conjugate(targets, keys, grams, scale2, damp)
+    both = conjugate(targets, systems, scale2, damp)
     gram = jnp.zeros((DK, DK), F32)
     cross = jnp.zeros((DK, DK), F32)
     for j in range(CHUNKS):
@@ -364,8 +369,8 @@
 
 def grads_body(seq, tables, need, made, put, dk_buf, dw_buf, out):
     (place,) = tables
-    k_in, v_in, dk_part, dv_part = [need(n) for n in range(4)]
-    gram_after, cross_after = total_of(need, 4)
+    k_in, v_in, dk_part, dv_part, dq_in = [need(n) for n in range(5)]
+    gram_after, cross_after = total_of(need, 5)
     gram_tall, cross_tall, cross_wide = tall(gram_after), tall(cross_after), wide(cross_after)
     for j in range(CHUNKS):
         k, v = k_in[chunk(j), :], v_in[chunk(j), :]
@@ -377,8 +382,9 @@
         dk_buf[chunk(j), :] = dk
         out[j, :DK] = dk.astype(F32)
         dv = dv_part[j] + rk * nt(kk, cross_wide)
-        out[j, DK:] = dv.astype(BF16).astype(F32)
-    dw_buf[...] = jnp.transpose(tn(dk_buf[...], need(8)[...]))
+        out[j, DK : 2 * DK] = dv.astype(BF16).astype(F32)
+        out[j, 2 * DK :] = dq_in[j]
+    dw_buf[...] = jnp.transpose(tn(dk_buf[...], need(9)[...]))
     rows = made[0].shape[0]
     for step in range(seq):
         start = pl.multiple_of(lax.rem(place[0] + step, seq) * rows, rows)
@@ -389,18 +395,17 @@
         put(seq + step)
 
 
-def input_grad_body(tables, need, made, put, dk_cat, dv_cat):
+def input_grad_body(tables, need, made, put, *sides):
     (place,) = tables
-    dq_cat = jnp.concatenate([need(0)[h].astype(BF16) for h in range(HEADS)], axis=1)
-    total = nt(dq_cat, need(1)[...])
     for step in range(HEADS):
-        piece = need(4 + step)
+        piece = need(step)
         head = lax.rem(place[1] + HEADS - step, HEADS)
         cols = pl.ds(pl.multiple_of(head * DK, DK), DK)
-        dk_cat[:, cols] = piece[:DK].astype(BF16)
-        dv_cat[:, cols] = piece[DK:].astype(BF16)
-    total = total + nt(dk_cat[...], need(2)[...])
-    total = total + nt(dv_cat[...], need(3)[...])
+        for n, side in enumerate(sides):
+            side[:, cols] = piece[chunk(n), :].astype(BF16)
+    total = nt(sides[0][...], need(HEADS)[...])
+    for n in (1, 2):
+        total = total + nt(sides[n][...], need(HEADS + n)[...])
     made[0][...] = total.astype(BF16)
 
 
@@ -458,8 +463,7 @@
     pieces, where = gather_plane(low, high)
     slots = tuple((slot, start) for _, slot, start in pieces)
     pieces = [p for p, _, _ in pieces]
-    upstream, _ = lax.optimization_barrier((grad_out[0], pieces[4]))
-    (upstream,) = call(upstream_body, [shaped(HEADS, tokens, DK)], [upstream], 0)
+    (upstream,) = call(upstream_body, [shaped(HEADS, tokens, DK)], [grad_out[0]], 0)
     xb, k, v, first_tot = call(
         functools.partial(project_body, slots),
         [shaped(plane, width, dtype=BF16), brick, brick, state],
@@ -482,8 +486,6 @@
     )
     after = exclusive(second_tot, -1)
     dq, dk_part, dv_part = call(local_body, [blocks, blocks, blocks], [q, k, v, g, z, u], unit * 30)
-    dq_all = exchange(dq, PLANE)
-
     seq = lax.axis_size("seq")
     ctx = ("z", "y", "core")
     spread = lax.axis_size(ctx)
@@ -493,11 +495,11 @@
     ).astype(jnp.int32)
     pieces = call(
         functools.partial(grads_body, seq),
-        [shaped(width // seq, DK)] * seq + [shaped(2 * tokens, DK)] * CHUNKS,
-        [k, v, dk_part, dv_part, *after, xb], unit * 14, tables=[place],
+        [shaped(width // seq, DK)] * seq + [shaped(3 * tokens, DK)] * CHUNKS,
+        [k, v, dk_part, dv_part, dq, *after, xb], unit * 14, tables=[place],
         scratch=[
             pltpu.VMEM((plane, DK), BF16), pltpu.VMEM((width, DK), F32),
-            pltpu.VMEM((CHUNKS, 2 * tokens, DK), F32),
+            pltpu.VMEM((CHUNKS, 3 * tokens, DK), F32),
         ],
     )
     dw, dkv = pieces[:seq], pieces[seq:]
@@ -509,8 +511,8 @@
 
     (grad_inputs,) = call(
         input_grad_body, [shaped(tokens, width, dtype=BF16)],
-        [dq_all, w_query, w_key, w_value, *dkv], unit * 24, tables=[place],
-        scratch=[pltpu.VMEM((tokens, width), BF16)] * 2,
+        [*dkv, w_key, w_value, w_query], unit * 24, tables=[place],
+        scratch=[pltpu.VMEM((tokens, width), BF16)] * 3,
     )
     return (grad_inputs[None], grad_weights)
 

time: 159 us -> 150 us (0.943)
  the two profiles are of different devices: /device:TPU:2 before, /device:TPU:15 now
where the time goes in v3:
time: 150 us; the launch traced here: 149 us
  starting transfers between devices  64.6 us (43%)
  Pallas kernels  40.5 us (27%)
  waiting for transfers between devices  33.9 us (23%)
  other arithmetic  4.75 us (3%)
  local copies, waits for them, and re-layouts  4.25 us (3%)
    ppermute x32, starting transfers between devices, shift(): return lax.ppermute(x, axis, pairs)  51.3 us
    pallas_call x9, Pallas kernels, call(): pl.pallas_call(kernel, out_shape=tuple(outs), in_specs=[pl.BlockSpec(memo...  40.5 us
    ppermute x32, waiting for transfers between devices, shift(): return lax.ppermute(x, axis, pairs)  33.9 us
    all_to_all x2, starting transfers between devices, exchange(): return lax.all_to_all(x, axis, 0, 0)  13.3 us
    unnamed x58, local copies, waits for them, and re-layouts  3.64 us
  transfers between devices with their start and end apart: 34, of which 11 were waited for; matrix products, arithmetic and copies ran while one was open for 3% of the time, Pallas kernels for 15%

profile of v3, /device:TPU:15, one launch (start us, length us, event | category | flops | bytes accessed | tf_op | source)
XLA Modules:
  0.0 149.2 jit_solution(10735810169515070865)
XLA Ops:
  0.6 1.8 %shard_map.77 = (f32[64,1024]{1,0:T(8,128)}, f32[64,1024]{1,0:T(8,128)}) custom-call(bf16[128,1024]{1,0:T(8,128)(2,1)} %bitcast.21), custom_call_target="tpu_custom_call" | custom-call | bytes 786432 | tf_op jit(solution)/shard_map/pallas_call | solution.py:177
  6.5 4.7 %collective-permute-done.2.refs_7_ = f32[64,1024]{1,0:T(8,128)S(1)} collective-permute-done((f32[64,1024]{1,0:T(8,128)}, f32[64,1024]{1,0:T(8,128)S(1)}, u32[]{:S(2)}, u32[]{:S(2)}) %collective-permute-start.2) | collective-permute-done | bytes 262176 | tf_op jit(solution)/shard_map/ppermute | solution.py:415
  11.2 1.5 %collective-permute-start.3 = (f32[64,1024]{1,0:T(8,128)S(1)}, f32[64,1024]{1,0:T(8,128)S(1)}, u32[]{:S(2)}, u32[]{:S(2)}) collective-permute-start(f32[64,1024]{1,0:T(8,128)S(1)} %collective-permute-done.2.refs_7_), channel_id=1, source_target_pairs={{0,1},{1,0},{2,3},{3,2},{4,5},{5,4},{6,7},{7,6},{8,9},{9,8},{10,11... | collective-permute-start | bytes 786440 | tf_op jit(solution)/shard_map/ppermute | solution.py:415
  12.7 1.3 collective-permute-start.10
  14.1 2.6 %collective-permute-done.6.refs_11_ = f32[64,1024]{1,0:T(8,128)S(1)} collective-permute-done((f32[64,1024]{1,0:T(8,128)}, f32[64,1024]{1,0:T(8,128)S(1)}, u32[]{:S(2)}, u32[]{:S(2)}) %collective-permute-start.6) | collective-permute-done | bytes 262176 | tf_op jit(solution)/shard_map/ppermute | solution.py:415
  16.8 1.5 %collective-permute-start.5 = (f32[64,1024]{1,0:T(8,128)S(1)}, f32[64,1024]{1,0:T(8,128)S(1)}, u32[]{:S(2)}, u32[]{:S(2)}) collective-permute-start(f32[64,1024]{1,0:T(8,128)S(1)} %collective-permute-done.4.refs_9_), channel_id=1, source_target_pairs={{0,1},{1,0},{2,3},{3,2},{4,5},{5,4},{6,7},{7,6},{8,9},{9,8},{10,11... | collective-permute-start | bytes 786440 | tf_op jit(solution)/shard_map/ppermute | solution.py:415
  18.4 1.6 %collective-permute-start.7 = (f32[64,1024]{1,0:T(8,128)S(1)}, f32[64,1024]{1,0:T(8,128)S(1)}, u32[]{:S(2)}, u32[]{:S(2)}) collective-permute-start(f32[64,1024]{1,0:T(8,128)S(1)} %collective-permute-done.6.refs_11_), channel_id=1, source_target_pairs={{0,1},{1,0},{2,3},{3,2},{4,5},{5,4},{6,7},{7,6},{8,9},{9,8},{10,11... | collective-permute-start | bytes 786440 | tf_op jit(solution)/shard_map/ppermute | solution.py:415
  20.1 2.3 %collective-permute-done.10.refs_15_ = f32[64,1024]{1,0:T(8,128)S(1)} collective-permute-done((f32[64,1024]{1,0:T(8,128)S(1)}, f32[64,1024]{1,0:T(8,128)S(1)}, u32[]{:S(2)}, u32[]{:S(2)}) %collective-permute-start.10) | collective-permute-done | bytes 262176 | tf_op jit(solution)/shard_map/ppermute | solution.py:415
  25.0 1.8 %shard_map.80 = f32[8,128,128]{2,1,0:T(8,128)} custom-call(bf16[128,1024]{1,0:T(8,128)(2,1)} %bitcast.19), custom_call_target="tpu_custom_call" | custom-call | bytes 786432 | tf_op jit(solution)/shard_map/pallas_call | solution.py:177
  28.4 5.0 %shard_map.78 = (bf16[1024,1024]{1,0:T(8,128)(2,1)}, bf16[1024,128]{1,0:T(8,128)(2,1)}, bf16[1024,128]{1,0:T(8,128)(2,1)}, f32[200,128]{1,0:T(8,128)}) custom-call(s32[9]{0:T(128)} %stack.48.refs_0_, bf16[1024,1024]{1,0:T(8,128)(2,1)} %refs_9_.1, bf16[1024,1024]{1,0:T(8,128)(2,1)} %refs_10_.1, f32[64,1024]{1,0:T(8,128)} %get-tuple-element.29.refs_3_, ...), custom_call_target="tpu_custom_call" | custom-call | flops 939524096 | bytes 6918144 | tf_op jit(solution)/shard_map/pallas_call | solution.py:177
  33.4 4.4 %all-to-all-start = ((f32[8,128,128]{2,1,0:T(8,128)}), f32[8,128,128]{2,1,0:T(8,128)S(1)}, u32[]{:S(2)}, u32[]{:S(2)}) async-start(f32[8,128,128]{2,1,0:T(8,128)} %shard_map.80), calls=%async_computation | async-start | bytes 1048576 | tf_op jit(solution)/shard_map/all_to_all | solution.py:425
  37.8 3.5 %collective-permute-start.14 = (f32[200,128]{1,0:T(8,128)}, f32[200,128]{1,0:T(8,128)S(1)}, u32[]{:S(2)}, u32[]{:S(2)}) collective-permute-start(f32[200,128]{1,0:T(8,128)} %get-tuple-element.35), channel_id=1, source_target_pairs={{0,8},{8,16},{16,24},{24,32},{32,40},{40,48},{48,56},{1,9},{9,17},... | collective-permute-start | bytes 307208 | tf_op jit(solution)/shard_map/ppermute | solution.py:415
  41.3 4.9 %collective-permute-start.15 = (f32[200,128]{1,0:T(8,128)}, f32[200,128]{1,0:T(8,128)S(1)}, u32[]{:S(2)}, u32[]{:S(2)}) collective-permute-start(f32[200,128]{1,0:T(8,128)} %get-tuple-element.35), channel_id=1, source_target_pairs={{0,16},{8,24},{16,32},{24,40},{32,48},{40,56},{1,17},{9,25},{17,33... | collective-permute-start | bytes 307208 | tf_op jit(solution)/shard_map/ppermute | solution.py:415
  46.3 1.9 %collective-permute-done.15.refs_8_ = f32[200,128]{1,0:T(8,128)S(1)} collective-permute-done((f32[200,128]{1,0:T(8,128)}, f32[200,128]{1,0:T(8,128)S(1)}, u32[]{:S(2)}, u32[]{:S(2)}) %collective-permute-start.15) | collective-permute-done | bytes 102432 | tf_op jit(solution)/shard_map/ppermute | solution.py:415
  49.2 8.5 %collective-permute-start.16 = (f32[200,128]{1,0:T(8,128)S(1)}, f32[200,128]{1,0:T(8,128)S(1)}, u32[]{:S(2)}, u32[]{:S(2)}) collective-permute-start(f32[200,128]{1,0:T(8,128)S(1)} %add_add_fusion.2), channel_id=1, source_target_pairs={{0,24},{8,32},{16,40},{24,48},{32,56},{1,25},{9,33},{17,41},{25,49... | collective-permute-start | bytes 307208 | tf_op jit(solution)/shard_map/ppermute | solution.py:415
  57.7 1.5 collective-permute-start.17
  59.2 3.8 %shard_map.79 = (bf16[1024,128]{1,0:T(8,128)(2,1)}, f32[8,128,128]{2,1,0:T(8,128)}) custom-call(s32[9]{0:T(128)} %stack.48.refs_0_, bf16[1024,1024]{1,0:T(8,128)(2,1)} %refs_11_.1, bf16[1024,128]{1,0:T(8,128)(2,1)} %get-tuple-element.31.refs_2_.refs_0_.refs_1_, bf16[1024,1024]{1,0:T(8,128)(2,1)} %get-tuple-element.33.refs_3_.refs_10_), custom_call_target="tpu_custom_call" | custom-call | flops 335544320 | bytes 3145728 | tf_op jit(solution)/shard_map/pallas_call | solution.py:177
  63.9 3.6 %shard_map.81.refs_4_ = f32[8,128,128]{2,1,0:T(8,128)} custom-call(bf16[1024,128]{1,0:T(8,128)(2,1)} %get-tuple-element.31.refs_2_.refs_0_.refs_1_, bf16[1024,128]{1,0:T(8,128)(2,1)} %get-tuple-element.32.refs_1_.refs_2_, f32[8,128,128]{2,1,0:T(8,128)} %copy-done), custom_call_target="tpu_custom_call" | custom-call | flops 268435456 | bytes 1572864 | tf_op jit(solution)/shard_map/pallas_call | solution.py:177
  68.1 6.4 %shard_map.82 = (f32[8,128,128]{2,1,0:T(8,128)}, f32[8,128,128]{2,1,0:T(8,128)}, f32[200,128]{1,0:T(8,128)}) custom-call(s32[9]{0:T(128)} %stack.48.refs_0_, bf16[1024,128]{1,0:T(8,128)(2,1)} %get-tuple-element.34.refs_1_.refs_0_, bf16[1024,128]{1,0:T(8,128)(2,1)} %get-tuple-element.31.refs_2_.refs_0_.refs_1_, f32[8,128,128]{2,1,0:T(8,128)} %get-tuple-element.37.refs_3_, ...), custom_call_target="tpu_custom_call" | custom-call | flops 1342177280 | bytes 3661824 | tf_op jit(solution)/shard_map/pallas_call | solution.py:177
  77.2 4.6 %collective-permute-done.18.refs_6_ = f32[200,128]{1,0:T(8,128)S(1)} collective-permute-done((f32[200,128]{1,0:T(8,128)}, f32[200,128]{1,0:T(8,128)S(1)}, u32[]{:S(2)}, u32[]{:S(2)}) %collective-permute-start.18) | collective-permute-done | bytes 102432 | tf_op jit(solution)/shard_map/ppermute | solution.py:415
  81.8 5.0 %collective-permute-done.19.refs_7_ = f32[200,128]{1,0:T(8,128)S(1)} collective-permute-done((f32[200,128]{1,0:T(8,128)}, f32[200,128]{1,0:T(8,128)S(1)}, u32[]{:S(2)}, u32[]{:S(2)}) %collective-permute-start.19) | collective-permute-done | bytes 102432 | tf_op jit(solution)/shard_map/ppermute | solution.py:415
  91.0 6.2 %shard_map.83 = (f32[8,128,128]{2,1,0:T(8,128)}, f32[8,128,128]{2,1,0:T(8,128)}, f32[8,128,128]{2,1,0:T(8,128)}) custom-call(bf16[1024,128]{1,0:T(8,128)(2,1)} %get-tuple-element.34.refs_1_.refs_0_, bf16[1024,128]{1,0:T(8,128)(2,1)} %get-tuple-element.31.refs_2_.refs_0_.refs_1_, bf16[1024,128]{1,0:T(8,128)(2,1)} %get-tuple-element.32.refs_1_.refs_2_, ...), custom_call_target="tpu_custom_call" | custom-call | flops 1006632960 | bytes 3932160 | tf_op jit(solution)/shard_map/pallas_call | solution.py:177
  97.9 5.3 %shard_map.84 = (f32[256,128]{1,0:T(8,128)}, f32[256,128]{1,0:T(8,128)}, f32[256,128]{1,0:T(8,128)}, f32[256,128]{1,0:T(8,128)}, f32[384,128]{1,0:T(8,128)}, /*i...) custom-call(s32[2]{0:T(128)} %pad_add_fusion.refs_0_, ...), custom_call_target="tpu_custom_call" | custom-call | flops 469762048 | bytes 6701056 | tf_op jit(solution)/shard_map/pallas_call | solution.py:177
  103.3 5.3 %collective-permute-start.22 = (f32[384,128]{1,0:T(8,128)}, f32[384,128]{1,0:T(8,128)S(1)}, u32[]{:S(2)}, u32[]{:S(2)}) collective-permute-start(f32[384,128]{1,0:T(8,128)} %get-tuple-element.45), channel_id=1, source_target_pairs={{0,1},{1,2},{2,3},{3,4},{4,5},{5,6},{6,7},{7,0},{8,9},{9,10},{10,1... | collective-permute-start | bytes 589832 | tf_op jit(solution)/shard_map/ppermute | solution.py:415
  110.8 1.8 %collective-permute-start.29 = (f32[256,128]{1,0:T(8,128)}, f32[256,128]{1,0:T(8,128)S(1)}, u32[]{:S(2)}, u32[]{:S(2)}) collective-permute-start(f32[256,128]{1,0:T(8,128)} %get-tuple-element.53), channel_id=1, source_target_pairs={{0,64},{64,128},{128,192},{192,0},{1,65},{65,129},{129,193},{193,1... | collective-permute-start | bytes 393224 | tf_op jit(solution)/shard_map/ppermute | solution.py:415
  112.6 6.5 %collective-permute-done.31 = f32[256,128]{1,0:T(8,128)S(1)} collective-permute-done((f32[256,128]{1,0:T(8,128)}, f32[256,128]{1,0:T(8,128)S(1)}, u32[]{:S(2)}, u32[]{:S(2)}) %collective-permute-start.31) | collective-permute-done | bytes 131104 | tf_op jit(solution)/shard_map/ppermute | solution.py:415
  120.4 2.1 %collective-permute-start.25 = (f32[384,128]{1,0:T(8,128)}, f32[384,128]{1,0:T(8,128)S(1)}, u32[]{:S(2)}, u32[]{:S(2)}) collective-permute-start(f32[384,128]{1,0:T(8,128)} %get-tuple-element.48), channel_id=1, source_target_pairs={{0,4},{1,5},{2,6},{3,7},{4,0},{5,1},{6,2},{7,3},{8,12},{9,13},{10,... | collective-permute-start | bytes 589832 | tf_op jit(solution)/shard_map/ppermute | solution.py:415
  123.6 1.7 %collective-permute-start.28 = (f32[384,128]{1,0:T(8,128)}, f32[384,128]{1,0:T(8,128)S(1)}, u32[]{:S(2)}, u32[]{:S(2)}) collective-permute-start(f32[384,128]{1,0:T(8,128)} %get-tuple-element.51), channel_id=1, source_target_pairs={{0,7},{1,0},{2,1},{3,2},{4,3},{5,4},{6,5},{7,6},{8,15},{9,8},{10,9... | collective-permute-start | bytes 589832 | tf_op jit(solution)/shard_map/ppermute | solution.py:415
  125.3 1.6 %add_add_fusion = f32[256,128]{1,0:T(8,128)} fusion(f32[256,128]{1,0:T(8,128)S(1)} %collective-permute-done.31, f32[256,128]{1,0:T(8,128)S(1)} %collective-permute-done.30, f32[256,128]{1,0:T(8,128)} %get-tuple-element.52, f32[256,128]{1,0:T(8,128)S(1)} %collective-permute-done.29), kind=kLoop, calls=%fused_computation | loop fusion | flops 98304 | bytes 655360 | tf_op jit(solution)/shard_map/add | solution.py:506
  126.9 9.0 %all-to-all-start.1 = ((f32[64,4,128]{2,1,0:T(4,128)}), f32[64,4,128]{2,1,0:T(4,128)S(1)}, u32[]{:S(2)}, u32[]{:S(2)}) async-start(f32[64,4,128]{2,1,0:T(4,128)} %bitcast.13), calls=%async_computation.1 | async-start | bytes 262144 | tf_op jit(solution)/shard_map/all_to_all | solution.py:425
  135.9 5.0 %collective-permute-done.27.refs_7_ = f32[384,128]{1,0:T(8,128)S(1)} collective-permute-done((f32[384,128]{1,0:T(8,128)}, f32[384,128]{1,0:T(8,128)S(1)}, u32[]{:S(2)}, u32[]{:S(2)}) %collective-permute-start.27) | collective-permute-done | bytes 196640 | tf_op jit(solution)/shard_map/ppermute | solution.py:415
  142.0 6.5 %shard_map.85 = bf16[128,1024]{1,0:T(8,128)(2,1)} custom-call(s32[2]{0:T(128)} %pad_add_fusion.refs_0_, f32[384,128]{1,0:T(8,128)} %get-tuple-element.44.refs_1_, f32[384,128]{1,0:T(8,128)} %copy-done.16, f32[384,128]{1,0:T(8,128)} %copy-done.17, f32[384,128]{1,0:T(8,128)} %copy-done.18, f32[384,128]{1,0:T(8,128)} %copy-done.19, f32[384,128]{1,0:T(8,128)} %copy-done.20, ...), custom_call_target="tpu_custom_call" | custom-call | flops 805306368 | bytes 8126464 | tf_op jit(solution)/shard_map/pallas_call | solution.py:177
  (109 shorter events, 24.8 us)
Async XLA Ops:
  3.2 8.0 %collective-permute-start.2 = (f32[64,1024]{1,0:T(8,128)}, f32[64,1024]{1,0:T(8,128)S(1)}, u32[]{:S(2)}, u32[]{:S(2)}) collective-permute-start(f32[64,1024]{1,0:T(8,128)} %get-tuple-element.29.refs_3_), channel_id=1, source_target_pairs={{0,2},{2,4},{4,6},{6,0},{1,3},{3,5},{5,7},{7,1},{8,10},{10,12},{12... | collective-permute-start | bytes 786440 | tf_op jit(solution)/shard_map/ppermute | solution.py:415
  4.5 8.2 %collective-permute-start.1 = (f32[64,1024]{1,0:T(8,128)}, f32[64,1024]{1,0:T(8,128)S(1)}, u32[]{:S(2)}, u32[]{:S(2)}) collective-permute-start(f32[64,1024]{1,0:T(8,128)} %get-tuple-element.30.refs_4_), channel_id=1, source_target_pairs={{0,1},{1,0},{2,3},{3,2},{4,5},{5,4},{6,7},{7,6},{8,9},{9,8},{10,11... | collective-permute-start | bytes 786440 | tf_op jit(solution)/shard_map/ppermute | solution.py:415
  4.8 9.1 %collective-permute-start.4 = (f32[64,1024]{1,0:T(8,128)}, f32[64,1024]{1,0:T(8,128)S(1)}, u32[]{:S(2)}, u32[]{:S(2)}) collective-permute-start(f32[64,1024]{1,0:T(8,128)} %get-tuple-element.30.refs_4_), channel_id=1, source_target_pairs={{0,6},{2,0},{4,2},{6,4},{1,7},{3,1},{5,3},{7,5},{8,14},{10,8},{12,... | collective-permute-start | bytes 786440 | tf_op jit(solution)/shard_map/ppermute | solution.py:415
  5.0 11.8 %collective-permute-start.6 = (f32[64,1024]{1,0:T(8,128)}, f32[64,1024]{1,0:T(8,128)S(1)}, u32[]{:S(2)}, u32[]{:S(2)}) collective-permute-start(f32[64,1024]{1,0:T(8,128)} %get-tuple-element.30.refs_4_), channel_id=1, source_target_pairs={{0,2},{2,4},{4,6},{6,0},{1,3},{3,5},{5,7},{7,1},{8,10},{10,12},{12... | collective-permute-start | bytes 786440 | tf_op jit(solution)/shard_map/ppermute | solution.py:415
  6.3 12.1 %collective-permute-start.8 = (f32[64,1024]{1,0:T(8,128)}, f32[64,1024]{1,0:T(8,128)S(1)}, u32[]{:S(2)}, u32[]{:S(2)}) collective-permute-start(f32[64,1024]{1,0:T(8,128)} %get-tuple-element.29.refs_3_), channel_id=1, source_target_pairs={{0,6},{2,0},{4,2},{6,4},{1,7},{3,1},{5,3},{7,5},{8,14},{10,8},{12,... | collective-permute-start | bytes 786440 | tf_op jit(solution)/shard_map/ppermute | solution.py:415
  11.2 8.8 %collective-permute-start.3 = (f32[64,1024]{1,0:T(8,128)S(1)}, f32[64,1024]{1,0:T(8,128)S(1)}, u32[]{:S(2)}, u32[]{:S(2)}) collective-permute-start(f32[64,1024]{1,0:T(8,128)S(1)} %collective-permute-done.2.refs_7_), channel_id=1, source_target_pairs={{0,1},{1,0},{2,3},{3,2},{4,5},{5,4},{6,7},{7,6},{8,9},{9,8},{10,11... | collective-permute-start | bytes 786440 | tf_op jit(solution)/shard_map/ppermute | solution.py:415
  12.7 9.7 %collective-permute-start.10 = (f32[64,1024]{1,0:T(8,128)S(1)}, f32[64,1024]{1,0:T(8,128)S(1)}, u32[]{:S(2)}, u32[]{:S(2)}) collective-permute-start(f32[64,1024]{1,0:T(8,128)S(1)} %collective-permute-done.2.refs_7_), channel_id=1, source_target_pairs={{0,2},{2,4},{4,6},{6,0},{1,3},{3,5},{5,7},{7,1},{8,10},{10,12},{12... | collective-permute-start | bytes 786440 | tf_op jit(solution)/shard_map/ppermute | solution.py:415
  14.0 10.0 %collective-permute-start.12 = (f32[64,1024]{1,0:T(8,128)S(1)}, f32[64,1024]{1,0:T(8,128)S(1)}, u32[]{:S(2)}, u32[]{:S(2)}) collective-permute-start(f32[64,1024]{1,0:T(8,128)S(1)} %collective-permute-done.4.refs_9_), channel_id=1, source_target_pairs={{0,6},{2,0},{4,2},{6,4},{1,7},{3,1},{5,3},{7,5},{8,14},{10,8},{12,... | collective-permute-start | bytes 786440 | tf_op jit(solution)/shard_map/ppermute | solution.py:415
  16.8 10.6 %collective-permute-start.5 = (f32[64,1024]{1,0:T(8,128)S(1)}, f32[64,1024]{1,0:T(8,128)S(1)}, u32[]{:S(2)}, u32[]{:S(2)}) collective-permute-start(f32[64,1024]{1,0:T(8,128)S(1)} %collective-permute-done.4.refs_9_), channel_id=1, source_target_pairs={{0,1},{1,0},{2,3},{3,2},{4,5},{5,4},{6,7},{7,6},{8,9},{9,8},{10,11... | collective-permute-start | bytes 786440 | tf_op jit(solution)/shard_map/ppermute | solution.py:415
  18.4 9.0 %collective-permute-start.7 = (f32[64,1024]{1,0:T(8,128)S(1)}, f32[64,1024]{1,0:T(8,128)S(1)}, u32[]{:S(2)}, u32[]{:S(2)}) collective-permute-start(f32[64,1024]{1,0:T(8,128)S(1)} %collective-permute-done.6.refs_11_), channel_id=1, source_target_pairs={{0,1},{1,0},{2,3},{3,2},{4,5},{5,4},{6,7},{7,6},{8,9},{9,8},{10,11... | collective-permute-start | bytes 786440 | tf_op jit(solution)/shard_map/ppermute | solution.py:415
  20.0 7.4 %collective-permute-start.9 = (f32[64,1024]{1,0:T(8,128)S(1)}, f32[64,1024]{1,0:T(8,128)S(1)}, u32[]{:S(2)}, u32[]{:S(2)}) collective-permute-start(f32[64,1024]{1,0:T(8,128)S(1)} %collective-permute-done.8.refs_13_), channel_id=1, source_target_pairs={{0,1},{1,0},{2,3},{3,2},{4,5},{5,4},{6,7},{7,6},{8,9},{9,8},{10,11... | collective-permute-start | bytes 786440 | tf_op jit(solution)/shard_map/ppermute | solution.py:415
  22.4 5.1 %collective-permute-start.11 = (f32[64,1024]{1,0:T(8,128)S(1)}, f32[64,1024]{1,0:T(8,128)S(1)}, u32[]{:S(2)}, u32[]{:S(2)}) collective-permute-start(f32[64,1024]{1,0:T(8,128)S(1)} %collective-permute-done.10.refs_15_), channel_id=1, source_target_pairs={{0,1},{1,0},{2,3},{3,2},{4,5},{5,4},{6,7},{7,6},{8,9},{9,8},{10,11... | collective-permute-start | bytes 786440 | tf_op jit(solution)/shard_map/ppermute | solution.py:415
  33.4 29.6 %all-to-all-start = ((f32[8,128,128]{2,1,0:T(8,128)}), f32[8,128,128]{2,1,0:T(8,128)S(1)}, u32[]{:S(2)}, u32[]{:S(2)}) async-start(f32[8,128,128]{2,1,0:T(8,128)} %shard_map.80), calls=%async_computation | async-start | bytes 1048576 | tf_op jit(solution)/shard_map/all_to_all | solution.py:425
  37.8 8.4 %collective-permute-start.14 = (f32[200,128]{1,0:T(8,128)}, f32[200,128]{1,0:T(8,128)S(1)}, u32[]{:S(2)}, u32[]{:S(2)}) collective-permute-start(f32[200,128]{1,0:T(8,128)} %get-tuple-element.35), channel_id=1, source_target_pairs={{0,8},{8,16},{16,24},{24,32},{32,40},{40,48},{48,56},{1,9},{9,17},... | collective-permute-start | bytes 307208 | tf_op jit(solution)/shard_map/ppermute | solution.py:415
  41.3 6.9 %collective-permute-start.15 = (f32[200,128]{1,0:T(8,128)}, f32[200,128]{1,0:T(8,128)S(1)}, u32[]{:S(2)}, u32[]{:S(2)}) collective-permute-start(f32[200,128]{1,0:T(8,128)} %get-tuple-element.35), channel_id=1, source_target_pairs={{0,16},{8,24},{16,32},{24,40},{32,48},{40,56},{1,17},{9,25},{17,33... | collective-permute-start | bytes 307208 | tf_op jit(solution)/shard_map/ppermute | solution.py:415
  49.2 18.3 %collective-permute-start.16 = (f32[200,128]{1,0:T(8,128)S(1)}, f32[200,128]{1,0:T(8,128)S(1)}, u32[]{:S(2)}, u32[]{:S(2)}) collective-permute-start(f32[200,128]{1,0:T(8,128)S(1)} %add_add_fusion.2), channel_id=1, source_target_pairs={{0,24},{8,32},{16,40},{24,48},{32,56},{1,25},{9,33},{17,41},{25,49... | collective-permute-start | bytes 307208 | tf_op jit(solution)/shard_map/ppermute | solution.py:415
  57.7 9.8 %collective-permute-start.17 = (f32[200,128]{1,0:T(8,128)S(1)}, f32[200,128]{1,0:T(8,128)S(1)}, u32[]{:S(2)}, u32[]{:S(2)}) collective-permute-start(f32[200,128]{1,0:T(8,128)S(1)} %add_add_fusion.2), channel_id=1, source_target_pairs={{0,48},{8,56},{1,49},{9,57},{2,50},{10,58},{3,51},{11,59},{4,52},{... | collective-permute-start | bytes 307208 | tf_op jit(solution)/shard_map/ppermute | solution.py:415
  74.6 7.2 %collective-permute-start.18 = (f32[200,128]{1,0:T(8,128)}, f32[200,128]{1,0:T(8,128)S(1)}, u32[]{:S(2)}, u32[]{:S(2)}) collective-permute-start(f32[200,128]{1,0:T(8,128)} %get-tuple-element.43), channel_id=1, source_target_pairs={{8,0},{16,8},{24,16},{32,24},{40,32},{48,40},{56,48},{9,1},{17,9},... | collective-permute-start | bytes 307208 | tf_op jit(solution)/shard_map/ppermute | solution.py:415
  75.9 10.9 %collective-permute-start.19 = (f32[200,128]{1,0:T(8,128)}, f32[200,128]{1,0:T(8,128)S(1)}, u32[]{:S(2)}, u32[]{:S(2)}) collective-permute-start(f32[200,128]{1,0:T(8,128)} %get-tuple-element.43), channel_id=1, source_target_pairs={{16,0},{24,8},{32,16},{40,24},{48,32},{56,40},{17,1},{25,9},{33,17... | collective-permute-start | bytes 307208 | tf_op jit(solution)/shard_map/ppermute | solution.py:415
  87.8 9.5 %collective-permute-start.20 = (f32[200,128]{1,0:T(8,128)S(1)}, f32[200,128]{1,0:T(8,128)S(1)}, u32[]{:S(2)}, u32[]{:S(2)}) collective-permute-start(f32[200,128]{1,0:T(8,128)S(1)} %add_add_fusion.1), channel_id=1, source_target_pairs={{24,0},{32,8},{40,16},{48,24},{56,32},{25,1},{33,9},{41,17},{49,25... | collective-permute-start | bytes 307208 | tf_op jit(solution)/shard_map/ppermute | solution.py:415
  89.1 8.2 %collective-permute-start.21 = (f32[200,128]{1,0:T(8,128)S(1)}, f32[200,128]{1,0:T(8,128)S(1)}, u32[]{:S(2)}, u32[]{:S(2)}) collective-permute-start(f32[200,128]{1,0:T(8,128)S(1)} %add_add_fusion.1), channel_id=1, source_target_pairs={{48,0},{56,8},{49,1},{57,9},{50,2},{58,10},{51,3},{59,11},{52,4},{... | collective-permute-start | bytes 307208 | tf_op jit(solution)/shard_map/ppermute | solution.py:415
  103.3 19.5 %collective-permute-start.22 = (f32[384,128]{1,0:T(8,128)}, f32[384,128]{1,0:T(8,128)S(1)}, u32[]{:S(2)}, u32[]{:S(2)}) collective-permute-start(f32[384,128]{1,0:T(8,128)} %get-tuple-element.45), channel_id=1, source_target_pairs={{0,1},{1,2},{2,3},{3,4},{4,5},{5,6},{6,7},{7,0},{8,9},{9,10},{10,1... | collective-permute-start | bytes 589832 | tf_op jit(solution)/shard_map/ppermute | solution.py:415
  108.5 15.1 %collective-permute-start.23 = (f32[384,128]{1,0:T(8,128)}, f32[384,128]{1,0:T(8,128)S(1)}, u32[]{:S(2)}, u32[]{:S(2)}) collective-permute-start(f32[384,128]{1,0:T(8,128)} %get-tuple-element.46), channel_id=1, source_target_pairs={{0,2},{1,3},{2,4},{3,5},{4,6},{5,7},{6,0},{7,1},{8,10},{9,11},{10,... | collective-permute-start | bytes 589832 | tf_op jit(solution)/shard_map/ppermute | solution.py:415
  109.5 9.7 %collective-permute-start.31 = (f32[256,128]{1,0:T(8,128)}, f32[256,128]{1,0:T(8,128)S(1)}, u32[]{:S(2)}, u32[]{:S(2)}) collective-permute-start(f32[256,128]{1,0:T(8,128)} %get-tuple-element.55), channel_id=1, source_target_pairs={{0,192},{64,0},{128,64},{192,128},{1,193},{65,1},{129,65},{193,129... | collective-permute-start | bytes 393224 | tf_op jit(solution)/shard_map/ppermute | solution.py:415
  110.0 10.4 %collective-permute-start.30 = (f32[256,128]{1,0:T(8,128)}, f32[256,128]{1,0:T(8,128)S(1)}, u32[]{:S(2)}, u32[]{:S(2)}) collective-permute-start(f32[256,128]{1,0:T(8,128)} %get-tuple-element.54), channel_id=1, source_target_pairs={{0,128},{64,192},{128,0},{192,64},{1,129},{65,193},{129,1},{193,65... | collective-permute-start | bytes 393224 | tf_op jit(solution)/shard_map/ppermute | solution.py:415
  110.8 11.6 %collective-permute-start.29 = (f32[256,128]{1,0:T(8,128)}, f32[256,128]{1,0:T(8,128)S(1)}, u32[]{:S(2)}, u32[]{:S(2)}) collective-permute-start(f32[256,128]{1,0:T(8,128)} %get-tuple-element.53), channel_id=1, source_target_pairs={{0,64},{64,128},{128,192},{192,0},{1,65},{65,129},{129,193},{193,1... | collective-permute-start | bytes 393224 | tf_op jit(solution)/shard_map/ppermute | solution.py:415
  119.2 16.7 %collective-permute-start.24 = (f32[384,128]{1,0:T(8,128)}, f32[384,128]{1,0:T(8,128)S(1)}, u32[]{:S(2)}, u32[]{:S(2)}) collective-permute-start(f32[384,128]{1,0:T(8,128)} %get-tuple-element.47), channel_id=1, source_target_pairs={{0,3},{1,4},{2,5},{3,6},{4,7},{5,0},{6,1},{7,2},{8,11},{9,12},{10,... | collective-permute-start | bytes 589832 | tf_op jit(solution)/shard_map/ppermute | solution.py:415
  120.4 15.5 %collective-permute-start.25 = (f32[384,128]{1,0:T(8,128)}, f32[384,128]{1,0:T(8,128)S(1)}, u32[]{:S(2)}, u32[]{:S(2)}) collective-permute-start(f32[384,128]{1,0:T(8,128)} %get-tuple-element.48), channel_id=1, source_target_pairs={{0,4},{1,5},{2,6},{3,7},{4,0},{5,1},{6,2},{7,3},{8,12},{9,13},{10,... | collective-permute-start | bytes 589832 | tf_op jit(solution)/shard_map/ppermute | solution.py:415
  122.5 13.5 %collective-permute-start.26 = (f32[384,128]{1,0:T(8,128)}, f32[384,128]{1,0:T(8,128)S(1)}, u32[]{:S(2)}, u32[]{:S(2)}) collective-permute-start(f32[384,128]{1,0:T(8,128)} %get-tuple-element.49), channel_id=1, source_target_pairs={{0,5},{1,6},{2,7},{3,0},{4,1},{5,2},{6,3},{7,4},{8,13},{9,14},{10,... | collective-permute-start | bytes 589832 | tf_op jit(solution)/shard_map/ppermute | solution.py:415
  122.8 18.1 %collective-permute-start.27 = (f32[384,128]{1,0:T(8,128)}, f32[384,128]{1,0:T(8,128)S(1)}, u32[]{:S(2)}, u32[]{:S(2)}) collective-permute-start(f32[384,128]{1,0:T(8,128)} %get-tuple-element.50), channel_id=1, source_target_pairs={{0,6},{1,7},{2,0},{3,1},{4,2},{5,3},{6,4},{7,5},{8,14},{9,15},{10,... | collective-permute-start | bytes 589832 | tf_op jit(solution)/shard_map/ppermute | solution.py:415
  123.6 17.7 %collective-permute-start.28 = (f32[384,128]{1,0:T(8,128)}, f32[384,128]{1,0:T(8,128)S(1)}, u32[]{:S(2)}, u32[]{:S(2)}) collective-permute-start(f32[384,128]{1,0:T(8,128)} %get-tuple-element.51), channel_id=1, source_target_pairs={{0,7},{1,0},{2,1},{3,2},{4,3},{5,4},{6,5},{7,6},{8,15},{9,8},{10,9... | collective-permute-start | bytes 589832 | tf_op jit(solution)/shard_map/ppermute | solution.py:415
  126.9 21.6 %all-to-all-start.1 = ((f32[64,4,128]{2,1,0:T(4,128)}), f32[64,4,128]{2,1,0:T(4,128)S(1)}, u32[]{:S(2)}, u32[]{:S(2)}) async-start(f32[64,4,128]{2,1,0:T(4,128)} %bitcast.13), calls=%async_computation.1 | async-start | bytes 262144 | tf_op jit(solution)/shard_map/all_to_all | solution.py:425
  (31 other events, 227.6 us)

commit v4 on v3

--- a/solution.py
+++ b/solution.py
@@ -436,10 +436,11 @@
     far_high = shift(next_high, "y", -1, True)
     pieces = [(low, 0, 0), (high, 0, rows)]
     pieces += [(shift(low, "core", 1, True), 4, 0), (shift(high, "core", 1, True), 4, rows)]
-    for piece, slot, start in (
+    near = (
         (prev_low, 1, 0), (next_high, 2, rows), (prev_high, 1, rows), (next_low, 2, 0),
         (far_low, 3, 0), (far_high, 3, rows),
-    ):
+    )
+    for piece, slot, start in near:
         pieces.append((piece, slot, start))
         pieces.append((shift(piece, "core", 1, True), slot + 4, start))
     ysize = lax.axis_size("y")
@@ -471,7 +472,6 @@
         scratch=[pltpu.VMEM((width, 2 * DK), BF16), pltpu.SemaphoreType.DMA((2,))],
     )
     prior = exclusive(first_tot, 1)
-    upstream, _ = lax.optimization_barrier((upstream, first_tot))
     g = exchange(upstream, PLANE)
     q, gram_pre = call(
         states_body, [brick, shaped(CHUNKS, DK, DK)], [k, xb], unit * 10,

time: 150 us -> 150 us (level)
  the two profiles are of different devices: /device:TPU:15 before, /device:TPU:2 now
where the time goes in v4:
time: 150 us; the launch traced here: 147 us
  starting transfers between devices  61.4 us (41%)
  Pallas kernels  40.6 us (27%)
  waiting for transfers between devices  34.6 us (23%)
  other arithmetic  4.88 us (3%)
  local copies, waits for them, and re-layouts  4.15 us (3%)
    ppermute x32, starting transfers between devices, shift(): return lax.ppermute(x, axis, pairs)  47.2 us
    pallas_call x9, Pallas kernels, call(): pl.pallas_call(kernel, out_shape=tuple(outs), in_specs=[pl.BlockSpec(memo...  40.6 us
    ppermute x32, waiting for transfers between devices, shift(): return lax.ppermute(x, axis, pairs)  31.7 us
    all_to_all x2, starting transfers between devices, exchange(): return lax.all_to_all(x, axis, 0, 0)  14.2 us
    unnamed x54, local copies, waits for them, and re-layouts  3.49 us
  transfers between devices with their start and end apart: 34, of which 13 were waited for; matrix products, arithmetic and copies ran while one was open for 3% of the time, Pallas kernels for 18%

profile of v4, /device:TPU:2, one launch (start us, length us, event | category | flops | bytes accessed | tf_op | source)
XLA Modules:
  0.0 146.8 jit_solution(6649118305983811540)
XLA Ops:
  0.6 1.8 %shard_map.77 = (f32[64,1024]{1,0:T(8,128)}, f32[64,1024]{1,0:T(8,128)}) custom-call(bf16[128,1024]{1,0:T(8,128)(2,1)} %bitcast.21), custom_call_target="tpu_custom_call" | custom-call | bytes 786432 | tf_op jit(solution)/shard_map/pallas_call | solution.py:177
  2.5 1.7 %collective-permute-start.2 = (f32[64,1024]{1,0:T(8,128)}, f32[64,1024]{1,0:T(8,128)S(1)}, u32[]{:S(2)}, u32[]{:S(2)}) collective-permute-start(f32[64,1024]{1,0:T(8,128)} %get-tuple-element.28.refs_3_), channel_id=1, source_target_pairs={{0,2},{2,4},{4,6},{6,0},{1,3},{3,5},{5,7},{7,1},{8,10},{10,12},{12... | collective-permute-start | bytes 786440 | tf_op jit(solution)/shard_map/ppermute | solution.py:415
  4.3 1.7 %collective-permute-start.4 = (f32[64,1024]{1,0:T(8,128)}, f32[64,1024]{1,0:T(8,128)S(1)}, u32[]{:S(2)}, u32[]{:S(2)}) collective-permute-start(f32[64,1024]{1,0:T(8,128)} %get-tuple-element.29.refs_4_), channel_id=1, source_target_pairs={{0,6},{2,0},{4,2},{6,4},{1,7},{3,1},{5,3},{7,5},{8,14},{10,8},{12,... | collective-permute-start | bytes 786440 | tf_op jit(solution)/shard_map/ppermute | solution.py:415
  6.3 2.9 %collective-permute-start.8 = (f32[64,1024]{1,0:T(8,128)}, f32[64,1024]{1,0:T(8,128)S(1)}, u32[]{:S(2)}, u32[]{:S(2)}) collective-permute-start(f32[64,1024]{1,0:T(8,128)} %get-tuple-element.28.refs_3_), channel_id=1, source_target_pairs={{0,6},{2,0},{4,2},{6,4},{1,7},{3,1},{5,3},{7,5},{8,14},{10,8},{12,... | collective-permute-start | bytes 786440 | tf_op jit(solution)/shard_map/ppermute | solution.py:415
  9.3 3.9 %collective-permute-done.2.refs_7_ = f32[64,1024]{1,0:T(8,128)S(1)} collective-permute-done((f32[64,1024]{1,0:T(8,128)}, f32[64,1024]{1,0:T(8,128)S(1)}, u32[]{:S(2)}, u32[]{:S(2)}) %collective-permute-start.2) | collective-permute-done | bytes 262176 | tf_op jit(solution)/shard_map/ppermute | solution.py:415
  13.7 2.9 %collective-permute-start.12 = (f32[64,1024]{1,0:T(8,128)S(1)}, f32[64,1024]{1,0:T(8,128)S(1)}, u32[]{:S(2)}, u32[]{:S(2)}) collective-permute-start(f32[64,1024]{1,0:T(8,128)S(1)} %collective-permute-done.4.refs_9_), channel_id=1, source_target_pairs={{0,6},{2,0},{4,2},{6,4},{1,7},{3,1},{5,3},{7,5},{8,14},{10,8},{12,... | collective-permute-start | bytes 786440 | tf_op jit(solution)/shard_map/ppermute | solution.py:415
  16.6 2.2 %collective-permute-done.6.refs_11_ = f32[64,1024]{1,0:T(8,128)S(1)} collective-permute-done((f32[64,1024]{1,0:T(8,128)}, f32[64,1024]{1,0:T(8,128)S(1)}, u32[]{:S(2)}, u32[]{:S(2)}) %collective-permute-start.6) | collective-permute-done | bytes 262176 | tf_op jit(solution)/shard_map/ppermute | solution.py:415
  19.8 4.1 %collective-permute-done.10.refs_15_ = f32[64,1024]{1,0:T(8,128)S(1)} collective-permute-done((f32[64,1024]{1,0:T(8,128)S(1)}, f32[64,1024]{1,0:T(8,128)S(1)}, u32[]{:S(2)}, u32[]{:S(2)}) %collective-permute-start.10) | collective-permute-done | bytes 262176 | tf_op jit(solution)/shard_map/ppermute | solution.py:415
  24.5 1.8 %shard_map.80 = f32[8,128,128]{2,1,0:T(8,128)} custom-call(bf16[128,1024]{1,0:T(8,128)(2,1)} %bitcast.19), custom_call_target="tpu_custom_call" | custom-call | bytes 786432 | tf_op jit(solution)/shard_map/pallas_call | solution.py:177
  26.3 4.2 %all-to-all-start = ((f32[8,128,128]{2,1,0:T(8,128)}), f32[8,128,128]{2,1,0:T(8,128)S(1)}, u32[]{:S(2)}, u32[]{:S(2)}) async-start(f32[8,128,128]{2,1,0:T(8,128)} %shard_map.80), calls=%async_computation | async-start | bytes 1048576 | tf_op jit(solution)/shard_map/all_to_all | solution.py:425
  31.9 5.0 %shard_map.78 = (bf16[1024,1024]{1,0:T(8,128)(2,1)}, bf16[1024,128]{1,0:T(8,128)(2,1)}, bf16[1024,128]{1,0:T(8,128)(2,1)}, f32[200,128]{1,0:T(8,128)}) custom-call(s32[9]{0:T(128)} %stack.48.refs_0_, bf16[1024,1024]{1,0:T(8,128)(2,1)} %refs_9_.1, bf16[1024,1024]{1,0:T(8,128)(2,1)} %refs_10_.1, f32[64,1024]{1,0:T(8,128)} %get-tuple-element.28.refs_3_, ...), custom_call_target="tpu_custom_call" | custom-call | flops 939524096 | bytes 6918144 | tf_op jit(solution)/shard_map/pallas_call | solution.py:177
  37.0 3.8 %collective-permute-start.14 = (f32[200,128]{1,0:T(8,128)}, f32[200,128]{1,0:T(8,128)S(1)}, u32[]{:S(2)}, u32[]{:S(2)}) collective-permute-start(f32[200,128]{1,0:T(8,128)} %get-tuple-element.35), channel_id=1, source_target_pairs={{0,8},{8,16},{16,24},{24,32},{32,40},{40,48},{48,56},{1,9},{9,17},... | collective-permute-start | bytes 307208 | tf_op jit(solution)/shard_map/ppermute | solution.py:415
  40.8 5.2 %collective-permute-start.15 = (f32[200,128]{1,0:T(8,128)}, f32[200,128]{1,0:T(8,128)S(1)}, u32[]{:S(2)}, u32[]{:S(2)}) collective-permute-start(f32[200,128]{1,0:T(8,128)} %get-tuple-element.35), channel_id=1, source_target_pairs={{0,16},{8,24},{16,32},{24,40},{32,48},{40,56},{1,17},{9,25},{17,33... | collective-permute-start | bytes 307208 | tf_op jit(solution)/shard_map/ppermute | solution.py:415
  46.0 2.8 %collective-permute-done.15.refs_8_ = f32[200,128]{1,0:T(8,128)S(1)} collective-permute-done((f32[200,128]{1,0:T(8,128)}, f32[200,128]{1,0:T(8,128)S(1)}, u32[]{:S(2)}, u32[]{:S(2)}) %collective-permute-start.15) | collective-permute-done | bytes 102432 | tf_op jit(solution)/shard_map/ppermute | solution.py:415
  49.8 8.4 %collective-permute-start.16 = (f32[200,128]{1,0:T(8,128)S(1)}, f32[200,128]{1,0:T(8,128)S(1)}, u32[]{:S(2)}, u32[]{:S(2)}) collective-permute-start(f32[200,128]{1,0:T(8,128)S(1)} %add_add_fusion.2), channel_id=1, source_target_pairs={{0,24},{8,32},{16,40},{24,48},{32,56},{1,25},{9,33},{17,41},{25,49... | collective-permute-start | bytes 307208 | tf_op jit(solution)/shard_map/ppermute | solution.py:415
  60.4 3.6 %shard_map.81.refs_4_ = f32[8,128,128]{2,1,0:T(8,128)} custom-call(bf16[1024,128]{1,0:T(8,128)(2,1)} %get-tuple-element.30.refs_2_.refs_0_.refs_1_, bf16[1024,128]{1,0:T(8,128)(2,1)} %get-tuple-element.31.refs_1_.refs_2_, f32[8,128,128]{2,1,0:T(8,128)} %copy-done), custom_call_target="tpu_custom_call" | custom-call | flops 268435456 | bytes 1572864 | tf_op jit(solution)/shard_map/pallas_call | solution.py:177
  64.0 3.8 %shard_map.79 = (bf16[1024,128]{1,0:T(8,128)(2,1)}, f32[8,128,128]{2,1,0:T(8,128)}) custom-call(s32[9]{0:T(128)} %stack.48.refs_0_, bf16[1024,1024]{1,0:T(8,128)(2,1)} %refs_11_.1, bf16[1024,128]{1,0:T(8,128)(2,1)} %get-tuple-element.30.refs_2_.refs_0_.refs_1_, bf16[1024,1024]{1,0:T(8,128)(2,1)} %get-tuple-element.32.refs_3_.refs_10_), custom_call_target="tpu_custom_call" | custom-call | flops 335544320 | bytes 3145728 | tf_op jit(solution)/shard_map/pallas_call | solution.py:177
  68.6 6.5 %shard_map.82 = (f32[8,128,128]{2,1,0:T(8,128)}, f32[8,128,128]{2,1,0:T(8,128)}, f32[200,128]{1,0:T(8,128)}) custom-call(s32[9]{0:T(128)} %stack.48.refs_0_, bf16[1024,128]{1,0:T(8,128)(2,1)} %get-tuple-element.33.refs_1_.refs_0_, bf16[1024,128]{1,0:T(8,128)(2,1)} %get-tuple-element.30.refs_2_.refs_0_.refs_1_, f32[8,128,128]{2,1,0:T(8,128)} %get-tuple-element.34.refs_3_, ...), custom_call_target="tpu_custom_call" | custom-call | flops 1342177280 | bytes 3661824 | tf_op jit(solution)/shard_map/pallas_call | solution.py:177
  77.6 5.9 %collective-permute-done.18.refs_6_ = f32[200,128]{1,0:T(8,128)S(1)} collective-permute-done((f32[200,128]{1,0:T(8,128)}, f32[200,128]{1,0:T(8,128)S(1)}, u32[]{:S(2)}, u32[]{:S(2)}) %collective-permute-start.18) | collective-permute-done | bytes 102432 | tf_op jit(solution)/shard_map/ppermute | solution.py:415
  83.6 5.8 %collective-permute-done.19.refs_7_ = f32[200,128]{1,0:T(8,128)S(1)} collective-permute-done((f32[200,128]{1,0:T(8,128)}, f32[200,128]{1,0:T(8,128)S(1)}, u32[]{:S(2)}, u32[]{:S(2)}) %collective-permute-start.19) | collective-permute-done | bytes 102432 | tf_op jit(solution)/shard_map/ppermute | solution.py:415
  93.6 6.3 %shard_map.83 = (f32[8,128,128]{2,1,0:T(8,128)}, f32[8,128,128]{2,1,0:T(8,128)}, f32[8,128,128]{2,1,0:T(8,128)}) custom-call(bf16[1024,128]{1,0:T(8,128)(2,1)} %get-tuple-element.33.refs_1_.refs_0_, bf16[1024,128]{1,0:T(8,128)(2,1)} %get-tuple-element.30.refs_2_.refs_0_.refs_1_, bf16[1024,128]{1,0:T(8,128)(2,1)} %get-tuple-element.31.refs_1_.refs_2_, ...), custom_call_target="tpu_custom_call" | custom-call | flops 1006632960 | bytes 3932160 | tf_op jit(solution)/shard_map/pallas_call | solution.py:177
  101.6 5.3 %shard_map.84 = (f32[256,128]{1,0:T(8,128)}, f32[256,128]{1,0:T(8,128)}, f32[256,128]{1,0:T(8,128)}, f32[256,128]{1,0:T(8,128)}, f32[384,128]{1,0:T(8,128)}, /*i...) custom-call(s32[2]{0:T(128)} %pad_add_fusion.refs_0_, ...), custom_call_target="tpu_custom_call" | custom-call | flops 469762048 | bytes 6701056 | tf_op jit(solution)/shard_map/pallas_call | solution.py:177
  108.9 2.5 %collective-permute-start.30 = (f32[256,128]{1,0:T(8,128)}, f32[256,128]{1,0:T(8,128)S(1)}, u32[]{:S(2)}, u32[]{:S(2)}) collective-permute-start(f32[256,128]{1,0:T(8,128)} %get-tuple-element.52), channel_id=1, source_target_pairs={{0,128},{64,192},{128,0},{192,64},{1,129},{65,193},{129,1},{193,65... | collective-permute-start | bytes 393224 | tf_op jit(solution)/shard_map/ppermute | solution.py:415
  111.3 1.7 %collective-permute-start.29 = (f32[256,128]{1,0:T(8,128)}, f32[256,128]{1,0:T(8,128)S(1)}, u32[]{:S(2)}, u32[]{:S(2)}) collective-permute-start(f32[256,128]{1,0:T(8,128)} %get-tuple-element.51), channel_id=1, source_target_pairs={{0,64},{64,128},{128,192},{192,0},{1,65},{65,129},{129,193},{193,1... | collective-permute-start | bytes 393224 | tf_op jit(solution)/shard_map/ppermute | solution.py:415
  113.1 1.6 %collective-permute-done.31 = f32[256,128]{1,0:T(8,128)S(1)} collective-permute-done((f32[256,128]{1,0:T(8,128)}, f32[256,128]{1,0:T(8,128)S(1)}, u32[]{:S(2)}, u32[]{:S(2)}) %collective-permute-start.31) | collective-permute-done | bytes 131104 | tf_op jit(solution)/shard_map/ppermute | solution.py:415
  115.9 2.6 %collective-permute-done.30 = f32[256,128]{1,0:T(8,128)S(1)} collective-permute-done((f32[256,128]{1,0:T(8,128)}, f32[256,128]{1,0:T(8,128)S(1)}, u32[]{:S(2)}, u32[]{:S(2)}) %collective-permute-start.30) | collective-permute-done | bytes 131104 | tf_op jit(solution)/shard_map/ppermute | solution.py:415
  118.5 2.3 %collective-permute-start.25 = (f32[384,128]{1,0:T(8,128)}, f32[384,128]{1,0:T(8,128)S(1)}, u32[]{:S(2)}, u32[]{:S(2)}) collective-permute-start(f32[384,128]{1,0:T(8,128)} %get-tuple-element.46), channel_id=1, source_target_pairs={{0,4},{1,5},{2,6},{3,7},{4,0},{5,1},{6,2},{7,3},{8,12},{9,13},{10,... | collective-permute-start | bytes 589832 | tf_op jit(solution)/shard_map/ppermute | solution.py:415
  121.5 1.9 %collective-permute-start.27 = (f32[384,128]{1,0:T(8,128)}, f32[384,128]{1,0:T(8,128)S(1)}, u32[]{:S(2)}, u32[]{:S(2)}) collective-permute-start(f32[384,128]{1,0:T(8,128)} %get-tuple-element.48), channel_id=1, source_target_pairs={{0,6},{1,7},{2,0},{3,1},{4,2},{5,3},{6,4},{7,5},{8,14},{9,15},{10,... | collective-permute-start | bytes 589832 | tf_op jit(solution)/shard_map/ppermute | solution.py:415
  123.4 1.7 %add_add_fusion = f32[256,128]{1,0:T(8,128)} fusion(f32[256,128]{1,0:T(8,128)S(1)} %collective-permute-done.31, f32[256,128]{1,0:T(8,128)S(1)} %collective-permute-done.30, f32[256,128]{1,0:T(8,128)} %get-tuple-element.50, f32[256,128]{1,0:T(8,128)S(1)} %collective-permute-done.29), kind=kLoop, calls=%fused_computation | loop fusion | flops 98304 | bytes 655360 | tf_op jit(solution)/shard_map/add | solution.py:506
  125.1 10.1 %all-to-all-start.1 = ((f32[64,4,128]{2,1,0:T(4,128)}), f32[64,4,128]{2,1,0:T(4,128)S(1)}, u32[]{:S(2)}, u32[]{:S(2)}) async-start(f32[64,4,128]{2,1,0:T(4,128)} %bitcast.13), calls=%async_computation.1 | async-start | bytes 262144 | tf_op jit(solution)/shard_map/all_to_all | solution.py:425
  136.7 6.5 %shard_map.85 = bf16[128,1024]{1,0:T(8,128)(2,1)} custom-call(s32[2]{0:T(128)} %pad_add_fusion.refs_0_, f32[384,128]{1,0:T(8,128)} %get-tuple-element.42.refs_1_, f32[384,128]{1,0:T(8,128)} %copy-done.14, f32[384,128]{1,0:T(8,128)} %copy-done.15, f32[384,128]{1,0:T(8,128)} %copy-done.16, f32[384,128]{1,0:T(8,128)} %copy-done.17, f32[384,128]{1,0:T(8,128)} %copy-done.18, ...), custom_call_target="tpu_custom_call" | custom-call | flops 805306368 | bytes 8126464 | tf_op jit(solution)/shard_map/pallas_call | solution.py:177
  143.3 2.9 %all-to-all-done.1 = f32[64,4,128]{2,1,0:T(4,128)S(1)} async-done(((f32[64,4,128]{2,1,0:T(4,128)}), f32[64,4,128]{2,1,0:T(4,128)S(1)}, u32[]{:S(2)}, u32[]{:S(2)}) %all-to-all-start.1) | async-done | bytes 131104 | tf_op jit(solution)/shard_map/all_to_all | solution.py:425
  (105 shorter events, 22.2 us)
Async XLA Ops:
  2.5 10.7 %collective-permute-start.2 = (f32[64,1024]{1,0:T(8,128)}, f32[64,1024]{1,0:T(8,128)S(1)}, u32[]{:S(2)}, u32[]{:S(2)}) collective-permute-start(f32[64,1024]{1,0:T(8,128)} %get-tuple-element.28.refs_3_), channel_id=1, source_target_pairs={{0,2},{2,4},{4,6},{6,0},{1,3},{3,5},{5,7},{7,1},{8,10},{10,12},{12... | collective-permute-start | bytes 786440 | tf_op jit(solution)/shard_map/ppermute | solution.py:415
  4.2 9.0 %collective-permute-start.1 = (f32[64,1024]{1,0:T(8,128)}, f32[64,1024]{1,0:T(8,128)S(1)}, u32[]{:S(2)}, u32[]{:S(2)}) collective-permute-start(f32[64,1024]{1,0:T(8,128)} %get-tuple-element.29.refs_4_), channel_id=1, source_target_pairs={{0,1},{1,0},{2,3},{3,2},{4,5},{5,4},{6,7},{7,6},{8,9},{9,8},{10,11... | collective-permute-start | bytes 786440 | tf_op jit(solution)/shard_map/ppermute | solution.py:415
  4.3 9.4 %collective-permute-start.4 = (f32[64,1024]{1,0:T(8,128)}, f32[64,1024]{1,0:T(8,128)S(1)}, u32[]{:S(2)}, u32[]{:S(2)}) collective-permute-start(f32[64,1024]{1,0:T(8,128)} %get-tuple-element.29.refs_4_), channel_id=1, source_target_pairs={{0,6},{2,0},{4,2},{6,4},{1,7},{3,1},{5,3},{7,5},{8,14},{10,8},{12,... | collective-permute-start | bytes 786440 | tf_op jit(solution)/shard_map/ppermute | solution.py:415
  6.0 12.8 %collective-permute-start.6 = (f32[64,1024]{1,0:T(8,128)}, f32[64,1024]{1,0:T(8,128)S(1)}, u32[]{:S(2)}, u32[]{:S(2)}) collective-permute-start(f32[64,1024]{1,0:T(8,128)} %get-tuple-element.29.refs_4_), channel_id=1, source_target_pairs={{0,2},{2,4},{4,6},{6,0},{1,3},{3,5},{5,7},{7,1},{8,10},{10,12},{12... | collective-permute-start | bytes 786440 | tf_op jit(solution)/shard_map/ppermute | solution.py:415
  6.3 13.0 %collective-permute-start.8 = (f32[64,1024]{1,0:T(8,128)}, f32[64,1024]{1,0:T(8,128)S(1)}, u32[]{:S(2)}, u32[]{:S(2)}) collective-permute-start(f32[64,1024]{1,0:T(8,128)} %get-tuple-element.28.refs_3_), channel_id=1, source_target_pairs={{0,6},{2,0},{4,2},{6,4},{1,7},{3,1},{5,3},{7,5},{8,14},{10,8},{12,... | collective-permute-start | bytes 786440 | tf_op jit(solution)/shard_map/ppermute | solution.py:415
  13.2 10.7 %collective-permute-start.10 = (f32[64,1024]{1,0:T(8,128)S(1)}, f32[64,1024]{1,0:T(8,128)S(1)}, u32[]{:S(2)}, u32[]{:S(2)}) collective-permute-start(f32[64,1024]{1,0:T(8,128)S(1)} %collective-permute-done.2.refs_7_), channel_id=1, source_target_pairs={{0,2},{2,4},{4,6},{6,0},{1,3},{3,5},{5,7},{7,1},{8,10},{10,12},{12... | collective-permute-start | bytes 786440 | tf_op jit(solution)/shard_map/ppermute | solution.py:415
  13.7 10.6 %collective-permute-start.12 = (f32[64,1024]{1,0:T(8,128)S(1)}, f32[64,1024]{1,0:T(8,128)S(1)}, u32[]{:S(2)}, u32[]{:S(2)}) collective-permute-start(f32[64,1024]{1,0:T(8,128)S(1)} %collective-permute-done.4.refs_9_), channel_id=1, source_target_pairs={{0,6},{2,0},{4,2},{6,4},{1,7},{3,1},{5,3},{7,5},{8,14},{10,8},{12,... | collective-permute-start | bytes 786440 | tf_op jit(solution)/shard_map/ppermute | solution.py:415
  18.8 12.3 %collective-permute-start.5 = (f32[64,1024]{1,0:T(8,128)S(1)}, f32[64,1024]{1,0:T(8,128)S(1)}, u32[]{:S(2)}, u32[]{:S(2)}) collective-permute-start(f32[64,1024]{1,0:T(8,128)S(1)} %collective-permute-done.4.refs_9_), channel_id=1, source_target_pairs={{0,1},{1,0},{2,3},{3,2},{4,5},{5,4},{6,7},{7,6},{8,9},{9,8},{10,11... | collective-permute-start | bytes 786440 | tf_op jit(solution)/shard_map/ppermute | solution.py:415
  19.3 11.8 %collective-permute-start.7 = (f32[64,1024]{1,0:T(8,128)S(1)}, f32[64,1024]{1,0:T(8,128)S(1)}, u32[]{:S(2)}, u32[]{:S(2)}) collective-permute-start(f32[64,1024]{1,0:T(8,128)S(1)} %collective-permute-done.6.refs_11_), channel_id=1, source_target_pairs={{0,1},{1,0},{2,3},{3,2},{4,5},{5,4},{6,7},{7,6},{8,9},{9,8},{10,11... | collective-permute-start | bytes 786440 | tf_op jit(solution)/shard_map/ppermute | solution.py:415
  19.3 11.8 %collective-permute-start.9 = (f32[64,1024]{1,0:T(8,128)S(1)}, f32[64,1024]{1,0:T(8,128)}, u32[]{:S(2)}, u32[]{:S(2)}) collective-permute-start(f32[64,1024]{1,0:T(8,128)S(1)} %collective-permute-done.8.refs_13_), channel_id=1, source_target_pairs={{0,1},{1,0},{2,3},{3,2},{4,5},{5,4},{6,7},{7,6},{8,9},{9,8},{10,11... | collective-permute-start | bytes 786440 | tf_op jit(solution)/shard_map/ppermute | solution.py:415
  23.9 7.2 %collective-permute-start.11 = (f32[64,1024]{1,0:T(8,128)S(1)}, f32[64,1024]{1,0:T(8,128)}, u32[]{:S(2)}, u32[]{:S(2)}) collective-permute-start(f32[64,1024]{1,0:T(8,128)S(1)} %collective-permute-done.10.refs_15_), channel_id=1, source_target_pairs={{0,1},{1,0},{2,3},{3,2},{4,5},{5,4},{6,7},{7,6},{8,9},{9,8},{10,11... | collective-permute-start | bytes 786440 | tf_op jit(solution)/shard_map/ppermute | solution.py:415
  24.3 6.8 %collective-permute-start.13 = (f32[64,1024]{1,0:T(8,128)S(1)}, f32[64,1024]{1,0:T(8,128)}, u32[]{:S(2)}, u32[]{:S(2)}) collective-permute-start(f32[64,1024]{1,0:T(8,128)S(1)} %collective-permute-done.12.refs_17_), channel_id=1, source_target_pairs={{0,1},{1,0},{2,3},{3,2},{4,5},{5,4},{6,7},{7,6},{8,9},{9,8},{10,11... | collective-permute-start | bytes 786440 | tf_op jit(solution)/shard_map/ppermute | solution.py:415
  26.3 33.4 %all-to-all-start = ((f32[8,128,128]{2,1,0:T(8,128)}), f32[8,128,128]{2,1,0:T(8,128)S(1)}, u32[]{:S(2)}, u32[]{:S(2)}) async-start(f32[8,128,128]{2,1,0:T(8,128)} %shard_map.80), calls=%async_computation | async-start | bytes 1048576 | tf_op jit(solution)/shard_map/all_to_all | solution.py:425
  37.0 9.0 %collective-permute-start.14 = (f32[200,128]{1,0:T(8,128)}, f32[200,128]{1,0:T(8,128)S(1)}, u32[]{:S(2)}, u32[]{:S(2)}) collective-permute-start(f32[200,128]{1,0:T(8,128)} %get-tuple-element.35), channel_id=1, source_target_pairs={{0,8},{8,16},{16,24},{24,32},{32,40},{40,48},{48,56},{1,9},{9,17},... | collective-permute-start | bytes 307208 | tf_op jit(solution)/shard_map/ppermute | solution.py:415
  40.8 8.0 %collective-permute-start.15 = (f32[200,128]{1,0:T(8,128)}, f32[200,128]{1,0:T(8,128)S(1)}, u32[]{:S(2)}, u32[]{:S(2)}) collective-permute-start(f32[200,128]{1,0:T(8,128)} %get-tuple-element.35), channel_id=1, source_target_pairs={{0,16},{8,24},{16,32},{24,40},{32,48},{40,56},{1,17},{9,25},{17,33... | collective-permute-start | bytes 307208 | tf_op jit(solution)/shard_map/ppermute | solution.py:415
  49.8 18.1 %collective-permute-start.16 = (f32[200,128]{1,0:T(8,128)S(1)}, f32[200,128]{1,0:T(8,128)S(1)}, u32[]{:S(2)}, u32[]{:S(2)}) collective-permute-start(f32[200,128]{1,0:T(8,128)S(1)} %add_add_fusion.2), channel_id=1, source_target_pairs={{0,24},{8,32},{16,40},{24,48},{32,56},{1,25},{9,33},{17,41},{25,49... | collective-permute-start | bytes 307208 | tf_op jit(solution)/shard_map/ppermute | solution.py:415
  58.1 9.8 %collective-permute-start.17 = (f32[200,128]{1,0:T(8,128)S(1)}, f32[200,128]{1,0:T(8,128)S(1)}, u32[]{:S(2)}, u32[]{:S(2)}) collective-permute-start(f32[200,128]{1,0:T(8,128)S(1)} %add_add_fusion.2), channel_id=1, source_target_pairs={{0,48},{8,56},{1,49},{9,57},{2,50},{10,58},{3,51},{11,59},{4,52},{... | collective-permute-start | bytes 307208 | tf_op jit(solution)/shard_map/ppermute | solution.py:415
  75.0 8.5 %collective-permute-start.18 = (f32[200,128]{1,0:T(8,128)}, f32[200,128]{1,0:T(8,128)S(1)}, u32[]{:S(2)}, u32[]{:S(2)}) collective-permute-start(f32[200,128]{1,0:T(8,128)} %get-tuple-element.41), channel_id=1, source_target_pairs={{8,0},{16,8},{24,16},{32,24},{40,32},{48,40},{56,48},{9,1},{17,9},... | collective-permute-start | bytes 307208 | tf_op jit(solution)/shard_map/ppermute | solution.py:415
  76.3 13.1 %collective-permute-start.19 = (f32[200,128]{1,0:T(8,128)}, f32[200,128]{1,0:T(8,128)S(1)}, u32[]{:S(2)}, u32[]{:S(2)}) collective-permute-start(f32[200,128]{1,0:T(8,128)} %get-tuple-element.41), channel_id=1, source_target_pairs={{16,0},{24,8},{32,16},{40,24},{48,32},{56,40},{17,1},{25,9},{33,17... | collective-permute-start | bytes 307208 | tf_op jit(solution)/shard_map/ppermute | solution.py:415
  90.4 10.5 %collective-permute-start.20 = (f32[200,128]{1,0:T(8,128)S(1)}, f32[200,128]{1,0:T(8,128)S(1)}, u32[]{:S(2)}, u32[]{:S(2)}) collective-permute-start(f32[200,128]{1,0:T(8,128)S(1)} %add_add_fusion.1), channel_id=1, source_target_pairs={{24,0},{32,8},{40,16},{48,24},{56,32},{25,1},{33,9},{41,17},{49,25... | collective-permute-start | bytes 307208 | tf_op jit(solution)/shard_map/ppermute | solution.py:415
  91.7 9.2 %collective-permute-start.21 = (f32[200,128]{1,0:T(8,128)S(1)}, f32[200,128]{1,0:T(8,128)S(1)}, u32[]{:S(2)}, u32[]{:S(2)}) collective-permute-start(f32[200,128]{1,0:T(8,128)S(1)} %add_add_fusion.1), channel_id=1, source_target_pairs={{48,0},{56,8},{49,1},{57,9},{50,2},{58,10},{51,3},{59,11},{52,4},{... | collective-permute-start | bytes 307208 | tf_op jit(solution)/shard_map/ppermute | solution.py:415
  106.9 14.6 %collective-permute-start.22 = (f32[384,128]{1,0:T(8,128)}, f32[384,128]{1,0:T(8,128)S(1)}, u32[]{:S(2)}, u32[]{:S(2)}) collective-permute-start(f32[384,128]{1,0:T(8,128)} %get-tuple-element.43), channel_id=1, source_target_pairs={{0,1},{1,2},{2,3},{3,4},{4,5},{5,6},{6,7},{7,0},{8,9},{9,10},{10,1... | collective-permute-start | bytes 589832 | tf_op jit(solution)/shard_map/ppermute | solution.py:415
  106.9 16.5 %collective-permute-start.23 = (f32[384,128]{1,0:T(8,128)}, f32[384,128]{1,0:T(8,128)S(1)}, u32[]{:S(2)}, u32[]{:S(2)}) collective-permute-start(f32[384,128]{1,0:T(8,128)} %get-tuple-element.44), channel_id=1, source_target_pairs={{0,2},{1,3},{2,4},{3,5},{4,6},{5,7},{6,0},{7,1},{8,10},{9,11},{10,... | collective-permute-start | bytes 589832 | tf_op jit(solution)/shard_map/ppermute | solution.py:415
  108.3 6.3 %collective-permute-start.31 = (f32[256,128]{1,0:T(8,128)}, f32[256,128]{1,0:T(8,128)S(1)}, u32[]{:S(2)}, u32[]{:S(2)}) collective-permute-start(f32[256,128]{1,0:T(8,128)} %get-tuple-element.53), channel_id=1, source_target_pairs={{0,192},{64,0},{128,64},{192,128},{1,193},{65,1},{129,65},{193,129... | collective-permute-start | bytes 393224 | tf_op jit(solution)/shard_map/ppermute | solution.py:415
  108.9 9.6 %collective-permute-start.30 = (f32[256,128]{1,0:T(8,128)}, f32[256,128]{1,0:T(8,128)S(1)}, u32[]{:S(2)}, u32[]{:S(2)}) collective-permute-start(f32[256,128]{1,0:T(8,128)} %get-tuple-element.52), channel_id=1, source_target_pairs={{0,128},{64,192},{128,0},{192,64},{1,129},{65,193},{129,1},{193,65... | collective-permute-start | bytes 393224 | tf_op jit(solution)/shard_map/ppermute | solution.py:415
  111.3 9.5 %collective-permute-start.29 = (f32[256,128]{1,0:T(8,128)}, f32[256,128]{1,0:T(8,128)S(1)}, u32[]{:S(2)}, u32[]{:S(2)}) collective-permute-start(f32[256,128]{1,0:T(8,128)} %get-tuple-element.51), channel_id=1, source_target_pairs={{0,64},{64,128},{128,192},{192,0},{1,65},{65,129},{129,193},{193,1... | collective-permute-start | bytes 393224 | tf_op jit(solution)/shard_map/ppermute | solution.py:415
  114.7 20.5 %collective-permute-start.24 = (f32[384,128]{1,0:T(8,128)}, f32[384,128]{1,0:T(8,128)S(1)}, u32[]{:S(2)}, u32[]{:S(2)}) collective-permute-start(f32[384,128]{1,0:T(8,128)} %get-tuple-element.45), channel_id=1, source_target_pairs={{0,3},{1,4},{2,5},{3,6},{4,7},{5,0},{6,1},{7,2},{8,11},{9,12},{10,... | collective-permute-start | bytes 589832 | tf_op jit(solution)/shard_map/ppermute | solution.py:415
  118.5 16.7 %collective-permute-start.25 = (f32[384,128]{1,0:T(8,128)}, f32[384,128]{1,0:T(8,128)S(1)}, u32[]{:S(2)}, u32[]{:S(2)}) collective-permute-start(f32[384,128]{1,0:T(8,128)} %get-tuple-element.46), channel_id=1, source_target_pairs={{0,4},{1,5},{2,6},{3,7},{4,0},{5,1},{6,2},{7,3},{8,12},{9,13},{10,... | collective-permute-start | bytes 589832 | tf_op jit(solution)/shard_map/ppermute | solution.py:415
  120.8 14.4 %collective-permute-start.26 = (f32[384,128]{1,0:T(8,128)}, f32[384,128]{1,0:T(8,128)S(1)}, u32[]{:S(2)}, u32[]{:S(2)}) collective-permute-start(f32[384,128]{1,0:T(8,128)} %get-tuple-element.47), channel_id=1, source_target_pairs={{0,5},{1,6},{2,7},{3,0},{4,1},{5,2},{6,3},{7,4},{8,13},{9,14},{10,... | collective-permute-start | bytes 589832 | tf_op jit(solution)/shard_map/ppermute | solution.py:415
  121.5 13.7 %collective-permute-start.27 = (f32[384,128]{1,0:T(8,128)}, f32[384,128]{1,0:T(8,128)S(1)}, u32[]{:S(2)}, u32[]{:S(2)}) collective-permute-start(f32[384,128]{1,0:T(8,128)} %get-tuple-element.48), channel_id=1, source_target_pairs={{0,6},{1,7},{2,0},{3,1},{4,2},{5,3},{6,4},{7,5},{8,14},{9,15},{10,... | collective-permute-start | bytes 589832 | tf_op jit(solution)/shard_map/ppermute | solution.py:415
  123.4 12.6 %collective-permute-start.28 = (f32[384,128]{1,0:T(8,128)}, f32[384,128]{1,0:T(8,128)S(1)}, u32[]{:S(2)}, u32[]{:S(2)}) collective-permute-start(f32[384,128]{1,0:T(8,128)} %get-tuple-element.49), channel_id=1, source_target_pairs={{0,7},{1,0},{2,1},{3,2},{4,3},{5,4},{6,5},{7,6},{8,15},{9,8},{10,9... | collective-permute-start | bytes 589832 | tf_op jit(solution)/shard_map/ppermute | solution.py:415
  125.1 21.1 %all-to-all-start.1 = ((f32[64,4,128]{2,1,0:T(4,128)}), f32[64,4,128]{2,1,0:T(4,128)S(1)}, u32[]{:S(2)}, u32[]{:S(2)}) async-start(f32[64,4,128]{2,1,0:T(4,128)} %bitcast.13), calls=%async_computation.1 | async-start | bytes 262144 | tf_op jit(solution)/shard_map/all_to_all | solution.py:425
  (29 other events, 244.6 us)

commit v5 on v4

--- a/solution.py
+++ b/solution.py
@@ -119,14 +119,15 @@
     return solution
 
 
-def staged(body, counts, tables, *refs):
+def staged(body, counts, parts, tables, *refs):
     n_in, n_out = counts
     sources, refs = refs[:n_in], refs[n_in:]
     targets, refs = refs[:n_out], refs[n_out:]
     held, refs = refs[:n_in], refs[n_in:]
     made, (in_sems, out_sems, *rest) = refs[:n_out], refs[n_out:]
     loads = [
-        pltpu.make_async_copy(s, h, in_sems.at[n]) for n, (s, h) in enumerate(zip(sources, held))
+        pltpu.make_async_copy(s.at[part] if part else s, h, in_sems.at[n])
+        for n, (s, h, part) in enumerate(zip(sources, held, parts))
     ]
     stores = [
         pltpu.make_async_copy(m, t, out_sems.at[n]) for n, (m, t) in enumerate(zip(made, targets))
@@ -163,11 +164,17 @@
 
 
 def call(body, outs, args, flops, tables=(), raw=(), scratch=()):
+    parts = [a[1] if isinstance(a, tuple) else None for a in args]
+    args = [a[0] if isinstance(a, tuple) else a for a in args]
+    held = [
+        (p.stop - p.start, *a.shape[1:]) if p else a.shape for a, p in zip(args, parts)
+    ]
+
     def kernel(*refs):
         t, r = len(tables), len(raw)
         operands = refs[t + r :]
         staged(
-            functools.partial(body, *refs[t : t + r]), (len(args), len(outs)), refs[:t],
+            functools.partial(body, *refs[t : t + r]), (len(args), len(outs)), parts, refs[:t],
             *operands,
         )
 
@@ -180,7 +187,7 @@
         in_specs=[pl.BlockSpec(memory_space=pltpu.SMEM)] * len(tables)
         + [ANYWHERE] * (len(raw) + len(args)),
         out_specs=tuple([ANYWHERE] * len(outs)),
-        scratch_shapes=[pltpu.VMEM(a.shape, a.dtype) for a in args]
+        scratch_shapes=[pltpu.VMEM(h, a.dtype) for h, a in zip(held, args)]
         + [pltpu.VMEM(o.shape, o.dtype) for o in outs]
         + [pltpu.SemaphoreType.DMA((len(args),)), pltpu.SemaphoreType.DMA((len(outs),))]
         + list(scratch),
@@ -390,8 +397,11 @@
         start = pl.multiple_of(lax.rem(place[0] + step, seq) * rows, rows)
         made[step][...] = dw_buf[pl.ds(start, rows), :]
         put(step)
-    for step in range(CHUNKS):
-        made[seq + step][...] = out[lax.rem(place[1] + step, CHUNKS)]
+    core = place[2]
+    for step in range(CHUNKS // 2):
+        block = lax.rem(place[1] + step, CHUNKS // 2) * 2
+        made[seq + step][: 3 * DK] = out[block + core]
+        made[seq + step][3 * DK :] = out[block + 1 - core]
         put(seq + step)
 
 
@@ -399,7 +409,9 @@
     (place,) = tables
     for step in range(HEADS):
         piece = need(step)
-        head = lax.rem(place[1] + HEADS - step, HEADS)
+        chips = HEADS // 2
+        core = place[2] if step < chips else 1 - place[2]
+        head = lax.rem(place[1] + chips - step % chips, chips) * 2 + core
         cols = pl.ds(pl.multiple_of(head * DK, DK), DK)
         for n, side in enumerate(sides):
             side[:, cols] = piece[chunk(n), :].astype(BF16)
@@ -491,11 +503,11 @@
     spread = lax.axis_size(ctx)
     rows = width // (seq * spread)
     place = jnp.stack(
-        [lax.axis_index("seq"), lax.axis_index("y") * 2 + lax.axis_index("core")]
+        [lax.axis_index("seq"), lax.axis_index("y"), lax.axis_index("core")]
     ).astype(jnp.int32)
     pieces = call(
         functools.partial(grads_body, seq),
-        [shaped(width // seq, DK)] * seq + [shaped(3 * tokens, DK)] * CHUNKS,
+        [shaped(width // seq, DK)] * seq + [shaped(6 * tokens, DK)] * (CHUNKS // 2),
         [k, v, dk_part, dv_part, dq, *after, xb], unit * 14, tables=[place],
         scratch=[
             pltpu.VMEM((plane, DK), BF16), pltpu.VMEM((width, DK), F32),
@@ -504,14 +516,17 @@
     )
     dw, dkv = pieces[:seq], pieces[seq:]
     dw = sum((shift(part, "seq", step, True) for step, part in enumerate(dw) if step), dw[0])
-    dkv = [shift(p, PLANE, step, True) if step else p for step, p in enumerate(dkv)]
+    dkv = [shift(p, "y", step, True) if step else p for step, p in enumerate(dkv)]
     dw = exchange(dw.reshape(spread, rows, DK), ctx)
+    other = [shift(p, "core", 1, True) for p in dkv]
     dw = dw.reshape(spread // HEADS, HEADS, rows, DK)
     grad_weights = jnp.sum(dw, axis=0).transpose(1, 0, 2).reshape(rows, HEADS * DK)
 
+    mine_of = [(p, slice(0, 3 * tokens)) for p in dkv]
+    other_of = [(p, slice(3 * tokens, 6 * tokens)) for p in other]
     (grad_inputs,) = call(
         input_grad_body, [shaped(tokens, width, dtype=BF16)],
-        [*dkv, w_key, w_value, w_query], unit * 24, tables=[place],
+        [*mine_of, *other_of, w_key, w_value, w_query], unit * 24, tables=[place],
         scratch=[pltpu.VMEM((tokens, width), BF16)] * 3,
     )
     return (grad_inputs[None], grad_weights)

time: 150 us -> 158 us (1.053)
  blocking collectives: 0 us -> 20 us
  starting transfers between devices: 61.4 us -> 49.6 us
    all_to_all x0 -> x1, blocking collectives: none -> 20 us  [exchange(): return lax.all_to_all(x, axis, 0, 0)]
    all_to_all x2 -> x1, starting transfers between devices: 14.2 us -> 4.18 us  [exchange(): return lax.all_to_all(x, axis, 0, 0)]
    ppermute x32, waiting for transfers between devices: 31.7 us -> 35.4 us  [shift(): return lax.ppermute(x, axis, pairs)]
    all_to_all x2 -> x1, waiting for transfers between devices: 2.93 us -> 0.01 us  [exchange(): return lax.all_to_all(x, axis, 0, 0)]
    ppermute x32, starting transfers between devices: 47.2 us -> 45.4 us  [shift(): return lax.ppermute(x, axis, pairs)]
  transfers between devices with their start and end apart: 34 -> 33, of which waited for: 13 -> 13; matrix products, arithmetic and copies ran while one was open for 3% -> 3% of each run, Pallas kernels for 18% -> 13%
where the time goes in v5:
time: 158 us; the launch traced here: 156 us
  starting transfers between devices  49.6 us (31%)
  Pallas kernels  40.5 us (26%)
  waiting for transfers between devices  35.4 us (22%)
  blocking collectives  20 us (13%)
  local copies, waits for them, and re-layouts  5.2 us (3%)
  other arithmetic  4.25 us (3%)
    ppermute x32, starting transfers between devices, shift(): return lax.ppermute(x, axis, pairs)  45.4 us
    pallas_call x9, Pallas kernels, call(): pl.pallas_call(kernel, out_shape=tuple(outs), in_specs=[pl.BlockSpec(memo...  40.5 us
    ppermute x32, waiting for transfers between devices, shift(): return lax.ppermute(x, axis, pairs)  35.4 us
    all_to_all x1, blocking collectives, exchange(): return lax.all_to_all(x, axis, 0, 0)  20 us
    unnamed x54, local copies, waits for them, and re-layouts  4.52 us
    all_to_all x1, starting transfers between devices, exchange(): return lax.all_to_all(x, axis, 0, 0)  4.18 us
  transfers between devices with their start and end apart: 33, of which 13 were waited for; matrix products, arithmetic and copies ran while one was open for 3% of the time, Pallas kernels for 13%

profile of v5, /device:TPU:2, one launch (start us, length us, event | category | flops | bytes accessed | tf_op | source)
XLA Modules:
  0.0 156.2 jit_solution(1225428940521236134)
XLA Ops:
  0.6 1.8 %shard_map.77 = (f32[64,1024]{1,0:T(8,128)}, f32[64,1024]{1,0:T(8,128)}) custom-call(bf16[128,1024]{1,0:T(8,128)(2,1)} %bitcast.24), custom_call_target="tpu_custom_call" | custom-call | bytes 786432 | tf_op jit(solution)/shard_map/pallas_call | solution.py:184
  2.5 1.7 %collective-permute-start.2 = (f32[64,1024]{1,0:T(8,128)}, f32[64,1024]{1,0:T(8,128)S(1)}, u32[]{:S(2)}, u32[]{:S(2)}) collective-permute-start(f32[64,1024]{1,0:T(8,128)} %get-tuple-element.24.refs_3_), channel_id=1, source_target_pairs={{0,2},{2,4},{4,6},{6,0},{1,3},{3,5},{5,7},{7,1},{8,10},{10,12},{12... | collective-permute-start | bytes 786440 | tf_op jit(solution)/shard_map/ppermute | solution.py:427
  4.3 1.7 %collective-permute-start.4 = (f32[64,1024]{1,0:T(8,128)}, f32[64,1024]{1,0:T(8,128)S(1)}, u32[]{:S(2)}, u32[]{:S(2)}) collective-permute-start(f32[64,1024]{1,0:T(8,128)} %get-tuple-element.25.refs_4_), channel_id=1, source_target_pairs={{0,6},{2,0},{4,2},{6,4},{1,7},{3,1},{5,3},{7,5},{8,14},{10,8},{12,... | collective-permute-start | bytes 786440 | tf_op jit(solution)/shard_map/ppermute | solution.py:427
  6.3 2.9 %collective-permute-start.8 = (f32[64,1024]{1,0:T(8,128)}, f32[64,1024]{1,0:T(8,128)S(1)}, u32[]{:S(2)}, u32[]{:S(2)}) collective-permute-start(f32[64,1024]{1,0:T(8,128)} %get-tuple-element.24.refs_3_), channel_id=1, source_target_pairs={{0,6},{2,0},{4,2},{6,4},{1,7},{3,1},{5,3},{7,5},{8,14},{10,8},{12,... | collective-permute-start | bytes 786440 | tf_op jit(solution)/shard_map/ppermute | solution.py:427
  9.3 3.9 %collective-permute-done.2.refs_7_ = f32[64,1024]{1,0:T(8,128)S(1)} collective-permute-done((f32[64,1024]{1,0:T(8,128)}, f32[64,1024]{1,0:T(8,128)S(1)}, u32[]{:S(2)}, u32[]{:S(2)}) %collective-permute-start.2) | collective-permute-done | bytes 262176 | tf_op jit(solution)/shard_map/ppermute | solution.py:427
  13.7 2.9 %collective-permute-start.12 = (f32[64,1024]{1,0:T(8,128)S(1)}, f32[64,1024]{1,0:T(8,128)S(1)}, u32[]{:S(2)}, u32[]{:S(2)}) collective-permute-start(f32[64,1024]{1,0:T(8,128)S(1)} %collective-permute-done.4.refs_9_), channel_id=1, source_target_pairs={{0,6},{2,0},{4,2},{6,4},{1,7},{3,1},{5,3},{7,5},{8,14},{10,8},{12,... | collective-permute-start | bytes 786440 | tf_op jit(solution)/shard_map/ppermute | solution.py:427
  16.6 2.2 %collective-permute-done.6.refs_11_ = f32[64,1024]{1,0:T(8,128)S(1)} collective-permute-done((f32[64,1024]{1,0:T(8,128)}, f32[64,1024]{1,0:T(8,128)S(1)}, u32[]{:S(2)}, u32[]{:S(2)}) %collective-permute-start.6) | collective-permute-done | bytes 262176 | tf_op jit(solution)/shard_map/ppermute | solution.py:427
  19.8 4.1 %collective-permute-done.10.refs_15_ = f32[64,1024]{1,0:T(8,128)S(1)} collective-permute-done((f32[64,1024]{1,0:T(8,128)S(1)}, f32[64,1024]{1,0:T(8,128)S(1)}, u32[]{:S(2)}, u32[]{:S(2)}) %collective-permute-start.10) | collective-permute-done | bytes 262176 | tf_op jit(solution)/shard_map/ppermute | solution.py:427
  24.5 1.8 %shard_map.80 = f32[8,128,128]{2,1,0:T(8,128)} custom-call(bf16[128,1024]{1,0:T(8,128)(2,1)} %bitcast.22), custom_call_target="tpu_custom_call" | custom-call | bytes 786432 | tf_op jit(solution)/shard_map/pallas_call | solution.py:184
  26.2 4.2 %all-to-all-start = ((f32[8,128,128]{2,1,0:T(8,128)}), f32[8,128,128]{2,1,0:T(8,128)S(1)}, u32[]{:S(2)}, u32[]{:S(2)}) async-start(f32[8,128,128]{2,1,0:T(8,128)} %shard_map.80), calls=%async_computation | async-start | bytes 1048576 | tf_op jit(solution)/shard_map/all_to_all | solution.py:437
  31.9 5.0 %shard_map.78 = (bf16[1024,1024]{1,0:T(8,128)(2,1)}, bf16[1024,128]{1,0:T(8,128)(2,1)}, bf16[1024,128]{1,0:T(8,128)(2,1)}, f32[200,128]{1,0:T(8,128)}) custom-call(s32[9]{0:T(128)} %stack.55.refs_0_, bf16[1024,1024]{1,0:T(8,128)(2,1)} %refs_9_.1, bf16[1024,1024]{1,0:T(8,128)(2,1)} %refs_10_.1, f32[64,1024]{1,0:T(8,128)} %get-tuple-element.24.refs_3_, ...), custom_call_target="tpu_custom_call" | custom-call | flops 939524096 | bytes 6918144 | tf_op jit(solution)/shard_map/pallas_call | solution.py:184
  37.0 3.8 %collective-permute-start.14 = (f32[200,128]{1,0:T(8,128)}, f32[200,128]{1,0:T(8,128)S(1)}, u32[]{:S(2)}, u32[]{:S(2)}) collective-permute-start(f32[200,128]{1,0:T(8,128)} %get-tuple-element.31), channel_id=1, source_target_pairs={{0,8},{8,16},{16,24},{24,32},{32,40},{40,48},{48,56},{1,9},{9,17},... | collective-permute-start | bytes 307208 | tf_op jit(solution)/shard_map/ppermute | solution.py:427
  40.8 5.2 %collective-permute-start.15 = (f32[200,128]{1,0:T(8,128)}, f32[200,128]{1,0:T(8,128)S(1)}, u32[]{:S(2)}, u32[]{:S(2)}) collective-permute-start(f32[200,128]{1,0:T(8,128)} %get-tuple-element.31), channel_id=1, source_target_pairs={{0,16},{8,24},{16,32},{24,40},{32,48},{40,56},{1,17},{9,25},{17,33... | collective-permute-start | bytes 307208 | tf_op jit(solution)/shard_map/ppermute | solution.py:427
  46.0 2.8 %collective-permute-done.15.refs_8_ = f32[200,128]{1,0:T(8,128)S(1)} collective-permute-done((f32[200,128]{1,0:T(8,128)}, f32[200,128]{1,0:T(8,128)S(1)}, u32[]{:S(2)}, u32[]{:S(2)}) %collective-permute-start.15) | collective-permute-done | bytes 102432 | tf_op jit(solution)/shard_map/ppermute | solution.py:427
  49.8 8.4 %collective-permute-start.16 = (f32[200,128]{1,0:T(8,128)S(1)}, f32[200,128]{1,0:T(8,128)S(1)}, u32[]{:S(2)}, u32[]{:S(2)}) collective-permute-start(f32[200,128]{1,0:T(8,128)S(1)} %add_add_fusion.2), channel_id=1, source_target_pairs={{0,24},{8,32},{16,40},{24,48},{32,56},{1,25},{9,33},{17,41},{25,49... | collective-permute-start | bytes 307208 | tf_op jit(solution)/shard_map/ppermute | solution.py:427
  58.1 1.5 collective-permute-start.17
  60.4 3.6 %shard_map.81.refs_4_ = f32[8,128,128]{2,1,0:T(8,128)} custom-call(bf16[1024,128]{1,0:T(8,128)(2,1)} %get-tuple-element.26.refs_2_.refs_0_.refs_1_, bf16[1024,128]{1,0:T(8,128)(2,1)} %get-tuple-element.27.refs_1_.refs_2_, f32[8,128,128]{2,1,0:T(8,128)} %copy-done), custom_call_target="tpu_custom_call" | custom-call | flops 268435456 | bytes 1572864 | tf_op jit(solution)/shard_map/pallas_call | solution.py:184
  64.0 3.8 %shard_map.79 = (bf16[1024,128]{1,0:T(8,128)(2,1)}, f32[8,128,128]{2,1,0:T(8,128)}) custom-call(s32[9]{0:T(128)} %stack.55.refs_0_, bf16[1024,1024]{1,0:T(8,128)(2,1)} %refs_11_.1, bf16[1024,128]{1,0:T(8,128)(2,1)} %get-tuple-element.26.refs_2_.refs_0_.refs_1_, bf16[1024,1024]{1,0:T(8,128)(2,1)} %get-tuple-element.28.refs_3_.refs_10_), custom_call_target="tpu_custom_call" | custom-call | flops 335544320 | bytes 3145728 | tf_op jit(solution)/shard_map/pallas_call | solution.py:184
  68.6 6.4 %shard_map.82 = (f32[8,128,128]{2,1,0:T(8,128)}, f32[8,128,128]{2,1,0:T(8,128)}, f32[200,128]{1,0:T(8,128)}) custom-call(s32[9]{0:T(128)} %stack.55.refs_0_, bf16[1024,128]{1,0:T(8,128)(2,1)} %get-tuple-element.29.refs_1_.refs_0_, bf16[1024,128]{1,0:T(8,128)(2,1)} %get-tuple-element.26.refs_2_.refs_0_.refs_1_, f32[8,128,128]{2,1,0:T(8,128)} %get-tuple-element.30.refs_3_, ...), custom_call_target="tpu_custom_call" | custom-call | flops 1342177280 | bytes 3661824 | tf_op jit(solution)/shard_map/pallas_call | solution.py:184
  77.6 5.9 %collective-permute-done.18.refs_6_ = f32[200,128]{1,0:T(8,128)S(1)} collective-permute-done((f32[200,128]{1,0:T(8,128)}, f32[200,128]{1,0:T(8,128)S(1)}, u32[]{:S(2)}, u32[]{:S(2)}) %collective-permute-start.18) | collective-permute-done | bytes 102432 | tf_op jit(solution)/shard_map/ppermute | solution.py:427
  83.6 5.8 %collective-permute-done.19.refs_7_ = f32[200,128]{1,0:T(8,128)S(1)} collective-permute-done((f32[200,128]{1,0:T(8,128)}, f32[200,128]{1,0:T(8,128)S(1)}, u32[]{:S(2)}, u32[]{:S(2)}) %collective-permute-start.19) | collective-permute-done | bytes 102432 | tf_op jit(solution)/shard_map/ppermute | solution.py:427
  93.6 6.3 %shard_map.83 = (f32[8,128,128]{2,1,0:T(8,128)}, f32[8,128,128]{2,1,0:T(8,128)}, f32[8,128,128]{2,1,0:T(8,128)}) custom-call(bf16[1024,128]{1,0:T(8,128)(2,1)} %get-tuple-element.29.refs_1_.refs_0_, bf16[1024,128]{1,0:T(8,128)(2,1)} %get-tuple-element.26.refs_2_.refs_0_.refs_1_, bf16[1024,128]{1,0:T(8,128)(2,1)} %get-tuple-element.27.refs_1_.refs_2_, ...), custom_call_target="tpu_custom_call" | custom-call | flops 1006632960 | bytes 3932160 | tf_op jit(solution)/shard_map/pallas_call | solution.py:184
  101.5 5.3 %shard_map.84 = (f32[256,128]{1,0:T(8,128)}, f32[256,128]{1,0:T(8,128)}, f32[256,128]{1,0:T(8,128)}, f32[256,128]{1,0:T(8,128)}, f32[768,128]{1,0:T(8,128)}, /*i...) custom-call(s32[3]{0:T(128)} %pad_add_fusion.refs_0_, ...), custom_call_target="tpu_custom_call" | custom-call | flops 469762048 | bytes 6701056 | tf_op jit(solution)/shard_map/pallas_call | solution.py:184
  106.8 1.4 collective-permute-start.22
  108.3 2.7 %collective-permute-start.23 = (f32[768,128]{1,0:T(8,128)}, f32[768,128]{1,0:T(8,128)S(1)}, u32[]{:S(2)}, u32[]{:S(2)}) collective-permute-start(f32[768,128]{1,0:T(8,128)} %get-tuple-element.40), channel_id=1, source_target_pairs={{0,4},{2,6},{4,0},{6,2},{1,5},{3,7},{5,1},{7,3},{8,12},{10,14},{12... | collective-permute-start | bytes 1179656 | tf_op jit(solution)/shard_map/ppermute | solution.py:427
  110.9 1.5 collective-permute-start.24
  112.9 2.4 %collective-permute-start.30 = (f32[256,128]{1,0:T(8,128)}, f32[256,128]{1,0:T(8,128)S(1)}, u32[]{:S(2)}, u32[]{:S(2)}) collective-permute-start(f32[256,128]{1,0:T(8,128)} %get-tuple-element.44), channel_id=1, source_target_pairs={{0,128},{64,192},{128,0},{192,64},{1,129},{65,193},{129,1},{193,65... | collective-permute-start | bytes 393224 | tf_op jit(solution)/shard_map/ppermute | solution.py:427
  115.4 2.2 %collective-permute-done.31 = f32[256,128]{1,0:T(8,128)S(1)} collective-permute-done((f32[256,128]{1,0:T(8,128)}, f32[256,128]{1,0:T(8,128)S(1)}, u32[]{:S(2)}, u32[]{:S(2)}) %collective-permute-start.31) | collective-permute-done | bytes 131104 | tf_op jit(solution)/shard_map/ppermute | solution.py:427
  117.6 1.5 collective-permute-start.29
  119.9 5.5 %collective-permute-done.22.refs_2_ = f32[768,128]{1,0:T(8,128)S(1)} collective-permute-done((f32[768,128]{1,0:T(8,128)}, f32[768,128]{1,0:T(8,128)S(1)}, u32[]{:S(2)}, u32[]{:S(2)}) %collective-permute-start.22) | collective-permute-done | bytes 393248 | tf_op jit(solution)/shard_map/ppermute | solution.py:427
  127.2 20.0 %all_to_all.10 = f32[64,4,128]{2,1,0:T(4,128)S(1)} all-to-all(f32[64,4,128]{2,1,0:T(4,128)S(1)} %bitcast.20), channel_id=1, replica_groups=mesh['seq'=4,'z'=8,'y'=4,'core'=2] {'z','y','core'}, dimensions={0} | all-to-all | bytes 262144 | tf_op jit(solution)/shard_map/all_to_all | solution.py:437
  149.5 6.5 %shard_map.85 = bf16[128,1024]{1,0:T(8,128)(2,1)} custom-call(s32[3]{0:T(128)} %pad_add_fusion.refs_0_, f32[768,128]{1,0:T(8,128)} %get-tuple-element.38.refs_1_, f32[768,128]{1,0:T(8,128)} %copy-done.3, f32[768,128]{1,0:T(8,128)} %copy-done.4, f32[768,128]{1,0:T(8,128)} %copy-done.5, f32[768,128]{1,0:T(8,128)} %copy-done.6, f32[768,128]{1,0:T(8,128)} %copy-done.7, ...), custom_call_target="tpu_custom_call" | custom-call | flops 805306368 | bytes 9699328 | tf_op jit(solution)/shard_map/pallas_call | solution.py:184
  (104 shorter events, 20.2 us)
Async XLA Ops:
  2.5 10.7 %collective-permute-start.2 = (f32[64,1024]{1,0:T(8,128)}, f32[64,1024]{1,0:T(8,128)S(1)}, u32[]{:S(2)}, u32[]{:S(2)}) collective-permute-start(f32[64,1024]{1,0:T(8,128)} %get-tuple-element.24.refs_3_), channel_id=1, source_target_pairs={{0,2},{2,4},{4,6},{6,0},{1,3},{3,5},{5,7},{7,1},{8,10},{10,12},{12... | collective-permute-start | bytes 786440 | tf_op jit(solution)/shard_map/ppermute | solution.py:427
  4.2 9.0 %collective-permute-start.1 = (f32[64,1024]{1,0:T(8,128)}, f32[64,1024]{1,0:T(8,128)S(1)}, u32[]{:S(2)}, u32[]{:S(2)}) collective-permute-start(f32[64,1024]{1,0:T(8,128)} %get-tuple-element.25.refs_4_), channel_id=1, source_target_pairs={{0,1},{1,0},{2,3},{3,2},{4,5},{5,4},{6,7},{7,6},{8,9},{9,8},{10,11... | collective-permute-start | bytes 786440 | tf_op jit(solution)/shard_map/ppermute | solution.py:427
  4.3 9.4 %collective-permute-start.4 = (f32[64,1024]{1,0:T(8,128)}, f32[64,1024]{1,0:T(8,128)S(1)}, u32[]{:S(2)}, u32[]{:S(2)}) collective-permute-start(f32[64,1024]{1,0:T(8,128)} %get-tuple-element.25.refs_4_), channel_id=1, source_target_pairs={{0,6},{2,0},{4,2},{6,4},{1,7},{3,1},{5,3},{7,5},{8,14},{10,8},{12,... | collective-permute-start | bytes 786440 | tf_op jit(solution)/shard_map/ppermute | solution.py:427
  6.0 12.8 %collective-permute-start.6 = (f32[64,1024]{1,0:T(8,128)}, f32[64,1024]{1,0:T(8,128)S(1)}, u32[]{:S(2)}, u32[]{:S(2)}) collective-permute-start(f32[64,1024]{1,0:T(8,128)} %get-tuple-element.25.refs_4_), channel_id=1, source_target_pairs={{0,2},{2,4},{4,6},{6,0},{1,3},{3,5},{5,7},{7,1},{8,10},{10,12},{12... | collective-permute-start | bytes 786440 | tf_op jit(solution)/shard_map/ppermute | solution.py:427
  6.3 13.0 %collective-permute-start.8 = (f32[64,1024]{1,0:T(8,128)}, f32[64,1024]{1,0:T(8,128)S(1)}, u32[]{:S(2)}, u32[]{:S(2)}) collective-permute-start(f32[64,1024]{1,0:T(8,128)} %get-tuple-element.24.refs_3_), channel_id=1, source_target_pairs={{0,6},{2,0},{4,2},{6,4},{1,7},{3,1},{5,3},{7,5},{8,14},{10,8},{12,... | collective-permute-start | bytes 786440 | tf_op jit(solution)/shard_map/ppermute | solution.py:427
  13.2 6.1 %collective-permute-start.3 = (f32[64,1024]{1,0:T(8,128)S(1)}, f32[64,1024]{1,0:T(8,128)S(1)}, u32[]{:S(2)}, u32[]{:S(2)}) collective-permute-start(f32[64,1024]{1,0:T(8,128)S(1)} %collective-permute-done.2.refs_7_), channel_id=1, source_target_pairs={{0,1},{1,0},{2,3},{3,2},{4,5},{5,4},{6,7},{7,6},{8,9},{9,8},{10,11... | collective-permute-start | bytes 786440 | tf_op jit(solution)/shard_map/ppermute | solution.py:427
  13.2 10.7 %collective-permute-start.10 = (f32[64,1024]{1,0:T(8,128)S(1)}, f32[64,1024]{1,0:T(8,128)S(1)}, u32[]{:S(2)}, u32[]{:S(2)}) collective-permute-start(f32[64,1024]{1,0:T(8,128)S(1)} %collective-permute-done.2.refs_7_), channel_id=1, source_target_pairs={{0,2},{2,4},{4,6},{6,0},{1,3},{3,5},{5,7},{7,1},{8,10},{10,12},{12... | collective-permute-start | bytes 786440 | tf_op jit(solution)/shard_map/ppermute | solution.py:427
  13.7 10.6 %collective-permute-start.12 = (f32[64,1024]{1,0:T(8,128)S(1)}, f32[64,1024]{1,0:T(8,128)S(1)}, u32[]{:S(2)}, u32[]{:S(2)}) collective-permute-start(f32[64,1024]{1,0:T(8,128)S(1)} %collective-permute-done.4.refs_9_), channel_id=1, source_target_pairs={{0,6},{2,0},{4,2},{6,4},{1,7},{3,1},{5,3},{7,5},{8,14},{10,8},{12,... | collective-permute-start | bytes 786440 | tf_op jit(solution)/shard_map/ppermute | solution.py:427
  18.8 12.3 %collective-permute-start.5 = (f32[64,1024]{1,0:T(8,128)S(1)}, f32[64,1024]{1,0:T(8,128)S(1)}, u32[]{:S(2)}, u32[]{:S(2)}) collective-permute-start(f32[64,1024]{1,0:T(8,128)S(1)} %collective-permute-done.4.refs_9_), channel_id=1, source_target_pairs={{0,1},{1,0},{2,3},{3,2},{4,5},{5,4},{6,7},{7,6},{8,9},{9,8},{10,11... | collective-permute-start | bytes 786440 | tf_op jit(solution)/shard_map/ppermute | solution.py:427
  19.3 11.8 %collective-permute-start.7 = (f32[64,1024]{1,0:T(8,128)S(1)}, f32[64,1024]{1,0:T(8,128)S(1)}, u32[]{:S(2)}, u32[]{:S(2)}) collective-permute-start(f32[64,1024]{1,0:T(8,128)S(1)} %collective-permute-done.6.refs_11_), channel_id=1, source_target_pairs={{0,1},{1,0},{2,3},{3,2},{4,5},{5,4},{6,7},{7,6},{8,9},{9,8},{10,11... | collective-permute-start | bytes 786440 | tf_op jit(solution)/shard_map/ppermute | solution.py:427
  19.3 11.8 %collective-permute-start.9 = (f32[64,1024]{1,0:T(8,128)S(1)}, f32[64,1024]{1,0:T(8,128)}, u32[]{:S(2)}, u32[]{:S(2)}) collective-permute-start(f32[64,1024]{1,0:T(8,128)S(1)} %collective-permute-done.8.refs_13_), channel_id=1, source_target_pairs={{0,1},{1,0},{2,3},{3,2},{4,5},{5,4},{6,7},{7,6},{8,9},{9,8},{10,11... | collective-permute-start | bytes 786440 | tf_op jit(solution)/shard_map/ppermute | solution.py:427
  23.9 7.2 %collective-permute-start.11 = (f32[64,1024]{1,0:T(8,128)S(1)}, f32[64,1024]{1,0:T(8,128)}, u32[]{:S(2)}, u32[]{:S(2)}) collective-permute-start(f32[64,1024]{1,0:T(8,128)S(1)} %collective-permute-done.10.refs_15_), channel_id=1, source_target_pairs={{0,1},{1,0},{2,3},{3,2},{4,5},{5,4},{6,7},{7,6},{8,9},{9,8},{10,11... | collective-permute-start | bytes 786440 | tf_op jit(solution)/shard_map/ppermute | solution.py:427
  24.3 6.8 %collective-permute-start.13 = (f32[64,1024]{1,0:T(8,128)S(1)}, f32[64,1024]{1,0:T(8,128)}, u32[]{:S(2)}, u32[]{:S(2)}) collective-permute-start(f32[64,1024]{1,0:T(8,128)S(1)} %collective-permute-done.12.refs_17_), channel_id=1, source_target_pairs={{0,1},{1,0},{2,3},{3,2},{4,5},{5,4},{6,7},{7,6},{8,9},{9,8},{10,11... | collective-permute-start | bytes 786440 | tf_op jit(solution)/shard_map/ppermute | solution.py:427
  26.2 33.4 %all-to-all-start = ((f32[8,128,128]{2,1,0:T(8,128)}), f32[8,128,128]{2,1,0:T(8,128)S(1)}, u32[]{:S(2)}, u32[]{:S(2)}) async-start(f32[8,128,128]{2,1,0:T(8,128)} %shard_map.80), calls=%async_computation | async-start | bytes 1048576 | tf_op jit(solution)/shard_map/all_to_all | solution.py:437
  37.0 9.0 %collective-permute-start.14 = (f32[200,128]{1,0:T(8,128)}, f32[200,128]{1,0:T(8,128)S(1)}, u32[]{:S(2)}, u32[]{:S(2)}) collective-permute-start(f32[200,128]{1,0:T(8,128)} %get-tuple-element.31), channel_id=1, source_target_pairs={{0,8},{8,16},{16,24},{24,32},{32,40},{40,48},{48,56},{1,9},{9,17},... | collective-permute-start | bytes 307208 | tf_op jit(solution)/shard_map/ppermute | solution.py:427
  40.8 8.0 %collective-permute-start.15 = (f32[200,128]{1,0:T(8,128)}, f32[200,128]{1,0:T(8,128)S(1)}, u32[]{:S(2)}, u32[]{:S(2)}) collective-permute-start(f32[200,128]{1,0:T(8,128)} %get-tuple-element.31), channel_id=1, source_target_pairs={{0,16},{8,24},{16,32},{24,40},{32,48},{40,56},{1,17},{9,25},{17,33... | collective-permute-start | bytes 307208 | tf_op jit(solution)/shard_map/ppermute | solution.py:427
  49.8 18.1 %collective-permute-start.16 = (f32[200,128]{1,0:T(8,128)S(1)}, f32[200,128]{1,0:T(8,128)S(1)}, u32[]{:S(2)}, u32[]{:S(2)}) collective-permute-start(f32[200,128]{1,0:T(8,128)S(1)} %add_add_fusion.2), channel_id=1, source_target_pairs={{0,24},{8,32},{16,40},{24,48},{32,56},{1,25},{9,33},{17,41},{25,49... | collective-permute-start | bytes 307208 | tf_op jit(solution)/shard_map/ppermute | solution.py:427
  58.1 9.8 %collective-permute-start.17 = (f32[200,128]{1,0:T(8,128)S(1)}, f32[200,128]{1,0:T(8,128)S(1)}, u32[]{:S(2)}, u32[]{:S(2)}) collective-permute-start(f32[200,128]{1,0:T(8,128)S(1)} %add_add_fusion.2), channel_id=1, source_target_pairs={{0,48},{8,56},{1,49},{9,57},{2,50},{10,58},{3,51},{11,59},{4,52},{... | collective-permute-start | bytes 307208 | tf_op jit(solution)/shard_map/ppermute | solution.py:427
  75.0 8.5 %collective-permute-start.18 = (f32[200,128]{1,0:T(8,128)}, f32[200,128]{1,0:T(8,128)S(1)}, u32[]{:S(2)}, u32[]{:S(2)}) collective-permute-start(f32[200,128]{1,0:T(8,128)} %get-tuple-element.37), channel_id=1, source_target_pairs={{8,0},{16,8},{24,16},{32,24},{40,32},{48,40},{56,48},{9,1},{17,9},... | collective-permute-start | bytes 307208 | tf_op jit(solution)/shard_map/ppermute | solution.py:427
  76.3 13.1 %collective-permute-start.19 = (f32[200,128]{1,0:T(8,128)}, f32[200,128]{1,0:T(8,128)S(1)}, u32[]{:S(2)}, u32[]{:S(2)}) collective-permute-start(f32[200,128]{1,0:T(8,128)} %get-tuple-element.37), channel_id=1, source_target_pairs={{16,0},{24,8},{32,16},{40,24},{48,32},{56,40},{17,1},{25,9},{33,17... | collective-permute-start | bytes 307208 | tf_op jit(solution)/shard_map/ppermute | solution.py:427
  90.4 10.5 %collective-permute-start.20 = (f32[200,128]{1,0:T(8,128)S(1)}, f32[200,128]{1,0:T(8,128)S(1)}, u32[]{:S(2)}, u32[]{:S(2)}) collective-permute-start(f32[200,128]{1,0:T(8,128)S(1)} %add_add_fusion.1), channel_id=1, source_target_pairs={{24,0},{32,8},{40,16},{48,24},{56,32},{25,1},{33,9},{41,17},{49,25... | collective-permute-start | bytes 307208 | tf_op jit(solution)/shard_map/ppermute | solution.py:427
  91.7 9.2 %collective-permute-start.21 = (f32[200,128]{1,0:T(8,128)S(1)}, f32[200,128]{1,0:T(8,128)S(1)}, u32[]{:S(2)}, u32[]{:S(2)}) collective-permute-start(f32[200,128]{1,0:T(8,128)S(1)} %add_add_fusion.1), channel_id=1, source_target_pairs={{48,0},{56,8},{49,1},{57,9},{50,2},{58,10},{51,3},{59,11},{52,4},{... | collective-permute-start | bytes 307208 | tf_op jit(solution)/shard_map/ppermute | solution.py:427
  106.8 18.6 %collective-permute-start.22 = (f32[768,128]{1,0:T(8,128)}, f32[768,128]{1,0:T(8,128)S(1)}, u32[]{:S(2)}, u32[]{:S(2)}) collective-permute-start(f32[768,128]{1,0:T(8,128)} %get-tuple-element.39), channel_id=1, source_target_pairs={{0,2},{2,4},{4,6},{6,0},{1,3},{3,5},{5,7},{7,1},{8,10},{10,12},{12... | collective-permute-start | bytes 1179656 | tf_op jit(solution)/shard_map/ppermute | solution.py:427
  108.3 17.2 %collective-permute-start.23 = (f32[768,128]{1,0:T(8,128)}, f32[768,128]{1,0:T(8,128)S(1)}, u32[]{:S(2)}, u32[]{:S(2)}) collective-permute-start(f32[768,128]{1,0:T(8,128)} %get-tuple-element.40), channel_id=1, source_target_pairs={{0,4},{2,6},{4,0},{6,2},{1,5},{3,7},{5,1},{7,3},{8,12},{10,14},{12... | collective-permute-start | bytes 1179656 | tf_op jit(solution)/shard_map/ppermute | solution.py:427
  110.9 15.1 %collective-permute-start.24 = (f32[768,128]{1,0:T(8,128)}, f32[768,128]{1,0:T(8,128)S(1)}, u32[]{:S(2)}, u32[]{:S(2)}) collective-permute-start(f32[768,128]{1,0:T(8,128)} %get-tuple-element.41), channel_id=1, source_target_pairs={{0,6},{2,0},{4,2},{6,4},{1,7},{3,1},{5,3},{7,5},{8,14},{10,8},{12,... | collective-permute-start | bytes 1179656 | tf_op jit(solution)/shard_map/ppermute | solution.py:427
  112.4 5.2 %collective-permute-start.31 = (f32[256,128]{1,0:T(8,128)}, f32[256,128]{1,0:T(8,128)S(1)}, u32[]{:S(2)}, u32[]{:S(2)}) collective-permute-start(f32[256,128]{1,0:T(8,128)} %get-tuple-element.45), channel_id=1, source_target_pairs={{0,192},{64,0},{128,64},{192,128},{1,193},{65,1},{129,65},{193,129... | collective-permute-start | bytes 393224 | tf_op jit(solution)/shard_map/ppermute | solution.py:427
  112.9 7.0 %collective-permute-start.30 = (f32[256,128]{1,0:T(8,128)}, f32[256,128]{1,0:T(8,128)S(1)}, u32[]{:S(2)}, u32[]{:S(2)}) collective-permute-start(f32[256,128]{1,0:T(8,128)} %get-tuple-element.44), channel_id=1, source_target_pairs={{0,128},{64,192},{128,0},{192,64},{1,129},{65,193},{129,1},{193,65... | collective-permute-start | bytes 393224 | tf_op jit(solution)/shard_map/ppermute | solution.py:427
  117.6 8.5 %collective-permute-start.29 = (f32[256,128]{1,0:T(8,128)}, f32[256,128]{1,0:T(8,128)S(1)}, u32[]{:S(2)}, u32[]{:S(2)}) collective-permute-start(f32[256,128]{1,0:T(8,128)} %get-tuple-element.43), channel_id=1, source_target_pairs={{0,64},{64,128},{128,192},{192,0},{1,65},{65,129},{129,193},{193,1... | collective-permute-start | bytes 393224 | tf_op jit(solution)/shard_map/ppermute | solution.py:427
  119.9 27.8 %collective-permute-start.25 = (f32[768,128]{1,0:T(8,128)}, f32[768,128]{1,0:T(8,128)S(1)}, u32[]{:S(2)}, u32[]{:S(2)}) collective-permute-start(f32[768,128]{1,0:T(8,128)} %get-tuple-element.38.refs_1_), channel_id=1, source_target_pairs={{0,1},{1,0},{2,3},{3,2},{4,5},{5,4},{6,7},{7,6},{8,9},{9,8},{10,11... | collective-permute-start | bytes 1179656 | tf_op jit(solution)/shard_map/ppermute | solution.py:427
  125.4 22.3 %collective-permute-start.26 = (f32[768,128]{1,0:T(8,128)S(1)}, f32[768,128]{1,0:T(8,128)S(1)}, u32[]{:S(2)}, u32[]{:S(2)}) collective-permute-start(f32[768,128]{1,0:T(8,128)S(1)} %collective-permute-done.22.refs_2_), channel_id=1, source_target_pairs={{0,1},{1,0},{2,3},{3,2},{4,5},{5,4},{6,7},{7,6},{8,9},{9,8},{10,11... | collective-permute-start | bytes 1179656 | tf_op jit(solution)/shard_map/ppermute | solution.py:427
  125.5 22.3 %collective-permute-start.27 = (f32[768,128]{1,0:T(8,128)S(1)}, f32[768,128]{1,0:T(8,128)S(1)}, u32[]{:S(2)}, u32[]{:S(2)}) collective-permute-start(f32[768,128]{1,0:T(8,128)S(1)} %collective-permute-done.23.refs_3_), channel_id=1, source_target_pairs={{0,1},{1,0},{2,3},{3,2},{4,5},{5,4},{6,7},{7,6},{8,9},{9,8},{10,11... | collective-permute-start | bytes 1179656 | tf_op jit(solution)/shard_map/ppermute | solution.py:427
  126.1 21.7 %collective-permute-start.28 = (f32[768,128]{1,0:T(8,128)S(1)}, f32[768,128]{1,0:T(8,128)S(1)}, u32[]{:S(2)}, u32[]{:S(2)}) collective-permute-start(f32[768,128]{1,0:T(8,128)S(1)} %collective-permute-done.24.refs_4_), channel_id=1, source_target_pairs={{0,1},{1,0},{2,3},{3,2},{4,5},{5,4},{6,7},{7,6},{8,9},{9,8},{10,11... | collective-permute-start | bytes 1179656 | tf_op jit(solution)/shard_map/ppermute | solution.py:427
  (28 other events, 277.2 us)

commit v6 on v5

--- a/solution.py
+++ b/solution.py
@@ -342,7 +342,7 @@
 
 def local_body(tables, need, made, put):
     q_in, k_in, v_in, g_in, z_in, u_in = [need(n) for n in range(6)]
-    dq_out, dk_out, dv_out = made
+    dq_out, dk_out = made
     keep = causal(DK)
     for j in range(CHUNKS):
         q, u = q_in[chunk(j), :], u_in[j]
@@ -367,17 +367,31 @@
         dkn = fold_rows(fold_cols(tn(wide(left), right)))
         dkn = dkn + nn(twice_wide(v), tall(cross))
         dk_out[j] = dkn - rk * nn(kk, tall(gram))
-        dv_out[j] = rk * nt(kk, wide(cross)) + tn(tall(pair[DK:]), twice_tall(g))
         if j:
             swapped = jnp.concatenate([u_wide, z_wide], axis=0)
             gram = gram + fold_rows(fold_cols(tn(swapped, right)))
             cross = cross + fold_cols(tn(g, z_wide))
 
 
+def value_terms_body(tables, need, made, put):
+    k_in, g_in, z_in = [need(n) for n in range(3)]
+    keep = causal(DK)
+    cross = jnp.zeros((DK, DK), F32)
+    for j in reversed(range(CHUNKS)):
+        k, g = k_in[chunk(j), :], g_in[j].astype(BF16)
+        rk = inv_norm(k)
+        kk = twice_wide(k)
+        z_wide = wide(z_in[j])
+        scores = nt(z_wide, kk) * jnp.where(keep, across(rk), 0.0)
+        made[0][j] = rk * nt(kk, wide(cross)) + tn(tall(scores), twice_tall(g))
+        if j:
+            cross = cross + fold_cols(tn(g, z_wide))
+
+
 def grads_body(seq, tables, need, made, put, dk_buf, dw_buf, out):
     (place,) = tables
-    k_in, v_in, dk_part, dv_part, dq_in = [need(n) for n in range(5)]
-    gram_after, cross_after = total_of(need, 5)
+    k_in, v_in, dk_part, dv_part = [need(n) for n in range(4)]
+    gram_after, cross_after = total_of(need, 4)
     gram_tall, cross_tall, cross_wide = tall(gram_after), tall(cross_after), wide(cross_after)
     for j in range(CHUNKS):
         k, v = k_in[chunk(j), :], v_in[chunk(j), :]
@@ -389,9 +403,8 @@
         dk_buf[chunk(j), :] = dk
         out[j, :DK] = dk.astype(F32)
         dv = dv_part[j] + rk * nt(kk, cross_wide)
-        out[j, DK : 2 * DK] = dv.astype(BF16).astype(F32)
-        out[j, 2 * DK :] = dq_in[j]
-    dw_buf[...] = jnp.transpose(tn(dk_buf[...], need(9)[...]))
+        out[j, DK:] = dv.astype(BF16).astype(F32)
+    dw_buf[...] = jnp.transpose(tn(dk_buf[...], need(8)[...]))
     rows = made[0].shape[0]
     for step in range(seq):
         start = pl.multiple_of(lax.rem(place[0] + step, seq) * rows, rows)
@@ -400,9 +413,14 @@
     core = place[2]
     for step in range(CHUNKS // 2):
         block = lax.rem(place[1] + step, CHUNKS // 2) * 2
-        made[seq + step][: 3 * DK] = out[block + core]
-        made[seq + step][3 * DK :] = out[block + 1 - core]
+        made[seq + step][: 2 * DK] = out[block + core]
+        made[seq + step][2 * DK :] = out[block + 1 - core]
         put(seq + step)
+
+
+def query_part_body(tables, need, made, put):
+    cat = jnp.concatenate([need(0)[h].astype(BF16) for h in range(HEADS)], axis=1)
+    made[0][...] = nt(cat, need(1)[...])
 
 
 def input_grad_body(tables, need, made, put, *sides):
@@ -415,9 +433,9 @@
         cols = pl.ds(pl.multiple_of(head * DK, DK), DK)
         for n, side in enumerate(sides):
             side[:, cols] = piece[chunk(n), :].astype(BF16)
-    total = nt(sides[0][...], need(HEADS)[...])
-    for n in (1, 2):
-        total = total + nt(sides[n][...], need(HEADS + n)[...])
+    total = need(HEADS)[...]
+    for n, side in enumerate(sides):
+        total = total + nt(side[...], need(HEADS + 1 + n)[...])
     made[0][...] = total.astype(BF16)
 
 
@@ -430,7 +448,9 @@
 def exclusive(total, sign):
     one, two = shift(total, "z", sign, False), shift(total, "z", 2 * sign, False)
     third = total + one + two
-    return one, two, shift(third, "z", 3 * sign, False), shift(third, "z", 6 * sign, False)
+    six = shift(third, "z", 6 * sign, False)
+    three = shift(third, "z", 3 * sign, False)
+    return one, two, three, six
 
 
 def exchange(x, axis):
@@ -497,7 +517,11 @@
         [q, k, gram_pre, part, g, damping, *prior], unit * 40, tables=[where],
     )
     after = exclusive(second_tot, -1)
-    dq, dk_part, dv_part = call(local_body, [blocks, blocks, blocks], [q, k, v, g, z, u], unit * 30)
+    dq, dk_part = call(local_body, [blocks, blocks], [q, k, v, g, z, u], unit * 26)
+    (dv_part,) = call(value_terms_body, [blocks], [k, g, z], unit * 8)
+    dq_all = exchange(dq, PLANE)
+    (partial,) = call(query_part_body, [shaped(tokens, width)], [dq_all, w_query], unit * 8)
+
     seq = lax.axis_size("seq")
     ctx = ("z", "y", "core")
     spread = lax.axis_size(ctx)
@@ -507,11 +531,11 @@
     ).astype(jnp.int32)
     pieces = call(
         functools.partial(grads_body, seq),
-        [shaped(width // seq, DK)] * seq + [shaped(6 * tokens, DK)] * (CHUNKS // 2),
-        [k, v, dk_part, dv_part, dq, *after, xb], unit * 14, tables=[place],
+        [shaped(width // seq, DK)] * seq + [shaped(4 * tokens, DK)] * (CHUNKS // 2),
+        [k, v, dk_part, dv_part, *after, xb], unit * 14, tables=[place],
         scratch=[
             pltpu.VMEM((plane, DK), BF16), pltpu.VMEM((width, DK), F32),
-            pltpu.VMEM((CHUNKS, 3 * tokens, DK), F32),
+            pltpu.VMEM((CHUNKS, 2 * tokens, DK), F32),
         ],
     )
     dw, dkv = pieces[:seq], pieces[seq:]
@@ -522,12 +546,12 @@
     dw = dw.reshape(spread // HEADS, HEADS, rows, DK)
     grad_weights = jnp.sum(dw, axis=0).transpose(1, 0, 2).reshape(rows, HEADS * DK)
 
-    mine_of = [(p, slice(0, 3 * tokens)) for p in dkv]
-    other_of = [(p, slice(3 * tokens, 6 * tokens)) for p in other]
+    mine_of = [(p, slice(0, 2 * tokens)) for p in dkv]
+    other_of = [(p, slice(2 * tokens, 4 * tokens)) for p in other]
     (grad_inputs,) = call(
         input_grad_body, [shaped(tokens, width, dtype=BF16)],
-        [*mine_of, *other_of, w_key, w_value, w_query], unit * 24, tables=[place],
-        scratch=[pltpu.VMEM((tokens, width), BF16)] * 3,
+        [*mine_of, *other_of, partial, w_key, w_value], unit * 16, tables=[place],
+        scratch=[pltpu.VMEM((tokens, width), BF16)] * 2,
     )
     return (grad_inputs[None], grad_weights)
 

time: 158 us -> 165 us (1.044)
  the two profiles are of different devices: /device:TPU:2 before, /device:TPU:1 now
where the time goes in v6:
time: 165 us; the launch traced here: 164 us
  starting transfers between devices  71.5 us (43%)
  Pallas kernels  46.2 us (28%)
  waiting for transfers between devices  35.1 us (21%)
  local copies, waits for them, and re-layouts  5.06 us (3%)
  other arithmetic  4.81 us (3%)
    ppermute x32, starting transfers between devices, shift(): return lax.ppermute(x, axis, pairs)  47.8 us
    pallas_call x11, Pallas kernels, call(): pl.pallas_call(kernel, out_shape=tuple(outs), in_specs=[pl.BlockSpec(memo...  46.2 us
    ppermute x32, waiting for transfers between devices, shift(): return lax.ppermute(x, axis, pairs)  27.4 us
    all_to_all x3, starting transfers between devices, exchange(): return lax.all_to_all(x, axis, 0, 0)  23.7 us
    all_to_all x3, waiting for transfers between devices, exchange(): return lax.all_to_all(x, axis, 0, 0)  7.67 us
    unnamed x56, local copies, waits for them, and re-layouts  4.38 us
  transfers between devices with their start and end apart: 35, of which 9 were waited for; matrix products, arithmetic and copies ran while one was open for 3% of the time, Pallas kernels for 17%

profile of v6, /device:TPU:1, one launch (start us, length us, event | category | flops | bytes accessed | tf_op | source)
XLA Modules:
  0.0 164.0 jit_solution(6284466665767779662)
XLA Ops:
  0.6 1.8 %shard_map.77 = (f32[64,1024]{1,0:T(8,128)}, f32[64,1024]{1,0:T(8,128)}) custom-call(bf16[128,1024]{1,0:T(8,128)(2,1)} %bitcast.23), custom_call_target="tpu_custom_call" | custom-call | bytes 786432 | tf_op jit(solution)/shard_map/pallas_call | solution.py:184
  2.4 3.3 %collective-permute-start = (f32[64,1024]{1,0:T(8,128)}, f32[64,1024]{1,0:T(8,128)S(1)}, u32[]{:S(2)}, u32[]{:S(2)}) collective-permute-start(f32[64,1024]{1,0:T(8,128)} %get-tuple-element.23.refs_3_), channel_id=1, source_target_pairs={{0,1},{1,0},{2,3},{3,2},{4,5},{5,4},{6,7},{7,6},{8,9},{9,8},{10,11... | collective-permute-start | bytes 786440 | tf_op jit(solution)/shard_map/ppermute | solution.py:445
  5.9 2.9 %collective-permute-start.4 = (f32[64,1024]{1,0:T(8,128)}, f32[64,1024]{1,0:T(8,128)S(1)}, u32[]{:S(2)}, u32[]{:S(2)}) collective-permute-start(f32[64,1024]{1,0:T(8,128)} %get-tuple-element.24.refs_4_), channel_id=1, source_target_pairs={{0,6},{2,0},{4,2},{6,4},{1,7},{3,1},{5,3},{7,5},{8,14},{10,8},{12,... | collective-permute-start | bytes 786440 | tf_op jit(solution)/shard_map/ppermute | solution.py:445
  8.8 2.7 %collective-permute-start.8 = (f32[64,1024]{1,0:T(8,128)}, f32[64,1024]{1,0:T(8,128)S(1)}, u32[]{:S(2)}, u32[]{:S(2)}) collective-permute-start(f32[64,1024]{1,0:T(8,128)} %get-tuple-element.23.refs_3_), channel_id=1, source_target_pairs={{0,6},{2,0},{4,2},{6,4},{1,7},{3,1},{5,3},{7,5},{8,14},{10,8},{12,... | collective-permute-start | bytes 786440 | tf_op jit(solution)/shard_map/ppermute | solution.py:445
  11.4 3.5 %collective-permute-done.2.refs_7_ = f32[64,1024]{1,0:T(8,128)S(1)} collective-permute-done((f32[64,1024]{1,0:T(8,128)}, f32[64,1024]{1,0:T(8,128)S(1)}, u32[]{:S(2)}, u32[]{:S(2)}) %collective-permute-start.2) | collective-permute-done | bytes 262176 | tf_op jit(solution)/shard_map/ppermute | solution.py:445
  16.4 2.7 %collective-permute-start.12 = (f32[64,1024]{1,0:T(8,128)S(1)}, f32[64,1024]{1,0:T(8,128)S(1)}, u32[]{:S(2)}, u32[]{:S(2)}) collective-permute-start(f32[64,1024]{1,0:T(8,128)S(1)} %collective-permute-done.4.refs_9_), channel_id=1, source_target_pairs={{0,6},{2,0},{4,2},{6,4},{1,7},{3,1},{5,3},{7,5},{8,14},{10,8},{12,... | collective-permute-start | bytes 786440 | tf_op jit(solution)/shard_map/ppermute | solution.py:445
  22.5 3.6 %collective-permute-done.10.refs_15_ = f32[64,1024]{1,0:T(8,128)S(1)} collective-permute-done((f32[64,1024]{1,0:T(8,128)S(1)}, f32[64,1024]{1,0:T(8,128)S(1)}, u32[]{:S(2)}, u32[]{:S(2)}) %collective-permute-start.10) | collective-permute-done | bytes 262176 | tf_op jit(solution)/shard_map/ppermute | solution.py:445
  27.2 1.8 %shard_map.80 = f32[8,128,128]{2,1,0:T(8,128)} custom-call(bf16[128,1024]{1,0:T(8,128)(2,1)} %bitcast.22), custom_call_target="tpu_custom_call" | custom-call | bytes 786432 | tf_op jit(solution)/shard_map/pallas_call | solution.py:184
  29.0 4.6 %all-to-all-start = ((f32[8,128,128]{2,1,0:T(8,128)}), f32[8,128,128]{2,1,0:T(8,128)S(1)}, u32[]{:S(2)}, u32[]{:S(2)}) async-start(f32[8,128,128]{2,1,0:T(8,128)} %shard_map.80), calls=%async_computation | async-start | bytes 1048576 | tf_op jit(solution)/shard_map/all_to_all | solution.py:457
  35.1 5.0 %shard_map.78 = (bf16[1024,1024]{1,0:T(8,128)(2,1)}, bf16[1024,128]{1,0:T(8,128)(2,1)}, bf16[1024,128]{1,0:T(8,128)(2,1)}, f32[200,128]{1,0:T(8,128)}) custom-call(s32[9]{0:T(128)} %stack.55.refs_0_, bf16[1024,1024]{1,0:T(8,128)(2,1)} %refs_10_.1, bf16[1024,1024]{1,0:T(8,128)(2,1)} %refs_11_.1, f32[64,1024]{1,0:T(8,128)} %get-tuple-element.23.refs_3_, ...), custom_call_target="tpu_custom_call" | custom-call | flops 939524096 | bytes 6918144 | tf_op jit(solution)/shard_map/pallas_call | solution.py:184
  40.1 1.9 %collective-permute-start.14 = (f32[200,128]{1,0:T(8,128)}, f32[200,128]{1,0:T(8,128)S(1)}, u32[]{:S(2)}, u32[]{:S(2)}) collective-permute-start(f32[200,128]{1,0:T(8,128)} %get-tuple-element.30), channel_id=1, source_target_pairs={{0,8},{8,16},{16,24},{24,32},{32,40},{40,48},{48,56},{1,9},{9,17},... | collective-permute-start | bytes 307208 | tf_op jit(solution)/shard_map/ppermute | solution.py:445
  42.0 4.9 %collective-permute-start.15 = (f32[200,128]{1,0:T(8,128)}, f32[200,128]{1,0:T(8,128)S(1)}, u32[]{:S(2)}, u32[]{:S(2)}) collective-permute-start(f32[200,128]{1,0:T(8,128)} %get-tuple-element.30), channel_id=1, source_target_pairs={{0,16},{8,24},{16,32},{24,40},{32,48},{40,56},{1,17},{9,25},{17,33... | collective-permute-start | bytes 307208 | tf_op jit(solution)/shard_map/ppermute | solution.py:445
  46.9 2.2 %collective-permute-done.15.refs_8_ = f32[200,128]{1,0:T(8,128)S(1)} collective-permute-done((f32[200,128]{1,0:T(8,128)}, f32[200,128]{1,0:T(8,128)S(1)}, u32[]{:S(2)}, u32[]{:S(2)}) %collective-permute-start.15) | collective-permute-done | bytes 102432 | tf_op jit(solution)/shard_map/ppermute | solution.py:445
  50.1 8.6 %collective-permute-start.16 = (f32[200,128]{1,0:T(8,128)S(1)}, f32[200,128]{1,0:T(8,128)S(1)}, u32[]{:S(2)}, u32[]{:S(2)}) collective-permute-start(f32[200,128]{1,0:T(8,128)S(1)} %add_add_fusion.2), channel_id=1, source_target_pairs={{0,24},{8,32},{16,40},{24,48},{32,56},{1,25},{9,33},{17,41},{25,49... | collective-permute-start | bytes 307208 | tf_op jit(solution)/shard_map/ppermute | solution.py:445
  61.0 3.6 %shard_map.81.refs_4_ = f32[8,128,128]{2,1,0:T(8,128)} custom-call(bf16[1024,128]{1,0:T(8,128)(2,1)} %get-tuple-element.25.refs_2_.refs_0_.refs_1_, bf16[1024,128]{1,0:T(8,128)(2,1)} %get-tuple-element.26.refs_1_.refs_2_, f32[8,128,128]{2,1,0:T(8,128)} %copy-done), custom_call_target="tpu_custom_call" | custom-call | flops 268435456 | bytes 1572864 | tf_op jit(solution)/shard_map/pallas_call | solution.py:184
  64.6 3.8 %shard_map.79 = (bf16[1024,128]{1,0:T(8,128)(2,1)}, f32[8,128,128]{2,1,0:T(8,128)}) custom-call(s32[9]{0:T(128)} %stack.55.refs_0_, bf16[1024,1024]{1,0:T(8,128)(2,1)} %refs_1_.5, bf16[1024,128]{1,0:T(8,128)(2,1)} %get-tuple-element.25.refs_2_.refs_0_.refs_1_, bf16[1024,1024]{1,0:T(8,128)(2,1)} %get-tuple-element.27.refs_3_.refs_9_), custom_call_target="tpu_custom_call" | custom-call | flops 335544320 | bytes 3145728 | tf_op jit(solution)/shard_map/pallas_call | solution.py:184
  69.2 6.4 %shard_map.82 = (f32[8,128,128]{2,1,0:T(8,128)}, f32[8,128,128]{2,1,0:T(8,128)}, f32[200,128]{1,0:T(8,128)}) custom-call(s32[9]{0:T(128)} %stack.55.refs_0_, bf16[1024,128]{1,0:T(8,128)(2,1)} %get-tuple-element.28.refs_1_.refs_0_, bf16[1024,128]{1,0:T(8,128)(2,1)} %get-tuple-element.25.refs_2_.refs_0_.refs_1_, f32[8,128,128]{2,1,0:T(8,128)} %get-tuple-element.29.refs_3_, ...), custom_call_target="tpu_custom_call" | custom-call | flops 1342177280 | bytes 3661824 | tf_op jit(solution)/shard_map/pallas_call | solution.py:184
  78.9 4.0 %collective-permute-done.18.refs_5_ = f32[200,128]{1,0:T(8,128)S(1)} collective-permute-done((f32[200,128]{1,0:T(8,128)}, f32[200,128]{1,0:T(8,128)S(1)}, u32[]{:S(2)}, u32[]{:S(2)}) %collective-permute-start.18) | collective-permute-done | bytes 102432 | tf_op jit(solution)/shard_map/ppermute | solution.py:445
  82.8 6.2 %collective-permute-done.19.refs_6_ = f32[200,128]{1,0:T(8,128)S(1)} collective-permute-done((f32[200,128]{1,0:T(8,128)}, f32[200,128]{1,0:T(8,128)S(1)}, u32[]{:S(2)}, u32[]{:S(2)}) %collective-permute-start.19) | collective-permute-done | bytes 102432 | tf_op jit(solution)/shard_map/ppermute | solution.py:445
  92.6 4.2 %shard_map.84.refs_4_ = f32[8,128,128]{2,1,0:T(8,128)} custom-call(bf16[1024,128]{1,0:T(8,128)(2,1)} %get-tuple-element.25.refs_2_.refs_0_.refs_1_, f32[8,128,128]{2,1,0:T(8,128)} %copy-done, f32[8,128,128]{2,1,0:T(8,128)} %get-tuple-element.31.refs_4_.refs_2_), custom_call_target="tpu_custom_call" | custom-call | flops 268435456 | bytes 1835008 | tf_op jit(solution)/shard_map/pallas_call | solution.py:184
  96.9 5.9 %shard_map.83 = (f32[8,128,128]{2,1,0:T(8,128)}, f32[8,128,128]{2,1,0:T(8,128)}) custom-call(bf16[1024,128]{1,0:T(8,128)(2,1)} %get-tuple-element.28.refs_1_.refs_0_, bf16[1024,128]{1,0:T(8,128)(2,1)} %get-tuple-element.25.refs_2_.refs_0_.refs_1_, bf16[1024,128]{1,0:T(8,128)(2,1)} %get-tuple-element.26.refs_1_.refs_2_, f32[8,128,128]{2,1,0:T(8,128)} %copy-done, ...), custom_call_target="tpu_custom_call" | custom-call | flops 872415232 | bytes 3407872 | tf_op jit(solution)/shard_map/pallas_call | solution.py:184
  103.5 4.9 %shard_map.85 = (f32[256,128]{1,0:T(8,128)}, f32[256,128]{1,0:T(8,128)}, f32[256,128]{1,0:T(8,128)}, f32[256,128]{1,0:T(8,128)}, f32[512,128]{1,0:T(8,128)}, /*i...) custom-call(s32[3]{0:T(128)} %pad_add_fusion.refs_0_, ...), custom_call_target="tpu_custom_call" | custom-call | flops 469762048 | bytes 5652480 | tf_op jit(solution)/shard_map/pallas_call | solution.py:184
  108.7 2.2 %collective-permute-start.23 = (f32[512,128]{1,0:T(8,128)}, f32[512,128]{1,0:T(8,128)S(1)}, u32[]{:S(2)}, u32[]{:S(2)}) collective-permute-start(f32[512,128]{1,0:T(8,128)} %get-tuple-element.37), channel_id=1, source_target_pairs={{0,4},{2,6},{4,0},{6,2},{1,5},{3,7},{5,1},{7,3},{8,12},{10,14},{12... | collective-permute-start | bytes 786440 | tf_op jit(solution)/shard_map/ppermute | solution.py:445
  112.1 2.5 %collective-permute-start.31 = (f32[256,128]{1,0:T(8,128)}, f32[256,128]{1,0:T(8,128)S(1)}, u32[]{:S(2)}, u32[]{:S(2)}) collective-permute-start(f32[256,128]{1,0:T(8,128)} %get-tuple-element.43), channel_id=1, source_target_pairs={{0,192},{64,0},{128,64},{192,128},{1,193},{65,1},{129,65},{193,129... | collective-permute-start | bytes 393224 | tf_op jit(solution)/shard_map/ppermute | solution.py:445
  114.6 7.7 %all-to-all-start.1 = ((f32[8,128,128]{2,1,0:T(8,128)}), f32[8,128,128]{2,1,0:T(8,128)S(1)}, u32[]{:S(2)}, u32[]{:S(2)}) async-start(f32[8,128,128]{2,1,0:T(8,128)} %get-tuple-element.39), calls=%async_computation.1 | async-start | bytes 1048576 | tf_op jit(solution)/shard_map/all_to_all | solution.py:457
  123.4 5.5 %collective-permute-done.30 = f32[256,128]{1,0:T(8,128)S(1)} collective-permute-done((f32[256,128]{1,0:T(8,128)}, f32[256,128]{1,0:T(8,128)S(1)}, u32[]{:S(2)}, u32[]{:S(2)}) %collective-permute-start.30) | collective-permute-done | bytes 131104 | tf_op jit(solution)/shard_map/ppermute | solution.py:445
  128.9 1.7 %collective-permute-start.25 = (f32[512,128]{1,0:T(8,128)}, f32[512,128]{1,0:T(8,128)S(1)}, u32[]{:S(2)}, u32[]{:S(2)}) collective-permute-start(f32[512,128]{1,0:T(8,128)} %get-tuple-element.35.refs_1_), channel_id=1, source_target_pairs={{0,1},{1,0},{2,3},{3,2},{4,5},{5,4},{6,7},{7,6},{8,9},{9,8},{10,11... | collective-permute-start | bytes 786440 | tf_op jit(solution)/shard_map/ppermute | solution.py:445
  132.2 1.6 add_add_fusion
  133.8 11.4 %all-to-all-start.2 = ((f32[64,4,128]{2,1,0:T(4,128)}), f32[64,4,128]{2,1,0:T(4,128)S(1)}, u32[]{:S(2)}, u32[]{:S(2)}) async-start(f32[64,4,128]{2,1,0:T(4,128)} %bitcast.15), calls=%async_computation.2 | async-start | bytes 262144 | tf_op jit(solution)/shard_map/all_to_all | solution.py:457
  145.2 3.4 %shard_map.86.refs_9_ = f32[128,1024]{1,0:T(8,128)} custom-call(f32[8,128,128]{2,1,0:T(8,128)} %copy-done.1, bf16[1024,1024]{1,0:T(8,128)(2,1)} %refs_1_.5), custom_call_target="tpu_custom_call" | custom-call | flops 268435456 | bytes 3145728 | tf_op jit(solution)/shard_map/pallas_call | solution.py:184
  148.7 7.7 %all-to-all-done.2 = f32[64,4,128]{2,1,0:T(4,128)S(1)} async-done(((f32[64,4,128]{2,1,0:T(4,128)}), f32[64,4,128]{2,1,0:T(4,128)S(1)}, u32[]{:S(2)}, u32[]{:S(2)}) %all-to-all-start.2) | async-done | bytes 131104 | tf_op jit(solution)/shard_map/all_to_all | solution.py:457
  158.6 5.2 %shard_map.87 = bf16[128,1024]{1,0:T(8,128)(2,1)} custom-call(s32[3]{0:T(128)} %pad_add_fusion.refs_0_, f32[512,128]{1,0:T(8,128)} %get-tuple-element.35.refs_1_, f32[512,128]{1,0:T(8,128)} %copy-done.4, f32[512,128]{1,0:T(8,128)} %copy-done.5, f32[512,128]{1,0:T(8,128)} %copy-done.6, f32[512,128]{1,0:T(8,128)} %copy-done.7, f32[512,128]{1,0:T(8,128)} %copy-done.8, ...), custom_call_target="tpu_custom_call" | custom-call | flops 536870912 | bytes 7077888 | tf_op jit(solution)/shard_map/pallas_call | solution.py:184
  (111 shorter events, 25.4 us)
Async XLA Ops:
  5.7 9.2 %collective-permute-start.2 = (f32[64,1024]{1,0:T(8,128)}, f32[64,1024]{1,0:T(8,128)S(1)}, u32[]{:S(2)}, u32[]{:S(2)}) collective-permute-start(f32[64,1024]{1,0:T(8,128)} %get-tuple-element.23.refs_3_), channel_id=1, source_target_pairs={{0,2},{2,4},{4,6},{6,0},{1,3},{3,5},{5,7},{7,1},{8,10},{10,12},{12... | collective-permute-start | bytes 786440 | tf_op jit(solution)/shard_map/ppermute | solution.py:445
  5.7 10.7 %collective-permute-start.1 = (f32[64,1024]{1,0:T(8,128)}, f32[64,1024]{1,0:T(8,128)S(1)}, u32[]{:S(2)}, u32[]{:S(2)}) collective-permute-start(f32[64,1024]{1,0:T(8,128)} %get-tuple-element.24.refs_4_), channel_id=1, source_target_pairs={{0,1},{1,0},{2,3},{3,2},{4,5},{5,4},{6,7},{7,6},{8,9},{9,8},{10,11... | collective-permute-start | bytes 786440 | tf_op jit(solution)/shard_map/ppermute | solution.py:445
  5.9 10.5 %collective-permute-start.4 = (f32[64,1024]{1,0:T(8,128)}, f32[64,1024]{1,0:T(8,128)S(1)}, u32[]{:S(2)}, u32[]{:S(2)}) collective-permute-start(f32[64,1024]{1,0:T(8,128)} %get-tuple-element.24.refs_4_), channel_id=1, source_target_pairs={{0,6},{2,0},{4,2},{6,4},{1,7},{3,1},{5,3},{7,5},{8,14},{10,8},{12,... | collective-permute-start | bytes 786440 | tf_op jit(solution)/shard_map/ppermute | solution.py:445
  8.7 11.8 %collective-permute-start.6 = (f32[64,1024]{1,0:T(8,128)}, f32[64,1024]{1,0:T(8,128)S(1)}, u32[]{:S(2)}, u32[]{:S(2)}) collective-permute-start(f32[64,1024]{1,0:T(8,128)} %get-tuple-element.24.refs_4_), channel_id=1, source_target_pairs={{0,2},{2,4},{4,6},{6,0},{1,3},{3,5},{5,7},{7,1},{8,10},{10,12},{12... | collective-permute-start | bytes 786440 | tf_op jit(solution)/shard_map/ppermute | solution.py:445
  8.8 13.3 %collective-permute-start.8 = (f32[64,1024]{1,0:T(8,128)}, f32[64,1024]{1,0:T(8,128)S(1)}, u32[]{:S(2)}, u32[]{:S(2)}) collective-permute-start(f32[64,1024]{1,0:T(8,128)} %get-tuple-element.23.refs_3_), channel_id=1, source_target_pairs={{0,6},{2,0},{4,2},{6,4},{1,7},{3,1},{5,3},{7,5},{8,14},{10,8},{12,... | collective-permute-start | bytes 786440 | tf_op jit(solution)/shard_map/ppermute | solution.py:445
  14.9 7.2 %collective-permute-start.3 = (f32[64,1024]{1,0:T(8,128)S(1)}, f32[64,1024]{1,0:T(8,128)S(1)}, u32[]{:S(2)}, u32[]{:S(2)}) collective-permute-start(f32[64,1024]{1,0:T(8,128)S(1)} %collective-permute-done.2.refs_7_), channel_id=1, source_target_pairs={{0,1},{1,0},{2,3},{3,2},{4,5},{5,4},{6,7},{7,6},{8,9},{9,8},{10,11... | collective-permute-start | bytes 786440 | tf_op jit(solution)/shard_map/ppermute | solution.py:445
  16.4 9.7 %collective-permute-start.10 = (f32[64,1024]{1,0:T(8,128)S(1)}, f32[64,1024]{1,0:T(8,128)S(1)}, u32[]{:S(2)}, u32[]{:S(2)}) collective-permute-start(f32[64,1024]{1,0:T(8,128)S(1)} %collective-permute-done.2.refs_7_), channel_id=1, source_target_pairs={{0,2},{2,4},{4,6},{6,0},{1,3},{3,5},{5,7},{7,1},{8,10},{10,12},{12... | collective-permute-start | bytes 786440 | tf_op jit(solution)/shard_map/ppermute | solution.py:445
  16.4 10.7 %collective-permute-start.12 = (f32[64,1024]{1,0:T(8,128)S(1)}, f32[64,1024]{1,0:T(8,128)S(1)}, u32[]{:S(2)}, u32[]{:S(2)}) collective-permute-start(f32[64,1024]{1,0:T(8,128)S(1)} %collective-permute-done.4.refs_9_), channel_id=1, source_target_pairs={{0,6},{2,0},{4,2},{6,4},{1,7},{3,1},{5,3},{7,5},{8,14},{10,8},{12,... | collective-permute-start | bytes 786440 | tf_op jit(solution)/shard_map/ppermute | solution.py:445
  20.5 13.8 %collective-permute-start.5 = (f32[64,1024]{1,0:T(8,128)S(1)}, f32[64,1024]{1,0:T(8,128)S(1)}, u32[]{:S(2)}, u32[]{:S(2)}) collective-permute-start(f32[64,1024]{1,0:T(8,128)S(1)} %collective-permute-done.4.refs_9_), channel_id=1, source_target_pairs={{0,1},{1,0},{2,3},{3,2},{4,5},{5,4},{6,7},{7,6},{8,9},{9,8},{10,11... | collective-permute-start | bytes 786440 | tf_op jit(solution)/shard_map/ppermute | solution.py:445
  22.0 12.3 %collective-permute-start.7 = (f32[64,1024]{1,0:T(8,128)S(1)}, f32[64,1024]{1,0:T(8,128)S(1)}, u32[]{:S(2)}, u32[]{:S(2)}) collective-permute-start(f32[64,1024]{1,0:T(8,128)S(1)} %collective-permute-done.6.refs_11_), channel_id=1, source_target_pairs={{0,1},{1,0},{2,3},{3,2},{4,5},{5,4},{6,7},{7,6},{8,9},{9,8},{10,11... | collective-permute-start | bytes 786440 | tf_op jit(solution)/shard_map/ppermute | solution.py:445
  22.1 12.2 %collective-permute-start.9 = (f32[64,1024]{1,0:T(8,128)S(1)}, f32[64,1024]{1,0:T(8,128)}, u32[]{:S(2)}, u32[]{:S(2)}) collective-permute-start(f32[64,1024]{1,0:T(8,128)S(1)} %collective-permute-done.8.refs_13_), channel_id=1, source_target_pairs={{0,1},{1,0},{2,3},{3,2},{4,5},{5,4},{6,7},{7,6},{8,9},{9,8},{10,11... | collective-permute-start | bytes 786440 | tf_op jit(solution)/shard_map/ppermute | solution.py:445
  26.1 8.2 %collective-permute-start.11 = (f32[64,1024]{1,0:T(8,128)S(1)}, f32[64,1024]{1,0:T(8,128)}, u32[]{:S(2)}, u32[]{:S(2)}) collective-permute-start(f32[64,1024]{1,0:T(8,128)S(1)} %collective-permute-done.10.refs_15_), channel_id=1, source_target_pairs={{0,1},{1,0},{2,3},{3,2},{4,5},{5,4},{6,7},{7,6},{8,9},{9,8},{10,11... | collective-permute-start | bytes 786440 | tf_op jit(solution)/shard_map/ppermute | solution.py:445
  27.1 7.2 %collective-permute-start.13 = (f32[64,1024]{1,0:T(8,128)S(1)}, f32[64,1024]{1,0:T(8,128)}, u32[]{:S(2)}, u32[]{:S(2)}) collective-permute-start(f32[64,1024]{1,0:T(8,128)S(1)} %collective-permute-done.12.refs_17_), channel_id=1, source_target_pairs={{0,1},{1,0},{2,3},{3,2},{4,5},{5,4},{6,7},{7,6},{8,9},{9,8},{10,11... | collective-permute-start | bytes 786440 | tf_op jit(solution)/shard_map/ppermute | solution.py:445
  29.0 31.2 %all-to-all-start = ((f32[8,128,128]{2,1,0:T(8,128)}), f32[8,128,128]{2,1,0:T(8,128)S(1)}, u32[]{:S(2)}, u32[]{:S(2)}) async-start(f32[8,128,128]{2,1,0:T(8,128)} %shard_map.80), calls=%async_computation | async-start | bytes 1048576 | tf_op jit(solution)/shard_map/all_to_all | solution.py:457
  42.0 7.2 %collective-permute-start.15 = (f32[200,128]{1,0:T(8,128)}, f32[200,128]{1,0:T(8,128)S(1)}, u32[]{:S(2)}, u32[]{:S(2)}) collective-permute-start(f32[200,128]{1,0:T(8,128)} %get-tuple-element.30), channel_id=1, source_target_pairs={{0,16},{8,24},{16,32},{24,40},{32,48},{40,56},{1,17},{9,25},{17,33... | collective-permute-start | bytes 307208 | tf_op jit(solution)/shard_map/ppermute | solution.py:445
  50.1 18.3 %collective-permute-start.16 = (f32[200,128]{1,0:T(8,128)S(1)}, f32[200,128]{1,0:T(8,128)S(1)}, u32[]{:S(2)}, u32[]{:S(2)}) collective-permute-start(f32[200,128]{1,0:T(8,128)S(1)} %add_add_fusion.2), channel_id=1, source_target_pairs={{0,24},{8,32},{16,40},{24,48},{32,56},{1,25},{9,33},{17,41},{25,49... | collective-permute-start | bytes 307208 | tf_op jit(solution)/shard_map/ppermute | solution.py:445
  58.7 9.8 %collective-permute-start.17 = (f32[200,128]{1,0:T(8,128)S(1)}, f32[200,128]{1,0:T(8,128)S(1)}, u32[]{:S(2)}, u32[]{:S(2)}) collective-permute-start(f32[200,128]{1,0:T(8,128)S(1)} %add_add_fusion.2), channel_id=1, source_target_pairs={{0,48},{8,56},{1,49},{9,57},{2,50},{10,58},{3,51},{11,59},{4,52},{... | collective-permute-start | bytes 307208 | tf_op jit(solution)/shard_map/ppermute | solution.py:445
  75.6 7.2 %collective-permute-start.18 = (f32[200,128]{1,0:T(8,128)}, f32[200,128]{1,0:T(8,128)S(1)}, u32[]{:S(2)}, u32[]{:S(2)}) collective-permute-start(f32[200,128]{1,0:T(8,128)} %get-tuple-element.34), channel_id=1, source_target_pairs={{8,0},{16,8},{24,16},{32,24},{40,32},{48,40},{56,48},{9,1},{17,9},... | collective-permute-start | bytes 307208 | tf_op jit(solution)/shard_map/ppermute | solution.py:445
  76.9 12.1 %collective-permute-start.19 = (f32[200,128]{1,0:T(8,128)}, f32[200,128]{1,0:T(8,128)S(1)}, u32[]{:S(2)}, u32[]{:S(2)}) collective-permute-start(f32[200,128]{1,0:T(8,128)} %get-tuple-element.34), channel_id=1, source_target_pairs={{16,0},{24,8},{32,16},{40,24},{48,32},{56,40},{17,1},{25,9},{33,17... | collective-permute-start | bytes 307208 | tf_op jit(solution)/shard_map/ppermute | solution.py:445
  90.0 12.8 %collective-permute-start.20 = (f32[200,128]{1,0:T(8,128)S(1)}, f32[200,128]{1,0:T(8,128)S(1)}, u32[]{:S(2)}, u32[]{:S(2)}) collective-permute-start(f32[200,128]{1,0:T(8,128)S(1)} %add_add_fusion.1), channel_id=1, source_target_pairs={{24,0},{32,8},{40,16},{48,24},{56,32},{25,1},{33,9},{41,17},{49,25... | collective-permute-start | bytes 307208 | tf_op jit(solution)/shard_map/ppermute | solution.py:445
  91.3 11.5 %collective-permute-start.21 = (f32[200,128]{1,0:T(8,128)S(1)}, f32[200,128]{1,0:T(8,128)S(1)}, u32[]{:S(2)}, u32[]{:S(2)}) collective-permute-start(f32[200,128]{1,0:T(8,128)S(1)} %add_add_fusion.1), channel_id=1, source_target_pairs={{48,0},{56,8},{49,1},{57,9},{50,2},{58,10},{51,3},{59,11},{52,4},{... | collective-permute-start | bytes 307208 | tf_op jit(solution)/shard_map/ppermute | solution.py:445
  108.4 22.2 %collective-permute-start.22 = (f32[512,128]{1,0:T(8,128)}, f32[512,128]{1,0:T(8,128)S(1)}, u32[]{:S(2)}, u32[]{:S(2)}) collective-permute-start(f32[512,128]{1,0:T(8,128)} %get-tuple-element.36), channel_id=1, source_target_pairs={{0,2},{2,4},{4,6},{6,0},{1,3},{3,5},{5,7},{7,1},{8,10},{10,12},{12... | collective-permute-start | bytes 786440 | tf_op jit(solution)/shard_map/ppermute | solution.py:445
  108.7 22.0 %collective-permute-start.23 = (f32[512,128]{1,0:T(8,128)}, f32[512,128]{1,0:T(8,128)S(1)}, u32[]{:S(2)}, u32[]{:S(2)}) collective-permute-start(f32[512,128]{1,0:T(8,128)} %get-tuple-element.37), channel_id=1, source_target_pairs={{0,4},{2,6},{4,0},{6,2},{1,5},{3,7},{5,1},{7,3},{8,12},{10,14},{12... | collective-permute-start | bytes 786440 | tf_op jit(solution)/shard_map/ppermute | solution.py:445
  110.9 20.2 %collective-permute-start.24 = (f32[512,128]{1,0:T(8,128)}, f32[512,128]{1,0:T(8,128)S(1)}, u32[]{:S(2)}, u32[]{:S(2)}) collective-permute-start(f32[512,128]{1,0:T(8,128)} %get-tuple-element.38), channel_id=1, source_target_pairs={{0,6},{2,0},{4,2},{6,4},{1,7},{3,1},{5,3},{7,5},{8,14},{10,8},{12,... | collective-permute-start | bytes 786440 | tf_op jit(solution)/shard_map/ppermute | solution.py:445
  112.1 10.7 %collective-permute-start.31 = (f32[256,128]{1,0:T(8,128)}, f32[256,128]{1,0:T(8,128)S(1)}, u32[]{:S(2)}, u32[]{:S(2)}) collective-permute-start(f32[256,128]{1,0:T(8,128)} %get-tuple-element.43), channel_id=1, source_target_pairs={{0,192},{64,0},{128,64},{192,128},{1,193},{65,1},{129,65},{193,129... | collective-permute-start | bytes 393224 | tf_op jit(solution)/shard_map/ppermute | solution.py:445
  114.6 19.2 %all-to-all-start.1 = ((f32[8,128,128]{2,1,0:T(8,128)}), f32[8,128,128]{2,1,0:T(8,128)S(1)}, u32[]{:S(2)}, u32[]{:S(2)}) async-start(f32[8,128,128]{2,1,0:T(8,128)} %get-tuple-element.39), calls=%async_computation.1 | async-start | bytes 1048576 | tf_op jit(solution)/shard_map/all_to_all | solution.py:457
  122.8 9.4 %collective-permute-start.29 = (f32[256,128]{1,0:T(8,128)}, f32[256,128]{1,0:T(8,128)S(1)}, u32[]{:S(2)}, u32[]{:S(2)}) collective-permute-start(f32[256,128]{1,0:T(8,128)} %get-tuple-element.41), channel_id=1, source_target_pairs={{0,64},{64,128},{128,192},{192,0},{1,65},{65,129},{129,193},{193,1... | collective-permute-start | bytes 393224 | tf_op jit(solution)/shard_map/ppermute | solution.py:445
  128.9 28.1 %collective-permute-start.25 = (f32[512,128]{1,0:T(8,128)}, f32[512,128]{1,0:T(8,128)S(1)}, u32[]{:S(2)}, u32[]{:S(2)}) collective-permute-start(f32[512,128]{1,0:T(8,128)} %get-tuple-element.35.refs_1_), channel_id=1, source_target_pairs={{0,1},{1,0},{2,3},{3,2},{4,5},{5,4},{6,7},{7,6},{8,9},{9,8},{10,11... | collective-permute-start | bytes 786440 | tf_op jit(solution)/shard_map/ppermute | solution.py:445
  130.6 26.4 %collective-permute-start.26 = (f32[512,128]{1,0:T(8,128)S(1)}, f32[512,128]{1,0:T(8,128)S(1)}, u32[]{:S(2)}, u32[]{:S(2)}) collective-permute-start(f32[512,128]{1,0:T(8,128)S(1)} %collective-permute-done.22.refs_2_), channel_id=1, source_target_pairs={{0,1},{1,0},{2,3},{3,2},{4,5},{5,4},{6,7},{7,6},{8,9},{9,8},{10,11... | collective-permute-start | bytes 786440 | tf_op jit(solution)/shard_map/ppermute | solution.py:445
  130.7 26.3 %collective-permute-start.27 = (f32[512,128]{1,0:T(8,128)S(1)}, f32[512,128]{1,0:T(8,128)S(1)}, u32[]{:S(2)}, u32[]{:S(2)}) collective-permute-start(f32[512,128]{1,0:T(8,128)S(1)} %collective-permute-done.23.refs_3_), channel_id=1, source_target_pairs={{0,1},{1,0},{2,3},{3,2},{4,5},{5,4},{6,7},{7,6},{8,9},{9,8},{10,11... | collective-permute-start | bytes 786440 | tf_op jit(solution)/shard_map/ppermute | solution.py:445
  131.1 25.9 %collective-permute-start.28 = (f32[512,128]{1,0:T(8,128)S(1)}, f32[512,128]{1,0:T(8,128)S(1)}, u32[]{:S(2)}, u32[]{:S(2)}) collective-permute-start(f32[512,128]{1,0:T(8,128)S(1)} %collective-permute-done.24.refs_4_), channel_id=1, source_target_pairs={{0,1},{1,0},{2,3},{3,2},{4,5},{5,4},{6,7},{7,6},{8,9},{9,8},{10,11... | collective-permute-start | bytes 786440 | tf_op jit(solution)/shard_map/ppermute | solution.py:445
  133.8 22.5 %all-to-all-start.2 = ((f32[64,4,128]{2,1,0:T(4,128)}), f32[64,4,128]{2,1,0:T(4,128)S(1)}, u32[]{:S(2)}, u32[]{:S(2)}) async-start(f32[64,4,128]{2,1,0:T(4,128)} %bitcast.15), calls=%async_computation.2 | async-start | bytes 262144 | tf_op jit(solution)/shard_map/all_to_all | solution.py:457
  (31 other events, 327.2 us)

commit v7 on v6

--- a/solution.py
+++ b/solution.py
@@ -342,7 +342,7 @@
 
 def local_body(tables, need, made, put):
     q_in, k_in, v_in, g_in, z_in, u_in = [need(n) for n in range(6)]
-    dq_out, dk_out = made
+    dq_out, dk_out, dv_out = made
     keep = causal(DK)
     for j in range(CHUNKS):
         q, u = q_in[chunk(j), :], u_in[j]
@@ -367,24 +367,10 @@
         dkn = fold_rows(fold_cols(tn(wide(left), right)))
         dkn = dkn + nn(twice_wide(v), tall(cross))
         dk_out[j] = dkn - rk * nn(kk, tall(gram))
+        dv_out[j] = rk * nt(kk, wide(cross)) + tn(tall(pair[DK:]), twice_tall(g))
         if j:
             swapped = jnp.concatenate([u_wide, z_wide], axis=0)
             gram = gram + fold_rows(fold_cols(tn(swapped, right)))
-            cross = cross + fold_cols(tn(g, z_wide))
-
-
-def value_terms_body(tables, need, made, put):
-    k_in, g_in, z_in = [need(n) for n in range(3)]
-    keep = causal(DK)
-    cross = jnp.zeros((DK, DK), F32)
-    for j in reversed(range(CHUNKS)):
-        k, g = k_in[chunk(j), :], g_in[j].astype(BF16)
-        rk = inv_norm(k)
-        kk = twice_wide(k)
-        z_wide = wide(z_in[j])
-        scores = nt(z_wide, kk) * jnp.where(keep, across(rk), 0.0)
-        made[0][j] = rk * nt(kk, wide(cross)) + tn(tall(scores), twice_tall(g))
-        if j:
             cross = cross + fold_cols(tn(g, z_wide))
 
 
@@ -517,8 +503,7 @@
         [q, k, gram_pre, part, g, damping, *prior], unit * 40, tables=[where],
     )
     after = exclusive(second_tot, -1)
-    dq, dk_part = call(local_body, [blocks, blocks], [q, k, v, g, z, u], unit * 26)
-    (dv_part,) = call(value_terms_body, [blocks], [k, g, z], unit * 8)
+    dq, dk_part, dv_part = call(local_body, [blocks, blocks, blocks], [q, k, v, g, z, u], unit * 30)
     dq_all = exchange(dq, PLANE)
     (partial,) = call(query_part_body, [shaped(tokens, width)], [dq_all, w_query], unit * 8)
 

time: 165 us -> 161 us (0.976)
  Pallas kernels: 46.2 us -> 42.3 us
    pallas_call x11 -> x10, Pallas kernels: 46.2 us -> 42.3 us  [call(): pl.pallas_call(kernel, out_shape=tuple(outs), in_specs=[pl.BlockSpec(memo...]
  transfers between devices with their start and end apart: 35 -> 35, of which waited for: 9 -> 9; matrix products, arithmetic and copies ran while one was open for 3% -> 3% of each run, Pallas kernels for 17% -> 15%
where the time goes in v7:
time: 161 us
  starting transfers between devices  71.2 us (44%)
  Pallas kernels  42.3 us (26%)
  waiting for transfers between devices  35.8 us (22%)
  local copies, waits for them, and re-layouts  5.04 us (3%)
  other arithmetic  4.81 us (3%)
    ppermute x32, starting transfers between devices, shift(): return lax.ppermute(x, axis, pairs)  47.5 us
    pallas_call x10, Pallas kernels, call(): pl.pallas_call(kernel, out_shape=tuple(outs), in_specs=[pl.BlockSpec(memo...  42.3 us
    ppermute x32, waiting for transfers between devices, shift(): return lax.ppermute(x, axis, pairs)  28.2 us
    all_to_all x3, starting transfers between devices, exchange(): return lax.all_to_all(x, axis, 0, 0)  23.7 us
    all_to_all x3, waiting for transfers between devices, exchange(): return lax.all_to_all(x, axis, 0, 0)  7.67 us
    unnamed x56, local copies, waits for them, and re-layouts  4.37 us
  transfers between devices with their start and end apart: 35, of which 9 were waited for; matrix products, arithmetic and copies ran while one was open for 3% of the time, Pallas kernels for 15%

profile of v7, /device:TPU:1, one launch (start us, length us, event | category | flops | bytes accessed | tf_op | source)
XLA Modules:
  0.0 160.5 jit_solution(18404900312387336912)
XLA Ops:
  0.6 1.8 %shard_map.77 = (f32[64,1024]{1,0:T(8,128)}, f32[64,1024]{1,0:T(8,128)}) custom-call(bf16[128,1024]{1,0:T(8,128)(2,1)} %bitcast.23), custom_call_target="tpu_custom_call" | custom-call | bytes 786432 | tf_op jit(solution)/shard_map/pallas_call | solution.py:184
  2.4 3.3 %collective-permute-start = (f32[64,1024]{1,0:T(8,128)}, f32[64,1024]{1,0:T(8,128)S(1)}, u32[]{:S(2)}, u32[]{:S(2)}) collective-permute-start(f32[64,1024]{1,0:T(8,128)} %get-tuple-element.24.refs_3_), channel_id=1, source_target_pairs={{0,1},{1,0},{2,3},{3,2},{4,5},{5,4},{6,7},{7,6},{8,9},{9,8},{10,11... | collective-permute-start | bytes 786440 | tf_op jit(solution)/shard_map/ppermute | solution.py:431
  5.9 2.9 %collective-permute-start.4 = (f32[64,1024]{1,0:T(8,128)}, f32[64,1024]{1,0:T(8,128)S(1)}, u32[]{:S(2)}, u32[]{:S(2)}) collective-permute-start(f32[64,1024]{1,0:T(8,128)} %get-tuple-element.25.refs_4_), channel_id=1, source_target_pairs={{0,6},{2,0},{4,2},{6,4},{1,7},{3,1},{5,3},{7,5},{8,14},{10,8},{12,... | collective-permute-start | bytes 786440 | tf_op jit(solution)/shard_map/ppermute | solution.py:431
  8.8 2.7 %collective-permute-start.8 = (f32[64,1024]{1,0:T(8,128)}, f32[64,1024]{1,0:T(8,128)S(1)}, u32[]{:S(2)}, u32[]{:S(2)}) collective-permute-start(f32[64,1024]{1,0:T(8,128)} %get-tuple-element.24.refs_3_), channel_id=1, source_target_pairs={{0,6},{2,0},{4,2},{6,4},{1,7},{3,1},{5,3},{7,5},{8,14},{10,8},{12,... | collective-permute-start | bytes 786440 | tf_op jit(solution)/shard_map/ppermute | solution.py:431
  11.4 3.5 %collective-permute-done.2.refs_7_ = f32[64,1024]{1,0:T(8,128)S(1)} collective-permute-done((f32[64,1024]{1,0:T(8,128)}, f32[64,1024]{1,0:T(8,128)S(1)}, u32[]{:S(2)}, u32[]{:S(2)}) %collective-permute-start.2) | collective-permute-done | bytes 262176 | tf_op jit(solution)/shard_map/ppermute | solution.py:431
  14.9 1.5 collective-permute-start.3
  16.4 2.7 %collective-permute-start.12 = (f32[64,1024]{1,0:T(8,128)S(1)}, f32[64,1024]{1,0:T(8,128)S(1)}, u32[]{:S(2)}, u32[]{:S(2)}) collective-permute-start(f32[64,1024]{1,0:T(8,128)S(1)} %collective-permute-done.4.refs_9_), channel_id=1, source_target_pairs={{0,6},{2,0},{4,2},{6,4},{1,7},{3,1},{5,3},{7,5},{8,14},{10,8},{12,... | collective-permute-start | bytes 786440 | tf_op jit(solution)/shard_map/ppermute | solution.py:431
  22.5 3.6 %collective-permute-done.10.refs_15_ = f32[64,1024]{1,0:T(8,128)S(1)} collective-permute-done((f32[64,1024]{1,0:T(8,128)S(1)}, f32[64,1024]{1,0:T(8,128)S(1)}, u32[]{:S(2)}, u32[]{:S(2)}) %collective-permute-start.10) | collective-permute-done | bytes 262176 | tf_op jit(solution)/shard_map/ppermute | solution.py:431
  27.2 1.8 %shard_map.80 = f32[8,128,128]{2,1,0:T(8,128)} custom-call(bf16[128,1024]{1,0:T(8,128)(2,1)} %bitcast.22), custom_call_target="tpu_custom_call" | custom-call | bytes 786432 | tf_op jit(solution)/shard_map/pallas_call | solution.py:184
  29.0 4.6 %all-to-all-start = ((f32[8,128,128]{2,1,0:T(8,128)}), f32[8,128,128]{2,1,0:T(8,128)S(1)}, u32[]{:S(2)}, u32[]{:S(2)}) async-start(f32[8,128,128]{2,1,0:T(8,128)} %shard_map.80), calls=%async_computation | async-start | bytes 1048576 | tf_op jit(solution)/shard_map/all_to_all | solution.py:443
  35.1 5.0 %shard_map.78 = (bf16[1024,1024]{1,0:T(8,128)(2,1)}, bf16[1024,128]{1,0:T(8,128)(2,1)}, bf16[1024,128]{1,0:T(8,128)(2,1)}, f32[200,128]{1,0:T(8,128)}) custom-call(s32[9]{0:T(128)} %stack.55.refs_0_, bf16[1024,1024]{1,0:T(8,128)(2,1)} %refs_10_.1, bf16[1024,1024]{1,0:T(8,128)(2,1)} %refs_11_.1, f32[64,1024]{1,0:T(8,128)} %get-tuple-element.24.refs_3_, ...), custom_call_target="tpu_custom_call" | custom-call | flops 939524096 | bytes 6918144 | tf_op jit(solution)/shard_map/pallas_call | solution.py:184
  40.1 1.9 %collective-permute-start.14 = (f32[200,128]{1,0:T(8,128)}, f32[200,128]{1,0:T(8,128)S(1)}, u32[]{:S(2)}, u32[]{:S(2)}) collective-permute-start(f32[200,128]{1,0:T(8,128)} %get-tuple-element.31), channel_id=1, source_target_pairs={{0,8},{8,16},{16,24},{24,32},{32,40},{40,48},{48,56},{1,9},{9,17},... | collective-permute-start | bytes 307208 | tf_op jit(solution)/shard_map/ppermute | solution.py:431
  42.0 4.9 %collective-permute-start.15 = (f32[200,128]{1,0:T(8,128)}, f32[200,128]{1,0:T(8,128)S(1)}, u32[]{:S(2)}, u32[]{:S(2)}) collective-permute-start(f32[200,128]{1,0:T(8,128)} %get-tuple-element.31), channel_id=1, source_target_pairs={{0,16},{8,24},{16,32},{24,40},{32,48},{40,56},{1,17},{9,25},{17,33... | collective-permute-start | bytes 307208 | tf_op jit(solution)/shard_map/ppermute | solution.py:431
  46.9 2.2 %collective-permute-done.15.refs_8_ = f32[200,128]{1,0:T(8,128)S(1)} collective-permute-done((f32[200,128]{1,0:T(8,128)}, f32[200,128]{1,0:T(8,128)S(1)}, u32[]{:S(2)}, u32[]{:S(2)}) %collective-permute-start.15) | collective-permute-done | bytes 102432 | tf_op jit(solution)/shard_map/ppermute | solution.py:431
  50.1 8.6 %collective-permute-start.16 = (f32[200,128]{1,0:T(8,128)S(1)}, f32[200,128]{1,0:T(8,128)S(1)}, u32[]{:S(2)}, u32[]{:S(2)}) collective-permute-start(f32[200,128]{1,0:T(8,128)S(1)} %add_add_fusion.2), channel_id=1, source_target_pairs={{0,24},{8,32},{16,40},{24,48},{32,56},{1,25},{9,33},{17,41},{25,49... | collective-permute-start | bytes 307208 | tf_op jit(solution)/shard_map/ppermute | solution.py:431
  61.0 3.6 %shard_map.81.refs_4_ = f32[8,128,128]{2,1,0:T(8,128)} custom-call(bf16[1024,128]{1,0:T(8,128)(2,1)} %get-tuple-element.26.refs_2_.refs_0_.refs_1_, bf16[1024,128]{1,0:T(8,128)(2,1)} %get-tuple-element.27.refs_1_.refs_2_, f32[8,128,128]{2,1,0:T(8,128)} %copy-done), custom_call_target="tpu_custom_call" | custom-call | flops 268435456 | bytes 1572864 | tf_op jit(solution)/shard_map/pallas_call | solution.py:184
  64.6 3.8 %shard_map.79 = (bf16[1024,128]{1,0:T(8,128)(2,1)}, f32[8,128,128]{2,1,0:T(8,128)}) custom-call(s32[9]{0:T(128)} %stack.55.refs_0_, bf16[1024,1024]{1,0:T(8,128)(2,1)} %refs_1_.5, bf16[1024,128]{1,0:T(8,128)(2,1)} %get-tuple-element.26.refs_2_.refs_0_.refs_1_, bf16[1024,1024]{1,0:T(8,128)(2,1)} %get-tuple-element.28.refs_3_.refs_9_), custom_call_target="tpu_custom_call" | custom-call | flops 335544320 | bytes 3145728 | tf_op jit(solution)/shard_map/pallas_call | solution.py:184
  69.2 6.4 %shard_map.82 = (f32[8,128,128]{2,1,0:T(8,128)}, f32[8,128,128]{2,1,0:T(8,128)}, f32[200,128]{1,0:T(8,128)}) custom-call(s32[9]{0:T(128)} %stack.55.refs_0_, bf16[1024,128]{1,0:T(8,128)(2,1)} %get-tuple-element.29.refs_1_.refs_0_, bf16[1024,128]{1,0:T(8,128)(2,1)} %get-tuple-element.26.refs_2_.refs_0_.refs_1_, f32[8,128,128]{2,1,0:T(8,128)} %get-tuple-element.30.refs_3_, ...), custom_call_target="tpu_custom_call" | custom-call | flops 1342177280 | bytes 3661824 | tf_op jit(solution)/shard_map/pallas_call | solution.py:184
  78.2 4.6 %collective-permute-done.18.refs_5_ = f32[200,128]{1,0:T(8,128)S(1)} collective-permute-done((f32[200,128]{1,0:T(8,128)}, f32[200,128]{1,0:T(8,128)S(1)}, u32[]{:S(2)}, u32[]{:S(2)}) %collective-permute-start.18) | collective-permute-done | bytes 102432 | tf_op jit(solution)/shard_map/ppermute | solution.py:431
  82.9 6.2 %collective-permute-done.19.refs_6_ = f32[200,128]{1,0:T(8,128)S(1)} collective-permute-done((f32[200,128]{1,0:T(8,128)}, f32[200,128]{1,0:T(8,128)S(1)}, u32[]{:S(2)}, u32[]{:S(2)}) %collective-permute-start.19) | collective-permute-done | bytes 102432 | tf_op jit(solution)/shard_map/ppermute | solution.py:431
  93.3 6.3 %shard_map.83 = (f32[8,128,128]{2,1,0:T(8,128)}, f32[8,128,128]{2,1,0:T(8,128)}, f32[8,128,128]{2,1,0:T(8,128)}) custom-call(bf16[1024,128]{1,0:T(8,128)(2,1)} %get-tuple-element.29.refs_1_.refs_0_, bf16[1024,128]{1,0:T(8,128)(2,1)} %get-tuple-element.26.refs_2_.refs_0_.refs_1_, bf16[1024,128]{1,0:T(8,128)(2,1)} %get-tuple-element.27.refs_1_.refs_2_, ...), custom_call_target="tpu_custom_call" | custom-call | flops 1006632960 | bytes 3932160 | tf_op jit(solution)/shard_map/pallas_call | solution.py:184
  100.3 4.9 %shard_map.84 = (f32[256,128]{1,0:T(8,128)}, f32[256,128]{1,0:T(8,128)}, f32[256,128]{1,0:T(8,128)}, f32[256,128]{1,0:T(8,128)}, f32[512,128]{1,0:T(8,128)}, /*i...) custom-call(s32[3]{0:T(128)} %pad_add_fusion.refs_0_, ...), custom_call_target="tpu_custom_call" | custom-call | flops 469762048 | bytes 5652480 | tf_op jit(solution)/shard_map/pallas_call | solution.py:184
  105.3 2.1 %collective-permute-start.23 = (f32[512,128]{1,0:T(8,128)}, f32[512,128]{1,0:T(8,128)S(1)}, u32[]{:S(2)}, u32[]{:S(2)}) collective-permute-start(f32[512,128]{1,0:T(8,128)} %get-tuple-element.39), channel_id=1, source_target_pairs={{0,4},{2,6},{4,0},{6,2},{1,5},{3,7},{5,1},{7,3},{8,12},{10,14},{12... | collective-permute-start | bytes 786440 | tf_op jit(solution)/shard_map/ppermute | solution.py:431
  108.7 2.4 %collective-permute-start.31 = (f32[256,128]{1,0:T(8,128)}, f32[256,128]{1,0:T(8,128)S(1)}, u32[]{:S(2)}, u32[]{:S(2)}) collective-permute-start(f32[256,128]{1,0:T(8,128)} %get-tuple-element.45), channel_id=1, source_target_pairs={{0,192},{64,0},{128,64},{192,128},{1,193},{65,1},{129,65},{193,129... | collective-permute-start | bytes 393224 | tf_op jit(solution)/shard_map/ppermute | solution.py:431
  111.1 8.6 %all-to-all-start.1 = ((f32[8,128,128]{2,1,0:T(8,128)}), f32[8,128,128]{2,1,0:T(8,128)S(1)}, u32[]{:S(2)}, u32[]{:S(2)}) async-start(f32[8,128,128]{2,1,0:T(8,128)} %get-tuple-element.41), calls=%async_computation.1 | async-start | bytes 1048576 | tf_op jit(solution)/shard_map/all_to_all | solution.py:443
  120.9 5.5 %collective-permute-done.30 = f32[256,128]{1,0:T(8,128)S(1)} collective-permute-done((f32[256,128]{1,0:T(8,128)}, f32[256,128]{1,0:T(8,128)S(1)}, u32[]{:S(2)}, u32[]{:S(2)}) %collective-permute-start.30) | collective-permute-done | bytes 131104 | tf_op jit(solution)/shard_map/ppermute | solution.py:431
  126.4 1.7 %collective-permute-start.25 = (f32[512,128]{1,0:T(8,128)}, f32[512,128]{1,0:T(8,128)S(1)}, u32[]{:S(2)}, u32[]{:S(2)}) collective-permute-start(f32[512,128]{1,0:T(8,128)} %get-tuple-element.37.refs_1_), channel_id=1, source_target_pairs={{0,1},{1,0},{2,3},{3,2},{4,5},{5,4},{6,7},{7,6},{8,9},{9,8},{10,11... | collective-permute-start | bytes 786440 | tf_op jit(solution)/shard_map/ppermute | solution.py:431
  129.7 1.6 add_add_fusion
  131.3 10.5 %all-to-all-start.2 = ((f32[64,4,128]{2,1,0:T(4,128)}), f32[64,4,128]{2,1,0:T(4,128)S(1)}, u32[]{:S(2)}, u32[]{:S(2)}) async-start(f32[64,4,128]{2,1,0:T(4,128)} %bitcast.15), calls=%async_computation.2 | async-start | bytes 262144 | tf_op jit(solution)/shard_map/all_to_all | solution.py:443
  141.8 3.4 %shard_map.85.refs_9_ = f32[128,1024]{1,0:T(8,128)} custom-call(f32[8,128,128]{2,1,0:T(8,128)} %copy-done.1, bf16[1024,1024]{1,0:T(8,128)(2,1)} %refs_1_.5), custom_call_target="tpu_custom_call" | custom-call | flops 268435456 | bytes 3145728 | tf_op jit(solution)/shard_map/pallas_call | solution.py:184
  145.2 7.7 %all-to-all-done.2 = f32[64,4,128]{2,1,0:T(4,128)S(1)} async-done(((f32[64,4,128]{2,1,0:T(4,128)}), f32[64,4,128]{2,1,0:T(4,128)S(1)}, u32[]{:S(2)}, u32[]{:S(2)}) %all-to-all-start.2) | async-done | bytes 131104 | tf_op jit(solution)/shard_map/all_to_all | solution.py:443
  155.1 5.2 %shard_map.86 = bf16[128,1024]{1,0:T(8,128)(2,1)} custom-call(s32[3]{0:T(128)} %pad_add_fusion.refs_0_, f32[512,128]{1,0:T(8,128)} %get-tuple-element.37.refs_1_, f32[512,128]{1,0:T(8,128)} %copy-done.4, f32[512,128]{1,0:T(8,128)} %copy-done.5, f32[512,128]{1,0:T(8,128)} %copy-done.6, f32[512,128]{1,0:T(8,128)} %copy-done.7, f32[512,128]{1,0:T(8,128)} %copy-done.8, ...), custom_call_target="tpu_custom_call" | custom-call | flops 536870912 | bytes 7077888 | tf_op jit(solution)/shard_map/pallas_call | solution.py:184
  (110 shorter events, 23.7 us)
Async XLA Ops:
  5.7 9.2 %collective-permute-start.2 = (f32[64,1024]{1,0:T(8,128)}, f32[64,1024]{1,0:T(8,128)S(1)}, u32[]{:S(2)}, u32[]{:S(2)}) collective-permute-start(f32[64,1024]{1,0:T(8,128)} %get-tuple-element.24.refs_3_), channel_id=1, source_target_pairs={{0,2},{2,4},{4,6},{6,0},{1,3},{3,5},{5,7},{7,1},{8,10},{10,12},{12... | collective-permute-start | bytes 786440 | tf_op jit(solution)/shard_map/ppermute | solution.py:431
  5.7 10.7 %collective-permute-start.1 = (f32[64,1024]{1,0:T(8,128)}, f32[64,1024]{1,0:T(8,128)S(1)}, u32[]{:S(2)}, u32[]{:S(2)}) collective-permute-start(f32[64,1024]{1,0:T(8,128)} %get-tuple-element.25.refs_4_), channel_id=1, source_target_pairs={{0,1},{1,0},{2,3},{3,2},{4,5},{5,4},{6,7},{7,6},{8,9},{9,8},{10,11... | collective-permute-start | bytes 786440 | tf_op jit(solution)/shard_map/ppermute | solution.py:431
  5.9 10.5 %collective-permute-start.4 = (f32[64,1024]{1,0:T(8,128)}, f32[64,1024]{1,0:T(8,128)S(1)}, u32[]{:S(2)}, u32[]{:S(2)}) collective-permute-start(f32[64,1024]{1,0:T(8,128)} %get-tuple-element.25.refs_4_), channel_id=1, source_target_pairs={{0,6},{2,0},{4,2},{6,4},{1,7},{3,1},{5,3},{7,5},{8,14},{10,8},{12,... | collective-permute-start | bytes 786440 | tf_op jit(solution)/shard_map/ppermute | solution.py:431
  8.7 11.8 %collective-permute-start.6 = (f32[64,1024]{1,0:T(8,128)}, f32[64,1024]{1,0:T(8,128)S(1)}, u32[]{:S(2)}, u32[]{:S(2)}) collective-permute-start(f32[64,1024]{1,0:T(8,128)} %get-tuple-element.25.refs_4_), channel_id=1, source_target_pairs={{0,2},{2,4},{4,6},{6,0},{1,3},{3,5},{5,7},{7,1},{8,10},{10,12},{12... | collective-permute-start | bytes 786440 | tf_op jit(solution)/shard_map/ppermute | solution.py:431
  8.8 13.3 %collective-permute-start.8 = (f32[64,1024]{1,0:T(8,128)}, f32[64,1024]{1,0:T(8,128)S(1)}, u32[]{:S(2)}, u32[]{:S(2)}) collective-permute-start(f32[64,1024]{1,0:T(8,128)} %get-tuple-element.24.refs_3_), channel_id=1, source_target_pairs={{0,6},{2,0},{4,2},{6,4},{1,7},{3,1},{5,3},{7,5},{8,14},{10,8},{12,... | collective-permute-start | bytes 786440 | tf_op jit(solution)/shard_map/ppermute | solution.py:431
  14.9 7.2 %collective-permute-start.3 = (f32[64,1024]{1,0:T(8,128)S(1)}, f32[64,1024]{1,0:T(8,128)S(1)}, u32[]{:S(2)}, u32[]{:S(2)}) collective-permute-start(f32[64,1024]{1,0:T(8,128)S(1)} %collective-permute-done.2.refs_7_), channel_id=1, source_target_pairs={{0,1},{1,0},{2,3},{3,2},{4,5},{5,4},{6,7},{7,6},{8,9},{9,8},{10,11... | collective-permute-start | bytes 786440 | tf_op jit(solution)/shard_map/ppermute | solution.py:431
  16.4 9.7 %collective-permute-start.10 = (f32[64,1024]{1,0:T(8,128)S(1)}, f32[64,1024]{1,0:T(8,128)S(1)}, u32[]{:S(2)}, u32[]{:S(2)}) collective-permute-start(f32[64,1024]{1,0:T(8,128)S(1)} %collective-permute-done.2.refs_7_), channel_id=1, source_target_pairs={{0,2},{2,4},{4,6},{6,0},{1,3},{3,5},{5,7},{7,1},{8,10},{10,12},{12... | collective-permute-start | bytes 786440 | tf_op jit(solution)/shard_map/ppermute | solution.py:431
  16.4 10.7 %collective-permute-start.12 = (f32[64,1024]{1,0:T(8,128)S(1)}, f32[64,1024]{1,0:T(8,128)S(1)}, u32[]{:S(2)}, u32[]{:S(2)}) collective-permute-start(f32[64,1024]{1,0:T(8,128)S(1)} %collective-permute-done.4.refs_9_), channel_id=1, source_target_pairs={{0,6},{2,0},{4,2},{6,4},{1,7},{3,1},{5,3},{7,5},{8,14},{10,8},{12,... | collective-permute-start | bytes 786440 | tf_op jit(solution)/shard_map/ppermute | solution.py:431
  20.5 13.8 %collective-permute-start.5 = (f32[64,1024]{1,0:T(8,128)S(1)}, f32[64,1024]{1,0:T(8,128)S(1)}, u32[]{:S(2)}, u32[]{:S(2)}) collective-permute-start(f32[64,1024]{1,0:T(8,128)S(1)} %collective-permute-done.4.refs_9_), channel_id=1, source_target_pairs={{0,1},{1,0},{2,3},{3,2},{4,5},{5,4},{6,7},{7,6},{8,9},{9,8},{10,11... | collective-permute-start | bytes 786440 | tf_op jit(solution)/shard_map/ppermute | solution.py:431
  22.0 12.3 %collective-permute-start.7 = (f32[64,1024]{1,0:T(8,128)S(1)}, f32[64,1024]{1,0:T(8,128)S(1)}, u32[]{:S(2)}, u32[]{:S(2)}) collective-permute-start(f32[64,1024]{1,0:T(8,128)S(1)} %collective-permute-done.6.refs_11_), channel_id=1, source_target_pairs={{0,1},{1,0},{2,3},{3,2},{4,5},{5,4},{6,7},{7,6},{8,9},{9,8},{10,11... | collective-permute-start | bytes 786440 | tf_op jit(solution)/shard_map/ppermute | solution.py:431
  22.1 12.2 %collective-permute-start.9 = (f32[64,1024]{1,0:T(8,128)S(1)}, f32[64,1024]{1,0:T(8,128)}, u32[]{:S(2)}, u32[]{:S(2)}) collective-permute-start(f32[64,1024]{1,0:T(8,128)S(1)} %collective-permute-done.8.refs_13_), channel_id=1, source_target_pairs={{0,1},{1,0},{2,3},{3,2},{4,5},{5,4},{6,7},{7,6},{8,9},{9,8},{10,11... | collective-permute-start | bytes 786440 | tf_op jit(solution)/shard_map/ppermute | solution.py:431
  26.1 8.2 %collective-permute-start.11 = (f32[64,1024]{1,0:T(8,128)S(1)}, f32[64,1024]{1,0:T(8,128)}, u32[]{:S(2)}, u32[]{:S(2)}) collective-permute-start(f32[64,1024]{1,0:T(8,128)S(1)} %collective-permute-done.10.refs_15_), channel_id=1, source_target_pairs={{0,1},{1,0},{2,3},{3,2},{4,5},{5,4},{6,7},{7,6},{8,9},{9,8},{10,11... | collective-permute-start | bytes 786440 | tf_op jit(solution)/shard_map/ppermute | solution.py:431
  27.1 7.2 %collective-permute-start.13 = (f32[64,1024]{1,0:T(8,128)S(1)}, f32[64,1024]{1,0:T(8,128)}, u32[]{:S(2)}, u32[]{:S(2)}) collective-permute-start(f32[64,1024]{1,0:T(8,128)S(1)} %collective-permute-done.12.refs_17_), channel_id=1, source_target_pairs={{0,1},{1,0},{2,3},{3,2},{4,5},{5,4},{6,7},{7,6},{8,9},{9,8},{10,11... | collective-permute-start | bytes 786440 | tf_op jit(solution)/shard_map/ppermute | solution.py:431
  29.0 31.2 %all-to-all-start = ((f32[8,128,128]{2,1,0:T(8,128)}), f32[8,128,128]{2,1,0:T(8,128)S(1)}, u32[]{:S(2)}, u32[]{:S(2)}) async-start(f32[8,128,128]{2,1,0:T(8,128)} %shard_map.80), calls=%async_computation | async-start | bytes 1048576 | tf_op jit(solution)/shard_map/all_to_all | solution.py:443
  42.0 7.2 %collective-permute-start.15 = (f32[200,128]{1,0:T(8,128)}, f32[200,128]{1,0:T(8,128)S(1)}, u32[]{:S(2)}, u32[]{:S(2)}) collective-permute-start(f32[200,128]{1,0:T(8,128)} %get-tuple-element.31), channel_id=1, source_target_pairs={{0,16},{8,24},{16,32},{24,40},{32,48},{40,56},{1,17},{9,25},{17,33... | collective-permute-start | bytes 307208 | tf_op jit(solution)/shard_map/ppermute | solution.py:431
  50.1 18.3 %collective-permute-start.16 = (f32[200,128]{1,0:T(8,128)S(1)}, f32[200,128]{1,0:T(8,128)S(1)}, u32[]{:S(2)}, u32[]{:S(2)}) collective-permute-start(f32[200,128]{1,0:T(8,128)S(1)} %add_add_fusion.2), channel_id=1, source_target_pairs={{0,24},{8,32},{16,40},{24,48},{32,56},{1,25},{9,33},{17,41},{25,49... | collective-permute-start | bytes 307208 | tf_op jit(solution)/shard_map/ppermute | solution.py:431
  58.7 9.8 %collective-permute-start.17 = (f32[200,128]{1,0:T(8,128)S(1)}, f32[200,128]{1,0:T(8,128)S(1)}, u32[]{:S(2)}, u32[]{:S(2)}) collective-permute-start(f32[200,128]{1,0:T(8,128)S(1)} %add_add_fusion.2), channel_id=1, source_target_pairs={{0,48},{8,56},{1,49},{9,57},{2,50},{10,58},{3,51},{11,59},{4,52},{... | collective-permute-start | bytes 307208 | tf_op jit(solution)/shard_map/ppermute | solution.py:431
  75.6 7.3 %collective-permute-start.18 = (f32[200,128]{1,0:T(8,128)}, f32[200,128]{1,0:T(8,128)S(1)}, u32[]{:S(2)}, u32[]{:S(2)}) collective-permute-start(f32[200,128]{1,0:T(8,128)} %get-tuple-element.36), channel_id=1, source_target_pairs={{8,0},{16,8},{24,16},{32,24},{40,32},{48,40},{56,48},{9,1},{17,9},... | collective-permute-start | bytes 307208 | tf_op jit(solution)/shard_map/ppermute | solution.py:431
  76.9 12.2 %collective-permute-start.19 = (f32[200,128]{1,0:T(8,128)}, f32[200,128]{1,0:T(8,128)S(1)}, u32[]{:S(2)}, u32[]{:S(2)}) collective-permute-start(f32[200,128]{1,0:T(8,128)} %get-tuple-element.36), channel_id=1, source_target_pairs={{16,0},{24,8},{32,16},{40,24},{48,32},{56,40},{17,1},{25,9},{33,17... | collective-permute-start | bytes 307208 | tf_op jit(solution)/shard_map/ppermute | solution.py:431
  90.0 9.6 %collective-permute-start.20 = (f32[200,128]{1,0:T(8,128)S(1)}, f32[200,128]{1,0:T(8,128)S(1)}, u32[]{:S(2)}, u32[]{:S(2)}) collective-permute-start(f32[200,128]{1,0:T(8,128)S(1)} %add_add_fusion.1), channel_id=1, source_target_pairs={{24,0},{32,8},{40,16},{48,24},{56,32},{25,1},{33,9},{41,17},{49,25... | collective-permute-start | bytes 307208 | tf_op jit(solution)/shard_map/ppermute | solution.py:431
  91.3 8.3 %collective-permute-start.21 = (f32[200,128]{1,0:T(8,128)S(1)}, f32[200,128]{1,0:T(8,128)S(1)}, u32[]{:S(2)}, u32[]{:S(2)}) collective-permute-start(f32[200,128]{1,0:T(8,128)S(1)} %add_add_fusion.1), channel_id=1, source_target_pairs={{48,0},{56,8},{49,1},{57,9},{50,2},{58,10},{51,3},{59,11},{52,4},{... | collective-permute-start | bytes 307208 | tf_op jit(solution)/shard_map/ppermute | solution.py:431
  105.2 22.9 %collective-permute-start.22 = (f32[512,128]{1,0:T(8,128)}, f32[512,128]{1,0:T(8,128)S(1)}, u32[]{:S(2)}, u32[]{:S(2)}) collective-permute-start(f32[512,128]{1,0:T(8,128)} %get-tuple-element.38), channel_id=1, source_target_pairs={{0,2},{2,4},{4,6},{6,0},{1,3},{3,5},{5,7},{7,1},{8,10},{10,12},{12... | collective-permute-start | bytes 786440 | tf_op jit(solution)/shard_map/ppermute | solution.py:431
  105.3 22.9 %collective-permute-start.23 = (f32[512,128]{1,0:T(8,128)}, f32[512,128]{1,0:T(8,128)S(1)}, u32[]{:S(2)}, u32[]{:S(2)}) collective-permute-start(f32[512,128]{1,0:T(8,128)} %get-tuple-element.39), channel_id=1, source_target_pairs={{0,4},{2,6},{4,0},{6,2},{1,5},{3,7},{5,1},{7,3},{8,12},{10,14},{12... | collective-permute-start | bytes 786440 | tf_op jit(solution)/shard_map/ppermute | solution.py:431
  107.4 21.2 %collective-permute-start.24 = (f32[512,128]{1,0:T(8,128)}, f32[512,128]{1,0:T(8,128)S(1)}, u32[]{:S(2)}, u32[]{:S(2)}) collective-permute-start(f32[512,128]{1,0:T(8,128)} %get-tuple-element.40), channel_id=1, source_target_pairs={{0,6},{2,0},{4,2},{6,4},{1,7},{3,1},{5,3},{7,5},{8,14},{10,8},{12,... | collective-permute-start | bytes 786440 | tf_op jit(solution)/shard_map/ppermute | solution.py:431
  108.7 11.6 %collective-permute-start.31 = (f32[256,128]{1,0:T(8,128)}, f32[256,128]{1,0:T(8,128)S(1)}, u32[]{:S(2)}, u32[]{:S(2)}) collective-permute-start(f32[256,128]{1,0:T(8,128)} %get-tuple-element.45), channel_id=1, source_target_pairs={{0,192},{64,0},{128,64},{192,128},{1,193},{65,1},{129,65},{193,129... | collective-permute-start | bytes 393224 | tf_op jit(solution)/shard_map/ppermute | solution.py:431
  111.1 20.2 %all-to-all-start.1 = ((f32[8,128,128]{2,1,0:T(8,128)}), f32[8,128,128]{2,1,0:T(8,128)S(1)}, u32[]{:S(2)}, u32[]{:S(2)}) async-start(f32[8,128,128]{2,1,0:T(8,128)} %get-tuple-element.41), calls=%async_computation.1 | async-start | bytes 1048576 | tf_op jit(solution)/shard_map/all_to_all | solution.py:443
  120.3 9.4 %collective-permute-start.29 = (f32[256,128]{1,0:T(8,128)}, f32[256,128]{1,0:T(8,128)S(1)}, u32[]{:S(2)}, u32[]{:S(2)}) collective-permute-start(f32[256,128]{1,0:T(8,128)} %get-tuple-element.43), channel_id=1, source_target_pairs={{0,64},{64,128},{128,192},{192,0},{1,65},{65,129},{129,193},{193,1... | collective-permute-start | bytes 393224 | tf_op jit(solution)/shard_map/ppermute | solution.py:431
  126.4 27.1 %collective-permute-start.25 = (f32[512,128]{1,0:T(8,128)}, f32[512,128]{1,0:T(8,128)S(1)}, u32[]{:S(2)}, u32[]{:S(2)}) collective-permute-start(f32[512,128]{1,0:T(8,128)} %get-tuple-element.37.refs_1_), channel_id=1, source_target_pairs={{0,1},{1,0},{2,3},{3,2},{4,5},{5,4},{6,7},{7,6},{8,9},{9,8},{10,11... | collective-permute-start | bytes 786440 | tf_op jit(solution)/shard_map/ppermute | solution.py:431
  128.1 25.5 %collective-permute-start.26 = (f32[512,128]{1,0:T(8,128)S(1)}, f32[512,128]{1,0:T(8,128)S(1)}, u32[]{:S(2)}, u32[]{:S(2)}) collective-permute-start(f32[512,128]{1,0:T(8,128)S(1)} %collective-permute-done.22.refs_2_), channel_id=1, source_target_pairs={{0,1},{1,0},{2,3},{3,2},{4,5},{5,4},{6,7},{7,6},{8,9},{9,8},{10,11... | collective-permute-start | bytes 786440 | tf_op jit(solution)/shard_map/ppermute | solution.py:431
  128.2 25.4 %collective-permute-start.27 = (f32[512,128]{1,0:T(8,128)S(1)}, f32[512,128]{1,0:T(8,128)S(1)}, u32[]{:S(2)}, u32[]{:S(2)}) collective-permute-start(f32[512,128]{1,0:T(8,128)S(1)} %collective-permute-done.23.refs_3_), channel_id=1, source_target_pairs={{0,1},{1,0},{2,3},{3,2},{4,5},{5,4},{6,7},{7,6},{8,9},{9,8},{10,11... | collective-permute-start | bytes 786440 | tf_op jit(solution)/shard_map/ppermute | solution.py:431
  128.6 25.0 %collective-permute-start.28 = (f32[512,128]{1,0:T(8,128)S(1)}, f32[512,128]{1,0:T(8,128)S(1)}, u32[]{:S(2)}, u32[]{:S(2)}) collective-permute-start(f32[512,128]{1,0:T(8,128)S(1)} %collective-permute-done.24.refs_4_), channel_id=1, source_target_pairs={{0,1},{1,0},{2,3},{3,2},{4,5},{5,4},{6,7},{7,6},{8,9},{9,8},{10,11... | collective-permute-start | bytes 786440 | tf_op jit(solution)/shard_map/ppermute | solution.py:431
  131.3 21.6 %all-to-all-start.2 = ((f32[64,4,128]{2,1,0:T(4,128)}), f32[64,4,128]{2,1,0:T(4,128)S(1)}, u32[]{:S(2)}, u32[]{:S(2)}) async-start(f32[64,4,128]{2,1,0:T(4,128)} %bitcast.15), calls=%async_computation.2 | async-start | bytes 262144 | tf_op jit(solution)/shard_map/all_to_all | solution.py:443
  (31 other events, 317.1 us)

commit v8 on v7

--- a/solution.py
+++ b/solution.py
@@ -230,14 +230,6 @@
 
 def chunk(j):
     return slice(j * DK, (j + 1) * DK)
-
-
-def prepare_body(tables, need, made, put):
-    x, (low, high) = need(0), made
-    rows = low.shape[0]
-    low[...] = x[:rows].astype(F32)
-    put(0)
-    high[...] = x[rows:].astype(F32)
 
 
 def upstream_body(tables, need, made, put):
@@ -477,8 +469,7 @@
     state = shaped(STATE, DK)
     unit = 2 * plane * DK * DK
 
-    half = shaped(tokens // 2, width)
-    low, high = call(prepare_body, [half, half], [mine], 0)
+    low, high = mine[: tokens // 2].astype(F32), mine[tokens // 2 :].astype(F32)
     pieces, where = gather_plane(low, high)
     slots = tuple((slot, start) for _, slot, start in pieces)
     pieces = [p for p, _, _ in pieces]

time: 161 us -> 160 us (level)
  Pallas kernels: 42.3 us -> 40.6 us
    pallas_call x10 -> x9, Pallas kernels: 42.3 us -> 40.6 us  [call(): pl.pallas_call(kernel, out_shape=tuple(outs), in_specs=[pl.BlockSpec(memo...]
where the time goes in v8:
time: 160 us; the launch traced here: 159 us
  starting transfers between devices  71.3 us (45%)
  Pallas kernels  40.6 us (25%)
  waiting for transfers between devices  35.5 us (22%)
  other arithmetic  5.82 us (4%)
  local copies, waits for them, and re-layouts  4.39 us (3%)
    ppermute x32, starting transfers between devices, shift(): return lax.ppermute(x, axis, pairs)  47.6 us
    pallas_call x9, Pallas kernels, call(): pl.pallas_call(kernel, out_shape=tuple(outs), in_specs=[pl.BlockSpec(memo...  40.6 us
    ppermute x32, waiting for transfers between devices, shift(): return lax.ppermute(x, axis, pairs)  27.8 us
    all_to_all x3, starting transfers between devices, exchange(): return lax.all_to_all(x, axis, 0, 0)  23.7 us
    all_to_all x3, waiting for transfers between devices, exchange(): return lax.all_to_all(x, axis, 0, 0)  7.67 us
    unnamed x56, local copies, waits for them, and re-layouts  3.71 us
  transfers between devices with their start and end apart: 35, of which 9 were waited for; matrix products, arithmetic and copies ran while one was open for 3% of the time, Pallas kernels for 15%

profile of v8, /device:TPU:1, one launch (start us, length us, event | category | flops | bytes accessed | tf_op | source)
XLA Modules:
  0.0 158.9 jit_solution(3251954253541175371)
XLA Ops:
  1.7 3.3 %collective-permute-start = (f32[64,1024]{1,0:T(8,128)S(1)}, f32[64,1024]{1,0:T(8,128)S(1)}, u32[]{:S(2)}, u32[]{:S(2)}) collective-permute-start(f32[64,1024]{1,0:T(8,128)S(1)} %get-tuple-element.43.refs_3_), channel_id=1, source_target_pairs={{0,1},{1,0},{2,3},{3,2},{4,5},{5,4},{6,7},{7,6},{8,9},{9,8},{10,11... | collective-permute-start | bytes 786440 | tf_op jit(solution)/shard_map/ppermute | solution.py:423
  5.1 2.9 %collective-permute-start.4 = (f32[64,1024]{1,0:T(8,128)S(1)}, f32[64,1024]{1,0:T(8,128)S(1)}, u32[]{:S(2)}, u32[]{:S(2)}) collective-permute-start(f32[64,1024]{1,0:T(8,128)S(1)} %get-tuple-element.42.refs_4_), channel_id=1, source_target_pairs={{0,6},{2,0},{4,2},{6,4},{1,7},{3,1},{5,3},{7,5},{8,14},{10,8},{12,... | collective-permute-start | bytes 786440 | tf_op jit(solution)/shard_map/ppermute | solution.py:423
  8.0 2.7 %collective-permute-start.8 = (f32[64,1024]{1,0:T(8,128)S(1)}, f32[64,1024]{1,0:T(8,128)S(1)}, u32[]{:S(2)}, u32[]{:S(2)}) collective-permute-start(f32[64,1024]{1,0:T(8,128)S(1)} %get-tuple-element.43.refs_3_), channel_id=1, source_target_pairs={{0,6},{2,0},{4,2},{6,4},{1,7},{3,1},{5,3},{7,5},{8,14},{10,8},{12,... | collective-permute-start | bytes 786440 | tf_op jit(solution)/shard_map/ppermute | solution.py:423
  10.7 3.3 %collective-permute-done.2.refs_7_ = f32[64,1024]{1,0:T(8,128)S(1)} collective-permute-done((f32[64,1024]{1,0:T(8,128)S(1)}, f32[64,1024]{1,0:T(8,128)S(1)}, u32[]{:S(2)}, u32[]{:S(2)}) %collective-permute-start.2) | collective-permute-done | bytes 262176 | tf_op jit(solution)/shard_map/ppermute | solution.py:423
  13.9 1.5 collective-permute-start.3
  15.5 2.7 %collective-permute-start.12 = (f32[64,1024]{1,0:T(8,128)S(1)}, f32[64,1024]{1,0:T(8,128)S(1)}, u32[]{:S(2)}, u32[]{:S(2)}) collective-permute-start(f32[64,1024]{1,0:T(8,128)S(1)} %collective-permute-done.4.refs_9_), channel_id=1, source_target_pairs={{0,6},{2,0},{4,2},{6,4},{1,7},{3,1},{5,3},{7,5},{8,14},{10,8},{12,... | collective-permute-start | bytes 786440 | tf_op jit(solution)/shard_map/ppermute | solution.py:423
  19.6 1.5 collective-permute-start.5
  21.6 3.6 %collective-permute-done.10.refs_15_ = f32[64,1024]{1,0:T(8,128)S(1)} collective-permute-done((f32[64,1024]{1,0:T(8,128)S(1)}, f32[64,1024]{1,0:T(8,128)S(1)}, u32[]{:S(2)}, u32[]{:S(2)}) %collective-permute-start.10) | collective-permute-done | bytes 262176 | tf_op jit(solution)/shard_map/ppermute | solution.py:423
  26.2 1.8 %shard_map.79 = f32[8,128,128]{2,1,0:T(8,128)} custom-call(bf16[128,1024]{1,0:T(8,128)(2,1)} %bitcast.27), custom_call_target="tpu_custom_call" | custom-call | bytes 786432 | tf_op jit(solution)/shard_map/pallas_call | solution.py:184
  28.0 4.6 %all-to-all-start = ((f32[8,128,128]{2,1,0:T(8,128)}), f32[8,128,128]{2,1,0:T(8,128)S(1)}, u32[]{:S(2)}, u32[]{:S(2)}) async-start(f32[8,128,128]{2,1,0:T(8,128)} %shard_map.79), calls=%async_computation | async-start | bytes 1048576 | tf_op jit(solution)/shard_map/all_to_all | solution.py:435
  33.5 5.1 %shard_map.77 = (bf16[1024,1024]{1,0:T(8,128)(2,1)}, bf16[1024,128]{1,0:T(8,128)(2,1)}, bf16[1024,128]{1,0:T(8,128)(2,1)}, f32[200,128]{1,0:T(8,128)}) custom-call(s32[9]{0:T(128)} %stack.55.refs_0_, bf16[1024,1024]{1,0:T(8,128)(2,1)} %refs_10_.1, bf16[1024,1024]{1,0:T(8,128)(2,1)} %refs_11_.1, f32[64,1024]{1,0:T(8,128)} %copy-done.3, f32[64,1024]{1,0:T(8,128)} %copy-done.2, ...), custom_call_target="tpu_custom_call" | custom-call | flops 939524096 | bytes 6918144 | tf_op jit(solution)/shard_map/pallas_call | solution.py:184
  38.5 1.9 %collective-permute-start.14 = (f32[200,128]{1,0:T(8,128)}, f32[200,128]{1,0:T(8,128)S(1)}, u32[]{:S(2)}, u32[]{:S(2)}) collective-permute-start(f32[200,128]{1,0:T(8,128)} %get-tuple-element.27), channel_id=1, source_target_pairs={{0,8},{8,16},{16,24},{24,32},{32,40},{40,48},{48,56},{1,9},{9,17},... | collective-permute-start | bytes 307208 | tf_op jit(solution)/shard_map/ppermute | solution.py:423
  40.4 4.9 %collective-permute-start.15 = (f32[200,128]{1,0:T(8,128)}, f32[200,128]{1,0:T(8,128)S(1)}, u32[]{:S(2)}, u32[]{:S(2)}) collective-permute-start(f32[200,128]{1,0:T(8,128)} %get-tuple-element.27), channel_id=1, source_target_pairs={{0,16},{8,24},{16,32},{24,40},{32,48},{40,56},{1,17},{9,25},{17,33... | collective-permute-start | bytes 307208 | tf_op jit(solution)/shard_map/ppermute | solution.py:423
  45.3 2.2 %collective-permute-done.15.refs_8_ = f32[200,128]{1,0:T(8,128)S(1)} collective-permute-done((f32[200,128]{1,0:T(8,128)}, f32[200,128]{1,0:T(8,128)S(1)}, u32[]{:S(2)}, u32[]{:S(2)}) %collective-permute-start.15) | collective-permute-done | bytes 102432 | tf_op jit(solution)/shard_map/ppermute | solution.py:423
  48.5 8.6 %collective-permute-start.16 = (f32[200,128]{1,0:T(8,128)S(1)}, f32[200,128]{1,0:T(8,128)S(1)}, u32[]{:S(2)}, u32[]{:S(2)}) collective-permute-start(f32[200,128]{1,0:T(8,128)S(1)} %add_add_fusion.2), channel_id=1, source_target_pairs={{0,24},{8,32},{16,40},{24,48},{32,56},{1,25},{9,33},{17,41},{25,49... | collective-permute-start | bytes 307208 | tf_op jit(solution)/shard_map/ppermute | solution.py:423
  59.4 3.6 %shard_map.80.refs_4_ = f32[8,128,128]{2,1,0:T(8,128)} custom-call(bf16[1024,128]{1,0:T(8,128)(2,1)} %get-tuple-element.22.refs_2_.refs_0_.refs_1_, bf16[1024,128]{1,0:T(8,128)(2,1)} %get-tuple-element.23.refs_1_.refs_2_, f32[8,128,128]{2,1,0:T(8,128)} %copy-done), custom_call_target="tpu_custom_call" | custom-call | flops 268435456 | bytes 1572864 | tf_op jit(solution)/shard_map/pallas_call | solution.py:184
  63.0 3.8 %shard_map.78 = (bf16[1024,128]{1,0:T(8,128)(2,1)}, f32[8,128,128]{2,1,0:T(8,128)}) custom-call(s32[9]{0:T(128)} %stack.55.refs_0_, bf16[1024,1024]{1,0:T(8,128)(2,1)} %refs_1_.5, bf16[1024,128]{1,0:T(8,128)(2,1)} %get-tuple-element.22.refs_2_.refs_0_.refs_1_, bf16[1024,1024]{1,0:T(8,128)(2,1)} %get-tuple-element.24.refs_3_.refs_9_), custom_call_target="tpu_custom_call" | custom-call | flops 335544320 | bytes 3145728 | tf_op jit(solution)/shard_map/pallas_call | solution.py:184
  67.6 6.4 %shard_map.81 = (f32[8,128,128]{2,1,0:T(8,128)}, f32[8,128,128]{2,1,0:T(8,128)}, f32[200,128]{1,0:T(8,128)}) custom-call(s32[9]{0:T(128)} %stack.55.refs_0_, bf16[1024,128]{1,0:T(8,128)(2,1)} %get-tuple-element.25.refs_1_.refs_0_, bf16[1024,128]{1,0:T(8,128)(2,1)} %get-tuple-element.22.refs_2_.refs_0_.refs_1_, f32[8,128,128]{2,1,0:T(8,128)} %get-tuple-element.26.refs_3_, ...), custom_call_target="tpu_custom_call" | custom-call | flops 1342177280 | bytes 3661824 | tf_op jit(solution)/shard_map/pallas_call | solution.py:184
  76.6 4.6 %collective-permute-done.18.refs_5_ = f32[200,128]{1,0:T(8,128)S(1)} collective-permute-done((f32[200,128]{1,0:T(8,128)}, f32[200,128]{1,0:T(8,128)S(1)}, u32[]{:S(2)}, u32[]{:S(2)}) %collective-permute-start.18) | collective-permute-done | bytes 102432 | tf_op jit(solution)/shard_map/ppermute | solution.py:423
  81.2 6.2 %collective-permute-done.19.refs_6_ = f32[200,128]{1,0:T(8,128)S(1)} collective-permute-done((f32[200,128]{1,0:T(8,128)}, f32[200,128]{1,0:T(8,128)S(1)}, u32[]{:S(2)}, u32[]{:S(2)}) %collective-permute-start.19) | collective-permute-done | bytes 102432 | tf_op jit(solution)/shard_map/ppermute | solution.py:423
  91.7 6.3 %shard_map.82 = (f32[8,128,128]{2,1,0:T(8,128)}, f32[8,128,128]{2,1,0:T(8,128)}, f32[8,128,128]{2,1,0:T(8,128)}) custom-call(bf16[1024,128]{1,0:T(8,128)(2,1)} %get-tuple-element.25.refs_1_.refs_0_, bf16[1024,128]{1,0:T(8,128)(2,1)} %get-tuple-element.22.refs_2_.refs_0_.refs_1_, bf16[1024,128]{1,0:T(8,128)(2,1)} %get-tuple-element.23.refs_1_.refs_2_, ...), custom_call_target="tpu_custom_call" | custom-call | flops 1006632960 | bytes 3932160 | tf_op jit(solution)/shard_map/pallas_call | solution.py:184
  98.6 4.9 %shard_map.83 = (f32[256,128]{1,0:T(8,128)}, f32[256,128]{1,0:T(8,128)}, f32[256,128]{1,0:T(8,128)}, f32[256,128]{1,0:T(8,128)}, f32[512,128]{1,0:T(8,128)}, /*i...) custom-call(s32[3]{0:T(128)} %pad_add_fusion.refs_0_, ...), custom_call_target="tpu_custom_call" | custom-call | flops 469762048 | bytes 5652480 | tf_op jit(solution)/shard_map/pallas_call | solution.py:184
  103.7 2.3 %collective-permute-start.23 = (f32[512,128]{1,0:T(8,128)}, f32[512,128]{1,0:T(8,128)S(1)}, u32[]{:S(2)}, u32[]{:S(2)}) collective-permute-start(f32[512,128]{1,0:T(8,128)} %get-tuple-element.35), channel_id=1, source_target_pairs={{0,4},{2,6},{4,0},{6,2},{1,5},{3,7},{5,1},{7,3},{8,12},{10,14},{12... | collective-permute-start | bytes 786440 | tf_op jit(solution)/shard_map/ppermute | solution.py:423
  107.0 2.5 %collective-permute-start.31 = (f32[256,128]{1,0:T(8,128)}, f32[256,128]{1,0:T(8,128)S(1)}, u32[]{:S(2)}, u32[]{:S(2)}) collective-permute-start(f32[256,128]{1,0:T(8,128)} %get-tuple-element.41), channel_id=1, source_target_pairs={{0,192},{64,0},{128,64},{192,128},{1,193},{65,1},{129,65},{193,129... | collective-permute-start | bytes 393224 | tf_op jit(solution)/shard_map/ppermute | solution.py:423
  109.5 8.6 %all-to-all-start.1 = ((f32[8,128,128]{2,1,0:T(8,128)}), f32[8,128,128]{2,1,0:T(8,128)S(1)}, u32[]{:S(2)}, u32[]{:S(2)}) async-start(f32[8,128,128]{2,1,0:T(8,128)} %get-tuple-element.37), calls=%async_computation.1 | async-start | bytes 1048576 | tf_op jit(solution)/shard_map/all_to_all | solution.py:435
  119.3 5.5 %collective-permute-done.30 = f32[256,128]{1,0:T(8,128)S(1)} collective-permute-done((f32[256,128]{1,0:T(8,128)}, f32[256,128]{1,0:T(8,128)S(1)}, u32[]{:S(2)}, u32[]{:S(2)}) %collective-permute-start.30) | collective-permute-done | bytes 131104 | tf_op jit(solution)/shard_map/ppermute | solution.py:423
  124.8 1.7 %collective-permute-start.25 = (f32[512,128]{1,0:T(8,128)}, f32[512,128]{1,0:T(8,128)S(1)}, u32[]{:S(2)}, u32[]{:S(2)}) collective-permute-start(f32[512,128]{1,0:T(8,128)} %get-tuple-element.33.refs_1_), channel_id=1, source_target_pairs={{0,1},{1,0},{2,3},{3,2},{4,5},{5,4},{6,7},{7,6},{8,9},{9,8},{10,11... | collective-permute-start | bytes 786440 | tf_op jit(solution)/shard_map/ppermute | solution.py:423
  128.1 1.6 %add_add_fusion = f32[256,128]{1,0:T(8,128)} fusion(f32[256,128]{1,0:T(8,128)S(1)} %collective-permute-done.31, f32[256,128]{1,0:T(8,128)S(1)} %collective-permute-done.30, f32[256,128]{1,0:T(8,128)} %get-tuple-element.38, f32[256,128]{1,0:T(8,128)S(1)} %collective-permute-done.29), kind=kLoop, calls=%fused_computation.2 | loop fusion | flops 98304 | bytes 655360 | tf_op jit(solution)/shard_map/add | solution.py:518
  129.7 10.5 %all-to-all-start.2 = ((f32[64,4,128]{2,1,0:T(4,128)}), f32[64,4,128]{2,1,0:T(4,128)S(1)}, u32[]{:S(2)}, u32[]{:S(2)}) async-start(f32[64,4,128]{2,1,0:T(4,128)} %bitcast.18), calls=%async_computation.2 | async-start | bytes 262144 | tf_op jit(solution)/shard_map/all_to_all | solution.py:435
  140.2 3.4 %shard_map.84.refs_9_ = f32[128,1024]{1,0:T(8,128)} custom-call(f32[8,128,128]{2,1,0:T(8,128)} %copy-done.1, bf16[1024,1024]{1,0:T(8,128)(2,1)} %refs_1_.5), custom_call_target="tpu_custom_call" | custom-call | flops 268435456 | bytes 3145728 | tf_op jit(solution)/shard_map/pallas_call | solution.py:184
  143.6 7.7 %all-to-all-done.2 = f32[64,4,128]{2,1,0:T(4,128)S(1)} async-done(((f32[64,4,128]{2,1,0:T(4,128)}), f32[64,4,128]{2,1,0:T(4,128)S(1)}, u32[]{:S(2)}, u32[]{:S(2)}) %all-to-all-start.2) | async-done | bytes 131104 | tf_op jit(solution)/shard_map/all_to_all | solution.py:435
  153.5 5.2 %shard_map.85 = bf16[128,1024]{1,0:T(8,128)(2,1)} custom-call(s32[3]{0:T(128)} %pad_add_fusion.refs_0_, f32[512,128]{1,0:T(8,128)} %get-tuple-element.33.refs_1_, f32[512,128]{1,0:T(8,128)} %copy-done.6, f32[512,128]{1,0:T(8,128)} %copy-done.7, f32[512,128]{1,0:T(8,128)} %copy-done.8, f32[512,128]{1,0:T(8,128)} %copy-done.9, f32[512,128]{1,0:T(8,128)} %copy-done.10, ...), custom_call_target="tpu_custom_call" | custom-call | flops 536870912 | bytes 7077888 | tf_op jit(solution)/shard_map/pallas_call | solution.py:184
  (110 shorter events, 22.5 us)
Async XLA Ops:
  5.0 9.0 %collective-permute-start.2 = (f32[64,1024]{1,0:T(8,128)S(1)}, f32[64,1024]{1,0:T(8,128)S(1)}, u32[]{:S(2)}, u32[]{:S(2)}) collective-permute-start(f32[64,1024]{1,0:T(8,128)S(1)} %get-tuple-element.43.refs_3_), channel_id=1, source_target_pairs={{0,2},{2,4},{4,6},{6,0},{1,3},{3,5},{5,7},{7,1},{8,10},{10,12},{12... | collective-permute-start | bytes 786440 | tf_op jit(solution)/shard_map/ppermute | solution.py:423
  5.0 10.5 %collective-permute-start.1 = (f32[64,1024]{1,0:T(8,128)S(1)}, f32[64,1024]{1,0:T(8,128)S(1)}, u32[]{:S(2)}, u32[]{:S(2)}) collective-permute-start(f32[64,1024]{1,0:T(8,128)S(1)} %get-tuple-element.42.refs_4_), channel_id=1, source_target_pairs={{0,1},{1,0},{2,3},{3,2},{4,5},{5,4},{6,7},{7,6},{8,9},{9,8},{10,11... | collective-permute-start | bytes 786440 | tf_op jit(solution)/shard_map/ppermute | solution.py:423
  5.1 10.3 %collective-permute-start.4 = (f32[64,1024]{1,0:T(8,128)S(1)}, f32[64,1024]{1,0:T(8,128)S(1)}, u32[]{:S(2)}, u32[]{:S(2)}) collective-permute-start(f32[64,1024]{1,0:T(8,128)S(1)} %get-tuple-element.42.refs_4_), channel_id=1, source_target_pairs={{0,6},{2,0},{4,2},{6,4},{1,7},{3,1},{5,3},{7,5},{8,14},{10,8},{12,... | collective-permute-start | bytes 786440 | tf_op jit(solution)/shard_map/ppermute | solution.py:423
  8.0 11.6 %collective-permute-start.6 = (f32[64,1024]{1,0:T(8,128)S(1)}, f32[64,1024]{1,0:T(8,128)S(1)}, u32[]{:S(2)}, u32[]{:S(2)}) collective-permute-start(f32[64,1024]{1,0:T(8,128)S(1)} %get-tuple-element.42.refs_4_), channel_id=1, source_target_pairs={{0,2},{2,4},{4,6},{6,0},{1,3},{3,5},{5,7},{7,1},{8,10},{10,12},{12... | collective-permute-start | bytes 786440 | tf_op jit(solution)/shard_map/ppermute | solution.py:423
  8.0 13.0 %collective-permute-start.8 = (f32[64,1024]{1,0:T(8,128)S(1)}, f32[64,1024]{1,0:T(8,128)S(1)}, u32[]{:S(2)}, u32[]{:S(2)}) collective-permute-start(f32[64,1024]{1,0:T(8,128)S(1)} %get-tuple-element.43.refs_3_), channel_id=1, source_target_pairs={{0,6},{2,0},{4,2},{6,4},{1,7},{3,1},{5,3},{7,5},{8,14},{10,8},{12,... | collective-permute-start | bytes 786440 | tf_op jit(solution)/shard_map/ppermute | solution.py:423
  13.9 7.2 %collective-permute-start.3 = (f32[64,1024]{1,0:T(8,128)S(1)}, f32[64,1024]{1,0:T(8,128)S(1)}, u32[]{:S(2)}, u32[]{:S(2)}) collective-permute-start(f32[64,1024]{1,0:T(8,128)S(1)} %collective-permute-done.2.refs_7_), channel_id=1, source_target_pairs={{0,1},{1,0},{2,3},{3,2},{4,5},{5,4},{6,7},{7,6},{8,9},{9,8},{10,11... | collective-permute-start | bytes 786440 | tf_op jit(solution)/shard_map/ppermute | solution.py:423
  15.4 9.7 %collective-permute-start.10 = (f32[64,1024]{1,0:T(8,128)S(1)}, f32[64,1024]{1,0:T(8,128)S(1)}, u32[]{:S(2)}, u32[]{:S(2)}) collective-permute-start(f32[64,1024]{1,0:T(8,128)S(1)} %collective-permute-done.2.refs_7_), channel_id=1, source_target_pairs={{0,2},{2,4},{4,6},{6,0},{1,3},{3,5},{5,7},{7,1},{8,10},{10,12},{12... | collective-permute-start | bytes 786440 | tf_op jit(solution)/shard_map/ppermute | solution.py:423
  15.5 10.7 %collective-permute-start.12 = (f32[64,1024]{1,0:T(8,128)S(1)}, f32[64,1024]{1,0:T(8,128)S(1)}, u32[]{:S(2)}, u32[]{:S(2)}) collective-permute-start(f32[64,1024]{1,0:T(8,128)S(1)} %collective-permute-done.4.refs_9_), channel_id=1, source_target_pairs={{0,6},{2,0},{4,2},{6,4},{1,7},{3,1},{5,3},{7,5},{8,14},{10,8},{12,... | collective-permute-start | bytes 786440 | tf_op jit(solution)/shard_map/ppermute | solution.py:423
  19.6 13.8 %collective-permute-start.5 = (f32[64,1024]{1,0:T(8,128)S(1)}, f32[64,1024]{1,0:T(8,128)}, u32[]{:S(2)}, u32[]{:S(2)}) collective-permute-start(f32[64,1024]{1,0:T(8,128)S(1)} %collective-permute-done.4.refs_9_), channel_id=1, source_target_pairs={{0,1},{1,0},{2,3},{3,2},{4,5},{5,4},{6,7},{7,6},{8,9},{9,8},{10,11... | collective-permute-start | bytes 786440 | tf_op jit(solution)/shard_map/ppermute | solution.py:423
  21.1 12.3 %collective-permute-start.7 = (f32[64,1024]{1,0:T(8,128)S(1)}, f32[64,1024]{1,0:T(8,128)}, u32[]{:S(2)}, u32[]{:S(2)}) collective-permute-start(f32[64,1024]{1,0:T(8,128)S(1)} %collective-permute-done.6.refs_11_), channel_id=1, source_target_pairs={{0,1},{1,0},{2,3},{3,2},{4,5},{5,4},{6,7},{7,6},{8,9},{9,8},{10,11... | collective-permute-start | bytes 786440 | tf_op jit(solution)/shard_map/ppermute | solution.py:423
  21.2 12.2 %collective-permute-start.9 = (f32[64,1024]{1,0:T(8,128)S(1)}, f32[64,1024]{1,0:T(8,128)}, u32[]{:S(2)}, u32[]{:S(2)}) collective-permute-start(f32[64,1024]{1,0:T(8,128)S(1)} %collective-permute-done.8.refs_13_), channel_id=1, source_target_pairs={{0,1},{1,0},{2,3},{3,2},{4,5},{5,4},{6,7},{7,6},{8,9},{9,8},{10,11... | collective-permute-start | bytes 786440 | tf_op jit(solution)/shard_map/ppermute | solution.py:423
  25.2 8.2 %collective-permute-start.11 = (f32[64,1024]{1,0:T(8,128)S(1)}, f32[64,1024]{1,0:T(8,128)}, u32[]{:S(2)}, u32[]{:S(2)}) collective-permute-start(f32[64,1024]{1,0:T(8,128)S(1)} %collective-permute-done.10.refs_15_), channel_id=1, source_target_pairs={{0,1},{1,0},{2,3},{3,2},{4,5},{5,4},{6,7},{7,6},{8,9},{9,8},{10,11... | collective-permute-start | bytes 786440 | tf_op jit(solution)/shard_map/ppermute | solution.py:423
  26.1 7.2 %collective-permute-start.13 = (f32[64,1024]{1,0:T(8,128)S(1)}, f32[64,1024]{1,0:T(8,128)}, u32[]{:S(2)}, u32[]{:S(2)}) collective-permute-start(f32[64,1024]{1,0:T(8,128)S(1)} %collective-permute-done.12.refs_17_), channel_id=1, source_target_pairs={{0,1},{1,0},{2,3},{3,2},{4,5},{5,4},{6,7},{7,6},{8,9},{9,8},{10,11... | collective-permute-start | bytes 786440 | tf_op jit(solution)/shard_map/ppermute | solution.py:423
  28.0 30.6 %all-to-all-start = ((f32[8,128,128]{2,1,0:T(8,128)}), f32[8,128,128]{2,1,0:T(8,128)S(1)}, u32[]{:S(2)}, u32[]{:S(2)}) async-start(f32[8,128,128]{2,1,0:T(8,128)} %shard_map.79), calls=%async_computation | async-start | bytes 1048576 | tf_op jit(solution)/shard_map/all_to_all | solution.py:435
  40.4 7.2 %collective-permute-start.15 = (f32[200,128]{1,0:T(8,128)}, f32[200,128]{1,0:T(8,128)S(1)}, u32[]{:S(2)}, u32[]{:S(2)}) collective-permute-start(f32[200,128]{1,0:T(8,128)} %get-tuple-element.27), channel_id=1, source_target_pairs={{0,16},{8,24},{16,32},{24,40},{32,48},{40,56},{1,17},{9,25},{17,33... | collective-permute-start | bytes 307208 | tf_op jit(solution)/shard_map/ppermute | solution.py:423
  48.5 18.3 %collective-permute-start.16 = (f32[200,128]{1,0:T(8,128)S(1)}, f32[200,128]{1,0:T(8,128)S(1)}, u32[]{:S(2)}, u32[]{:S(2)}) collective-permute-start(f32[200,128]{1,0:T(8,128)S(1)} %add_add_fusion.2), channel_id=1, source_target_pairs={{0,24},{8,32},{16,40},{24,48},{32,56},{1,25},{9,33},{17,41},{25,49... | collective-permute-start | bytes 307208 | tf_op jit(solution)/shard_map/ppermute | solution.py:423
  57.1 9.8 %collective-permute-start.17 = (f32[200,128]{1,0:T(8,128)S(1)}, f32[200,128]{1,0:T(8,128)S(1)}, u32[]{:S(2)}, u32[]{:S(2)}) collective-permute-start(f32[200,128]{1,0:T(8,128)S(1)} %add_add_fusion.2), channel_id=1, source_target_pairs={{0,48},{8,56},{1,49},{9,57},{2,50},{10,58},{3,51},{11,59},{4,52},{... | collective-permute-start | bytes 307208 | tf_op jit(solution)/shard_map/ppermute | solution.py:423
  74.0 7.2 %collective-permute-start.18 = (f32[200,128]{1,0:T(8,128)}, f32[200,128]{1,0:T(8,128)S(1)}, u32[]{:S(2)}, u32[]{:S(2)}) collective-permute-start(f32[200,128]{1,0:T(8,128)} %get-tuple-element.32), channel_id=1, source_target_pairs={{8,0},{16,8},{24,16},{32,24},{40,32},{48,40},{56,48},{9,1},{17,9},... | collective-permute-start | bytes 307208 | tf_op jit(solution)/shard_map/ppermute | solution.py:423
  75.3 12.1 %collective-permute-start.19 = (f32[200,128]{1,0:T(8,128)}, f32[200,128]{1,0:T(8,128)S(1)}, u32[]{:S(2)}, u32[]{:S(2)}) collective-permute-start(f32[200,128]{1,0:T(8,128)} %get-tuple-element.32), channel_id=1, source_target_pairs={{16,0},{24,8},{32,16},{40,24},{48,32},{56,40},{17,1},{25,9},{33,17... | collective-permute-start | bytes 307208 | tf_op jit(solution)/shard_map/ppermute | solution.py:423
  88.4 9.6 %collective-permute-start.20 = (f32[200,128]{1,0:T(8,128)S(1)}, f32[200,128]{1,0:T(8,128)S(1)}, u32[]{:S(2)}, u32[]{:S(2)}) collective-permute-start(f32[200,128]{1,0:T(8,128)S(1)} %add_add_fusion.1), channel_id=1, source_target_pairs={{24,0},{32,8},{40,16},{48,24},{56,32},{25,1},{33,9},{41,17},{49,25... | collective-permute-start | bytes 307208 | tf_op jit(solution)/shard_map/ppermute | solution.py:423
  89.7 8.3 %collective-permute-start.21 = (f32[200,128]{1,0:T(8,128)S(1)}, f32[200,128]{1,0:T(8,128)S(1)}, u32[]{:S(2)}, u32[]{:S(2)}) collective-permute-start(f32[200,128]{1,0:T(8,128)S(1)} %add_add_fusion.1), channel_id=1, source_target_pairs={{48,0},{56,8},{49,1},{57,9},{50,2},{58,10},{51,3},{59,11},{52,4},{... | collective-permute-start | bytes 307208 | tf_op jit(solution)/shard_map/ppermute | solution.py:423
  103.6 22.9 %collective-permute-start.22 = (f32[512,128]{1,0:T(8,128)}, f32[512,128]{1,0:T(8,128)S(1)}, u32[]{:S(2)}, u32[]{:S(2)}) collective-permute-start(f32[512,128]{1,0:T(8,128)} %get-tuple-element.34), channel_id=1, source_target_pairs={{0,2},{2,4},{4,6},{6,0},{1,3},{3,5},{5,7},{7,1},{8,10},{10,12},{12... | collective-permute-start | bytes 786440 | tf_op jit(solution)/shard_map/ppermute | solution.py:423
  103.7 22.9 %collective-permute-start.23 = (f32[512,128]{1,0:T(8,128)}, f32[512,128]{1,0:T(8,128)S(1)}, u32[]{:S(2)}, u32[]{:S(2)}) collective-permute-start(f32[512,128]{1,0:T(8,128)} %get-tuple-element.35), channel_id=1, source_target_pairs={{0,4},{2,6},{4,0},{6,2},{1,5},{3,7},{5,1},{7,3},{8,12},{10,14},{12... | collective-permute-start | bytes 786440 | tf_op jit(solution)/shard_map/ppermute | solution.py:423
  105.9 21.1 %collective-permute-start.24 = (f32[512,128]{1,0:T(8,128)}, f32[512,128]{1,0:T(8,128)S(1)}, u32[]{:S(2)}, u32[]{:S(2)}) collective-permute-start(f32[512,128]{1,0:T(8,128)} %get-tuple-element.36), channel_id=1, source_target_pairs={{0,6},{2,0},{4,2},{6,4},{1,7},{3,1},{5,3},{7,5},{8,14},{10,8},{12,... | collective-permute-start | bytes 786440 | tf_op jit(solution)/shard_map/ppermute | solution.py:423
  107.0 11.6 %collective-permute-start.31 = (f32[256,128]{1,0:T(8,128)}, f32[256,128]{1,0:T(8,128)S(1)}, u32[]{:S(2)}, u32[]{:S(2)}) collective-permute-start(f32[256,128]{1,0:T(8,128)} %get-tuple-element.41), channel_id=1, source_target_pairs={{0,192},{64,0},{128,64},{192,128},{1,193},{65,1},{129,65},{193,129... | collective-permute-start | bytes 393224 | tf_op jit(solution)/shard_map/ppermute | solution.py:423
  109.5 20.2 %all-to-all-start.1 = ((f32[8,128,128]{2,1,0:T(8,128)}), f32[8,128,128]{2,1,0:T(8,128)S(1)}, u32[]{:S(2)}, u32[]{:S(2)}) async-start(f32[8,128,128]{2,1,0:T(8,128)} %get-tuple-element.37), calls=%async_computation.1 | async-start | bytes 1048576 | tf_op jit(solution)/shard_map/all_to_all | solution.py:435
  118.7 9.4 %collective-permute-start.29 = (f32[256,128]{1,0:T(8,128)}, f32[256,128]{1,0:T(8,128)S(1)}, u32[]{:S(2)}, u32[]{:S(2)}) collective-permute-start(f32[256,128]{1,0:T(8,128)} %get-tuple-element.39), channel_id=1, source_target_pairs={{0,64},{64,128},{128,192},{192,0},{1,65},{65,129},{129,193},{193,1... | collective-permute-start | bytes 393224 | tf_op jit(solution)/shard_map/ppermute | solution.py:423
  124.8 27.2 %collective-permute-start.25 = (f32[512,128]{1,0:T(8,128)}, f32[512,128]{1,0:T(8,128)S(1)}, u32[]{:S(2)}, u32[]{:S(2)}) collective-permute-start(f32[512,128]{1,0:T(8,128)} %get-tuple-element.33.refs_1_), channel_id=1, source_target_pairs={{0,1},{1,0},{2,3},{3,2},{4,5},{5,4},{6,7},{7,6},{8,9},{9,8},{10,11... | collective-permute-start | bytes 786440 | tf_op jit(solution)/shard_map/ppermute | solution.py:423
  126.5 25.5 %collective-permute-start.26 = (f32[512,128]{1,0:T(8,128)S(1)}, f32[512,128]{1,0:T(8,128)S(1)}, u32[]{:S(2)}, u32[]{:S(2)}) collective-permute-start(f32[512,128]{1,0:T(8,128)S(1)} %collective-permute-done.22.refs_2_), channel_id=1, source_target_pairs={{0,1},{1,0},{2,3},{3,2},{4,5},{5,4},{6,7},{7,6},{8,9},{9,8},{10,11... | collective-permute-start | bytes 786440 | tf_op jit(solution)/shard_map/ppermute | solution.py:423
  126.6 25.4 %collective-permute-start.27 = (f32[512,128]{1,0:T(8,128)S(1)}, f32[512,128]{1,0:T(8,128)S(1)}, u32[]{:S(2)}, u32[]{:S(2)}) collective-permute-start(f32[512,128]{1,0:T(8,128)S(1)} %collective-permute-done.23.refs_3_), channel_id=1, source_target_pairs={{0,1},{1,0},{2,3},{3,2},{4,5},{5,4},{6,7},{7,6},{8,9},{9,8},{10,11... | collective-permute-start | bytes 786440 | tf_op jit(solution)/shard_map/ppermute | solution.py:423
  127.0 25.0 %collective-permute-start.28 = (f32[512,128]{1,0:T(8,128)S(1)}, f32[512,128]{1,0:T(8,128)S(1)}, u32[]{:S(2)}, u32[]{:S(2)}) collective-permute-start(f32[512,128]{1,0:T(8,128)S(1)} %collective-permute-done.24.refs_4_), channel_id=1, source_target_pairs={{0,1},{1,0},{2,3},{3,2},{4,5},{5,4},{6,7},{7,6},{8,9},{9,8},{10,11... | collective-permute-start | bytes 786440 | tf_op jit(solution)/shard_map/ppermute | solution.py:423
  129.7 21.6 %all-to-all-start.2 = ((f32[64,4,128]{2,1,0:T(4,128)}), f32[64,4,128]{2,1,0:T(4,128)S(1)}, u32[]{:S(2)}, u32[]{:S(2)}) async-start(f32[64,4,128]{2,1,0:T(4,128)} %bitcast.18), calls=%async_computation.2 | async-start | bytes 262144 | tf_op jit(solution)/shard_map/all_to_all | solution.py:435
  (31 other events, 378.9 us)
